TPU v7x, 128 devices: a whole 4x4x4 slice. The times are simulated.
128 devices in a mesh: lat: 8 (over x, core), lon: 16 (over y, z).
Axes of the slice: x: 4, y: 4, z: 4, core: 2. Of those that a mesh axis runs over, the one named last changes fastest.
Arguments:
- node_latent: bfloat16 [128, 512, 512], P('lat', 'lon'), may hold values from -6 to 6
- edge_latent: bfloat16 [262144, 512], P(('lat', 'lon')), may hold values from -6 to 6
- sender: int32 [262144], P(('lat', 'lon')), may hold values from -1 to 65535, as said below
- receiver: int32 [262144], P(('lat', 'lon')), may hold values from -1 to 127, as said below
- block_tile: int32 [2048], P(('lat', 'lon')), may hold values from 0 to 3, as said below
- w_first: bfloat16 [1536, 512], replicated, may hold values from -0.15625 to 0.15625
- w_second: bfloat16 [512, 512], replicated, may hold values from -0.25 to 0.25
- edge_gain: float32 [512], replicated, may hold values from 0.5 to 1.5
- w_node_first: bfloat16 [1024, 512], replicated, may hold values from -0.1875 to 0.1875
- w_node_second: bfloat16 [512, 512], replicated, may hold values from -0.25 to 0.25
- node_gain: float32 [512], replicated, may hold values from 0.5 to 1.5
Outputs:
- node_out: bfloat16 [128, 512, 512], P('lat', 'lon')
- edge_out: bfloat16 [262144, 512], P(('lat', 'lon'))
Inputs may be any that keep to these rules, and one draw needn't show every extreme that they name: `sender`: -1 on padded slots; otherwise the id of one of the eight grid neighbours of the edge's receiver node (columns wrap around, rows do not), or of a node whose row and column are both multiples of 4, anywhere on the grid. `receiver`: padded slots (-1) stand at the end of each block, at least 32 slots of a block are live, and live values never fall within a block. `block_tile`: never falls from one block of a device to the next, over the device's 16 blocks.
All inputs are finite; a program needn't handle non-finite values.
Results may differ from a plain program's by a relative error of at most 0.008.
Values may be sent and summed in bfloat16 or wider, within the bound.
No kernel may reach another device: no remote copies, remote signals or barrier semaphores. Data moves between devices by JAX's collectives and lax.ppermute only.
A program may use at most 128 MiB of HBM per device.

v0:
```python
import jax
import jax.numpy as jnp
from jax import lax
from jax.sharding import PartitionSpec as P


def laid_out(pieces, dim):
    pieces = jnp.moveaxis(pieces, 0, dim)
    shape = pieces.shape
    return pieces.reshape(*shape[:dim], shape[dim] * shape[dim + 1], *shape[dim + 2 :])


def copy_for_each(value, axis):
    copies = jnp.broadcast_to(value, (lax.axis_size(axis), *value.shape))
    return lax.all_to_all(copies, axis, split_axis=0, concat_axis=0, tiled=True)


def gather_directly(value, axis, dim):
    return laid_out(copy_for_each(value, axis), dim)


def padded(value, sides, width, wrap):
    for axis, dim in sides:
        devices, length = (lax.axis_size(axis), value.shape[dim])
        up = [(i, (i + 1) % devices) for i in range(devices if wrap else devices - 1)]
        down = [(j, i) for i, j in up]
        last = lax.slice_in_dim(value, length - width, length, axis=dim)
        leading = lax.slice_in_dim(value, 0, width, axis=dim)
        before = lax.ppermute(last, axis, up)
        after = lax.ppermute(leading, axis, down)
        value = jnp.concatenate([before, value, after], axis=dim)
    return value


def layer_norm(values, gain_vec):
    average = jnp.mean(values, -1, keepdims=True)
    centred = values - average
    spread = jnp.mean(centred * centred, -1, keepdims=True)
    return centred * lax.rsqrt(spread + 1e-05) * gain_vec


def coarse_table(coarse_own):
    banded = gather_directly(coarse_own, "lon", 0)
    return lax.all_gather(banded, "lat", axis=0, tiled=True)


def per_device(
    node_latent,
    edge_latent,
    sender,
    receiver,
    block_tile,
    w_first,
    w_second,
    edge_gain,
    w_node_first,
    w_node_second,
    node_gain,
):
    patch_rows, patch_cols, features = node_latent.shape
    lon_count = lax.axis_size("lon")
    lat_index = lax.axis_index("lat")
    lon_index = lax.axis_index("lon")
    grid_cols = patch_cols * lon_count
    blocks = block_tile.shape[0]
    block_len = edge_latent.shape[0] // blocks
    tile_nodes = 4 * patch_cols
    node_count = patch_rows * patch_cols
    own_rows = node_latent.reshape(node_count, features)
    coarse_own = node_latent[::4, ::4].reshape(-1, features)
    widened = padded(node_latent, (("lon", 1),), 1, True)
    extended = padded(widened, (("lat", 0),), 1, False)
    ext_rows = extended.reshape(-1, features)
    ext_count = ext_rows.shape[0]
    coarse_rows = coarse_table(coarse_own)
    lookup = jnp.concatenate([ext_rows, coarse_rows], axis=0)
    senders = jnp.maximum(sender, 0)
    send_row = senders // grid_cols
    send_col = senders % grid_cols
    near_row = send_row - lat_index * patch_rows + 1
    near_col = (send_col - lon_index * patch_cols + 1) % grid_cols
    is_near = (near_row >= 0) & (near_row <= patch_rows + 1) & (near_col <= patch_cols + 1)
    near_index = jnp.clip(near_row, 0, patch_rows + 1) * (patch_cols + 2) + jnp.clip(
        near_col, 0, patch_cols + 1
    )
    coarse_per = patch_rows // 4 * (patch_cols // 4)
    far_index = (
        (send_row // patch_rows * lon_count + send_col // patch_cols) * coarse_per
        + send_row % patch_rows // 4 * (patch_cols // 4)
        + send_col % patch_cols // 4
    )
    table_index = jnp.where(is_near, near_index, ext_count + far_index)
    live_slot = receiver >= 0
    tile_of = jnp.broadcast_to(block_tile[:, None], (blocks, block_len)).reshape(-1)
    local_index = jnp.where(live_slot, tile_of * tile_nodes + receiver, -1)
    recv_index = jnp.maximum(local_index, 0)
    w_edge = w_first[:features]
    w_send = w_first[features : 2 * features]
    w_recv = w_first[2 * features :]
    edge_proj = jnp.dot(edge_latent, w_edge, preferred_element_type=jnp.float32)
    send_rows = lookup[table_index]
    recv_rows = own_rows[recv_index]
    first_sum = (
        edge_proj
        + jnp.dot(send_rows, w_send, preferred_element_type=jnp.float32)
        + jnp.dot(recv_rows, w_recv, preferred_element_type=jnp.float32)
    )
    hidden = jax.nn.silu(first_sum).astype(jnp.bfloat16)
    second_sum = jnp.dot(hidden, w_second, preferred_element_type=jnp.float32)
    message = layer_norm(second_sum, edge_gain).astype(jnp.bfloat16)
    updated = jnp.where(
        live_slot[:, None], edge_latent.astype(jnp.float32) + message.astype(jnp.float32), 0.0
    ).astype(jnp.bfloat16)
    one_hot = (jnp.arange(node_count, dtype=jnp.int32)[:, None] == local_index[None, :]).astype(
        jnp.bfloat16
    )
    summed = jnp.dot(one_hot, message, preferred_element_type=jnp.float32)
    aggregate = summed.astype(jnp.bfloat16)
    node_first = jnp.dot(
        own_rows, w_node_first[:features], preferred_element_type=jnp.float32
    ) + jnp.dot(aggregate, w_node_first[features:], preferred_element_type=jnp.float32)
    node_hidden = jax.nn.silu(node_first).astype(jnp.bfloat16)
    node_second = jnp.dot(node_hidden, w_node_second, preferred_element_type=jnp.float32)
    node_out = (own_rows.astype(jnp.float32) + layer_norm(node_second, node_gain)).astype(
        jnp.bfloat16
    )
    return (node_out.reshape(patch_rows, patch_cols, features), updated)


def solution(mesh):
    return jax.shard_map(
        per_device,
        mesh=mesh,
        in_specs=(
            P("lat", "lon", None),
            P(("lat", "lon"), None),
            P(("lat", "lon")),
            P(("lat", "lon")),
            P(("lat", "lon")),
            P(),
            P(),
            P(),
            P(),
            P(),
            P(),
        ),
        out_specs=(P("lat", "lon", None), P(("lat", "lon"), None)),
        check_vma=False,
    )
```

profile of v0, /device:TPU:1, one launch (start us, length us, event | category | flops | bytes accessed | tf_op | source)
XLA Modules:
  0.0 115.4 jit_solution(2201828013964012128)
XLA Ops:
  7.2 0.0 copy-start
  7.2 0.0 copy-start.3
  7.2 0.0 all-gather.2.cloned.1.call-start
  7.2 2.1 %slice.36 = bf16[4,8,512]{2,1,0:T(8,128)(2,1)S(1)} slice(bf16[16,32,512]{2,1,0:T(8,128)(2,1)} %param.11), slice={[0:16:4], [0:32:4], [0:512:1]} | slice | bytes 65536 | tf_op jit(solution)/shard_map/slice | solution.py:70
  9.4 18.8 %all_to_all.5 = bf16[16,32,512]{2,1,0:T(8,128)(2,1)} all-to-all(bf16[16,32,512]{2,1,0:T(8,128)(2,1)S(1)} %broadcast_in_dim.42), channel_id=1, replica_groups=mesh['lat'=8,'lon'=16] {'lon'}, dimensions={0} | all-to-all | bytes 1048576 | tf_op jit(solution)/shard_map/all_to_all | solution.py:15
  28.2 0.0 all-gather.2.cloned.1.call-update
  28.2 1.0 fusion.36
  29.2 0.6 collective-permute-start
  29.8 4.3 %collective-permute-start.1 = (bf16[16,1,512]{2,1,0:T(2,128)(2,1)S(1)}, bf16[16,1,512]{2,1,0:T(2,128)(2,1)S(1)}, u32[]{:S(2)}, u32[]{:S(2)}) collective-permute-start(bf16[16,1,512]{2,1,0:T(2,128)(2,1)S(1)} %get-tuple-element.9), channel_id=1, source_target_pairs={{1,0},{2,1},{3,2},{4,3},{5,4},{6,5},{7,6},{8,7},{9,8},{10,9},{11,1... | collective-permute-start | bytes 49160 | tf_op jit(solution)/shard_map/ppermute | solution.py:30
  34.1 0.7 broadcast_multiply_fusion.2
  34.8 0.8 maximum_clamp_fusion
  35.5 2.7 %fusion.11 = f32[512,512]{1,0:T(8,128)} fusion(bf16[512,512]{1,0:T(8,128)(2,1)} %bitcast.17, bf16[1024,512]{1,0:T(8,128)(2,1)} %param.19), kind=kOutput, calls=%fused_computation.23 | convolution fusion | flops 268435456 | bytes 2097152 | tf_op jit(solution)/shard_map/dot_general | solution.py:119
  38.2 0.0 copy-done.3
  38.2 0.0 copy-start.8
  38.2 0.0 copy-start.1
  38.2 0.0 copy-start.7
  38.2 4.4 %fusion.9 = f32[2048,512]{1,0:T(8,128)} fusion(bf16[2048,512]{1,0:T(8,128)(2,1)S(1)} %copy-done.3, bf16[1536,512]{1,0:T(8,128)(2,1)} %param.16), kind=kOutput, calls=%fused_computation.21 | convolution fusion | flops 1073741824 | bytes 6815744 | tf_op jit(solution)/shard_map/dot_general | solution.py:100
  42.6 0.0 copy-done.8
  42.6 0.1 fusion.33
  42.7 0.0 collective-permute-done
  42.7 0.0 collective-permute-done.1
  42.7 0.0 copy-done.1
  42.7 5.8 %collective-permute-start.2 = (bf16[1,34,512]{2,1,0:T(8,128)(2,1)S(1)}, bf16[1,34,512]{2,1,0:T(8,128)(2,1)S(1)}, u32[]{:S(2)}, u32[]{:S(2)}) collective-permute-start(bf16[1,34,512]{2,1,0:T(8,128)(2,1)S(1)} %get-tuple-element.6), channel_id=1, source_target_pairs={{0,16},{16,32},{32,48},{48,64},{64,80},{80,96},{96,112},{1,17},{17... | collective-permute-start | bytes 104456 | tf_op jit(solution)/shard_map/ppermute | solution.py:29
  48.5 2.1 %collective-permute-start.3 = (bf16[1,34,512]{2,1,0:T(8,128)(2,1)S(1)}, bf16[1,34,512]{2,1,0:T(8,128)(2,1)S(1)}, u32[]{:S(2)}, u32[]{:S(2)}) collective-permute-start(bf16[1,34,512]{2,1,0:T(8,128)(2,1)S(1)} %get-tuple-element.7), channel_id=1, source_target_pairs={{16,0},{32,16},{48,32},{64,48},{80,64},{96,80},{112,96},{17,1},{33... | collective-permute-start | bytes 104456 | tf_op jit(solution)/shard_map/ppermute | solution.py:30
  50.6 0.0 copy-done.7
  50.6 2.5 %copy.13 = bf16[2048,512]{0,1:T(8,128)(2,1)} copy(bf16[2048,512]{1,0:T(8,128)(2,1)S(1)} %copy-done.3) | data formatting | bytes 4194304 | tf_op args[1]
  53.1 9.2 %gather_fusion.1 = bf16[2048,512]{1,0:T(8,128)(2,1)} fusion(bf16[512,512]{1,0:T(8,128)(2,1)S(1)} %bitcast.18, s32[2048]{0:T(1024)S(1)} %get-tuple-element.4), kind=kCustom, calls=%fused_computation.1 | custom fusion | bytes 4202496 | tf_op jit(solution)/shard_map/gather | solution.py:102
  62.3 0.0 collective-permute-done.2
  62.3 0.0 collective-permute-done.3
  62.3 0.3 pad_maximum_fusion.1
  62.6 0.2 reshape.52
  62.8 0.0 all-gather.2.cloned.1.call-done
  62.8 5.4 %pad_maximum_fusion = bf16[4708,512]{1,0:T(8,128)(2,1)} fusion(bf16[4096,512]{1,0:T(8,128)(2,1)} %all-gather.2.cloned.1.call-done, bf16[612,512]{1,0:T(8,128)(2,1)S(1)} %reshape.52), kind=kLoop, calls=%fused_computation.2 | loop fusion | flops 9641984 | bytes 9641984 | tf_op jit(solution)/shard_map/concatenate | solution.py:76
  68.2 10.6 %gather_fusion = bf16[2048,512]{1,0:T(8,128)(2,1)S(1)} fusion(bf16[4708,512]{1,0:T(8,128)(2,1)} %pad_maximum_fusion, s32[2048]{0:T(1024)S(1)} %fusion.33), kind=kCustom, calls=%fused_computation | custom fusion | bytes 4202496 | tf_op jit(solution)/shard_map/gather | solution.py:101
  78.8 4.3 %fusion.7 = f32[2048,512]{1,0:T(8,128)} fusion(bf16[2048,512]{1,0:T(8,128)(2,1)S(1)} %gather_fusion, bf16[1536,512]{1,0:T(8,128)(2,1)} %param.16), kind=kOutput, calls=%fused_computation.19 | convolution fusion | flops 1073741824 | bytes 6815744 | tf_op jit(solution)/shard_map/dot_general | solution.py:105
  83.1 0.0 copy-done
  83.1 0.0 copy-start.4
  83.1 9.3 %fusion.37 = (f32[2048]{0:T(1024)S(1)}, f32[2048,512]{0,1:T(8,128)}) fusion(bf16[512,512]{1,0:T(8,128)(2,1)S(1)} %copy-done, f32[2048,512]{1,0:T(8,128)} %fusion.9, f32[2048,512]{1,0:T(8,128)} %fusion.7, bf16[2048,512]{1,0:T(8,128)(2,1)} %gather_fusion.1, bf16[1536,512]{1,0:T(8,128)(2,1)} %param.16), kind=kOutput, calls=%fused_computation.89 | convolution fusion | flops 2155870208 | bytes 15736832 | tf_op jit(solution)/shard_map/dot_general | solution.py:109
  92.4 0.0 copy-start.2
  92.4 0.0 copy-start.10
  92.4 2.8 %multiply_reduce_fusion = f32[2048]{0:T(1024)S(1)} fusion(f32[2048,512]{0,1:T(8,128)} %get-tuple-element.11, f32[2048]{0:T(1024)S(1)} %broadcast_multiply_fusion), kind=kLoop, calls=%fused_computation.5 | loop fusion | flops 3143680 | bytes 4210688 | tf_op jit(solution)/shard_map/reduce_sum | solution.py:38
  95.2 0.0 copy-done.4
  95.2 0.6 copy-done.2
  95.9 0.0 copy-done.10
  95.9 2.6 %select_convert_fusion = bf16[2048,512]{0,1:T(8,128)(2,1)} fusion(bf16[2048,512]{0,1:T(8,128)(2,1)S(1)} %copy-done.4, pred[2048]{0:T(1024)(128)(4,1)S(1)} %broadcast_compare_fusion, f32[512]{0:T(512)S(1)} %copy-done.10, f32[2048]{0:T(1024)S(1)} %add_rsqrt_fusion, f32[2048,512]{0,1:T(8,128)S(1)} %copy-done.2, f32[2048]{0:T(1024)S(1)} %broadcast_multiply_fusion), kind=kLoop, calls=%fused_computation.3 | loop fusion | flops 9437184 | bytes 8409088 | tf_op jit(solution)/shard_map/convert_element_type | solution.py:113
  98.4 0.0 copy-start.5
  98.4 4.0 %copy.14 = bf16[2048,512]{1,0:T(8,128)(2,1)} copy(bf16[2048,512]{0,1:T(8,128)(2,1)} %select_convert_fusion) | data formatting | bytes 4194304
  102.4 0.0 copy-done.5
  102.4 0.0 copy-start.6
  102.4 0.0 copy-start.9
  102.4 4.2 %multiply_convert_fusion.2 = bf16[512,512]{1,0:T(8,128)(2,1)S(1)} fusion(f32[512,512]{1,0:T(8,128)S(1)} %copy-done.5, s32[2048]{0:T(1024)S(1)} %get-tuple-element.5, bf16[1024,512]{1,0:T(8,128)(2,1)} %param.19, f32[2048,512]{0,1:T(8,128)} %get-tuple-element.11, f32[512]{0:T(512)S(1)} %copy-done.10, f32[2048]{0:T(1024)S(1)} %add_rsqrt_fusion, ...), kind=kOutput, calls=%fused_computation.15 | convolution fusion | flops 1349255168 | bytes 6318080 | tf_op jit(solution)/shard_map/dot_general | solution.py:121
  106.6 0.0 copy-done.6
  106.7 0.5 fusion.40
  107.2 0.3 multiply_reduce_fusion.1
  107.5 0.0 copy-done.9
  107.5 1.1 add_convert_fusion
  (7 shorter events, 0.1 us)
Async XLA Ops:
  7.2 76.0 %copy-start = (bf16[512,512]{1,0:T(8,128)(2,1)S(1)}, bf16[512,512]{1,0:T(8,128)(2,1)}, u32[]{:S(2)}) copy-start(bf16[512,512]{1,0:T(8,128)(2,1)} %param.17) | copy-start | bytes 1572868
  7.2 31.0 %copy-start.3 = (bf16[2048,512]{1,0:T(8,128)(2,1)S(1)}, bf16[2048,512]{1,0:T(8,128)(2,1)}, u32[]{:S(2)}) copy-start(bf16[2048,512]{1,0:T(8,128)(2,1)} %param.12) | copy-start | bytes 6291460
  7.2 55.6 %all-gather.2.cloned.1.call-start = ((), (), s32[]{:S(2)}) async-start(), calls=%async_computation.1 | async-start | bytes 4718592 | tf_op jit(solution)/shard_map/all_gather | solution.py:44
  29.2 13.4 %collective-permute-start = (bf16[16,1,512]{2,1,0:T(2,128)(2,1)S(1)}, bf16[16,1,512]{2,1,0:T(2,128)(2,1)S(1)}, u32[]{:S(2)}, u32[]{:S(2)}) collective-permute-start(bf16[16,1,512]{2,1,0:T(2,128)(2,1)S(1)} %get-tuple-element.8), channel_id=1, source_target_pairs={{0,1},{1,2},{2,3},{3,4},{4,5},{5,6},{6,7},{7,8},{8,9},{9,10},{10,1... | collective-permute-start | bytes 49160 | tf_op jit(solution)/shard_map/ppermute | solution.py:29
  29.8 12.8 %collective-permute-start.1 = (bf16[16,1,512]{2,1,0:T(2,128)(2,1)S(1)}, bf16[16,1,512]{2,1,0:T(2,128)(2,1)S(1)}, u32[]{:S(2)}, u32[]{:S(2)}) collective-permute-start(bf16[16,1,512]{2,1,0:T(2,128)(2,1)S(1)} %get-tuple-element.9), channel_id=1, source_target_pairs={{1,0},{2,1},{3,2},{4,3},{5,4},{6,5},{7,6},{8,7},{9,8},{10,9},{11,1... | collective-permute-start | bytes 49160 | tf_op jit(solution)/shard_map/ppermute | solution.py:30
  38.2 4.4 %copy-start.8 = (s32[2048]{0:T(1024)S(1)}, s32[2048]{0:T(1024)}, u32[]{:S(2)}) copy-start(s32[2048]{0:T(1024)} %param.13) | copy-start | bytes 24580
  38.2 4.5 %copy-start.1 = (bf16[16,32,512]{2,1,0:T(8,128)(2,1)S(1)}, bf16[16,32,512]{2,1,0:T(8,128)(2,1)}, u32[]{:S(2)}) copy-start(bf16[16,32,512]{2,1,0:T(8,128)(2,1)} %param.11) | copy-start | bytes 1572868
  38.2 12.4 %copy-start.7 = (s32[2048]{0:T(1024)S(1)}, s32[2048]{0:T(1024)}, u32[]{:S(2)}) copy-start(s32[2048]{0:T(1024)} %param.14) | copy-start | bytes 24580
  42.7 19.6 %collective-permute-start.2 = (bf16[1,34,512]{2,1,0:T(8,128)(2,1)S(1)}, bf16[1,34,512]{2,1,0:T(8,128)(2,1)S(1)}, u32[]{:S(2)}, u32[]{:S(2)}) collective-permute-start(bf16[1,34,512]{2,1,0:T(8,128)(2,1)S(1)} %get-tuple-element.6), channel_id=1, source_target_pairs={{0,16},{16,32},{32,48},{48,64},{64,80},{80,96},{96,112},{1,17},{17... | collective-permute-start | bytes 104456 | tf_op jit(solution)/shard_map/ppermute | solution.py:29
  48.5 13.8 %collective-permute-start.3 = (bf16[1,34,512]{2,1,0:T(8,128)(2,1)S(1)}, bf16[1,34,512]{2,1,0:T(8,128)(2,1)S(1)}, u32[]{:S(2)}, u32[]{:S(2)}) collective-permute-start(bf16[1,34,512]{2,1,0:T(8,128)(2,1)S(1)} %get-tuple-element.7), channel_id=1, source_target_pairs={{16,0},{32,16},{48,32},{64,48},{80,64},{96,80},{112,96},{17,1},{33... | collective-permute-start | bytes 104456 | tf_op jit(solution)/shard_map/ppermute | solution.py:30
  83.1 12.1 %copy-start.4 = (bf16[2048,512]{0,1:T(8,128)(2,1)S(1)}, bf16[2048,512]{0,1:T(8,128)(2,1)}, u32[]{:S(2)}) copy-start(bf16[2048,512]{0,1:T(8,128)(2,1)} %copy.13) | copy-start | bytes 6291460
  92.4 3.4 %copy-start.2 = (f32[2048,512]{0,1:T(8,128)S(1)}, f32[2048,512]{0,1:T(8,128)}, u32[]{:S(2)}) copy-start(f32[2048,512]{0,1:T(8,128)} %get-tuple-element.11) | copy-start | bytes 12582916
  92.4 3.4 %copy-start.10 = (f32[512]{0:T(512)S(1)}, f32[512]{0:T(512)}, u32[]{:S(2)}) copy-start(f32[512]{0:T(512)} %param.18) | copy-start | bytes 6148
  98.4 4.0 %copy-start.5 = (f32[512,512]{1,0:T(8,128)S(1)}, f32[512,512]{1,0:T(8,128)}, u32[]{:S(2)}) copy-start(f32[512,512]{1,0:T(8,128)} %fusion.11) | copy-start | bytes 3145732
  102.4 4.2 %copy-start.6 = (bf16[512,512]{1,0:T(8,128)(2,1)S(1)}, bf16[512,512]{1,0:T(8,128)(2,1)}, u32[]{:S(2)}) copy-start(bf16[512,512]{1,0:T(8,128)(2,1)} %param.20) | copy-start | bytes 1572868
  102.4 5.0 %copy-start.9 = (f32[512]{0:T(512)S(1)}, f32[512]{0:T(512)}, u32[]{:S(2)}) copy-start(f32[512]{0:T(512)} %param.21) | copy-start | bytes 6148
Sparse Core Ops, SparseCore 0:
  28.3 31.7 all-gather.1
where the time goes:
time: 116 us; the launch traced here: 115 us
  local copies, waits for them, and re-layouts  30.2 us (26%)
  matrix products  25.4 us (22%)
  blocking collectives  18.8 us (16%)
  between operations  14.2 us (12%)
  other arithmetic  13.9 us (12%)
  starting transfers between devices  12.8 us (11%)
    all_to_all x1, blocking collectives, copy_for_each(): return lax.all_to_all(copies, axis, split_axis=0, concat_axis=0, tiled=True)  18.8 us
    gather x1, local copies, waits for them, and re-layouts, per_device(): send_rows = lookup[table_index]  10.6 us
    dot_general x1, matrix products, per_device(): second_sum = jnp.dot(hidden, w_second, preferred_element_type=jnp.float32)  9.29 us
    gather x1, local copies, waits for them, and re-layouts, per_device(): recv_rows = own_rows[recv_index]  9.2 us
    unnamed x24, local copies, waits for them, and re-layouts  7.14 us
    ppermute x2, starting transfers between devices, padded(): after = lax.ppermute(leading, axis, down)  6.37 us
    ppermute x2, starting transfers between devices, padded(): before = lax.ppermute(last, axis, up)  6.34 us
    concatenate x1, other arithmetic, per_device(): lookup = jnp.concatenate([ext_rows, coarse_rows], axis=0)  5.38 us
  transfers between devices with their start and end apart: 5, of which 0 were waited for; matrix products, arithmetic and copies ran while one was open for 19% of the time, Pallas kernels for 0%

commit v1 on v0

v1 whole, which is shorter than its diff:
```python
import jax
import jax.numpy as jnp
from jax import lax
from jax.experimental import pallas as pl
from jax.experimental.pallas import tpu as pltpu
from jax.sharding import PartitionSpec as P

F = 512
BLK = 128
GROUP = 4
ROWS = GROUP * BLK
PIECE = 512
RIM = 40
BF = jnp.bfloat16
F32 = jnp.float32


def device_of(x, c, y, z):
    return (x % 4 * 2 + c) * 16 + y % 4 * 4 + z % 4


def shift(axis, by_core):
    pairs = []
    for x in range(4):
        for c in range(2):
            for y in range(4):
                for z in range(4):
                    to = {"x": x, "y": y, "z": z}
                    to[axis] += by_core[c]
                    pairs.append((device_of(x, c, y, z), device_of(to["x"], c, to["y"], to["z"])))
    return pairs


def other_core(value):
    pairs = [
        (device_of(x, c, y, z), device_of(x, 1 - c, y, z))
        for x in range(4)
        for c in range(2)
        for y in range(4)
        for z in range(4)
    ]
    return lax.ppermute(value, ("lat", "lon"), pairs)


def move(value, axis, by_core):
    return lax.ppermute(value, ("lat", "lon"), shift(axis, by_core))


def ring(own, axis):
    ahead = move(own, axis, (1, -1))
    behind = move(own, axis, (-1, 1))
    across = move(ahead, axis, (1, -1))
    return own, ahead, behind, across


def ring_place(offset, core):
    near = jnp.where((offset == 1) == (core == 1), 1, 2)
    return jnp.where(offset == 0, 0, jnp.where(offset == 2, 3, near))


def silu(v):
    half = 0.5 * v
    return half + half * jnp.tanh(half)


def normed(values, gain):
    centred = values - jnp.mean(values, -1, keepdims=True)
    spread = jnp.mean(centred * centred, -1, keepdims=True)
    return centred * lax.rsqrt(spread + 1e-05) * gain


def dot(a, b):
    return jnp.dot(a, b, preferred_element_type=F32)


def chosen(recv_row):
    return (lax.broadcasted_iota(jnp.int32, (BLK, BLK), 0) == recv_row).astype(BF)


def early_kernel(tiles, edge_ref, recv_ref, node_ref, we_ref, wr_ref, wn_ref, pre_ref, nf_ref, got_ref):
    step = pl.program_id(0)

    @pl.when(step == 0)
    def _():
        nf_ref[...] = dot(node_ref[...], wn_ref[...])

    for k in range(GROUP):
        tile = pl.multiple_of(tiles[step * GROUP + k] * BLK, BLK)
        hot = chosen(recv_ref[k : k + 1, :])
        rows = lax.dot_general(
            hot,
            node_ref[pl.ds(tile, BLK), :],
            (((0,), (0,)), ((), ())),
            preferred_element_type=F32,
        )
        got_ref[k * BLK : (k + 1) * BLK, :] = rows.astype(BF)
    pre_ref[...] = dot(edge_ref[...], we_ref[...]) + dot(got_ref[...], wr_ref[...])


def late_kernel(
    table_index,
    tiles,
    lives,
    *refs,
):
    pieces = refs[:13]
    (
        pre_ref,
        edge_ref,
        recv_ref,
        nf_ref,
        node_ref,
        ws_ref,
        w2_ref,
        eg_ref,
        wn_ref,
        wn2_ref,
        ng_ref,
        out_ref,
        node_out_ref,
        table,
        sent,
        agg,
        sem,
    ) = refs[13:]
    step = pl.program_id(0)

    @pl.when(step == 0)
    def _():
        copies = []
        start = 0
        for i, piece in enumerate(pieces):
            rows = piece.shape[0]
            copies.append(pltpu.make_async_copy(piece, table.at[pl.ds(start, rows)], sem.at[i]))
            start += rows
        for copy in copies:
            copy.start()
        agg[...] = jnp.zeros_like(agg)
        for copy in copies:
            copy.wait()

    def fetch(i, carry):
        for u in range(16):
            e = i * 16 + u
            row = table[table_index[step * ROWS + e]]
            sent[pl.ds(pl.multiple_of(e * 4, 4), 4), :] = row.astype(F32)
        return carry

    lax.fori_loop(0, ROWS // 16, fetch, 0)
    send = jnp.concatenate(
        [sent[pl.ds(j, ROWS, stride=4), :].astype(BF) for j in range(4)], axis=1
    )
    hidden = silu(pre_ref[...] + dot(send, ws_ref[...])).astype(BF)
    message = normed(dot(hidden, w2_ref[...]), eg_ref[...]).astype(BF)
    place = lax.broadcasted_iota(jnp.int32, (BLK, F), 0)
    for k in range(GROUP):
        part = message[k * BLK : (k + 1) * BLK, :]
        edge = edge_ref[k * BLK : (k + 1) * BLK, :]
        live = place < lives[step * GROUP + k]
        out_ref[k * BLK : (k + 1) * BLK, :] = jnp.where(
            live, edge.astype(F32) + part.astype(F32), 0.0
        ).astype(BF)
        tile = pl.multiple_of(tiles[step * GROUP + k] * BLK, BLK)
        agg[pl.ds(tile, BLK), :] += dot(chosen(recv_ref[k : k + 1, :]), part)

    @pl.when(step == pl.num_programs(0) - 1)
    def _():
        first = nf_ref[...] + dot(agg[...].astype(BF), wn_ref[...])
        second = dot(silu(first).astype(BF), wn2_ref[...])
        node_out_ref[...] = (
            node_ref[...].astype(F32) + normed(second, ng_ref[...])
        ).astype(BF)


def per_device(
    node_latent,
    edge_latent,
    sender,
    receiver,
    block_tile,
    w_first,
    w_second,
    edge_gain,
    w_node_first,
    w_node_second,
    node_gain,
):
    patch_rows, patch_cols, features = node_latent.shape
    lat_index = lax.axis_index("lat")
    lon_index = lax.axis_index("lon")
    lat_count, lon_count = lax.axis_size("lat"), lax.axis_size("lon")
    grid_cols = patch_cols * lon_count
    blocks = block_tile.shape[0]
    nodes = patch_rows * patch_cols
    own_rows = node_latent.reshape(nodes, features)

    coarse_own = node_latent[::4, ::4].reshape(-1, 4, 128)
    line = jnp.concatenate(ring(coarse_own, "z"), 0)
    plane = jnp.concatenate(ring(line, "y"), 0)
    halves = ring(plane, "x")
    far_pieces = list(halves) + [other_core(part) for part in halves]

    right = [(i, (i + 1) % lon_count) for i in range(lon_count)]
    left = [(j, i) for i, j in right]
    up = [(i, i + 1) for i in range(lat_count - 1)]
    down = [(j, i) for i, j in up]
    west = lax.ppermute(node_latent[:, -1:], "lon", right)
    east = lax.ppermute(node_latent[:, :1], "lon", left)
    row_of = lambda r: jnp.concatenate([west[r], node_latent[r], east[r]], 0)
    north = lax.ppermute(row_of(patch_rows - 1), "lat", up)
    south = lax.ppermute(row_of(0), "lat", down)
    lanes = lambda a: a.reshape(-1, 4, 128)
    pad = lambda a: jnp.pad(lanes(a), ((0, RIM - patch_cols - 2), (0, 0), (0, 0)))
    near_pieces = [lanes(own_rows), lanes(west), lanes(east), pad(north), pad(south)]

    senders = jnp.maximum(sender, 0)
    send_row = senders // grid_cols
    send_col = senders % grid_cols
    row = send_row - lat_index * patch_rows
    col = (send_col - lon_index * patch_cols + 1) % grid_cols - 1
    is_near = (row >= -1) & (row <= patch_rows) & (col <= patch_cols)
    side = jnp.where(col < 0, nodes + row, nodes + patch_rows + row)
    inner = jnp.where((col < 0) | (col >= patch_cols), side, row * patch_cols + col)
    rim = nodes + 2 * patch_rows
    near_index = jnp.where(
        row < 0, rim + col + 1, jnp.where(row >= patch_rows, rim + RIM + col + 1, inner)
    )
    near_count = rim + 2 * RIM
    src_lat, src_lon = send_row // patch_rows, send_col // patch_cols
    src_core, core = src_lat % 2, lat_index % 2
    at_x = ring_place((src_lat // 2 - lat_index // 2) % 4, src_core)
    at_y = ring_place((src_lon // 4 - lon_index // 4) % 4, src_core)
    at_z = ring_place((src_lon % 4 - lon_index % 4) % 4, src_core)
    half = jnp.where(src_core == core, 0, 1)
    within = send_row % patch_rows // 4 * (patch_cols // 4) + send_col % patch_cols // 4
    per = patch_rows // 4 * (patch_cols // 4)
    far_index = near_count + ((((half * 4 + at_x) * 4 + at_y) * 4 + at_z) * per + within)
    table_index = jnp.where(is_near, near_index, far_index)
    recv_rows = receiver.reshape(blocks // GROUP, GROUP, BLK)
    lives = jnp.sum((receiver >= 0).astype(jnp.int32).reshape(blocks, BLK), 1)

    steps = blocks // GROUP
    whole = lambda shape: pl.BlockSpec(shape, lambda i, *_: (0,) * len(shape))
    part = pl.BlockSpec((ROWS, F), lambda i, *_: (i, 0))
    recv_spec = pl.BlockSpec((None, GROUP, BLK), lambda i, *_: (i, 0, 0))
    weight = lambda k: pl.BlockSpec((F, F), lambda i, *_: (k, 0))
    anywhere = pl.BlockSpec(memory_space=pl.ANY)
    pre, node_first = pl.pallas_call(
        early_kernel,
        name="early",
        grid_spec=pltpu.PrefetchScalarGridSpec(
            num_scalar_prefetch=1,
            grid=(steps,),
            in_specs=[part, recv_spec, whole((nodes, F)), weight(0), weight(2), weight(0)],
            out_specs=[part, whole((nodes, F))],
            scratch_shapes=[pltpu.VMEM((ROWS, F), BF)],
        ),
        out_shape=[
            jax.ShapeDtypeStruct((blocks * BLK, F), F32),
            jax.ShapeDtypeStruct((nodes, F), F32),
        ],
        compiler_params=pltpu.CompilerParams(vmem_limit_bytes=20 << 20),
        cost_estimate=pl.CostEstimate(
            flops=6 * 10**9, bytes_accessed=9 * 10**6, transcendentals=0
        ),
    )(block_tile, edge_latent, recv_rows, own_rows, w_first, w_first, w_node_first)

    pieces = near_pieces + far_pieces
    table_rows = sum(piece.shape[0] for piece in pieces)
    edge_out, node_out = pl.pallas_call(
        late_kernel,
        name="late",
        grid_spec=pltpu.PrefetchScalarGridSpec(
            num_scalar_prefetch=3,
            grid=(steps,),
            in_specs=[anywhere] * len(pieces)
            + [
                part,
                part,
                recv_spec,
                whole((nodes, F)),
                whole((nodes, F)),
                weight(1),
                whole((F, F)),
                whole((1, F)),
                weight(1),
                whole((F, F)),
                whole((1, F)),
            ],
            out_specs=[part, whole((nodes, F))],
            scratch_shapes=[
                pltpu.VMEM((table_rows, 4, 128), BF),
                pltpu.VMEM((ROWS * 4, 128), F32),
                pltpu.VMEM((nodes, F), F32),
                pltpu.SemaphoreType.DMA((len(pieces),)),
            ],
        ),
        out_shape=[
            jax.ShapeDtypeStruct((blocks * BLK, F), BF),
            jax.ShapeDtypeStruct((nodes, F), BF),
        ],
        compiler_params=pltpu.CompilerParams(vmem_limit_bytes=40 << 20),
        cost_estimate=pl.CostEstimate(
            flops=8 * 10**9, bytes_accessed=16 * 10**6, transcendentals=0
        ),
    )(
        table_index,
        block_tile,
        lives,
        *pieces,
        pre,
        edge_latent,
        recv_rows,
        node_first,
        own_rows,
        w_first,
        w_second,
        edge_gain.reshape(1, F),
        w_node_first,
        w_node_second,
        node_gain.reshape(1, F),
    )
    return node_out.reshape(patch_rows, patch_cols, features), edge_out


def solution(mesh):
    return jax.shard_map(
        per_device,
        mesh=mesh,
        in_specs=(
            P("lat", "lon", None),
            P(("lat", "lon"), None),
            P(("lat", "lon")),
            P(("lat", "lon")),
            P(("lat", "lon")),
            P(),
            P(),
            P(),
            P(),
            P(),
            P(),
        ),
        out_specs=(P("lat", "lon", None), P(("lat", "lon"), None)),
        check_vma=False,
    )
```

time: 116 us -> 93.4 us (0.81)
  starting transfers between devices: 12.8 us -> 42.4 us
  matrix products: 25.4 us -> 0 us
  Pallas kernels: 0 us -> 19.9 us
  blocking collectives: 18.8 us -> 0 us
  other arithmetic: 13.9 us -> 0.41 us
  between operations: 14.2 us -> 0.92 us
  local copies, waits for them, and re-layouts: 30.2 us -> 19.2 us
  waiting for transfers between devices: 0.05 us -> 9.91 us
    ppermute x4 -> x17, starting transfers between devices: 12.7 us -> 42.4 us  [the longest x4 18 us: other_core(): return lax.ppermute(value, ('lat', 'lon'), pairs)]
    dot_general x6 -> x0, matrix products: 25.4 us -> none  [the longest x1 9.29 us: per_device(): second_sum = jnp.dot(hidden, w_second, preferred_element_type=jnp.float32)]
    pallas_call x0 -> x2, Pallas kernels: none -> 19.9 us  [the longest x1 15.4 us: per_device(): pl.pallas_call(late_kernel, name='late', grid_spec=pltpu.PrefetchScalarGr...]
    gather x2 -> x0, local copies, waits for them, and re-layouts: 19.8 us -> none  [the longest x1 10.6 us: per_device(): send_rows = lookup[table_index]]
    all_to_all x1 -> x0, blocking collectives: 18.8 us -> none  [copy_for_each(): return lax.all_to_all(copies, axis, split_axis=0, concat_axis=0, tiled=True)]
    ppermute x4 -> x17, waiting for transfers between devices: 0.01 us -> 9.91 us  [the longest x9 5.54 us: move(): return lax.ppermute(value, ('lat', 'lon'), shift(axis, by_core))]
    unnamed x24 -> x45, local copies, waits for them, and re-layouts: 7.14 us -> 15.9 us
    concatenate x2, other arithmetic: 5.72 us -> 0.04 us  [per_device(): row_of = lambda r: jnp.concatenate([west[r], node_latent[r], east[r]], 0)]
  transfers between devices with their start and end apart: 5 -> 17, of which waited for: 0 -> 5; matrix products, arithmetic and copies ran while one was open for 19% -> 2% of each run, Pallas kernels for 0% -> 5%
where the time goes in v1:
time: 93.4 us; the launch traced here: 92.7 us
  starting transfers between devices  42.4 us (45%)
  Pallas kernels  19.9 us (21%)
  local copies, waits for them, and re-layouts  19.2 us (21%)
  waiting for transfers between devices  9.91 us (11%)
    ppermute x4, starting transfers between devices, other_core(): return lax.ppermute(value, ('lat', 'lon'), pairs)  18 us
    ppermute x9, starting transfers between devices, move(): return lax.ppermute(value, ('lat', 'lon'), shift(axis, by_core))  16.3 us
    unnamed x45, local copies, waits for them, and re-layouts  15.9 us
    pallas_call x1, Pallas kernels, per_device(): pl.pallas_call(late_kernel, name='late', grid_spec=pltpu.PrefetchScalarGr...  15.4 us
    ppermute x9, waiting for transfers between devices, move(): return lax.ppermute(value, ('lat', 'lon'), shift(axis, by_core))  5.54 us
    pallas_call x1, Pallas kernels, per_device(): pl.pallas_call(early_kernel, name='early', grid_spec=pltpu.PrefetchScalar...  4.48 us
    ppermute x1, starting transfers between devices, per_device(): east = lax.ppermute(node_latent[:, :1], 'lon', left)  4.12 us
    ppermute x1, waiting for transfers between devices, per_device(): south = lax.ppermute(row_of(0), 'lat', down)  3.2 us
  transfers between devices with their start and end apart: 17, of which 5 were waited for; matrix products, arithmetic and copies ran while one was open for 2% of the time, Pallas kernels for 5%

profile of v1, /device:TPU:1, one launch (start us, length us, event | category | flops | bytes accessed | tf_op | source)
XLA Modules:
  0.0 92.7 jit_solution(11682233567372615488)
XLA Ops:
  0.6 1.9 %slice.35 = bf16[4,8,512]{2,1,0:T(8,128)(2,1)S(1)} slice(bf16[16,32,512]{2,1,0:T(8,128)(2,1)} %param.11), slice={[0:16:4], [0:32:4], [0:512:1]} | slice | bytes 65536 | tf_op jit(solution)/shard_map/slice | solution.py:197
  2.6 2.5 %collective-permute-start.5 = (bf16[32,4,128]{2,1,0:T(4,128)(2,1)S(1)}, bf16[32,4,128]{2,1,0:T(4,128)(2,1)S(1)}, u32[]{:S(2)}, u32[]{:S(2)}) collective-permute-start(bf16[32,4,128]{2,1,0:T(4,128)(2,1)S(1)} %reshape.46), channel_id=1, source_target_pairs={{0,3},{1,0},{2,1},{3,2},{4,7},{5,4},{6,5},{7,6},{8,11},{9,8},{10,9... | collective-permute-start | bytes 98312 | tf_op jit(solution)/shard_map/ppermute | solution.py:46
  5.1 2.2 %collective-permute-start.4 = (bf16[32,4,128]{2,1,0:T(4,128)(2,1)S(1)}, bf16[32,4,128]{2,1,0:T(4,128)(2,1)S(1)}, u32[]{:S(2)}, u32[]{:S(2)}) collective-permute-start(bf16[32,4,128]{2,1,0:T(4,128)(2,1)S(1)} %reshape.46), channel_id=1, source_target_pairs={{0,1},{1,2},{2,3},{3,0},{4,5},{5,6},{6,7},{7,4},{8,9},{9,10},{10,1... | collective-permute-start | bytes 98312 | tf_op jit(solution)/shard_map/ppermute | solution.py:46
  7.4 1.0 %collective-permute-done.4 = bf16[32,4,128]{2,1,0:T(4,128)(2,1)S(1)} collective-permute-done((bf16[32,4,128]{2,1,0:T(4,128)(2,1)S(1)}, bf16[32,4,128]{2,1,0:T(4,128)(2,1)S(1)}, u32[]{:S(2)}, u32[]{:S(2)}) %collective-permute-start.4) | collective-permute-done | bytes 32800 | tf_op jit(solution)/shard_map/ppermute | solution.py:46
  8.4 3.0 %collective-permute-start.6 = (bf16[32,4,128]{2,1,0:T(4,128)(2,1)S(1)}, bf16[32,4,128]{2,1,0:T(4,128)(2,1)S(1)}, u32[]{:S(2)}, u32[]{:S(2)}) collective-permute-start(bf16[32,4,128]{2,1,0:T(4,128)(2,1)S(1)} %collective-permute-done.4), channel_id=1, source_target_pairs={{0,1},{1,2},{2,3},{3,0},{4,5},{5,6},{6,7},{7,4},{8,9},{9,10},{10,1... | collective-permute-start | bytes 98312 | tf_op jit(solution)/shard_map/ppermute | solution.py:46
  11.3 0.0 collective-permute-done.5
  11.4 0.9 %collective-permute-done.6 = bf16[32,4,128]{2,1,0:T(4,128)(2,1)S(1)} collective-permute-done((bf16[32,4,128]{2,1,0:T(4,128)(2,1)S(1)}, bf16[32,4,128]{2,1,0:T(4,128)(2,1)S(1)}, u32[]{:S(2)}, u32[]{:S(2)}) %collective-permute-start.6) | collective-permute-done | bytes 32800 | tf_op jit(solution)/shard_map/ppermute | solution.py:46
  12.4 1.4 %collective-permute-start.8 = (bf16[128,4,128]{2,1,0:T(4,128)(2,1)S(1)}, bf16[128,4,128]{2,1,0:T(4,128)(2,1)S(1)}, u32[]{:S(2)}, u32[]{:S(2)}) collective-permute-start(bf16[128,4,128]{2,1,0:T(4,128)(2,1)S(1)} %get-tuple-element.14), channel_id=1, source_target_pairs={{0,12},{1,13},{2,14},{3,15},{4,0},{5,1},{6,2},{7,3},{8,4},{9,5},{1... | collective-permute-start | bytes 393224 | tf_op jit(solution)/shard_map/ppermute | solution.py:46
  13.7 1.5 %collective-permute-start.7 = (bf16[128,4,128]{2,1,0:T(4,128)(2,1)S(1)}, bf16[128,4,128]{2,1,0:T(4,128)(2,1)S(1)}, u32[]{:S(2)}, u32[]{:S(2)}) collective-permute-start(bf16[128,4,128]{2,1,0:T(4,128)(2,1)S(1)} %get-tuple-element.14), channel_id=1, source_target_pairs={{0,4},{1,5},{2,6},{3,7},{4,8},{5,9},{6,10},{7,11},{8,12},{9,13},{1... | collective-permute-start | bytes 393224 | tf_op jit(solution)/shard_map/ppermute | solution.py:46
  15.3 1.0 %fusion.24 = (bf16[16,1,512]{2,1,0:T(2,128)(2,1)S(1)}, bf16[16,1,512]{2,1,0:T(2,128)(2,1)S(1)}) fusion(bf16[16,32,512]{2,1,0:T(8,128)(2,1)} %param.11), kind=kLoop, calls=%fused_computation.99 | loop fusion | bytes 65536 | tf_op jit(solution)/shard_map/slice | solution.py:208
  16.3 4.1 %collective-permute-start.1 = (bf16[16,1,512]{2,1,0:T(2,128)(2,1)S(1)}, bf16[16,1,512]{2,1,0:T(2,128)(2,1)S(1)}, u32[]{:S(2)}, u32[]{:S(2)}) collective-permute-start(bf16[16,1,512]{2,1,0:T(2,128)(2,1)S(1)} %get-tuple-element.12), channel_id=1, source_target_pairs={{1,0},{2,1},{3,2},{4,3},{5,4},{6,5},{7,6},{8,7},{9,8},{10,9},{11,1... | collective-permute-start | bytes 49160 | tf_op jit(solution)/shard_map/ppermute | solution.py:208
  20.4 0.0 collective-permute-start
  20.4 0.0 collective-permute-done.7
  20.4 0.5 collective-permute-start.9
  20.9 0.1 constant_dynamic-update-slice_fusion.6
  20.9 0.0 collective-permute-done.8
  20.9 0.1 constant_dynamic-update-slice_fusion.5
  21.0 3.6 %collective-permute-done.9 = bf16[128,4,128]{2,1,0:T(4,128)(2,1)S(1)} collective-permute-done((bf16[128,4,128]{2,1,0:T(4,128)(2,1)S(1)}, bf16[128,4,128]{2,1,0:T(4,128)(2,1)S(1)}, u32[]{:S(2)}, u32[]{:S(2)}) %collective-permute-start.9) | collective-permute-done | bytes 131104 | tf_op jit(solution)/shard_map/ppermute | solution.py:46
  24.6 0.1 constant_dynamic-update-slice_fusion.4.refs_5_
  24.7 2.5 %collective-permute-start.10 = (bf16[512,4,128]{2,1,0:T(4,128)(2,1)S(1)}, bf16[512,4,128]{2,1,0:T(4,128)(2,1)}, u32[]{:S(2)}, u32[]{:S(2)}) collective-permute-start(bf16[512,4,128]{2,1,0:T(4,128)(2,1)S(1)} %constant_dynamic-update-slice_fusion.4.refs_5_), channel_id=1, source_target_pairs={{0,32},{1,33},{2,34},{3,35},{4,36},{5,37},{6,38},{7,39},{8,40},{9,... | collective-permute-start | bytes 1572872 | tf_op jit(solution)/shard_map/ppermute | solution.py:46
  27.2 1.0 %copy-done = bf16[16,32,512]{2,1,0:T(8,128)(2,1)S(1)} copy-done((bf16[16,32,512]{2,1,0:T(8,128)(2,1)S(1)}, bf16[16,32,512]{2,1,0:T(8,128)(2,1)}, u32[]{:S(2)}) %copy-start) | copy-done | bytes 524312
  28.2 0.7 copy-done.2
  28.9 1.6 %copy-done.4 = bf16[2048,512]{1,0:T(8,128)(2,1)S(1)} copy-done((bf16[2048,512]{1,0:T(8,128)(2,1)S(1)}, bf16[2048,512]{1,0:T(8,128)(2,1)}, u32[]{:S(2)}) %copy-start.4) | copy-done | bytes 2097176
  30.5 1.4 %copy-done.6 = bf16[1536,512]{1,0:T(8,128)(2,1)S(1)} copy-done((bf16[1536,512]{1,0:T(8,128)(2,1)S(1)}, bf16[1536,512]{1,0:T(8,128)(2,1)}, u32[]{:S(2)}) %copy-start.6) | copy-done | bytes 1572888
  31.9 1.2 %copy-done.8 = bf16[1024,512]{1,0:T(8,128)(2,1)S(1)} copy-done((bf16[1024,512]{1,0:T(8,128)(2,1)S(1)}, bf16[1024,512]{1,0:T(8,128)(2,1)}, u32[]{:S(2)}) %copy-start.8) | copy-done | bytes 1048600
  33.2 0.7 copy-done.14
  33.8 0.0 copy-start.12
  33.8 0.0 copy-start.13
  33.9 0.0 copy-start.15
  33.9 4.5 %early.1 = (f32[2048,512]{1,0:T(8,128)S(1)}, f32[512,512]{1,0:T(8,128)S(1)}) custom-call(s32[16]{0:T(128)S(1)} %copy-done.14, bf16[2048,512]{1,0:T(8,128)(2,1)S(1)} %copy-done.4, s32[4,4,128]{2,1,0:T(4,128)S(1)} %bitcast.21, bf16[512,512]{1,0:T(8,128)(2,1)S(1)} %bitcast.19, bf16[1536,512]{1,0:T(8,128)(2,1)S(1)} %copy-done.6, ...), custom_call_target="tpu_custom_call" | custom-call | flops 6000000000 | bytes 9000000 | tf_op jit(solution)/shard_map/early/pallas_call | solution.py:248
  38.4 0.0 copy-start.16
  38.4 2.0 %copy-done.16 = f32[2048,512]{1,0:T(8,128)} copy-done((f32[2048,512]{1,0:T(8,128)}, f32[2048,512]{1,0:T(8,128)S(1)}, u32[]{:S(2)}) %copy-start.16) | copy-done | bytes 4194328
  40.3 1.0 %copy-done.17 = f32[512,512]{1,0:T(8,128)} copy-done((f32[512,512]{1,0:T(8,128)}, f32[512,512]{1,0:T(8,128)S(1)}, u32[]{:S(2)}) %copy-start.17) | copy-done | bytes 1048600
  41.3 0.0 collective-permute-start.11
  41.3 0.0 collective-permute-done.10.refs_6_
  41.3 2.7 %collective-permute-start.12 = (bf16[512,4,128]{2,1,0:T(4,128)(2,1)}, bf16[512,4,128]{2,1,0:T(4,128)(2,1)}, u32[]{:S(2)}, u32[]{:S(2)}) collective-permute-start(bf16[512,4,128]{2,1,0:T(4,128)(2,1)} %collective-permute-done.10.refs_6_), channel_id=1, source_target_pairs={{0,32},{1,33},{2,34},{3,35},{4,36},{5,37},{6,38},{7,39},{8,40},{9,... | collective-permute-start | bytes 1572872 | tf_op jit(solution)/shard_map/ppermute | solution.py:46
  44.0 0.1 fusion.12.table_index
  44.1 0.0 collective-permute-done.1
  44.1 7.8 %collective-permute-start.13 = (bf16[512,4,128]{2,1,0:T(4,128)(2,1)S(1)}, bf16[512,4,128]{2,1,0:T(4,128)(2,1)}, u32[]{:S(2)}, u32[]{:S(2)}) collective-permute-start(bf16[512,4,128]{2,1,0:T(4,128)(2,1)S(1)} %constant_dynamic-update-slice_fusion.4.refs_5_), channel_id=1, source_target_pairs={{0,16},{1,17},{2,18},{3,19},{4,20},{5,21},{6,22},{7,23},{8,24},{9,... | collective-permute-start | bytes 1572872 | tf_op jit(solution)/shard_map/ppermute | solution.py:42
  51.9 0.1 collective-permute-start.14
  52.0 0.0 collective-permute-done.11.refs_7_
  52.0 7.0 %collective-permute-start.15 = (bf16[512,4,128]{2,1,0:T(4,128)(2,1)}, bf16[512,4,128]{2,1,0:T(4,128)(2,1)}, u32[]{:S(2)}, u32[]{:S(2)}) collective-permute-start(bf16[512,4,128]{2,1,0:T(4,128)(2,1)} %collective-permute-done.11.refs_7_), channel_id=1, source_target_pairs={{0,16},{1,17},{2,18},{3,19},{4,20},{5,21},{6,22},{7,23},{8,24},{9,... | collective-permute-start | bytes 1572872 | tf_op jit(solution)/shard_map/ppermute | solution.py:42
  58.9 0.0 collective-permute-done.12.refs_8_
  58.9 3.2 %collective-permute-start.16 = (bf16[512,4,128]{2,1,0:T(4,128)(2,1)}, bf16[512,4,128]{2,1,0:T(4,128)(2,1)}, u32[]{:S(2)}, u32[]{:S(2)}) collective-permute-start(bf16[512,4,128]{2,1,0:T(4,128)(2,1)} %collective-permute-done.12.refs_8_), channel_id=1, source_target_pairs={{0,16},{1,17},{2,18},{3,19},{4,20},{5,21},{6,22},{7,23},{8,24},{9,... | collective-permute-start | bytes 1572872 | tf_op jit(solution)/shard_map/ppermute | solution.py:42
  62.1 0.0 collective-permute-done
  62.1 1.9 %collective-permute-start.2 = (bf16[34,512]{1,0:T(8,128)(2,1)S(1)}, bf16[34,512]{1,0:T(8,128)(2,1)S(1)}, u32[]{:S(2)}, u32[]{:S(2)}) collective-permute-start(bf16[34,512]{1,0:T(8,128)(2,1)S(1)} %pad_maximum_fusion), channel_id=1, source_target_pairs={{0,16},{16,32},{32,48},{48,64},{64,80},{80,96},{96,112},{1,17},{17... | collective-permute-start | bytes 104456 | tf_op jit(solution)/shard_map/ppermute | solution.py:210
  64.1 1.2 %collective-permute-done.2 = bf16[34,512]{1,0:T(8,128)(2,1)S(1)} collective-permute-done((bf16[34,512]{1,0:T(8,128)(2,1)S(1)}, bf16[34,512]{1,0:T(8,128)(2,1)S(1)}, u32[]{:S(2)}, u32[]{:S(2)}) %collective-permute-start.2) | collective-permute-done | bytes 34848 | tf_op jit(solution)/shard_map/ppermute | solution.py:210
  65.3 2.1 %collective-permute-start.3 = (bf16[34,512]{1,0:T(8,128)(2,1)S(1)}, bf16[34,512]{1,0:T(8,128)(2,1)S(1)}, u32[]{:S(2)}, u32[]{:S(2)}) collective-permute-start(bf16[34,512]{1,0:T(8,128)(2,1)S(1)} %pad_maximum_fusion.1), channel_id=1, source_target_pairs={{16,0},{32,16},{48,32},{64,48},{80,64},{96,80},{112,96},{17,1},{33... | collective-permute-start | bytes 104456 | tf_op jit(solution)/shard_map/ppermute | solution.py:211
  67.3 0.1 bitcast_reduce_fusion.lives
  67.5 0.1 reshape_reshape.3.refs_0_
  67.6 0.1 reduce.1
  67.7 0.1 reduce
  67.9 3.2 %collective-permute-done.3 = bf16[34,512]{1,0:T(8,128)(2,1)S(1)} collective-permute-done((bf16[34,512]{1,0:T(8,128)(2,1)S(1)}, bf16[34,512]{1,0:T(8,128)(2,1)S(1)}, u32[]{:S(2)}, u32[]{:S(2)}) %collective-permute-start.3) | collective-permute-done | bytes 34848 | tf_op jit(solution)/shard_map/ppermute | solution.py:211
  71.1 0.0 collective-permute-done.13.refs_9_
  71.1 0.0 collective-permute-done.15.refs_11_
  71.1 0.0 collective-permute-done.14.refs_10_
  71.1 0.0 collective-permute-done.16.refs_12_
  71.2 0.0 copy-start.5
  71.2 1.6 %copy-done.5 = bf16[2048,512]{1,0:T(8,128)(2,1)S(1)} copy-done((bf16[2048,512]{1,0:T(8,128)(2,1)S(1)}, bf16[2048,512]{1,0:T(8,128)(2,1)}, u32[]{:S(2)}) %copy-start.5) | copy-done | bytes 2097176
  72.8 1.2 %copy-done.9 = bf16[1024,512]{1,0:T(8,128)(2,1)S(1)} copy-done((bf16[1024,512]{1,0:T(8,128)(2,1)S(1)}, bf16[1024,512]{1,0:T(8,128)(2,1)}, u32[]{:S(2)}) %copy-start.9) | copy-done | bytes 1048600
  74.0 1.0 %copy-done.10 = bf16[512,512]{1,0:T(8,128)(2,1)S(1)} copy-done((bf16[512,512]{1,0:T(8,128)(2,1)S(1)}, bf16[512,512]{1,0:T(8,128)(2,1)}, u32[]{:S(2)}) %copy-start.10) | copy-done | bytes 524312
  75.0 1.0 %copy-done.11 = bf16[512,512]{1,0:T(8,128)(2,1)S(1)} copy-done((bf16[512,512]{1,0:T(8,128)(2,1)S(1)}, bf16[512,512]{1,0:T(8,128)(2,1)}, u32[]{:S(2)}) %copy-start.11) | copy-done | bytes 524312
  76.1 1.2 %copy-done.18 = f32[512,512]{1,0:T(8,128)S(1)} copy-done((f32[512,512]{1,0:T(8,128)S(1)}, f32[512,512]{1,0:T(8,128)}, u32[]{:S(2)}) %copy-start.18) | copy-done | bytes 1048600
  77.3 15.4 %late.1 = (bf16[2048,512]{1,0:T(8,128)(2,1)}, bf16[512,512]{1,0:T(8,128)(2,1)}) custom-call(s32[2048]{0:T(1024)S(1)} %fusion.12.table_index, s32[16]{0:T(128)S(1)} %copy-done.15, s32[16]{0:T(128)S(1)} %bitcast_reduce_fusion.lives, bf16[512,4,128]{2,1,0:T(4,128)(2,1)S(1)} %reshape_reshape.3.refs_0_, bf16[16,4,128]{2,1,0:T(4,128)(2,1)S(1)} %reshape.42.refs_1_, ...), custom_call_target="tpu_custom_call" | custom-call | flops 8000000000 | bytes 16000000 | tf_op jit(solution)/shard_map/late/pallas_call | solution.py:270
  (38 shorter events, 0.3 us)
Async XLA Ops:
  2.6 8.7 %collective-permute-start.5 = (bf16[32,4,128]{2,1,0:T(4,128)(2,1)S(1)}, bf16[32,4,128]{2,1,0:T(4,128)(2,1)S(1)}, u32[]{:S(2)}, u32[]{:S(2)}) collective-permute-start(bf16[32,4,128]{2,1,0:T(4,128)(2,1)S(1)} %reshape.46), channel_id=1, source_target_pairs={{0,3},{1,0},{2,1},{3,2},{4,7},{5,4},{6,5},{7,6},{8,11},{9,8},{10,9... | collective-permute-start | bytes 98312 | tf_op jit(solution)/shard_map/ppermute | solution.py:46
  5.1 3.2 %collective-permute-start.4 = (bf16[32,4,128]{2,1,0:T(4,128)(2,1)S(1)}, bf16[32,4,128]{2,1,0:T(4,128)(2,1)S(1)}, u32[]{:S(2)}, u32[]{:S(2)}) collective-permute-start(bf16[32,4,128]{2,1,0:T(4,128)(2,1)S(1)} %reshape.46), channel_id=1, source_target_pairs={{0,1},{1,2},{2,3},{3,0},{4,5},{5,6},{6,7},{7,4},{8,9},{9,10},{10,1... | collective-permute-start | bytes 98312 | tf_op jit(solution)/shard_map/ppermute | solution.py:46
  8.4 4.0 %collective-permute-start.6 = (bf16[32,4,128]{2,1,0:T(4,128)(2,1)S(1)}, bf16[32,4,128]{2,1,0:T(4,128)(2,1)S(1)}, u32[]{:S(2)}, u32[]{:S(2)}) collective-permute-start(bf16[32,4,128]{2,1,0:T(4,128)(2,1)S(1)} %collective-permute-done.4), channel_id=1, source_target_pairs={{0,1},{1,2},{2,3},{3,0},{4,5},{5,6},{6,7},{7,4},{8,9},{9,10},{10,1... | collective-permute-start | bytes 98312 | tf_op jit(solution)/shard_map/ppermute | solution.py:46
  12.4 8.6 %collective-permute-start.8 = (bf16[128,4,128]{2,1,0:T(4,128)(2,1)S(1)}, bf16[128,4,128]{2,1,0:T(4,128)(2,1)S(1)}, u32[]{:S(2)}, u32[]{:S(2)}) collective-permute-start(bf16[128,4,128]{2,1,0:T(4,128)(2,1)S(1)} %get-tuple-element.14), channel_id=1, source_target_pairs={{0,12},{1,13},{2,14},{3,15},{4,0},{5,1},{6,2},{7,3},{8,4},{9,5},{1... | collective-permute-start | bytes 393224 | tf_op jit(solution)/shard_map/ppermute | solution.py:46
  13.7 6.7 %collective-permute-start.7 = (bf16[128,4,128]{2,1,0:T(4,128)(2,1)S(1)}, bf16[128,4,128]{2,1,0:T(4,128)(2,1)S(1)}, u32[]{:S(2)}, u32[]{:S(2)}) collective-permute-start(bf16[128,4,128]{2,1,0:T(4,128)(2,1)S(1)} %get-tuple-element.14), channel_id=1, source_target_pairs={{0,4},{1,5},{2,6},{3,7},{4,8},{5,9},{6,10},{7,11},{8,12},{9,13},{1... | collective-permute-start | bytes 393224 | tf_op jit(solution)/shard_map/ppermute | solution.py:46
  16.3 27.8 %collective-permute-start.1 = (bf16[16,1,512]{2,1,0:T(2,128)(2,1)S(1)}, bf16[16,1,512]{2,1,0:T(2,128)(2,1)S(1)}, u32[]{:S(2)}, u32[]{:S(2)}) collective-permute-start(bf16[16,1,512]{2,1,0:T(2,128)(2,1)S(1)} %get-tuple-element.12), channel_id=1, source_target_pairs={{1,0},{2,1},{3,2},{4,3},{5,4},{6,5},{7,6},{8,7},{9,8},{10,9},{11,1... | collective-permute-start | bytes 49160 | tf_op jit(solution)/shard_map/ppermute | solution.py:208
  20.4 41.7 %collective-permute-start = (bf16[16,1,512]{2,1,0:T(2,128)(2,1)S(1)}, bf16[16,1,512]{2,1,0:T(2,128)(2,1)S(1)}, u32[]{:S(2)}, u32[]{:S(2)}) collective-permute-start(bf16[16,1,512]{2,1,0:T(2,128)(2,1)S(1)} %get-tuple-element.13), channel_id=1, source_target_pairs={{0,1},{1,2},{2,3},{3,4},{4,5},{5,6},{6,7},{7,8},{8,9},{9,10},{10,1... | collective-permute-start | bytes 49160 | tf_op jit(solution)/shard_map/ppermute | solution.py:207
  20.4 4.2 %collective-permute-start.9 = (bf16[128,4,128]{2,1,0:T(4,128)(2,1)S(1)}, bf16[128,4,128]{2,1,0:T(4,128)(2,1)S(1)}, u32[]{:S(2)}, u32[]{:S(2)}) collective-permute-start(bf16[128,4,128]{2,1,0:T(4,128)(2,1)S(1)} %collective-permute-done.7), channel_id=1, source_target_pairs={{0,4},{1,5},{2,6},{3,7},{4,8},{5,9},{6,10},{7,11},{8,12},{9,13},{1... | collective-permute-start | bytes 393224 | tf_op jit(solution)/shard_map/ppermute | solution.py:46
  24.7 16.6 %collective-permute-start.10 = (bf16[512,4,128]{2,1,0:T(4,128)(2,1)S(1)}, bf16[512,4,128]{2,1,0:T(4,128)(2,1)}, u32[]{:S(2)}, u32[]{:S(2)}) collective-permute-start(bf16[512,4,128]{2,1,0:T(4,128)(2,1)S(1)} %constant_dynamic-update-slice_fusion.4.refs_5_), channel_id=1, source_target_pairs={{0,32},{1,33},{2,34},{3,35},{4,36},{5,37},{6,38},{7,39},{8,40},{9,... | collective-permute-start | bytes 1572872 | tf_op jit(solution)/shard_map/ppermute | solution.py:46
  27.2 1.0 %copy-start = (bf16[16,32,512]{2,1,0:T(8,128)(2,1)S(1)}, bf16[16,32,512]{2,1,0:T(8,128)(2,1)}, u32[]{:S(2)}) copy-start(bf16[16,32,512]{2,1,0:T(8,128)(2,1)} %param.11) | copy-start | bytes 1572868
  28.2 0.7 copy-start.2
  28.9 1.6 %copy-start.4 = (bf16[2048,512]{1,0:T(8,128)(2,1)S(1)}, bf16[2048,512]{1,0:T(8,128)(2,1)}, u32[]{:S(2)}) copy-start(bf16[2048,512]{1,0:T(8,128)(2,1)} %refs_14_.1) | copy-start | bytes 6291460
  30.5 1.4 %copy-start.6 = (bf16[1536,512]{1,0:T(8,128)(2,1)S(1)}, bf16[1536,512]{1,0:T(8,128)(2,1)}, u32[]{:S(2)}) copy-start(bf16[1536,512]{1,0:T(8,128)(2,1)} %refs_18_.1) | copy-start | bytes 4718596
  31.9 1.2 %copy-start.8 = (bf16[1024,512]{1,0:T(8,128)(2,1)S(1)}, bf16[1024,512]{1,0:T(8,128)(2,1)}, u32[]{:S(2)}) copy-start(bf16[1024,512]{1,0:T(8,128)(2,1)} %refs_21_.1) | copy-start | bytes 3145732
  33.2 0.7 copy-start.14
  33.8 10.2 %copy-start.19 = (s32[2048]{0:T(1024)S(1)}, s32[2048]{0:T(1024)}, u32[]{:S(2)}) copy-start(s32[2048]{0:T(1024)} %param.13) | copy-start | bytes 24580
  33.8 33.5 %copy-start.3 = (s32[2048]{0:T(1024)S(1)}, s32[2048]{0:T(1024)}, u32[]{:S(2)}) copy-start(s32[2048]{0:T(1024)} %param.14) | copy-start | bytes 24580
  33.8 33.6 %copy-start.1 = (bf16[16,32,512]{2,1,0:T(8,128)(2,1)S(1)}, bf16[16,32,512]{2,1,0:T(8,128)(2,1)}, u32[]{:S(2)}) copy-start(bf16[16,32,512]{2,1,0:T(8,128)(2,1)} %param.11) | copy-start | bytes 1572868
  33.8 37.3 %copy-start.7 = (bf16[1536,512]{1,0:T(8,128)(2,1)S(1)}, bf16[1536,512]{1,0:T(8,128)(2,1)}, u32[]{:S(2)}) copy-start(bf16[1536,512]{1,0:T(8,128)(2,1)} %refs_18_.1) | copy-start | bytes 4718596
  33.8 37.3 %copy-start.12 = (f32[512]{0:T(512)S(1)}, f32[512]{0:T(512)}, u32[]{:S(2)}) copy-start(f32[512]{0:T(512)} %param.18) | copy-start | bytes 6148
  33.8 37.3 %copy-start.13 = (f32[512]{0:T(512)S(1)}, f32[512]{0:T(512)}, u32[]{:S(2)}) copy-start(f32[512]{0:T(512)} %param.21) | copy-start | bytes 6148
  33.9 37.3 %copy-start.15 = (s32[16]{0:T(128)S(1)}, s32[16]{0:T(128)}, u32[]{:S(2)}) copy-start(s32[16]{0:T(128)} %tiles.3) | copy-start | bytes 196
  38.4 2.0 %copy-start.16 = (f32[2048,512]{1,0:T(8,128)}, f32[2048,512]{1,0:T(8,128)S(1)}, u32[]{:S(2)}) copy-start(f32[2048,512]{1,0:T(8,128)S(1)} %get-tuple-element.6.refs_13_) | copy-start | bytes 12582916
  40.3 1.0 %copy-start.17 = (f32[512,512]{1,0:T(8,128)}, f32[512,512]{1,0:T(8,128)S(1)}, u32[]{:S(2)}) copy-start(f32[512,512]{1,0:T(8,128)S(1)} %get-tuple-element.7.refs_16_) | copy-start | bytes 3145732
  41.3 10.7 %collective-permute-start.11 = (bf16[512,4,128]{2,1,0:T(4,128)(2,1)S(1)}, bf16[512,4,128]{2,1,0:T(4,128)(2,1)}, u32[]{:S(2)}, u32[]{:S(2)}) collective-permute-start(bf16[512,4,128]{2,1,0:T(4,128)(2,1)S(1)} %constant_dynamic-update-slice_fusion.4.refs_5_), channel_id=1, source_target_pairs={{0,96},{1,97},{2,98},{3,99},{4,100},{5,101},{6,102},{7,103},{8,104... | collective-permute-start | bytes 1572872 | tf_op jit(solution)/shard_map/ppermute | solution.py:46
  41.3 17.6 %collective-permute-start.12 = (bf16[512,4,128]{2,1,0:T(4,128)(2,1)}, bf16[512,4,128]{2,1,0:T(4,128)(2,1)}, u32[]{:S(2)}, u32[]{:S(2)}) collective-permute-start(bf16[512,4,128]{2,1,0:T(4,128)(2,1)} %collective-permute-done.10.refs_6_), channel_id=1, source_target_pairs={{0,32},{1,33},{2,34},{3,35},{4,36},{5,37},{6,38},{7,39},{8,40},{9,... | collective-permute-start | bytes 1572872 | tf_op jit(solution)/shard_map/ppermute | solution.py:46
  44.1 27.0 %collective-permute-start.13 = (bf16[512,4,128]{2,1,0:T(4,128)(2,1)S(1)}, bf16[512,4,128]{2,1,0:T(4,128)(2,1)}, u32[]{:S(2)}, u32[]{:S(2)}) collective-permute-start(bf16[512,4,128]{2,1,0:T(4,128)(2,1)S(1)} %constant_dynamic-update-slice_fusion.4.refs_5_), channel_id=1, source_target_pairs={{0,16},{1,17},{2,18},{3,19},{4,20},{5,21},{6,22},{7,23},{8,24},{9,... | collective-permute-start | bytes 1572872 | tf_op jit(solution)/shard_map/ppermute | solution.py:42
  51.9 19.2 %collective-permute-start.14 = (bf16[512,4,128]{2,1,0:T(4,128)(2,1)}, bf16[512,4,128]{2,1,0:T(4,128)(2,1)}, u32[]{:S(2)}, u32[]{:S(2)}) collective-permute-start(bf16[512,4,128]{2,1,0:T(4,128)(2,1)} %collective-permute-done.10.refs_6_), channel_id=1, source_target_pairs={{0,16},{1,17},{2,18},{3,19},{4,20},{5,21},{6,22},{7,23},{8,24},{9,... | collective-permute-start | bytes 1572872 | tf_op jit(solution)/shard_map/ppermute | solution.py:42
  52.0 19.1 %collective-permute-start.15 = (bf16[512,4,128]{2,1,0:T(4,128)(2,1)}, bf16[512,4,128]{2,1,0:T(4,128)(2,1)}, u32[]{:S(2)}, u32[]{:S(2)}) collective-permute-start(bf16[512,4,128]{2,1,0:T(4,128)(2,1)} %collective-permute-done.11.refs_7_), channel_id=1, source_target_pairs={{0,16},{1,17},{2,18},{3,19},{4,20},{5,21},{6,22},{7,23},{8,24},{9,... | collective-permute-start | bytes 1572872 | tf_op jit(solution)/shard_map/ppermute | solution.py:42
  58.9 12.2 %collective-permute-start.16 = (bf16[512,4,128]{2,1,0:T(4,128)(2,1)}, bf16[512,4,128]{2,1,0:T(4,128)(2,1)}, u32[]{:S(2)}, u32[]{:S(2)}) collective-permute-start(bf16[512,4,128]{2,1,0:T(4,128)(2,1)} %collective-permute-done.12.refs_8_), channel_id=1, source_target_pairs={{0,16},{1,17},{2,18},{3,19},{4,20},{5,21},{6,22},{7,23},{8,24},{9,... | collective-permute-start | bytes 1572872 | tf_op jit(solution)/shard_map/ppermute | solution.py:42
  62.1 3.1 %collective-permute-start.2 = (bf16[34,512]{1,0:T(8,128)(2,1)S(1)}, bf16[34,512]{1,0:T(8,128)(2,1)S(1)}, u32[]{:S(2)}, u32[]{:S(2)}) collective-permute-start(bf16[34,512]{1,0:T(8,128)(2,1)S(1)} %pad_maximum_fusion), channel_id=1, source_target_pairs={{0,16},{16,32},{32,48},{48,64},{64,80},{80,96},{96,112},{1,17},{17... | collective-permute-start | bytes 104456 | tf_op jit(solution)/shard_map/ppermute | solution.py:210
  65.3 5.8 %collective-permute-start.3 = (bf16[34,512]{1,0:T(8,128)(2,1)S(1)}, bf16[34,512]{1,0:T(8,128)(2,1)S(1)}, u32[]{:S(2)}, u32[]{:S(2)}) collective-permute-start(bf16[34,512]{1,0:T(8,128)(2,1)S(1)} %pad_maximum_fusion.1), channel_id=1, source_target_pairs={{16,0},{32,16},{48,32},{64,48},{80,64},{96,80},{112,96},{17,1},{33... | collective-permute-start | bytes 104456 | tf_op jit(solution)/shard_map/ppermute | solution.py:211
  71.2 1.6 %copy-start.5 = (bf16[2048,512]{1,0:T(8,128)(2,1)S(1)}, bf16[2048,512]{1,0:T(8,128)(2,1)}, u32[]{:S(2)}) copy-start(bf16[2048,512]{1,0:T(8,128)(2,1)} %refs_14_.1) | copy-start | bytes 6291460
  72.8 1.2 %copy-start.9 = (bf16[1024,512]{1,0:T(8,128)(2,1)S(1)}, bf16[1024,512]{1,0:T(8,128)(2,1)}, u32[]{:S(2)}) copy-start(bf16[1024,512]{1,0:T(8,128)(2,1)} %refs_21_.1) | copy-start | bytes 3145732
  74.0 1.0 %copy-start.10 = (bf16[512,512]{1,0:T(8,128)(2,1)S(1)}, bf16[512,512]{1,0:T(8,128)(2,1)}, u32[]{:S(2)}) copy-start(bf16[512,512]{1,0:T(8,128)(2,1)} %refs_19_.1) | copy-start | bytes 1572868
  75.0 1.0 %copy-start.11 = (bf16[512,512]{1,0:T(8,128)(2,1)S(1)}, bf16[512,512]{1,0:T(8,128)(2,1)}, u32[]{:S(2)}) copy-start(bf16[512,512]{1,0:T(8,128)(2,1)} %refs_22_.1) | copy-start | bytes 1572868
  76.1 1.2 %copy-start.18 = (f32[512,512]{1,0:T(8,128)S(1)}, f32[512,512]{1,0:T(8,128)}, u32[]{:S(2)}) copy-start(f32[512,512]{1,0:T(8,128)} %copy-done.17) | copy-start | bytes 3145732

commit v2 on v1

--- a/solution.py
+++ b/solution.py
@@ -9,8 +9,10 @@
 BLK = 128
 GROUP = 4
 ROWS = GROUP * BLK
-PIECE = 512
 RIM = 40
+NEAR = 5
+FAR = 8
+VMEM = 56 << 20
 BF = jnp.bfloat16
 F32 = jnp.float32
 
@@ -77,13 +79,61 @@
     return (lax.broadcasted_iota(jnp.int32, (BLK, BLK), 0) == recv_row).astype(BF)
 
 
-def early_kernel(tiles, edge_ref, recv_ref, node_ref, we_ref, wr_ref, wn_ref, pre_ref, nf_ref, got_ref):
+def fetch(count, unroll, entry, table, sent):
+    def body(i, carry):
+        for u in range(unroll):
+            slot, row = entry(i * unroll + u)
+            sent[pl.ds(pl.multiple_of(slot * 4, 4), 4), :] = table[row].astype(F32)
+        return carry
+
+    lax.fori_loop(0, count, body, 0)
+
+
+def sent_rows(sent):
+    return jnp.concatenate(
+        [sent[pl.ds(j, ROWS, stride=4), :].astype(BF) for j in range(4)], axis=1
+    )
+
+
+def load_table(pieces, table, sem):
+    copies = []
+    start = 0
+    for i, piece in enumerate(pieces):
+        rows = piece.shape[0]
+        copies.append(pltpu.make_async_copy(piece, table.at[pl.ds(start, rows)], sem.at[i]))
+        start += rows
+    for copy in copies:
+        copy.start()
+    return copies
+
+
+def early_kernel(near_index, tiles, *refs):
+    pieces = refs[:NEAR]
+    (
+        edge_ref,
+        recv_ref,
+        node_ref,
+        we_ref,
+        ws_ref,
+        wr_ref,
+        wn_ref,
+        pre_ref,
+        nf_ref,
+        table,
+        sent,
+        got_ref,
+        sem,
+    ) = refs[NEAR:]
     step = pl.program_id(0)
 
     @pl.when(step == 0)
     def _():
+        copies = load_table(pieces, table, sem)
         nf_ref[...] = dot(node_ref[...], wn_ref[...])
-
+        for copy in copies:
+            copy.wait()
+
+    fetch(ROWS // 16, 16, lambda e: (e, near_index[step * ROWS + e]), table, sent)
     for k in range(GROUP):
         tile = pl.multiple_of(tiles[step * GROUP + k] * BLK, BLK)
         hot = chosen(recv_ref[k : k + 1, :])
@@ -94,16 +144,15 @@
             preferred_element_type=F32,
         )
         got_ref[k * BLK : (k + 1) * BLK, :] = rows.astype(BF)
-    pre_ref[...] = dot(edge_ref[...], we_ref[...]) + dot(got_ref[...], wr_ref[...])
-
-
-def late_kernel(
-    table_index,
-    tiles,
-    lives,
-    *refs,
-):
-    pieces = refs[:13]
+    pre_ref[...] = (
+        dot(edge_ref[...], we_ref[...])
+        + dot(got_ref[...], wr_ref[...])
+        + dot(sent_rows(sent), ws_ref[...])
+    )
+
+
+def late_kernel(far_list, far_count, tiles, lives, *refs):
+    pieces = refs[:FAR]
     (
         pre_ref,
         edge_ref,
@@ -122,35 +171,23 @@
         sent,
         agg,
         sem,
-    ) = refs[13:]
+    ) = refs[FAR:]
     step = pl.program_id(0)
+    sent[...] = jnp.zeros_like(sent)
 
     @pl.when(step == 0)
     def _():
-        copies = []
-        start = 0
-        for i, piece in enumerate(pieces):
-            rows = piece.shape[0]
-            copies.append(pltpu.make_async_copy(piece, table.at[pl.ds(start, rows)], sem.at[i]))
-            start += rows
-        for copy in copies:
-            copy.start()
+        copies = load_table(pieces, table, sem)
         agg[...] = jnp.zeros_like(agg)
         for copy in copies:
             copy.wait()
 
-    def fetch(i, carry):
-        for u in range(16):
-            e = i * 16 + u
-            row = table[table_index[step * ROWS + e]]
-            sent[pl.ds(pl.multiple_of(e * 4, 4), 4), :] = row.astype(F32)
-        return carry
-
-    lax.fori_loop(0, ROWS // 16, fetch, 0)
-    send = jnp.concatenate(
-        [sent[pl.ds(j, ROWS, stride=4), :].astype(BF) for j in range(4)], axis=1
-    )
-    hidden = silu(pre_ref[...] + dot(send, ws_ref[...])).astype(BF)
+    def entry(i):
+        packed = far_list[step * ROWS + i]
+        return packed % 1024, packed // 1024
+
+    fetch((far_count[step] + 7) // 8, 8, entry, table, sent)
+    hidden = silu(pre_ref[...] + dot(sent_rows(sent), ws_ref[...])).astype(BF)
     message = normed(dot(hidden, w2_ref[...]), eg_ref[...]).astype(BF)
     place = lax.broadcasted_iota(jnp.int32, (BLK, F), 0)
     for k in range(GROUP):
@@ -170,6 +207,17 @@
         node_out_ref[...] = (
             node_ref[...].astype(F32) + normed(second, ng_ref[...])
         ).astype(BF)
+
+
+def far_lists(is_far, far_index, steps):
+    place = jnp.arange(ROWS, dtype=jnp.int32)
+    far = is_far.reshape(steps, ROWS)
+    flag = far.astype(jnp.int32)
+    before = place[:, None] > place[None, :]
+    rank = jnp.sum(jnp.where(before[None], flag[:, None, :], 0), 2)
+    packed = far_index.reshape(steps, ROWS) * 1024 + place - ROWS
+    hit = (rank[:, None, :] == place[None, :, None]) & far[:, None, :]
+    return (ROWS + jnp.sum(jnp.where(hit, packed[:, None, :], 0), 2)).reshape(-1), jnp.sum(flag, 1)
 
 
 def per_device(
@@ -191,25 +239,28 @@
     lat_count, lon_count = lax.axis_size("lat"), lax.axis_size("lon")
     grid_cols = patch_cols * lon_count
     blocks = block_tile.shape[0]
+    steps = blocks // GROUP
     nodes = patch_rows * patch_cols
     own_rows = node_latent.reshape(nodes, features)
-
-    coarse_own = node_latent[::4, ::4].reshape(-1, 4, 128)
-    line = jnp.concatenate(ring(coarse_own, "z"), 0)
-    plane = jnp.concatenate(ring(line, "y"), 0)
-    halves = ring(plane, "x")
-    far_pieces = list(halves) + [other_core(part) for part in halves]
+    lanes = lambda a: a.reshape(-1, 4, 128)
 
     right = [(i, (i + 1) % lon_count) for i in range(lon_count)]
     left = [(j, i) for i, j in right]
     up = [(i, i + 1) for i in range(lat_count - 1)]
     down = [(j, i) for i, j in up]
+
+    coarse_own = lanes(node_latent[::4, ::4])
     west = lax.ppermute(node_latent[:, -1:], "lon", right)
     east = lax.ppermute(node_latent[:, :1], "lon", left)
+    line = jnp.concatenate(ring(coarse_own, "z"), 0)
+    line, west, east = lax.optimization_barrier((line, west, east))
     row_of = lambda r: jnp.concatenate([west[r], node_latent[r], east[r]], 0)
     north = lax.ppermute(row_of(patch_rows - 1), "lat", up)
     south = lax.ppermute(row_of(0), "lat", down)
-    lanes = lambda a: a.reshape(-1, 4, 128)
+    plane = jnp.concatenate(ring(line, "y"), 0)
+    plane, north, south = lax.optimization_barrier((plane, north, south))
+    own, ahead, behind, across = ring(plane, "x")
+
     pad = lambda a: jnp.pad(lanes(a), ((0, RIM - patch_cols - 2), (0, 0), (0, 0)))
     near_pieces = [lanes(own_rows), lanes(west), lanes(east), pad(north), pad(south)]
 
@@ -225,7 +276,8 @@
     near_index = jnp.where(
         row < 0, rim + col + 1, jnp.where(row >= patch_rows, rim + RIM + col + 1, inner)
     )
-    near_count = rim + 2 * RIM
+    no_row = rim + patch_cols + 2
+    near_index = jnp.where(is_near, near_index, no_row)
     src_lat, src_lon = send_row // patch_rows, send_col // patch_cols
     src_core, core = src_lat % 2, lat_index % 2
     at_x = ring_place((src_lat // 2 - lat_index // 2) % 4, src_core)
@@ -234,46 +286,65 @@
     half = jnp.where(src_core == core, 0, 1)
     within = send_row % patch_rows // 4 * (patch_cols // 4) + send_col % patch_cols // 4
     per = patch_rows // 4 * (patch_cols // 4)
-    far_index = near_count + ((((half * 4 + at_x) * 4 + at_y) * 4 + at_z) * per + within)
-    table_index = jnp.where(is_near, near_index, far_index)
-    recv_rows = receiver.reshape(blocks // GROUP, GROUP, BLK)
+    far_index = (((half * 4 + at_x) * 4 + at_y) * 4 + at_z) * per + within
+    far_list, far_count = far_lists((receiver >= 0) & ~is_near, far_index, steps)
+    recv_rows = receiver.reshape(steps, GROUP, BLK)
     lives = jnp.sum((receiver >= 0).astype(jnp.int32).reshape(blocks, BLK), 1)
 
-    steps = blocks // GROUP
     whole = lambda shape: pl.BlockSpec(shape, lambda i, *_: (0,) * len(shape))
     part = pl.BlockSpec((ROWS, F), lambda i, *_: (i, 0))
     recv_spec = pl.BlockSpec((None, GROUP, BLK), lambda i, *_: (i, 0, 0))
     weight = lambda k: pl.BlockSpec((F, F), lambda i, *_: (k, 0))
     anywhere = pl.BlockSpec(memory_space=pl.ANY)
+    near_rows = sum(piece.shape[0] for piece in near_pieces)
     pre, node_first = pl.pallas_call(
         early_kernel,
         name="early",
         grid_spec=pltpu.PrefetchScalarGridSpec(
-            num_scalar_prefetch=1,
+            num_scalar_prefetch=2,
             grid=(steps,),
-            in_specs=[part, recv_spec, whole((nodes, F)), weight(0), weight(2), weight(0)],
+            in_specs=[anywhere] * NEAR
+            + [part, recv_spec, whole((nodes, F)), weight(0), weight(1), weight(2), weight(0)],
             out_specs=[part, whole((nodes, F))],
-            scratch_shapes=[pltpu.VMEM((ROWS, F), BF)],
+            scratch_shapes=[
+                pltpu.VMEM((near_rows, 4, 128), BF),
+                pltpu.VMEM((ROWS * 4, 128), F32),
+                pltpu.VMEM((ROWS, F), BF),
+                pltpu.SemaphoreType.DMA((NEAR,)),
+            ],
         ),
         out_shape=[
             jax.ShapeDtypeStruct((blocks * BLK, F), F32),
             jax.ShapeDtypeStruct((nodes, F), F32),
         ],
-        compiler_params=pltpu.CompilerParams(vmem_limit_bytes=20 << 20),
+        compiler_params=pltpu.CompilerParams(vmem_limit_bytes=VMEM),
         cost_estimate=pl.CostEstimate(
-            flops=6 * 10**9, bytes_accessed=9 * 10**6, transcendentals=0
+            flops=4 * 10**9, bytes_accessed=10 * 10**6, transcendentals=0
         ),
-    )(block_tile, edge_latent, recv_rows, own_rows, w_first, w_first, w_node_first)
-
-    pieces = near_pieces + far_pieces
-    table_rows = sum(piece.shape[0] for piece in pieces)
+    )(
+        near_index,
+        block_tile,
+        *near_pieces,
+        edge_latent,
+        recv_rows,
+        own_rows,
+        w_first,
+        w_first,
+        w_first,
+        w_node_first,
+    )
+
+    across, pre = lax.optimization_barrier((across, pre))
+    halves = [own, ahead, behind, across]
+    far_pieces = halves + [other_core(piece) for piece in halves]
+    far_rows = sum(piece.shape[0] for piece in far_pieces)
     edge_out, node_out = pl.pallas_call(
         late_kernel,
         name="late",
         grid_spec=pltpu.PrefetchScalarGridSpec(
-            num_scalar_prefetch=3,
+            num_scalar_prefetch=4,
             grid=(steps,),
-            in_specs=[anywhere] * len(pieces)
+            in_specs=[anywhere] * FAR
             + [
                 part,
                 part,
@@ -289,25 +360,26 @@
             ],
             out_specs=[part, whole((nodes, F))],
             scratch_shapes=[
-                pltpu.VMEM((table_rows, 4, 128), BF),
-                pltpu.VMEM((ROWS * 4, 128), F32),
+                pltpu.VMEM((far_rows, 4, 128), BF),
+                pltpu.VMEM((ROWS * 4 + 32, 128), F32),
                 pltpu.VMEM((nodes, F), F32),
-                pltpu.SemaphoreType.DMA((len(pieces),)),
+                pltpu.SemaphoreType.DMA((FAR,)),
             ],
         ),
         out_shape=[
             jax.ShapeDtypeStruct((blocks * BLK, F), BF),
             jax.ShapeDtypeStruct((nodes, F), BF),
         ],
-        compiler_params=pltpu.CompilerParams(vmem_limit_bytes=40 << 20),
+        compiler_params=pltpu.CompilerParams(vmem_limit_bytes=VMEM),
         cost_estimate=pl.CostEstimate(
-            flops=8 * 10**9, bytes_accessed=16 * 10**6, transcendentals=0
+            flops=4 * 10**9, bytes_accessed=16 * 10**6, transcendentals=2 * 10**6
         ),
     )(
-        table_index,
+        far_list,
+        far_count,
         block_tile,
         lives,
-        *pieces,
+        *far_pieces,
         pre,
         edge_latent,
         recv_rows,

time: 93.4 us -> 92.9 us (level)
  the two profiles are of different devices: /device:TPU:1 before, /device:TPU:31 now
where the time goes in v2:
time: 92.9 us; the launch traced here: 92.7 us
  Pallas kernels  32.1 us (35%)
  starting transfers between devices  29 us (31%)
  waiting for transfers between devices  14.8 us (16%)
  local copies, waits for them, and re-layouts  9.95 us (11%)
  other arithmetic  5.86 us (6%)
  between operations  1.01 us (1%)
    pallas_call x1, Pallas kernels, per_device(): pl.pallas_call(late_kernel, name='late', grid_spec=pltpu.PrefetchScalarGr...  19.2 us
    ppermute x9, starting transfers between devices, move(): return lax.ppermute(value, ('lat', 'lon'), shift(axis, by_core))  17.6 us
    ppermute x9, waiting for transfers between devices, move(): return lax.ppermute(value, ('lat', 'lon'), shift(axis, by_core))  14.1 us
    pallas_call x1, Pallas kernels, per_device(): pl.pallas_call(early_kernel, name='early', grid_spec=pltpu.PrefetchScalar...  12.9 us
    ppermute x1, starting transfers between devices, per_device(): south = lax.ppermute(row_of(0), 'lat', down)  7.24 us
    another operation x1, local copies, waits for them, and re-layouts, per_device(): lanes = lambda a: a.reshape(-1, 4, 128)  1.96 us
    slice x1, local copies, waits for them, and re-layouts, per_device(): coarse_own = lanes(node_latent[::4, ::4])  1.94 us
  transfers between devices with their start and end apart: 17, of which 4 were waited for; matrix products, arithmetic and copies ran while one was open for 14% of the time, Pallas kernels for 14%

profile of v2, /device:TPU:31, one launch (start us, length us, event | category | flops | bytes accessed | tf_op | source)
XLA Modules:
  0.0 92.7 jit_solution(2448331187448404353)
XLA Ops:
  0.6 1.9 %slice.27 = bf16[4,8,512]{2,1,0:T(8,128)(2,1)S(1)} slice(bf16[16,32,512]{2,1,0:T(8,128)(2,1)} %param.11), slice={[0:16:4], [0:32:4], [0:512:1]} | slice | bytes 65536 | tf_op jit(solution)/shard_map/slice | solution.py:252
  2.6 1.7 %collective-permute-start.1 = (bf16[32,4,128]{2,1,0:T(4,128)(2,1)S(1)}, bf16[32,4,128]{2,1,0:T(4,128)(2,1)S(1)}, u32[]{:S(2)}, u32[]{:S(2)}) collective-permute-start(bf16[32,4,128]{2,1,0:T(4,128)(2,1)S(1)} %reshape.84), channel_id=1, source_target_pairs={{0,3},{1,0},{2,1},{3,2},{4,7},{5,4},{6,5},{7,6},{8,11},{9,8},{10,9... | collective-permute-start | bytes 98312 | tf_op jit(solution)/shard_map/ppermute | solution.py:48
  4.3 2.2 %collective-permute-start = (bf16[32,4,128]{2,1,0:T(4,128)(2,1)S(1)}, bf16[32,4,128]{2,1,0:T(4,128)(2,1)S(1)}, u32[]{:S(2)}, u32[]{:S(2)}) collective-permute-start(bf16[32,4,128]{2,1,0:T(4,128)(2,1)S(1)} %reshape.84), channel_id=1, source_target_pairs={{0,1},{1,2},{2,3},{3,0},{4,5},{5,6},{6,7},{7,4},{8,9},{9,10},{10,1... | collective-permute-start | bytes 98312 | tf_op jit(solution)/shard_map/ppermute | solution.py:48
  6.5 1.0 %fusion.24 = (bf16[16,1,512]{2,1,0:T(2,128)(2,1)S(1)}, bf16[16,1,512]{2,1,0:T(2,128)(2,1)S(1)}) fusion(bf16[16,32,512]{2,1,0:T(8,128)(2,1)} %param.11), kind=kLoop, calls=%fused_computation.96 | loop fusion | bytes 65536 | tf_op jit(solution)/shard_map/slice | solution.py:254
  7.5 1.6 %collective-permute-start.4 = (bf16[16,1,512]{2,1,0:T(2,128)(2,1)S(1)}, bf16[16,1,512]{2,1,0:T(2,128)(2,1)S(1)}, u32[]{:S(2)}, u32[]{:S(2)}) collective-permute-start(bf16[16,1,512]{2,1,0:T(2,128)(2,1)S(1)} %get-tuple-element.32), channel_id=1, source_target_pairs={{1,0},{2,1},{3,2},{4,3},{5,4},{6,5},{7,6},{8,7},{9,8},{10,9},{11,1... | collective-permute-start | bytes 49160 | tf_op jit(solution)/shard_map/ppermute | solution.py:254
  9.2 0.0 collective-permute-start.3
  9.2 0.8 slice_bitcast_fusion
  9.9 1.3 %select_select_fusion = (s32[2048]{0:T(1024)}, pred[2048]{0:T(1024)(128)(4,1)S(1)}, s32[2048]{0:T(1024)S(1)}) fusion(s32[]{:T(128)S(6)} %mul.40, s32[2048]{0:T(1024)} %param.13, s32[]{:T(128)S(6)} %mul.41, s32[]{:T(128)S(6)} %select_n.157, s32[]{:T(128)S(6)} %select_n.151, s32[]{:T(128)S(6)} %select_n.144, s32[]{:T(128)S(6)} %select_n.141), kind=kLoop, calls=%fused_computation.67 | loop fusion | flops 462848 | bytes 26648 | tf_op jit(solution)/shard_map/jit(_where)/select_n | solution.py:280
  11.3 0.0 collective-permute-done
  11.3 4.6 %collective-permute-start.2 = (bf16[32,4,128]{2,1,0:T(4,128)(2,1)S(1)}, bf16[32,4,128]{2,1,0:T(4,128)(2,1)S(1)}, u32[]{:S(2)}, u32[]{:S(2)}) collective-permute-start(bf16[32,4,128]{2,1,0:T(4,128)(2,1)S(1)} %collective-permute-done), channel_id=1, source_target_pairs={{0,1},{1,2},{2,3},{3,0},{4,5},{5,6},{6,7},{7,4},{8,9},{9,10},{10,1... | collective-permute-start | bytes 98312 | tf_op jit(solution)/shard_map/ppermute | solution.py:48
  15.9 1.4 %bitcast_reduce_fusion = (s32[16]{0:T(128)}, pred[2048]{0:T(1024)(128)(4,1)S(1)}) fusion(s32[2048]{0:T(1024)} %param.14), kind=kLoop, calls=%fused_computation.66 | loop fusion | flops 6128 | bytes 10304 | tf_op jit(solution)/shard_map/reduce_sum | solution.py:292
  17.3 2.0 %reshape_reshape.3.refs_0_ = bf16[512,4,128]{2,1,0:T(4,128)(2,1)} reshape(bf16[16,32,512]{2,1,0:T(8,128)(2,1)} %param.11) | data formatting | bytes 1048576 | tf_op jit(solution)/shard_map/reshape;reshape | solution.py:245
  19.3 0.0 collective-permute-done.1
  19.3 0.0 collective-permute-done.2
  19.3 0.1 pad_maximum_fusion.1
  19.4 0.0 collective-permute-done.4
  19.4 0.0 collective-permute-done.3
  19.4 0.1 collective-permute-start.6
  19.5 1.5 %collective-permute-start.5 = (bf16[128,4,128]{2,1,0:T(4,128)(2,1)S(1)}, bf16[128,4,128]{2,1,0:T(4,128)(2,1)S(1)}, u32[]{:S(2)}, u32[]{:S(2)}) collective-permute-start(bf16[128,4,128]{2,1,0:T(4,128)(2,1)S(1)} %pad_maximum_fusion.1), channel_id=1, source_target_pairs={{0,4},{1,5},{2,6},{3,7},{4,8},{5,9},{6,10},{7,11},{8,12},{9,13},{1... | collective-permute-start | bytes 393224 | tf_op jit(solution)/shard_map/ppermute | solution.py:48
  20.9 3.6 %collective-permute-done.5 = bf16[128,4,128]{2,1,0:T(4,128)(2,1)S(1)} collective-permute-done((bf16[128,4,128]{2,1,0:T(4,128)(2,1)S(1)}, bf16[128,4,128]{2,1,0:T(4,128)(2,1)S(1)}, u32[]{:S(2)}, u32[]{:S(2)}) %collective-permute-start.5) | collective-permute-done | bytes 131104 | tf_op jit(solution)/shard_map/ppermute | solution.py:48
  24.6 1.4 %collective-permute-start.7 = (bf16[128,4,128]{2,1,0:T(4,128)(2,1)S(1)}, bf16[128,4,128]{2,1,0:T(4,128)(2,1)S(1)}, u32[]{:S(2)}, u32[]{:S(2)}) collective-permute-start(bf16[128,4,128]{2,1,0:T(4,128)(2,1)S(1)} %collective-permute-done.5), channel_id=1, source_target_pairs={{0,4},{1,5},{2,6},{3,7},{4,8},{5,9},{6,10},{7,11},{8,12},{9,13},{1... | collective-permute-start | bytes 393224 | tf_op jit(solution)/shard_map/ppermute | solution.py:48
  26.0 1.3 %collective-permute-start.8 = (bf16[34,512]{1,0:T(8,128)(2,1)S(1)}, bf16[34,512]{1,0:T(8,128)(2,1)S(1)}, u32[]{:S(2)}, u32[]{:S(2)}) collective-permute-start(bf16[34,512]{1,0:T(8,128)(2,1)S(1)} %pad_maximum_fusion.2), channel_id=1, source_target_pairs={{0,16},{16,32},{32,48},{48,64},{64,80},{80,96},{96,112},{1,17},{17... | collective-permute-start | bytes 104456 | tf_op jit(solution)/shard_map/ppermute | solution.py:258
  27.3 7.2 %collective-permute-start.9 = (bf16[34,512]{1,0:T(8,128)(2,1)S(1)}, bf16[34,512]{1,0:T(8,128)(2,1)S(1)}, u32[]{:S(2)}, u32[]{:S(2)}) collective-permute-start(bf16[34,512]{1,0:T(8,128)(2,1)S(1)} %pad_maximum_fusion.3), channel_id=1, source_target_pairs={{16,0},{32,16},{48,32},{64,48},{80,64},{96,80},{112,96},{17,1},{33... | collective-permute-start | bytes 104456 | tf_op jit(solution)/shard_map/ppermute | solution.py:259
  34.6 0.0 collective-permute-done.6
  34.6 0.0 collective-permute-done.7
  34.6 0.4 pad_maximum_fusion.refs_0_
  35.0 0.0 copy-start
  35.0 0.0 collective-permute-done.8
  35.0 0.4 collective-permute-done.9
  35.4 3.9 %collective-permute-start.10 = (bf16[512,4,128]{2,1,0:T(4,128)(2,1)S(1)}, bf16[512,4,128]{2,1,0:T(4,128)(2,1)S(1)}, u32[]{:S(2)}, u32[]{:S(2)}) collective-permute-start(bf16[512,4,128]{2,1,0:T(4,128)(2,1)S(1)} %pad_maximum_fusion.refs_0_), channel_id=1, source_target_pairs={{0,32},{1,33},{2,34},{3,35},{4,36},{5,37},{6,38},{7,39},{8,40},{9,... | collective-permute-start | bytes 1572872 | tf_op jit(solution)/shard_map/ppermute | solution.py:48
  39.4 0.1 iota_compare_fusion.1
  39.5 0.1 collective-permute-start.11
  39.5 10.5 %collective-permute-done.10.refs_1_ = bf16[512,4,128]{2,1,0:T(4,128)(2,1)S(1)} collective-permute-done((bf16[512,4,128]{2,1,0:T(4,128)(2,1)S(1)}, bf16[512,4,128]{2,1,0:T(4,128)(2,1)S(1)}, u32[]{:S(2)}, u32[]{:S(2)}) %collective-permute-start.10) | collective-permute-done | bytes 524320 | tf_op jit(solution)/shard_map/ppermute | solution.py:48
  50.0 2.2 %collective-permute-start.12 = (bf16[512,4,128]{2,1,0:T(4,128)(2,1)S(1)}, bf16[512,4,128]{2,1,0:T(4,128)(2,1)S(1)}, u32[]{:S(2)}, u32[]{:S(2)}) collective-permute-start(bf16[512,4,128]{2,1,0:T(4,128)(2,1)S(1)} %collective-permute-done.10.refs_1_), channel_id=1, source_target_pairs={{0,32},{1,33},{2,34},{3,35},{4,36},{5,37},{6,38},{7,39},{8,40},{9,... | collective-permute-start | bytes 1572872 | tf_op jit(solution)/shard_map/ppermute | solution.py:48
  52.2 0.6 select_reduce_fusion.1
  52.8 0.1 reduce
  52.9 0.1 reduce.1
  53.0 0.6 reshape.86.refs_2_
  53.6 0.6 reshape.85.refs_1_
  54.3 0.3 collective-permute-start.13
  54.6 0.6 pad.7.refs_3_
  55.3 0.6 pad.8.refs_4_
  55.9 12.9 %early.1 = (f32[2048,512]{1,0:T(8,128)}, f32[512,512]{1,0:T(8,128)}) custom-call(s32[2048]{0:T(1024)} %get-tuple-element.26.near_index, s32[16]{0:T(128)} %tiles.3, bf16[512,4,128]{2,1,0:T(4,128)(2,1)} %reshape_reshape.3.refs_0_, bf16[16,4,128]{2,1,0:T(4,128)(2,1)} %reshape.85.refs_1_, bf16[16,4,128]{2,1,0:T(4,128)(2,1)} %reshape.86.refs_2_, ...), custom_call_target="tpu_custom_call" | custom-call | flops 4000000000 | bytes 10000000 | tf_op jit(solution)/shard_map/early/pallas_call | solution.py:300
  68.8 0.0 copy-done
  68.8 0.0 copy-done.1
  68.8 0.3 collective-permute-start.14
  69.1 0.0 collective-permute-done.11.refs_2_
  69.1 0.3 collective-permute-start.15
  69.4 0.0 collective-permute-done.12.refs_3_
  69.4 0.3 collective-permute-start.16
  69.7 1.0 %select_reduce_fusion = s32[4,512]{1,0:T(4,128)S(1)} fusion(s32[4,512]{1,0:T(4,128)S(1)} %add_add_fusion, s32[4,512]{1,0:T(4,128)S(1)} %select_reduce_fusion.1, pred[4,512]{1,0:T(4,128)(4,1)S(1)} %reshape.81), kind=kLoop, calls=%fused_computation | loop fusion | flops 4192256 | bytes 26624 | tf_op jit(solution)/shard_map/reduce_sum | solution.py:220
  70.7 0.6 copy.13
  71.3 0.7 convert_reduce_fusion.far_count
  72.0 0.0 collective-permute-done.13.refs_4_
  72.0 0.0 collective-permute-done.15.refs_6_
  72.0 0.0 collective-permute-done.14.refs_5_
  72.0 0.0 copy-start.5
  72.0 0.3 collective-permute-done.16.refs_7_
  72.3 0.0 copy-done.2
  72.3 0.5 copy-done.4
  72.8 0.2 copy-done.6
  73.0 0.2 copy-done.5
  73.2 0.2 copy-done.7
  73.4 19.2 %late.1 = (bf16[2048,512]{1,0:T(8,128)(2,1)}, bf16[512,512]{1,0:T(8,128)(2,1)}) custom-call(s32[2048]{0:T(1024)} %bitcast.26, s32[4]{0:T(128)} %convert_reduce_fusion.far_count, s32[16]{0:T(128)} %tiles.3, s32[16]{0:T(128)} %get-tuple-element.28.lives, bf16[512,4,128]{2,1,0:T(4,128)(2,1)} %copy-done, bf16[512,4,128]{2,1,0:T(4,128)(2,1)} %copy-done.1, ...), custom_call_target="tpu_custom_call" | custom-call | flops 4000000000 | bytes 16000000 | tf_op jit(solution)/shard_map/late/pallas_call | solution.py:341
  (19 shorter events, 0.2 us)
Async XLA Ops:
  2.6 16.7 %collective-permute-start.1 = (bf16[32,4,128]{2,1,0:T(4,128)(2,1)S(1)}, bf16[32,4,128]{2,1,0:T(4,128)(2,1)S(1)}, u32[]{:S(2)}, u32[]{:S(2)}) collective-permute-start(bf16[32,4,128]{2,1,0:T(4,128)(2,1)S(1)} %reshape.84), channel_id=1, source_target_pairs={{0,3},{1,0},{2,1},{3,2},{4,7},{5,4},{6,5},{7,6},{8,11},{9,8},{10,9... | collective-permute-start | bytes 98312 | tf_op jit(solution)/shard_map/ppermute | solution.py:48
  4.3 7.0 %collective-permute-start = (bf16[32,4,128]{2,1,0:T(4,128)(2,1)S(1)}, bf16[32,4,128]{2,1,0:T(4,128)(2,1)S(1)}, u32[]{:S(2)}, u32[]{:S(2)}) collective-permute-start(bf16[32,4,128]{2,1,0:T(4,128)(2,1)S(1)} %reshape.84), channel_id=1, source_target_pairs={{0,1},{1,2},{2,3},{3,0},{4,5},{5,6},{6,7},{7,4},{8,9},{9,10},{10,1... | collective-permute-start | bytes 98312 | tf_op jit(solution)/shard_map/ppermute | solution.py:48
  7.5 11.8 %collective-permute-start.4 = (bf16[16,1,512]{2,1,0:T(2,128)(2,1)S(1)}, bf16[16,1,512]{2,1,0:T(2,128)(2,1)S(1)}, u32[]{:S(2)}, u32[]{:S(2)}) collective-permute-start(bf16[16,1,512]{2,1,0:T(2,128)(2,1)S(1)} %get-tuple-element.32), channel_id=1, source_target_pairs={{1,0},{2,1},{3,2},{4,3},{5,4},{6,5},{7,6},{8,7},{9,8},{10,9},{11,1... | collective-permute-start | bytes 49160 | tf_op jit(solution)/shard_map/ppermute | solution.py:254
  9.2 10.2 %collective-permute-start.3 = (bf16[16,1,512]{2,1,0:T(2,128)(2,1)S(1)}, bf16[16,1,512]{2,1,0:T(2,128)(2,1)S(1)}, u32[]{:S(2)}, u32[]{:S(2)}) collective-permute-start(bf16[16,1,512]{2,1,0:T(2,128)(2,1)S(1)} %get-tuple-element.33), channel_id=1, source_target_pairs={{0,1},{1,2},{2,3},{3,4},{4,5},{5,6},{6,7},{7,8},{8,9},{9,10},{10,1... | collective-permute-start | bytes 49160 | tf_op jit(solution)/shard_map/ppermute | solution.py:253
  11.3 8.0 %collective-permute-start.2 = (bf16[32,4,128]{2,1,0:T(4,128)(2,1)S(1)}, bf16[32,4,128]{2,1,0:T(4,128)(2,1)S(1)}, u32[]{:S(2)}, u32[]{:S(2)}) collective-permute-start(bf16[32,4,128]{2,1,0:T(4,128)(2,1)S(1)} %collective-permute-done), channel_id=1, source_target_pairs={{0,1},{1,2},{2,3},{3,0},{4,5},{5,6},{6,7},{7,4},{8,9},{9,10},{10,1... | collective-permute-start | bytes 98312 | tf_op jit(solution)/shard_map/ppermute | solution.py:48
  19.4 15.2 %collective-permute-start.6 = (bf16[128,4,128]{2,1,0:T(4,128)(2,1)S(1)}, bf16[128,4,128]{2,1,0:T(4,128)(2,1)S(1)}, u32[]{:S(2)}, u32[]{:S(2)}) collective-permute-start(bf16[128,4,128]{2,1,0:T(4,128)(2,1)S(1)} %pad_maximum_fusion.1), channel_id=1, source_target_pairs={{0,12},{1,13},{2,14},{3,15},{4,0},{5,1},{6,2},{7,3},{8,4},{9,5},{1... | collective-permute-start | bytes 393224 | tf_op jit(solution)/shard_map/ppermute | solution.py:48
  19.5 5.1 %collective-permute-start.5 = (bf16[128,4,128]{2,1,0:T(4,128)(2,1)S(1)}, bf16[128,4,128]{2,1,0:T(4,128)(2,1)S(1)}, u32[]{:S(2)}, u32[]{:S(2)}) collective-permute-start(bf16[128,4,128]{2,1,0:T(4,128)(2,1)S(1)} %pad_maximum_fusion.1), channel_id=1, source_target_pairs={{0,4},{1,5},{2,6},{3,7},{4,8},{5,9},{6,10},{7,11},{8,12},{9,13},{1... | collective-permute-start | bytes 393224 | tf_op jit(solution)/shard_map/ppermute | solution.py:48
  24.6 10.0 %collective-permute-start.7 = (bf16[128,4,128]{2,1,0:T(4,128)(2,1)S(1)}, bf16[128,4,128]{2,1,0:T(4,128)(2,1)S(1)}, u32[]{:S(2)}, u32[]{:S(2)}) collective-permute-start(bf16[128,4,128]{2,1,0:T(4,128)(2,1)S(1)} %collective-permute-done.5), channel_id=1, source_target_pairs={{0,4},{1,5},{2,6},{3,7},{4,8},{5,9},{6,10},{7,11},{8,12},{9,13},{1... | collective-permute-start | bytes 393224 | tf_op jit(solution)/shard_map/ppermute | solution.py:48
  26.0 9.0 %collective-permute-start.8 = (bf16[34,512]{1,0:T(8,128)(2,1)S(1)}, bf16[34,512]{1,0:T(8,128)(2,1)S(1)}, u32[]{:S(2)}, u32[]{:S(2)}) collective-permute-start(bf16[34,512]{1,0:T(8,128)(2,1)S(1)} %pad_maximum_fusion.2), channel_id=1, source_target_pairs={{0,16},{16,32},{32,48},{48,64},{64,80},{80,96},{96,112},{1,17},{17... | collective-permute-start | bytes 104456 | tf_op jit(solution)/shard_map/ppermute | solution.py:258
  27.3 8.1 %collective-permute-start.9 = (bf16[34,512]{1,0:T(8,128)(2,1)S(1)}, bf16[34,512]{1,0:T(8,128)(2,1)S(1)}, u32[]{:S(2)}, u32[]{:S(2)}) collective-permute-start(bf16[34,512]{1,0:T(8,128)(2,1)S(1)} %pad_maximum_fusion.3), channel_id=1, source_target_pairs={{16,0},{32,16},{48,32},{64,48},{80,64},{96,80},{112,96},{17,1},{33... | collective-permute-start | bytes 104456 | tf_op jit(solution)/shard_map/ppermute | solution.py:259
  35.0 33.8 %copy-start = (bf16[512,4,128]{2,1,0:T(4,128)(2,1)}, bf16[512,4,128]{2,1,0:T(4,128)(2,1)S(1)}, u32[]{:S(2)}) copy-start(bf16[512,4,128]{2,1,0:T(4,128)(2,1)S(1)} %pad_maximum_fusion.refs_0_) | copy-start | bytes 1572868
  35.4 14.6 %collective-permute-start.10 = (bf16[512,4,128]{2,1,0:T(4,128)(2,1)S(1)}, bf16[512,4,128]{2,1,0:T(4,128)(2,1)S(1)}, u32[]{:S(2)}, u32[]{:S(2)}) collective-permute-start(bf16[512,4,128]{2,1,0:T(4,128)(2,1)S(1)} %pad_maximum_fusion.refs_0_), channel_id=1, source_target_pairs={{0,32},{1,33},{2,34},{3,35},{4,36},{5,37},{6,38},{7,39},{8,40},{9,... | collective-permute-start | bytes 1572872 | tf_op jit(solution)/shard_map/ppermute | solution.py:48
  39.5 29.6 %collective-permute-start.11 = (bf16[512,4,128]{2,1,0:T(4,128)(2,1)S(1)}, bf16[512,4,128]{2,1,0:T(4,128)(2,1)S(1)}, u32[]{:S(2)}, u32[]{:S(2)}) collective-permute-start(bf16[512,4,128]{2,1,0:T(4,128)(2,1)S(1)} %pad_maximum_fusion.refs_0_), channel_id=1, source_target_pairs={{0,96},{1,97},{2,98},{3,99},{4,100},{5,101},{6,102},{7,103},{8,104... | collective-permute-start | bytes 1572872 | tf_op jit(solution)/shard_map/ppermute | solution.py:48
  50.0 18.8 %copy-start.1 = (bf16[512,4,128]{2,1,0:T(4,128)(2,1)}, bf16[512,4,128]{2,1,0:T(4,128)(2,1)S(1)}, u32[]{:S(2)}) copy-start(bf16[512,4,128]{2,1,0:T(4,128)(2,1)S(1)} %collective-permute-done.10.refs_1_) | copy-start | bytes 1572868
  50.0 19.4 %collective-permute-start.12 = (bf16[512,4,128]{2,1,0:T(4,128)(2,1)S(1)}, bf16[512,4,128]{2,1,0:T(4,128)(2,1)S(1)}, u32[]{:S(2)}, u32[]{:S(2)}) collective-permute-start(bf16[512,4,128]{2,1,0:T(4,128)(2,1)S(1)} %collective-permute-done.10.refs_1_), channel_id=1, source_target_pairs={{0,32},{1,33},{2,34},{3,35},{4,36},{5,37},{6,38},{7,39},{8,40},{9,... | collective-permute-start | bytes 1572872 | tf_op jit(solution)/shard_map/ppermute | solution.py:48
  54.3 17.7 %collective-permute-start.13 = (bf16[512,4,128]{2,1,0:T(4,128)(2,1)S(1)}, bf16[512,4,128]{2,1,0:T(4,128)(2,1)S(1)}, u32[]{:S(2)}, u32[]{:S(2)}) collective-permute-start(bf16[512,4,128]{2,1,0:T(4,128)(2,1)S(1)} %pad_maximum_fusion.refs_0_), channel_id=1, source_target_pairs={{0,16},{1,17},{2,18},{3,19},{4,20},{5,21},{6,22},{7,23},{8,24},{9,... | collective-permute-start | bytes 1572872 | tf_op jit(solution)/shard_map/ppermute | solution.py:44
  68.8 3.2 %collective-permute-start.14 = (bf16[512,4,128]{2,1,0:T(4,128)(2,1)S(1)}, bf16[512,4,128]{2,1,0:T(4,128)(2,1)S(1)}, u32[]{:S(2)}, u32[]{:S(2)}) collective-permute-start(bf16[512,4,128]{2,1,0:T(4,128)(2,1)S(1)} %collective-permute-done.10.refs_1_), channel_id=1, source_target_pairs={{0,16},{1,17},{2,18},{3,19},{4,20},{5,21},{6,22},{7,23},{8,24},{9,... | collective-permute-start | bytes 1572872 | tf_op jit(solution)/shard_map/ppermute | solution.py:44
  69.1 3.2 %copy-start.2 = (bf16[512,4,128]{2,1,0:T(4,128)(2,1)}, bf16[512,4,128]{2,1,0:T(4,128)(2,1)S(1)}, u32[]{:S(2)}) copy-start(bf16[512,4,128]{2,1,0:T(4,128)(2,1)S(1)} %collective-permute-done.11.refs_2_) | copy-start | bytes 1572868
  69.1 2.9 %collective-permute-start.15 = (bf16[512,4,128]{2,1,0:T(4,128)(2,1)S(1)}, bf16[512,4,128]{2,1,0:T(4,128)(2,1)S(1)}, u32[]{:S(2)}, u32[]{:S(2)}) collective-permute-start(bf16[512,4,128]{2,1,0:T(4,128)(2,1)S(1)} %collective-permute-done.11.refs_2_), channel_id=1, source_target_pairs={{0,16},{1,17},{2,18},{3,19},{4,20},{5,21},{6,22},{7,23},{8,24},{9,... | collective-permute-start | bytes 1572872 | tf_op jit(solution)/shard_map/ppermute | solution.py:44
  69.4 2.9 %copy-start.3 = (bf16[512,4,128]{2,1,0:T(4,128)(2,1)}, bf16[512,4,128]{2,1,0:T(4,128)(2,1)S(1)}, u32[]{:S(2)}) copy-start(bf16[512,4,128]{2,1,0:T(4,128)(2,1)S(1)} %collective-permute-done.12.refs_3_) | copy-start | bytes 1572868
  69.4 2.9 %collective-permute-start.16 = (bf16[512,4,128]{2,1,0:T(4,128)(2,1)S(1)}, bf16[512,4,128]{2,1,0:T(4,128)(2,1)S(1)}, u32[]{:S(2)}, u32[]{:S(2)}) collective-permute-start(bf16[512,4,128]{2,1,0:T(4,128)(2,1)S(1)} %collective-permute-done.12.refs_3_), channel_id=1, source_target_pairs={{0,16},{1,17},{2,18},{3,19},{4,20},{5,21},{6,22},{7,23},{8,24},{9,... | collective-permute-start | bytes 1572872 | tf_op jit(solution)/shard_map/ppermute | solution.py:44
  72.0 0.8 copy-start.4
  72.0 1.0 %copy-start.6 = (bf16[512,4,128]{2,1,0:T(4,128)(2,1)}, bf16[512,4,128]{2,1,0:T(4,128)(2,1)S(1)}, u32[]{:S(2)}) copy-start(bf16[512,4,128]{2,1,0:T(4,128)(2,1)S(1)} %collective-permute-done.15.refs_6_) | copy-start | bytes 1572868
  72.0 1.2 %copy-start.5 = (bf16[512,4,128]{2,1,0:T(4,128)(2,1)}, bf16[512,4,128]{2,1,0:T(4,128)(2,1)S(1)}, u32[]{:S(2)}) copy-start(bf16[512,4,128]{2,1,0:T(4,128)(2,1)S(1)} %collective-permute-done.14.refs_5_) | copy-start | bytes 1572868
  72.3 1.1 %copy-start.7 = (bf16[512,4,128]{2,1,0:T(4,128)(2,1)}, bf16[512,4,128]{2,1,0:T(4,128)(2,1)S(1)}, u32[]{:S(2)}) copy-start(bf16[512,4,128]{2,1,0:T(4,128)(2,1)S(1)} %collective-permute-done.16.refs_7_) | copy-start | bytes 1572868

commit v3 on v2

v3 whole, which is shorter than its diff:
```python
import jax
import jax.numpy as jnp
from jax import lax
from jax.experimental import pallas as pl
from jax.experimental.pallas import tpu as pltpu
from jax.sharding import PartitionSpec as P

F = 512
BLK = 128
GROUP = 4
ROWS = GROUP * BLK
RIM = 40
NEAR = 5
FAR = 8
VMEM = 56 << 20
BF = jnp.bfloat16
F32 = jnp.float32


def device_of(x, c, y, z):
    return (x % 4 * 2 + c) * 16 + y % 4 * 4 + z % 4


def shift(axis, by_core):
    pairs = []
    for x in range(4):
        for c in range(2):
            for y in range(4):
                for z in range(4):
                    to = {"x": x, "y": y, "z": z}
                    to[axis] += by_core[c]
                    pairs.append((device_of(x, c, y, z), device_of(to["x"], c, to["y"], to["z"])))
    return pairs


def other_core(value):
    pairs = [
        (device_of(x, c, y, z), device_of(x, 1 - c, y, z))
        for x in range(4)
        for c in range(2)
        for y in range(4)
        for z in range(4)
    ]
    return lax.ppermute(value, ("lat", "lon"), pairs)


def move(value, axis, by_core):
    return lax.ppermute(value, ("lat", "lon"), shift(axis, by_core))


def ring_place(offset, core):
    near = jnp.where((offset == 1) == (core == 1), 1, 2)
    return jnp.where(offset == 0, 0, jnp.where(offset == 2, 3, near))


def silu(v):
    half = 0.5 * v
    return half + half * jnp.tanh(half)


def normed(values, gain):
    centred = values - jnp.mean(values, -1, keepdims=True)
    spread = jnp.mean(centred * centred, -1, keepdims=True)
    return centred * lax.rsqrt(spread + 1e-05) * gain


def dot(a, b):
    return jnp.dot(a, b, preferred_element_type=F32)


def chosen(recv_row):
    return (lax.broadcasted_iota(jnp.int32, (BLK, BLK), 0) == recv_row).astype(BF)


def fetch(count, unroll, entry, table, sent):
    def body(i, carry):
        for u in range(unroll):
            slot, row = entry(i * unroll + u)
            sent[pl.ds(pl.multiple_of(slot * 4, 4), 4), :] = table[row].astype(F32)
        return carry

    lax.fori_loop(0, count, body, 0)


def sent_rows(sent, base=0):
    return jnp.concatenate(
        [sent[pl.ds(base * 4 + j, ROWS, stride=4), :].astype(BF) for j in range(4)], axis=1
    )


def load_table(pieces, table, sem):
    copies = []
    start = 0
    for i, piece in enumerate(pieces):
        rows = piece.shape[0]
        copies.append(pltpu.make_async_copy(piece, table.at[pl.ds(start, rows)], sem.at[i]))
        start += rows
    for copy in copies:
        copy.start()
    return copies


def early_kernel(near_index, tiles, *refs):
    pieces = refs[:NEAR]
    (
        edge_ref,
        recv_ref,
        node_ref,
        we_ref,
        ws_ref,
        wr_ref,
        wn_ref,
        pre_ref,
        nf_ref,
        table,
        sent,
        got_ref,
        sem,
    ) = refs[NEAR:]
    step = pl.program_id(0)

    @pl.when(step == 0)
    def _():
        copies = load_table(pieces, table, sem)
        nf_ref[...] = dot(node_ref[...], wn_ref[...])
        for copy in copies:
            copy.wait()

    fetch(ROWS // 16, 16, lambda e: (e, near_index[step * ROWS + e]), table, sent)
    for k in range(GROUP):
        tile = pl.multiple_of(tiles[step * GROUP + k] * BLK, BLK)
        hot = chosen(recv_ref[k : k + 1, :])
        rows = lax.dot_general(
            hot,
            node_ref[pl.ds(tile, BLK), :],
            (((0,), (0,)), ((), ())),
            preferred_element_type=F32,
        )
        got_ref[k * BLK : (k + 1) * BLK, :] = rows.astype(BF)
    pre_ref[...] = (
        dot(edge_ref[...], we_ref[...])
        + dot(got_ref[...], wr_ref[...])
        + dot(sent_rows(sent), ws_ref[...])
    ).astype(BF)


def late_kernel(far_list, far_count, tiles, lives, *refs):
    pieces = refs[:FAR]
    (
        pre_hbm,
        edge_hbm,
        nf_hbm,
        node_hbm,
        w1_hbm,
        w2_hbm,
        wn_hbm,
        wn2_hbm,
        recv_ref,
        eg_ref,
        ng_ref,
        out_hbm,
        node_out_ref,
        table,
        sent,
        pre,
        edge,
        out,
        agg,
        nf,
        node,
        ws,
        w2,
        wn,
        wn2,
        sem,
        in_sem,
        out_sem,
    ) = refs[FAR:]
    steps = recv_ref.shape[0] // GROUP
    rows_of = lambda g: pl.ds(g * ROWS, ROWS)
    copies = load_table(pieces, table, sem)
    first = [
        pltpu.make_async_copy(w1_hbm.at[pl.ds(F, F)], ws, in_sem.at[0]),
        pltpu.make_async_copy(w2_hbm, w2, in_sem.at[1]),
    ]
    parts = []
    for g in range(steps):
        parts.append(
            [
                pltpu.make_async_copy(pre_hbm.at[rows_of(g)], pre.at[rows_of(g)], in_sem.at[6 + 2 * g]),
                pltpu.make_async_copy(edge_hbm.at[rows_of(g)], edge.at[rows_of(g)], in_sem.at[7 + 2 * g]),
            ]
        )
    last = [
        pltpu.make_async_copy(nf_hbm, nf, in_sem.at[2]),
        pltpu.make_async_copy(node_hbm, node, in_sem.at[3]),
        pltpu.make_async_copy(wn_hbm.at[pl.ds(F, F)], wn, in_sem.at[4]),
        pltpu.make_async_copy(wn2_hbm, wn2, in_sem.at[5]),
    ]
    for copy in first + sum(parts, []) + last:
        copy.start()
    sent[...] = jnp.zeros_like(sent)
    agg[...] = jnp.zeros_like(agg)
    for copy in copies:
        copy.wait()

    for g in range(steps):

        def entry(i):
            packed = far_list[g * ROWS + i]
            return packed & 4095, packed >> 12

        fetch((far_count[g] + 7) >> 3, 8, entry, table, sent)
    for copy in first:
        copy.wait()
    place = lax.broadcasted_iota(jnp.int32, (BLK, F), 0)
    stores = []
    for g in range(steps):
        for copy in parts[g]:
            copy.wait()
        base = g * ROWS
        total = pre[rows_of(g), :].astype(F32) + dot(sent_rows(sent, base), ws[...])
        message = normed(dot(silu(total).astype(BF), w2[...]), eg_ref[...]).astype(BF)
        for k in range(GROUP):
            b = g * GROUP + k
            part = message[k * BLK : (k + 1) * BLK, :]
            at = pl.ds(base + k * BLK, BLK)
            live = place < lives[b]
            out[at, :] = jnp.where(
                live, edge[at, :].astype(F32) + part.astype(F32), 0.0
            ).astype(BF)
            tile = pl.multiple_of(tiles[b] * BLK, BLK)
            agg[pl.ds(tile, BLK), :] += dot(chosen(recv_ref[b : b + 1, :]), part)
        store = pltpu.make_async_copy(out.at[rows_of(g)], out_hbm.at[rows_of(g)], out_sem.at[g])
        store.start()
        stores.append(store)
    for copy in last:
        copy.wait()
    first_sum = nf[...] + dot(agg[...].astype(BF), wn[...])
    second = dot(silu(first_sum).astype(BF), wn2[...])
    node_out_ref[...] = (node[...].astype(F32) + normed(second, ng_ref[...])).astype(BF)
    for store in stores:
        store.wait()


def far_lists(is_far, far_index, steps):
    place = jnp.arange(ROWS, dtype=jnp.int32)
    slots = steps * ROWS
    far = is_far.reshape(steps, ROWS)
    flag = far.astype(jnp.int32)
    before = place[:, None] > place[None, :]
    rank = jnp.sum(jnp.where(before[None], flag[:, None, :], 0), 2)
    packed = (far_index * 4096 + jnp.arange(slots, dtype=jnp.int32) - slots).reshape(steps, ROWS)
    hit = (rank[:, None, :] == place[None, :, None]) & far[:, None, :]
    return (slots + jnp.sum(jnp.where(hit, packed[:, None, :], 0), 2)).reshape(-1), jnp.sum(flag, 1)


def specs():
    whole = lambda shape: pl.BlockSpec(shape, lambda i, *_: (0,) * len(shape))
    part = pl.BlockSpec((ROWS, F), lambda i, *_: (i, 0))
    recv_spec = pl.BlockSpec((None, GROUP, BLK), lambda i, *_: (i, 0, 0))
    weight = lambda k: pl.BlockSpec((F, F), lambda i, *_: (k, 0))
    anywhere = pl.BlockSpec(memory_space=pl.ANY)
    return whole, part, recv_spec, weight, anywhere


def early_call(near_index, block_tile, near_pieces, edge_latent, recv_rows, own_rows, w_first, w_node_first):
    whole, part, recv_spec, weight, anywhere = specs()
    blocks, nodes = block_tile.shape[0], own_rows.shape[0]
    steps = blocks // GROUP
    near_rows = sum(piece.shape[0] for piece in near_pieces)
    return pl.pallas_call(
        early_kernel,
        name="early",
        grid_spec=pltpu.PrefetchScalarGridSpec(
            num_scalar_prefetch=2,
            grid=(steps,),
            in_specs=[anywhere] * NEAR
            + [part, recv_spec, whole((nodes, F)), weight(0), weight(1), weight(2), weight(0)],
            out_specs=[part, whole((nodes, F))],
            scratch_shapes=[
                pltpu.VMEM((near_rows, 4, 128), BF),
                pltpu.VMEM((ROWS * 4, 128), F32),
                pltpu.VMEM((ROWS, F), BF),
                pltpu.SemaphoreType.DMA((NEAR,)),
            ],
        ),
        out_shape=[
            jax.ShapeDtypeStruct((blocks * BLK, F), BF),
            jax.ShapeDtypeStruct((nodes, F), F32),
        ],
        compiler_params=pltpu.CompilerParams(vmem_limit_bytes=VMEM),
        cost_estimate=pl.CostEstimate(
            flops=4 * 10**9, bytes_accessed=10 * 10**6, transcendentals=0
        ),
    )(
        near_index,
        block_tile,
        *near_pieces,
        edge_latent,
        recv_rows,
        own_rows,
        w_first,
        w_first,
        w_first,
        w_node_first,
    )


def late_call(
    far_list,
    far_count,
    block_tile,
    lives,
    far_pieces,
    pre,
    edge_latent,
    receiver,
    node_first,
    own_rows,
    w_first,
    w_second,
    edge_gain,
    w_node_first,
    w_node_second,
    node_gain,
):
    blocks, nodes = block_tile.shape[0], own_rows.shape[0]
    slots, steps = blocks * BLK, blocks // GROUP
    far_rows = sum(piece.shape[0] for piece in far_pieces)
    anywhere = pl.BlockSpec(memory_space=pl.ANY)
    local = pl.BlockSpec(memory_space=pltpu.VMEM)
    scalars = pl.BlockSpec(memory_space=pltpu.SMEM)
    square = pltpu.VMEM((F, F), BF)
    return pl.pallas_call(
        late_kernel,
        name="late",
        in_specs=[scalars] * 4 + [anywhere] * (FAR + 8) + [local] * 3,
        out_specs=[anywhere, local],
        scratch_shapes=[
            pltpu.VMEM((far_rows, 4, 128), BF),
            pltpu.VMEM((slots * 4 + 32, 128), F32),
            pltpu.VMEM((slots, F), BF),
            pltpu.VMEM((slots, F), BF),
            pltpu.VMEM((slots, F), BF),
            pltpu.VMEM((nodes, F), F32),
            pltpu.VMEM((nodes, F), F32),
            pltpu.VMEM((nodes, F), BF),
            square,
            square,
            square,
            square,
            pltpu.SemaphoreType.DMA((FAR,)),
            pltpu.SemaphoreType.DMA((6 + 2 * steps,)),
            pltpu.SemaphoreType.DMA((steps,)),
        ],
        out_shape=[
            jax.ShapeDtypeStruct((slots, F), BF),
            jax.ShapeDtypeStruct((nodes, F), BF),
        ],
        compiler_params=pltpu.CompilerParams(vmem_limit_bytes=VMEM),
        cost_estimate=pl.CostEstimate(
            flops=4 * 10**9, bytes_accessed=14 * 10**6, transcendentals=2 * 10**6
        ),
    )(
        far_list,
        far_count,
        block_tile,
        lives,
        *far_pieces,
        pre,
        edge_latent,
        node_first,
        own_rows,
        w_first,
        w_second,
        w_node_first,
        w_node_second,
        receiver.reshape(blocks, BLK),
        edge_gain.reshape(1, F),
        node_gain.reshape(1, F),
    )


def per_device(
    node_latent,
    edge_latent,
    sender,
    receiver,
    block_tile,
    w_first,
    w_second,
    edge_gain,
    w_node_first,
    w_node_second,
    node_gain,
):
    patch_rows, patch_cols, features = node_latent.shape
    lat_index = lax.axis_index("lat")
    lon_index = lax.axis_index("lon")
    lat_count, lon_count = lax.axis_size("lat"), lax.axis_size("lon")
    grid_cols = patch_cols * lon_count
    blocks = block_tile.shape[0]
    steps = blocks // GROUP
    nodes = patch_rows * patch_cols
    own_rows = node_latent.reshape(nodes, features)
    lanes = lambda a: a.reshape(-1, 4, 128)

    right = [(i, (i + 1) % lon_count) for i in range(lon_count)]
    left = [(j, i) for i, j in right]
    up = [(i, i + 1) for i in range(lat_count - 1)]
    down = [(j, i) for i, j in up]

    coarse_own = lanes(node_latent[::4, ::4])
    copies = jnp.broadcast_to(coarse_own, (lon_count, *coarse_own.shape))
    copies, latent = lax.optimization_barrier((copies, node_latent))
    plane = lanes(lax.all_to_all(copies, "lon", split_axis=0, concat_axis=0, tiled=True))

    west = lax.ppermute(latent[:, -1:], "lon", right)
    east = lax.ppermute(latent[:, :1], "lon", left)
    row_of = lambda r: jnp.concatenate([west[r], latent[r], east[r]], 0)
    north = lax.ppermute(row_of(patch_rows - 1), "lat", up)
    south = lax.ppermute(row_of(0), "lat", down)
    plane, north, south = lax.optimization_barrier((plane, north, south))
    own, ahead, behind = plane, move(plane, "x", (1, -1)), move(plane, "x", (-1, 1))

    pad = lambda a: jnp.pad(lanes(a), ((0, RIM - patch_cols - 2), (0, 0), (0, 0)))
    near_pieces = [lanes(own_rows), lanes(west), lanes(east), pad(north), pad(south)]

    senders = jnp.maximum(sender, 0)
    send_row = senders // grid_cols
    send_col = senders % grid_cols
    row = send_row - lat_index * patch_rows
    col = (send_col - lon_index * patch_cols + 1) % grid_cols - 1
    is_near = (row >= -1) & (row <= patch_rows) & (col <= patch_cols)
    side = jnp.where(col < 0, nodes + row, nodes + patch_rows + row)
    inner = jnp.where((col < 0) | (col >= patch_cols), side, row * patch_cols + col)
    rim = nodes + 2 * patch_rows
    near_index = jnp.where(
        row < 0, rim + col + 1, jnp.where(row >= patch_rows, rim + RIM + col + 1, inner)
    )
    no_row = rim + patch_cols + 2
    near_index = jnp.where(is_near, near_index, no_row)
    src_lat, src_lon = send_row // patch_rows, send_col // patch_cols
    src_core, core = src_lat % 2, lat_index % 2
    at_x = ring_place((src_lat // 2 - lat_index // 2) % 4, src_core)
    half = jnp.where(src_core == core, 0, 1)
    within = send_row % patch_rows // 4 * (patch_cols // 4) + send_col % patch_cols // 4
    per = patch_rows // 4 * (patch_cols // 4)
    far_index = ((half * 4 + at_x) * lon_count + src_lon) * per + within
    far_list, far_count = far_lists((receiver >= 0) & ~is_near, far_index, steps)
    recv_rows = receiver.reshape(steps, GROUP, BLK)
    lives = jnp.sum((receiver >= 0).astype(jnp.int32).reshape(blocks, BLK), 1)

    pre, node_first = early_call(
        near_index, block_tile, near_pieces, edge_latent, recv_rows, own_rows, w_first, w_node_first
    )
    ahead, pre = lax.optimization_barrier((ahead, pre))
    across = move(ahead, "x", (1, -1))
    across, far_list, far_count = lax.optimization_barrier((across, far_list, far_count))
    halves = [own, ahead, behind, across]
    far_pieces = halves + [other_core(piece) for piece in halves]
    edge_out, node_out = late_call(
        far_list,
        far_count,
        block_tile,
        lives,
        far_pieces,
        pre,
        edge_latent,
        receiver,
        node_first,
        own_rows,
        w_first,
        w_second,
        edge_gain,
        w_node_first,
        w_node_second,
        node_gain,
    )
    return node_out.reshape(patch_rows, patch_cols, features), edge_out


def solution(mesh):
    return jax.shard_map(
        per_device,
        mesh=mesh,
        in_specs=(
            P("lat", "lon", None),
            P(("lat", "lon"), None),
            P(("lat", "lon")),
            P(("lat", "lon")),
            P(("lat", "lon")),
            P(),
            P(),
            P(),
            P(),
            P(),
            P(),
        ),
        out_specs=(P("lat", "lon", None), P(("lat", "lon"), None)),
        check_vma=False,
    )
```

time: 92.9 us -> 78.9 us (0.85)
  the two profiles are of different devices: /device:TPU:31 before, /device:TPU:1 now
where the time goes in v3:
time: 78.9 us; the launch traced here: 78.3 us
  Pallas kernels  26.8 us (34%)
  starting transfers between devices  26.2 us (33%)
  local copies, waits for them, and re-layouts  9.65 us (12%)
  waiting for transfers between devices  8.64 us (11%)
  other arithmetic  6 us (8%)
  between operations  1 us (1%)
    pallas_call x1, Pallas kernels, late_call(): pl.pallas_call(late_kernel, name='late', in_specs=[scalars] * 4 + [anywhe...  14.1 us
    pallas_call x1, Pallas kernels, early_call(): pl.pallas_call(early_kernel, name='early', grid_spec=pltpu.PrefetchScalar...  12.7 us
    all_to_all x1, starting transfers between devices, per_device(): lax.all_to_all(copies, 'lon', split_axis=0, concat_axis=0, tiled=True)  8.6 us
    ppermute x1, starting transfers between devices, per_device(): north = lax.ppermute(row_of(patch_rows - 1), 'lat', up)  5.2 us
    ppermute x3, waiting for transfers between devices, move(): return lax.ppermute(value, ('lat', 'lon'), shift(axis, by_core))  4.16 us
    ppermute x1, starting transfers between devices, per_device(): east = lax.ppermute(latent[:, :1], 'lon', left)  3.43 us
    ppermute x4, starting transfers between devices, other_core(): return lax.ppermute(value, ('lat', 'lon'), pairs)  2.86 us
    ppermute x3, starting transfers between devices, move(): return lax.ppermute(value, ('lat', 'lon'), shift(axis, by_core))  2.82 us
  transfers between devices with their start and end apart: 12, of which 4 were waited for; matrix products, arithmetic and copies ran while one was open for 15% of the time, Pallas kernels for 16%

profile of v3, /device:TPU:1, one launch (start us, length us, event | category | flops | bytes accessed | tf_op | source)
XLA Modules:
  0.0 78.3 jit_solution(12290107520558414000)
XLA Ops:
  0.6 0.0 copy-start
  0.6 2.0 %slice.27 = bf16[4,8,512]{2,1,0:T(8,128)(2,1)S(1)} slice(bf16[16,32,512]{2,1,0:T(8,128)(2,1)} %param.11), slice={[0:16:4], [0:32:4], [0:512:1]} | slice | bytes 65536 | tf_op jit(solution)/shard_map/slice | solution.py:414
  2.7 1.0 %broadcast_in_dim.54 = bf16[16,32,4,128]{3,2,1,0:T(4,128)(2,1)} broadcast(bf16[32,4,128]{2,1,0:T(4,128)(2,1)S(1)} %reshape.73), dimensions={1,2,3} | broadcast | bytes 557056 | tf_op jit(solution)/shard_map/broadcast_in_dim | solution.py:415
  3.7 8.6 %all-to-all-start = ((bf16[16,32,4,128]{3,2,1,0:T(4,128)(2,1)}), bf16[16,32,4,128]{3,2,1,0:T(4,128)(2,1)S(1)}, u32[]{:S(2)}, u32[]{:S(2)}) async-start(bf16[16,32,4,128]{3,2,1,0:T(4,128)(2,1)} %broadcast_in_dim.54), calls=%async_computation | async-start | bytes 1048576 | tf_op jit(solution)/shard_map/all_to_all | solution.py:417
  12.3 1.0 %fusion.24 = (bf16[16,1,512]{2,1,0:T(2,128)(2,1)S(1)}, bf16[16,1,512]{2,1,0:T(2,128)(2,1)S(1)}) fusion(bf16[16,32,512]{2,1,0:T(8,128)(2,1)} %param.11), kind=kLoop, calls=%fused_computation.81 | loop fusion | bytes 65536 | tf_op jit(solution)/shard_map/slice | solution.py:419
  13.3 1.4 %collective-permute-start = (bf16[16,1,512]{2,1,0:T(2,128)(2,1)S(1)}, bf16[16,1,512]{2,1,0:T(2,128)(2,1)S(1)}, u32[]{:S(2)}, u32[]{:S(2)}) collective-permute-start(bf16[16,1,512]{2,1,0:T(2,128)(2,1)S(1)} %get-tuple-element.36), channel_id=1, source_target_pairs={{0,1},{1,2},{2,3},{3,4},{4,5},{5,6},{6,7},{7,8},{8,9},{9,10},{10,1... | collective-permute-start | bytes 49160 | tf_op jit(solution)/shard_map/ppermute | solution.py:419
  14.7 3.4 %collective-permute-start.1 = (bf16[16,1,512]{2,1,0:T(2,128)(2,1)S(1)}, bf16[16,1,512]{2,1,0:T(2,128)(2,1)S(1)}, u32[]{:S(2)}, u32[]{:S(2)}) collective-permute-start(bf16[16,1,512]{2,1,0:T(2,128)(2,1)S(1)} %get-tuple-element.37), channel_id=1, source_target_pairs={{1,0},{2,1},{3,2},{4,3},{5,4},{6,5},{7,6},{8,7},{9,8},{10,9},{11,1... | collective-permute-start | bytes 49160 | tf_op jit(solution)/shard_map/ppermute | solution.py:420
  18.2 0.8 slice_bitcast_fusion
  18.9 1.3 %bitcast_reduce_fusion = (s32[16]{0:T(128)}, pred[2048]{0:T(1024)(128)(4,1)S(1)}) fusion(s32[2048]{0:T(1024)} %param.14), kind=kLoop, calls=%fused_computation.53 | loop fusion | flops 6128 | bytes 10304 | tf_op jit(solution)/shard_map/reduce_sum | solution.py:453
  20.2 0.7 not_and_fusion
  21.0 1.4 %fusion.9 = (s32[2048]{0:T(1024)S(1)}, s32[2048]{0:T(1024)}) fusion(s32[2048]{0:T(1024)} %param.13, s32[]{:T(128)S(6)} %select_n.109, s32[]{:T(128)S(6)} %select_n.106, pred[2048]{0:T(1024)(128)(4,1)S(1)} %get-tuple-element.33, s32[]{:T(128)S(6)} %mul.32, s32[]{:T(128)S(6)} %mul.31), kind=kLoop, calls=%fused_computation.48 | loop fusion | flops 335872 | bytes 26640 | tf_op jit(solution)/shard_map/sub | solution.py:253
  22.3 0.6 collective-permute-done
  22.9 0.0 collective-permute-done.1
  23.0 5.2 %collective-permute-start.2 = (bf16[34,512]{1,0:T(8,128)(2,1)S(1)}, bf16[34,512]{1,0:T(8,128)(2,1)S(1)}, u32[]{:S(2)}, u32[]{:S(2)}) collective-permute-start(bf16[34,512]{1,0:T(8,128)(2,1)S(1)} %pad_maximum_fusion), channel_id=1, source_target_pairs={{0,16},{16,32},{32,48},{48,64},{64,80},{80,96},{96,112},{1,17},{17... | collective-permute-start | bytes 104456 | tf_op jit(solution)/shard_map/ppermute | solution.py:422
  28.2 1.9 %collective-permute-start.3 = (bf16[34,512]{1,0:T(8,128)(2,1)S(1)}, bf16[34,512]{1,0:T(8,128)(2,1)S(1)}, u32[]{:S(2)}, u32[]{:S(2)}) collective-permute-start(bf16[34,512]{1,0:T(8,128)(2,1)S(1)} %pad_maximum_fusion.1), channel_id=1, source_target_pairs={{16,0},{32,16},{48,32},{64,48},{80,64},{96,80},{112,96},{17,1},{33... | collective-permute-start | bytes 104456 | tf_op jit(solution)/shard_map/ppermute | solution.py:423
  30.1 0.1 iota_compare_fusion.1
  30.2 0.0 copy-done
  30.2 0.9 %reshape_reshape.3.refs_0_ = bf16[512,4,128]{2,1,0:T(4,128)(2,1)} reshape(bf16[16,32,512]{2,1,0:T(8,128)(2,1)S(1)} %copy-done) | data formatting | bytes 1048576 | tf_op jit(solution)/shard_map/reshape;reshape | solution.py:407
  31.2 0.0 collective-permute-done.2
  31.2 2.3 %collective-permute-done.3 = bf16[34,512]{1,0:T(8,128)(2,1)S(1)} collective-permute-done((bf16[34,512]{1,0:T(8,128)(2,1)S(1)}, bf16[34,512]{1,0:T(8,128)(2,1)S(1)}, u32[]{:S(2)}, u32[]{:S(2)}) %collective-permute-start.3) | collective-permute-done | bytes 34848 | tf_op jit(solution)/shard_map/ppermute | solution.py:423
  33.5 0.0 all-to-all-done
  33.5 0.0 copy-start.1
  33.5 0.0 collective-permute-start.4
  33.5 0.6 select_reduce_fusion.1
  34.2 0.1 reduce
  34.3 0.6 reshape.75.refs_1_
  34.9 0.1 reduce.1
  35.0 0.6 reshape.76.refs_2_
  35.6 1.5 %collective-permute-start.6 = (bf16[512,4,128]{2,1,0:T(4,128)(2,1)S(1)}, bf16[512,4,128]{2,1,0:T(4,128)(2,1)S(1)}, u32[]{:S(2)}, u32[]{:S(2)}) collective-permute-start(bf16[512,4,128]{2,1,0:T(4,128)(2,1)S(1)} %bitcast.27), channel_id=1, source_target_pairs={{0,96},{1,97},{2,98},{3,99},{4,100},{5,101},{6,102},{7,103},{8,104... | collective-permute-start | bytes 1572872 | tf_op jit(solution)/shard_map/ppermute | solution.py:48
  37.1 0.6 pad.7.refs_3_
  37.7 0.6 pad.8.refs_4_
  38.4 12.7 %early.1 = (bf16[2048,512]{1,0:T(8,128)(2,1)}, f32[512,512]{1,0:T(8,128)}) custom-call(s32[2048]{0:T(1024)} %get-tuple-element.43.near_index, s32[16]{0:T(128)} %tiles.3, bf16[512,4,128]{2,1,0:T(4,128)(2,1)} %reshape_reshape.3.refs_0_, bf16[16,4,128]{2,1,0:T(4,128)(2,1)} %reshape.75.refs_1_, bf16[16,4,128]{2,1,0:T(4,128)(2,1)} %reshape.76.refs_2_, ...), custom_call_target="tpu_custom_call" | custom-call | flops 4000000000 | bytes 10000000 | tf_op jit(solution)/shard_map/early/pallas_call | solution.py:272
  51.1 0.0 collective-permute-done.4.refs_1_
  51.1 0.0 copy-start.2
  51.1 1.4 %collective-permute-start.5 = (bf16[512,4,128]{2,1,0:T(4,128)(2,1)S(1)}, bf16[512,4,128]{2,1,0:T(4,128)(2,1)S(1)}, u32[]{:S(2)}, u32[]{:S(2)}) collective-permute-start(bf16[512,4,128]{2,1,0:T(4,128)(2,1)S(1)} %collective-permute-done.4.refs_1_), channel_id=1, source_target_pairs={{0,32},{1,33},{2,34},{3,35},{4,36},{5,37},{6,38},{7,39},{8,40},{9,... | collective-permute-start | bytes 1572872 | tf_op jit(solution)/shard_map/ppermute | solution.py:48
  52.4 1.0 %select_reduce_fusion = s32[4,512]{1,0:T(4,128)S(1)} fusion(s32[4,512]{1,0:T(4,128)S(1)} %broadcast_in_dim.59, s32[4,512]{1,0:T(4,128)S(1)} %select_reduce_fusion.1, pred[4,512]{1,0:T(4,128)(4,1)S(1)} %reshape.81), kind=kLoop, calls=%fused_computation | loop fusion | flops 4192256 | bytes 26624 | tf_op jit(solution)/shard_map/reduce_sum | solution.py:255
  53.4 0.6 copy.13
  54.0 0.7 convert_reduce_fusion.far_count
  54.7 0.0 copy-done.1
  54.7 0.0 collective-permute-start.7
  54.7 0.5 collective-permute-start.8
  55.2 0.0 collective-permute-done.6.refs_2_
  55.2 0.0 copy-start.3
  55.2 0.1 collective-permute-start.9
  55.3 4.2 %collective-permute-done.5.refs_3_ = bf16[512,4,128]{2,1,0:T(4,128)(2,1)S(1)} collective-permute-done((bf16[512,4,128]{2,1,0:T(4,128)(2,1)S(1)}, bf16[512,4,128]{2,1,0:T(4,128)(2,1)S(1)}, u32[]{:S(2)}, u32[]{:S(2)}) %collective-permute-start.5) | collective-permute-done | bytes 524320 | tf_op jit(solution)/shard_map/ppermute | solution.py:48
  59.5 0.0 copy-start.4
  59.5 2.3 %collective-permute-start.10 = (bf16[512,4,128]{2,1,0:T(4,128)(2,1)S(1)}, bf16[512,4,128]{2,1,0:T(4,128)(2,1)S(1)}, u32[]{:S(2)}, u32[]{:S(2)}) collective-permute-start(bf16[512,4,128]{2,1,0:T(4,128)(2,1)S(1)} %collective-permute-done.5.refs_3_), channel_id=1, source_target_pairs={{0,16},{1,17},{2,18},{3,19},{4,20},{5,21},{6,22},{7,23},{8,24},{9,... | collective-permute-start | bytes 1572872 | tf_op jit(solution)/shard_map/ppermute | solution.py:44
  61.7 0.0 collective-permute-done.7.refs_4_
  61.8 0.0 copy-start.5
  61.8 0.0 collective-permute-done.9.refs_6_
  61.8 0.0 copy-start.7
  61.8 0.0 collective-permute-done.8.refs_5_
  61.8 0.0 copy-start.6
  61.8 1.5 %collective-permute-done.10.refs_7_ = bf16[512,4,128]{2,1,0:T(4,128)(2,1)S(1)} collective-permute-done((bf16[512,4,128]{2,1,0:T(4,128)(2,1)S(1)}, bf16[512,4,128]{2,1,0:T(4,128)(2,1)S(1)}, u32[]{:S(2)}, u32[]{:S(2)}) %collective-permute-start.10) | collective-permute-done | bytes 524320 | tf_op jit(solution)/shard_map/ppermute | solution.py:44
  63.3 0.0 copy-start.8
  63.3 0.0 copy-done.2
  63.3 0.0 copy-done.3
  63.3 0.0 copy-done.4
  63.3 0.0 copy-done.5
  63.3 0.0 copy-done.7
  63.3 0.0 copy-done.6
  63.3 0.7 copy-done.8
  64.1 14.1 %late.1 = (bf16[2048,512]{1,0:T(8,128)(2,1)}, bf16[512,512]{1,0:T(8,128)(2,1)}) custom-call(s32[2048]{0:T(1024)} %bitcast.32, s32[4]{0:T(128)} %convert_reduce_fusion.far_count, s32[16]{0:T(128)} %tiles.3, s32[16]{0:T(128)} %get-tuple-element.30.lives, bf16[512,4,128]{2,1,0:T(4,128)(2,1)} %bitcast.29, bf16[512,4,128]{2,1,0:T(4,128)(2,1)} %copy-done.2, ...), custom_call_target="tpu_custom_call" | custom-call | flops 4000000000 | bytes 14000000 | tf_op jit(solution)/shard_map/late/pallas_call | solution.py:335
  (11 shorter events, 0.1 us)
Async XLA Ops:
  0.6 29.6 %copy-start = (bf16[16,32,512]{2,1,0:T(8,128)(2,1)S(1)}, bf16[16,32,512]{2,1,0:T(8,128)(2,1)}, u32[]{:S(2)}) copy-start(bf16[16,32,512]{2,1,0:T(8,128)(2,1)} %param.11) | copy-start | bytes 1572868
  3.7 29.9 %all-to-all-start = ((bf16[16,32,4,128]{3,2,1,0:T(4,128)(2,1)}), bf16[16,32,4,128]{3,2,1,0:T(4,128)(2,1)S(1)}, u32[]{:S(2)}, u32[]{:S(2)}) async-start(bf16[16,32,4,128]{3,2,1,0:T(4,128)(2,1)} %broadcast_in_dim.54), calls=%async_computation | async-start | bytes 1048576 | tf_op jit(solution)/shard_map/all_to_all | solution.py:417
  13.3 9.6 %collective-permute-start = (bf16[16,1,512]{2,1,0:T(2,128)(2,1)S(1)}, bf16[16,1,512]{2,1,0:T(2,128)(2,1)S(1)}, u32[]{:S(2)}, u32[]{:S(2)}) collective-permute-start(bf16[16,1,512]{2,1,0:T(2,128)(2,1)S(1)} %get-tuple-element.36), channel_id=1, source_target_pairs={{0,1},{1,2},{2,3},{3,4},{4,5},{5,6},{6,7},{7,8},{8,9},{9,10},{10,1... | collective-permute-start | bytes 49160 | tf_op jit(solution)/shard_map/ppermute | solution.py:419
  14.7 8.2 %collective-permute-start.1 = (bf16[16,1,512]{2,1,0:T(2,128)(2,1)S(1)}, bf16[16,1,512]{2,1,0:T(2,128)(2,1)S(1)}, u32[]{:S(2)}, u32[]{:S(2)}) collective-permute-start(bf16[16,1,512]{2,1,0:T(2,128)(2,1)S(1)} %get-tuple-element.37), channel_id=1, source_target_pairs={{1,0},{2,1},{3,2},{4,3},{5,4},{6,5},{7,6},{8,7},{9,8},{10,9},{11,1... | collective-permute-start | bytes 49160 | tf_op jit(solution)/shard_map/ppermute | solution.py:420
  23.0 8.2 %collective-permute-start.2 = (bf16[34,512]{1,0:T(8,128)(2,1)S(1)}, bf16[34,512]{1,0:T(8,128)(2,1)S(1)}, u32[]{:S(2)}, u32[]{:S(2)}) collective-permute-start(bf16[34,512]{1,0:T(8,128)(2,1)S(1)} %pad_maximum_fusion), channel_id=1, source_target_pairs={{0,16},{16,32},{32,48},{48,64},{64,80},{80,96},{96,112},{1,17},{17... | collective-permute-start | bytes 104456 | tf_op jit(solution)/shard_map/ppermute | solution.py:422
  28.2 5.3 %collective-permute-start.3 = (bf16[34,512]{1,0:T(8,128)(2,1)S(1)}, bf16[34,512]{1,0:T(8,128)(2,1)S(1)}, u32[]{:S(2)}, u32[]{:S(2)}) collective-permute-start(bf16[34,512]{1,0:T(8,128)(2,1)S(1)} %pad_maximum_fusion.1), channel_id=1, source_target_pairs={{16,0},{32,16},{48,32},{64,48},{80,64},{96,80},{112,96},{17,1},{33... | collective-permute-start | bytes 104456 | tf_op jit(solution)/shard_map/ppermute | solution.py:423
  33.5 21.2 %copy-start.1 = (bf16[16,32,4,128]{3,2,1,0:T(4,128)(2,1)}, bf16[16,32,4,128]{3,2,1,0:T(4,128)(2,1)S(1)}, u32[]{:S(2)}) copy-start(bf16[16,32,4,128]{3,2,1,0:T(4,128)(2,1)S(1)} %all-to-all-done) | copy-start | bytes 1572868
  33.5 17.5 %collective-permute-start.4 = (bf16[512,4,128]{2,1,0:T(4,128)(2,1)S(1)}, bf16[512,4,128]{2,1,0:T(4,128)(2,1)S(1)}, u32[]{:S(2)}, u32[]{:S(2)}) collective-permute-start(bf16[512,4,128]{2,1,0:T(4,128)(2,1)S(1)} %bitcast.26), channel_id=1, source_target_pairs={{0,32},{1,33},{2,34},{3,35},{4,36},{5,37},{6,38},{7,39},{8,40},{9,... | collective-permute-start | bytes 1572872 | tf_op jit(solution)/shard_map/ppermute | solution.py:48
  35.6 19.6 %collective-permute-start.6 = (bf16[512,4,128]{2,1,0:T(4,128)(2,1)S(1)}, bf16[512,4,128]{2,1,0:T(4,128)(2,1)S(1)}, u32[]{:S(2)}, u32[]{:S(2)}) collective-permute-start(bf16[512,4,128]{2,1,0:T(4,128)(2,1)S(1)} %bitcast.27), channel_id=1, source_target_pairs={{0,96},{1,97},{2,98},{3,99},{4,100},{5,101},{6,102},{7,103},{8,104... | collective-permute-start | bytes 1572872 | tf_op jit(solution)/shard_map/ppermute | solution.py:48
  51.1 12.2 %copy-start.2 = (bf16[512,4,128]{2,1,0:T(4,128)(2,1)}, bf16[512,4,128]{2,1,0:T(4,128)(2,1)S(1)}, u32[]{:S(2)}) copy-start(bf16[512,4,128]{2,1,0:T(4,128)(2,1)S(1)} %collective-permute-done.4.refs_1_) | copy-start | bytes 1572868
  51.1 8.4 %collective-permute-start.5 = (bf16[512,4,128]{2,1,0:T(4,128)(2,1)S(1)}, bf16[512,4,128]{2,1,0:T(4,128)(2,1)S(1)}, u32[]{:S(2)}, u32[]{:S(2)}) collective-permute-start(bf16[512,4,128]{2,1,0:T(4,128)(2,1)S(1)} %collective-permute-done.4.refs_1_), channel_id=1, source_target_pairs={{0,32},{1,33},{2,34},{3,35},{4,36},{5,37},{6,38},{7,39},{8,40},{9,... | collective-permute-start | bytes 1572872 | tf_op jit(solution)/shard_map/ppermute | solution.py:48
  54.7 7.0 %collective-permute-start.7 = (bf16[512,4,128]{2,1,0:T(4,128)(2,1)S(1)}, bf16[512,4,128]{2,1,0:T(4,128)(2,1)S(1)}, u32[]{:S(2)}, u32[]{:S(2)}) collective-permute-start(bf16[512,4,128]{2,1,0:T(4,128)(2,1)S(1)} %bitcast.28), channel_id=1, source_target_pairs={{0,16},{1,17},{2,18},{3,19},{4,20},{5,21},{6,22},{7,23},{8,24},{9,... | collective-permute-start | bytes 1572872 | tf_op jit(solution)/shard_map/ppermute | solution.py:44
  54.7 7.0 %collective-permute-start.8 = (bf16[512,4,128]{2,1,0:T(4,128)(2,1)S(1)}, bf16[512,4,128]{2,1,0:T(4,128)(2,1)S(1)}, u32[]{:S(2)}, u32[]{:S(2)}) collective-permute-start(bf16[512,4,128]{2,1,0:T(4,128)(2,1)S(1)} %collective-permute-done.4.refs_1_), channel_id=1, source_target_pairs={{0,16},{1,17},{2,18},{3,19},{4,20},{5,21},{6,22},{7,23},{8,24},{9,... | collective-permute-start | bytes 1572872 | tf_op jit(solution)/shard_map/ppermute | solution.py:44
  55.2 8.1 %copy-start.3 = (bf16[512,4,128]{2,1,0:T(4,128)(2,1)}, bf16[512,4,128]{2,1,0:T(4,128)(2,1)S(1)}, u32[]{:S(2)}) copy-start(bf16[512,4,128]{2,1,0:T(4,128)(2,1)S(1)} %collective-permute-done.6.refs_2_) | copy-start | bytes 1572868
  55.2 6.5 %collective-permute-start.9 = (bf16[512,4,128]{2,1,0:T(4,128)(2,1)S(1)}, bf16[512,4,128]{2,1,0:T(4,128)(2,1)S(1)}, u32[]{:S(2)}, u32[]{:S(2)}) collective-permute-start(bf16[512,4,128]{2,1,0:T(4,128)(2,1)S(1)} %collective-permute-done.6.refs_2_), channel_id=1, source_target_pairs={{0,16},{1,17},{2,18},{3,19},{4,20},{5,21},{6,22},{7,23},{8,24},{9,... | collective-permute-start | bytes 1572872 | tf_op jit(solution)/shard_map/ppermute | solution.py:44
  59.5 3.8 %copy-start.4 = (bf16[512,4,128]{2,1,0:T(4,128)(2,1)}, bf16[512,4,128]{2,1,0:T(4,128)(2,1)S(1)}, u32[]{:S(2)}) copy-start(bf16[512,4,128]{2,1,0:T(4,128)(2,1)S(1)} %collective-permute-done.5.refs_3_) | copy-start | bytes 1572868
  59.5 3.8 %collective-permute-start.10 = (bf16[512,4,128]{2,1,0:T(4,128)(2,1)S(1)}, bf16[512,4,128]{2,1,0:T(4,128)(2,1)S(1)}, u32[]{:S(2)}, u32[]{:S(2)}) collective-permute-start(bf16[512,4,128]{2,1,0:T(4,128)(2,1)S(1)} %collective-permute-done.5.refs_3_), channel_id=1, source_target_pairs={{0,16},{1,17},{2,18},{3,19},{4,20},{5,21},{6,22},{7,23},{8,24},{9,... | collective-permute-start | bytes 1572872 | tf_op jit(solution)/shard_map/ppermute | solution.py:44
  61.8 1.5 %copy-start.5 = (bf16[512,4,128]{2,1,0:T(4,128)(2,1)}, bf16[512,4,128]{2,1,0:T(4,128)(2,1)S(1)}, u32[]{:S(2)}) copy-start(bf16[512,4,128]{2,1,0:T(4,128)(2,1)S(1)} %collective-permute-done.7.refs_4_) | copy-start | bytes 1572868
  61.8 1.6 %copy-start.7 = (bf16[512,4,128]{2,1,0:T(4,128)(2,1)}, bf16[512,4,128]{2,1,0:T(4,128)(2,1)S(1)}, u32[]{:S(2)}) copy-start(bf16[512,4,128]{2,1,0:T(4,128)(2,1)S(1)} %collective-permute-done.9.refs_6_) | copy-start | bytes 1572868
  61.8 1.5 %copy-start.6 = (bf16[512,4,128]{2,1,0:T(4,128)(2,1)}, bf16[512,4,128]{2,1,0:T(4,128)(2,1)S(1)}, u32[]{:S(2)}) copy-start(bf16[512,4,128]{2,1,0:T(4,128)(2,1)S(1)} %collective-permute-done.8.refs_5_) | copy-start | bytes 1572868
  63.3 0.8 %copy-start.8 = (bf16[512,4,128]{2,1,0:T(4,128)(2,1)}, bf16[512,4,128]{2,1,0:T(4,128)(2,1)S(1)}, u32[]{:S(2)}) copy-start(bf16[512,4,128]{2,1,0:T(4,128)(2,1)S(1)} %collective-permute-done.10.refs_7_) | copy-start | bytes 1572868

commit v4 on v3

--- a/solution.py
+++ b/solution.py
@@ -9,8 +9,7 @@
 BLK = 128
 GROUP = 4
 ROWS = GROUP * BLK
-RIM = 40
-NEAR = 5
+RIMS = 4
 FAR = 8
 VMEM = 56 << 20
 BF = jnp.bfloat16
@@ -100,33 +99,51 @@
     return copies
 
 
-def early_kernel(near_index, tiles, *refs):
-    pieces = refs[:NEAR]
-    (
-        edge_ref,
-        recv_ref,
-        node_ref,
-        we_ref,
-        ws_ref,
-        wr_ref,
-        wn_ref,
-        pre_ref,
-        nf_ref,
-        table,
-        sent,
-        got_ref,
-        sem,
-    ) = refs[NEAR:]
+def coarse_kernel(node_ref, out_hbm, west_ref, east_ref, top_ref, bottom_ref, wide, tall, block, sem):
+    nodes, sides, cols = node_ref.shape[0], west_ref.shape[0], top_ref.shape[0]
+    per = block.shape[0]
+    run = cols // 4
+    starts = []
+    at = 0
+    for rows in (per, sides, sides, cols, cols):
+        starts.append(at)
+        at += rows
+    for j in range(4):
+        wide[j * nodes : (j + 1) * nodes, :] = node_ref[:, j * 128 : (j + 1) * 128].astype(F32)
+
+    def take(start, count, j, first, stride):
+        source = pl.ds(j * nodes + first, count, stride=stride)
+        tall[pl.ds(start * 4 + j, count, stride=4), :] = wide[source, :]
+
+    for j in range(4):
+        for r in range(sides // 4):
+            take(starts[0] + r * run, run, j, 4 * r * cols, 4)
+        take(starts[1], sides, j, 0, cols)
+        take(starts[2], sides, j, cols - 1, cols)
+        take(starts[3], cols, j, 0, 1)
+        take(starts[4], cols, j, nodes - cols, 1)
+    outs = (block, west_ref, east_ref, top_ref, bottom_ref)
+    for start, out in zip(starts, outs):
+        for i in range(out.shape[0]):
+            out[i] = tall[(start + i) * 4 : (start + i) * 4 + 4, :].astype(BF)
+        if out is block:
+            stores = [
+                pltpu.make_async_copy(block, out_hbm.at[d], sem.at[d])
+                for d in range(out_hbm.shape[0])
+            ]
+            for store in stores:
+                store.start()
+    for store in stores:
+        store.wait()
+
+
+def early_kernel(tiles, edge_ref, recv_ref, node_ref, we_ref, wr_ref, wn_ref, part_ref, nf_ref, got_ref):
     step = pl.program_id(0)
 
     @pl.when(step == 0)
     def _():
-        copies = load_table(pieces, table, sem)
         nf_ref[...] = dot(node_ref[...], wn_ref[...])
-        for copy in copies:
-            copy.wait()
-
-    fetch(ROWS // 16, 16, lambda e: (e, near_index[step * ROWS + e]), table, sent)
+
     for k in range(GROUP):
         tile = pl.multiple_of(tiles[step * GROUP + k] * BLK, BLK)
         hot = chosen(recv_ref[k : k + 1, :])
@@ -137,11 +154,37 @@
             preferred_element_type=F32,
         )
         got_ref[k * BLK : (k + 1) * BLK, :] = rows.astype(BF)
-    pre_ref[...] = (
-        dot(edge_ref[...], we_ref[...])
-        + dot(got_ref[...], wr_ref[...])
-        + dot(sent_rows(sent), ws_ref[...])
-    ).astype(BF)
+    part_ref[...] = dot(edge_ref[...], we_ref[...]) + dot(got_ref[...], wr_ref[...])
+
+
+def near_kernel(near_index, node_ref, *refs):
+    rims = refs[:RIMS]
+    part_ref, ws_ref, pre_ref, tall, sent = refs[RIMS:]
+    nodes = node_ref.shape[0]
+    step = pl.program_id(0)
+
+    @pl.when(step == 0)
+    def _():
+        for j in range(4):
+            tall[pl.ds(j, nodes, stride=4), :] = node_ref[:, j * 128 : (j + 1) * 128].astype(F32)
+        at = nodes * 4
+        for rim in rims:
+            for i in range(rim.shape[0]):
+                tall[at : at + 4, :] = rim[i].astype(F32)
+                at += 4
+        tall[at : at + 4, :] = jnp.zeros((4, 128), F32)
+
+    def body(i, carry):
+        for u in range(16):
+            e = i * 16 + u
+            row = near_index[step * ROWS + e]
+            sent[pl.ds(pl.multiple_of(e * 4, 4), 4), :] = tall[
+                pl.ds(pl.multiple_of(row * 4, 4), 4), :
+            ]
+        return carry
+
+    lax.fori_loop(0, ROWS // 16, body, 0)
+    pre_ref[...] = (part_ref[...] + dot(sent_rows(sent), ws_ref[...])).astype(BF)
 
 
 def late_kernel(far_list, far_count, tiles, lives, *refs):
@@ -264,47 +307,53 @@
     return whole, part, recv_spec, weight, anywhere
 
 
-def early_call(near_index, block_tile, near_pieces, edge_latent, recv_rows, own_rows, w_first, w_node_first):
+def early_call(block_tile, edge_latent, recv_rows, own_rows, w_first, w_node_first):
     whole, part, recv_spec, weight, anywhere = specs()
     blocks, nodes = block_tile.shape[0], own_rows.shape[0]
-    steps = blocks // GROUP
-    near_rows = sum(piece.shape[0] for piece in near_pieces)
     return pl.pallas_call(
         early_kernel,
         name="early",
         grid_spec=pltpu.PrefetchScalarGridSpec(
-            num_scalar_prefetch=2,
-            grid=(steps,),
-            in_specs=[anywhere] * NEAR
-            + [part, recv_spec, whole((nodes, F)), weight(0), weight(1), weight(2), weight(0)],
+            num_scalar_prefetch=1,
+            grid=(blocks // GROUP,),
+            in_specs=[part, recv_spec, whole((nodes, F)), weight(0), weight(2), weight(0)],
             out_specs=[part, whole((nodes, F))],
-            scratch_shapes=[
-                pltpu.VMEM((near_rows, 4, 128), BF),
-                pltpu.VMEM((ROWS * 4, 128), F32),
-                pltpu.VMEM((ROWS, F), BF),
-                pltpu.SemaphoreType.DMA((NEAR,)),
-            ],
+            scratch_shapes=[pltpu.VMEM((ROWS, F), BF)],
         ),
         out_shape=[
-            jax.ShapeDtypeStruct((blocks * BLK, F), BF),
+            jax.ShapeDtypeStruct((blocks * BLK, F), F32),
             jax.ShapeDtypeStruct((nodes, F), F32),
         ],
         compiler_params=pltpu.CompilerParams(vmem_limit_bytes=VMEM),
         cost_estimate=pl.CostEstimate(
-            flops=4 * 10**9, bytes_accessed=10 * 10**6, transcendentals=0
+            flops=3 * 10**9, bytes_accessed=10 * 10**6, transcendentals=0
         ),
-    )(
-        near_index,
-        block_tile,
-        *near_pieces,
-        edge_latent,
-        recv_rows,
-        own_rows,
-        w_first,
-        w_first,
-        w_first,
-        w_node_first,
-    )
+    )(block_tile, edge_latent, recv_rows, own_rows, w_first, w_first, w_node_first)
+
+
+def near_call(near_index, own_rows, rims, partial, w_first):
+    whole, part, recv_spec, weight, anywhere = specs()
+    slots, nodes = partial.shape[0], own_rows.shape[0]
+    near_rows = nodes + sum(rim.shape[0] for rim in rims) + 1
+    return pl.pallas_call(
+        near_kernel,
+        name="near",
+        grid_spec=pltpu.PrefetchScalarGridSpec(
+            num_scalar_prefetch=1,
+            grid=(slots // ROWS,),
+            in_specs=[whole((nodes, F))] + [whole(rim.shape) for rim in rims] + [part, weight(1)],
+            out_specs=part,
+            scratch_shapes=[
+                pltpu.VMEM((near_rows * 4 + 4, 128), F32),
+                pltpu.VMEM((ROWS * 4, 128), F32),
+            ],
+        ),
+        out_shape=jax.ShapeDtypeStruct((slots, F), BF),
+        compiler_params=pltpu.CompilerParams(vmem_limit_bytes=VMEM),
+        cost_estimate=pl.CostEstimate(
+            flops=2 * 10**9, bytes_accessed=8 * 10**6, transcendentals=0
+        ),
+    )(near_index, own_rows, *rims, partial, w_first)
 
 
 def late_call(
@@ -411,21 +460,43 @@
     up = [(i, i + 1) for i in range(lat_count - 1)]
     down = [(j, i) for i, j in up]
 
-    coarse_own = lanes(node_latent[::4, ::4])
-    copies = jnp.broadcast_to(coarse_own, (lon_count, *coarse_own.shape))
-    copies, latent = lax.optimization_barrier((copies, node_latent))
+    per = patch_rows // 4 * (patch_cols // 4)
+    lane_rows = lambda rows: jax.ShapeDtypeStruct((rows, 4, 128), BF)
+    copies, first_col, last_col, top, bottom = pl.pallas_call(
+        coarse_kernel,
+        name="coarse",
+        in_specs=[pl.BlockSpec(memory_space=pltpu.VMEM)],
+        out_specs=[pl.BlockSpec(memory_space=pl.ANY)] + [pl.BlockSpec(memory_space=pltpu.VMEM)] * 4,
+        scratch_shapes=[
+            pltpu.VMEM((nodes * 4, 128), F32),
+            pltpu.VMEM((4 * (per + 2 * patch_rows + 2 * patch_cols), 128), F32),
+            pltpu.VMEM((per, 4, 128), BF),
+            pltpu.SemaphoreType.DMA((lon_count,)),
+        ],
+        out_shape=[
+            jax.ShapeDtypeStruct((lon_count, per, 4, 128), BF),
+            lane_rows(patch_rows),
+            lane_rows(patch_rows),
+            lane_rows(patch_cols),
+            lane_rows(patch_cols),
+        ],
+        compiler_params=pltpu.CompilerParams(vmem_limit_bytes=VMEM),
+    )(own_rows)
+    west = lax.ppermute(last_col, "lon", right)
+    east = lax.ppermute(first_col, "lon", left)
     plane = lanes(lax.all_to_all(copies, "lon", split_axis=0, concat_axis=0, tiled=True))
-
-    west = lax.ppermute(latent[:, -1:], "lon", right)
-    east = lax.ppermute(latent[:, :1], "lon", left)
-    row_of = lambda r: jnp.concatenate([west[r], latent[r], east[r]], 0)
-    north = lax.ppermute(row_of(patch_rows - 1), "lat", up)
-    south = lax.ppermute(row_of(0), "lat", down)
-    plane, north, south = lax.optimization_barrier((plane, north, south))
-    own, ahead, behind = plane, move(plane, "x", (1, -1)), move(plane, "x", (-1, 1))
-
-    pad = lambda a: jnp.pad(lanes(a), ((0, RIM - patch_cols - 2), (0, 0), (0, 0)))
-    near_pieces = [lanes(own_rows), lanes(west), lanes(east), pad(north), pad(south)]
+    wide = lambda r, rows: jnp.concatenate([west[r : r + 1], rows, east[r : r + 1]], 0)
+    north = lax.ppermute(wide(patch_rows - 1, bottom), "lat", up)
+    south = lax.ppermute(wide(0, top), "lat", down)
+    recv_rows = receiver.reshape(steps, GROUP, BLK)
+    copies, edges = lax.optimization_barrier((copies, edge_latent))
+    partial, node_first = early_call(
+        block_tile, edges, recv_rows, own_rows, w_first, w_node_first
+    )
+    plane, north, south, partial = lax.optimization_barrier((plane, north, south, partial))
+
+    ahead, behind = move(plane, "x", (1, -1)), move(plane, "x", (-1, 1))
+    plane_other = other_core(plane)
 
     senders = jnp.maximum(sender, 0)
     send_row = senders // grid_cols
@@ -435,31 +506,29 @@
     is_near = (row >= -1) & (row <= patch_rows) & (col <= patch_cols)
     side = jnp.where(col < 0, nodes + row, nodes + patch_rows + row)
     inner = jnp.where((col < 0) | (col >= patch_cols), side, row * patch_cols + col)
-    rim = nodes + 2 * patch_rows
+    rim, span = nodes + 2 * patch_rows, patch_cols + 2
     near_index = jnp.where(
-        row < 0, rim + col + 1, jnp.where(row >= patch_rows, rim + RIM + col + 1, inner)
-    )
-    no_row = rim + patch_cols + 2
-    near_index = jnp.where(is_near, near_index, no_row)
+        row < 0, rim + col + 1, jnp.where(row >= patch_rows, rim + span + col + 1, inner)
+    )
+    near_index = jnp.where(is_near, near_index, rim + 2 * span)
     src_lat, src_lon = send_row // patch_rows, send_col // patch_cols
     src_core, core = src_lat % 2, lat_index % 2
     at_x = ring_place((src_lat // 2 - lat_index // 2) % 4, src_core)
     half = jnp.where(src_core == core, 0, 1)
     within = send_row % patch_rows // 4 * (patch_cols // 4) + send_col % patch_cols // 4
-    per = patch_rows // 4 * (patch_cols // 4)
     far_index = ((half * 4 + at_x) * lon_count + src_lon) * per + within
     far_list, far_count = far_lists((receiver >= 0) & ~is_near, far_index, steps)
-    recv_rows = receiver.reshape(steps, GROUP, BLK)
     lives = jnp.sum((receiver >= 0).astype(jnp.int32).reshape(blocks, BLK), 1)
 
-    pre, node_first = early_call(
-        near_index, block_tile, near_pieces, edge_latent, recv_rows, own_rows, w_first, w_node_first
-    )
+    rims = [west, east, north, south]
+    pre = near_call(near_index, own_rows, rims, partial, w_first)
     ahead, pre = lax.optimization_barrier((ahead, pre))
     across = move(ahead, "x", (1, -1))
-    across, far_list, far_count = lax.optimization_barrier((across, far_list, far_count))
-    halves = [own, ahead, behind, across]
-    far_pieces = halves + [other_core(piece) for piece in halves]
+    across, far_list, far_count, lives = lax.optimization_barrier(
+        (across, far_list, far_count, lives)
+    )
+    far_pieces = [plane, ahead, behind, across, plane_other]
+    far_pieces += [other_core(piece) for piece in (ahead, behind, across)]
     edge_out, node_out = late_call(
         far_list,
         far_count,

time: 78.9 us -> 75.2 us (0.953)
  local copies, waits for them, and re-layouts: 9.65 us -> 1.43 us
  Pallas kernels: 26.8 us -> 33.7 us
  other arithmetic: 6 us -> 3.87 us
    pallas_call x0 -> x2, Pallas kernels: none -> 11.3 us  [the longest x1 8.64 us: near_call(): pl.pallas_call(near_kernel, name='near', grid_spec=pltpu.PrefetchScalarGr...]
    pallas_call x1, Pallas kernels: 12.7 us -> 8.21 us  [early_call(): pl.pallas_call(early_kernel, name='early', grid_spec=pltpu.PrefetchScalar...]
    slice x2, local copies, waits for them, and re-layouts: 3.02 us -> 0.01 us  [the longest x1 0.01 us: per_device(): east[r:r + 1]]
    reshape x5 -> x0, local copies, waits for them, and re-layouts: 1.27 us -> none  [per_device(): lanes = lambda a: a.reshape(-1, 4, 128)]
    pad x2 -> x0, local copies, waits for them, and re-layouts: 1.26 us -> none  [per_device(): jnp.pad(lanes(a), ((0, RIM - patch_cols - 2), (0, 0), (0, 0)))]
    broadcast_in_dim x1 -> x0, local copies, waits for them, and re-layouts: 1 us -> none  [per_device(): copies = jnp.broadcast_to(coarse_own, (lon_count, *coarse_own.shape))]
    another operation x1 -> x0, local copies, waits for them, and re-layouts: 0.92 us -> none  [per_device(): lanes = lambda a: a.reshape(-1, 4, 128)]
    squeeze x3 -> x0, local copies, waits for them, and re-layouts: 0.79 us -> none  [per_device(): row_of = lambda r: jnp.concatenate([west[r], latent[r], east[r]], 0)]
  transfers between devices with their start and end apart: 12 -> 12, of which waited for: 4 -> 3; matrix products, arithmetic and copies ran while one was open for 15% -> 6% of each run, Pallas kernels for 16% -> 23%
where the time goes in v4:
time: 75.2 us; the launch traced here: 74.7 us
  Pallas kernels  33.7 us (45%)
  starting transfers between devices  25.7 us (34%)
  waiting for transfers between devices  8.89 us (12%)
  other arithmetic  3.87 us (5%)
  local copies, waits for them, and re-layouts  1.43 us (2%)
  between operations  1.03 us (1%)
    pallas_call x1, Pallas kernels, late_call(): pl.pallas_call(late_kernel, name='late', in_specs=[scalars] * 4 + [anywhe...  14.1 us
    pallas_call x1, Pallas kernels, near_call(): pl.pallas_call(near_kernel, name='near', grid_spec=pltpu.PrefetchScalarGr...  8.64 us
    all_to_all x1, starting transfers between devices, per_device(): lax.all_to_all(copies, 'lon', split_axis=0, concat_axis=0, tiled=True)  8.61 us
    pallas_call x1, Pallas kernels, early_call(): pl.pallas_call(early_kernel, name='early', grid_spec=pltpu.PrefetchScalar...  8.21 us
    ppermute x1, starting transfers between devices, per_device(): north = lax.ppermute(wide(patch_rows - 1, bottom), 'lat', up)  4.52 us
    ppermute x3, waiting for transfers between devices, move(): return lax.ppermute(value, ('lat', 'lon'), shift(axis, by_core))  4.14 us
    ppermute x1, starting transfers between devices, per_device(): east = lax.ppermute(first_col, 'lon', left)  3.49 us
    ppermute x1, waiting for transfers between devices, per_device(): south = lax.ppermute(wide(0, top), 'lat', down)  3.24 us
  transfers between devices with their start and end apart: 12, of which 3 were waited for; matrix products, arithmetic and copies ran while one was open for 6% of the time, Pallas kernels for 23%

profile of v4, /device:TPU:1, one launch (start us, length us, event | category | flops | bytes accessed | tf_op | source)
XLA Modules:
  0.0 74.7 jit_solution(8731289322642548601)
XLA Ops:
  0.6 2.7 %coarse.1 = (bf16[16,32,4,128]{3,2,1,0:T(4,128)(2,1)}, bf16[16,4,128]{2,1,0:T(4,128)(2,1)}, bf16[16,4,128]{2,1,0:T(4,128)(2,1)}, bf16[32,4,128]{2,1,0:T(4,128)(2,1)}, bf16[32,4,128]{2,1,0:T(4,128)(2,1)}) custom-call(bf16[512,512]{1,0:T(8,128)(2,1)} %bitcast.12), custom_call_target="tpu_custom_call" | custom-call | tf_op jit(solution)/shard_map/coarse/pallas_call | solution.py:465
  3.3 8.6 %all-to-all-start = ((bf16[16,32,4,128]{3,2,1,0:T(4,128)(2,1)}), bf16[16,32,4,128]{3,2,1,0:T(4,128)(2,1)S(1)}, u32[]{:S(2)}, u32[]{:S(2)}) async-start(bf16[16,32,4,128]{3,2,1,0:T(4,128)(2,1)} %get-tuple-element.22), calls=%async_computation | async-start | bytes 1048576 | tf_op jit(solution)/shard_map/all_to_all | solution.py:487
  11.9 1.4 %collective-permute-start = (bf16[16,4,128]{2,1,0:T(4,128)(2,1)}, bf16[16,4,128]{2,1,0:T(4,128)(2,1)S(1)}, u32[]{:S(2)}, u32[]{:S(2)}) collective-permute-start(bf16[16,4,128]{2,1,0:T(4,128)(2,1)} %get-tuple-element.23), channel_id=1, source_target_pairs={{0,1},{1,2},{2,3},{3,4},{4,5},{5,6},{6,7},{7,8},{8,9},{9,10},{10,1... | collective-permute-start | bytes 49160 | tf_op jit(solution)/shard_map/ppermute | solution.py:485
  13.3 3.5 %collective-permute-start.1 = (bf16[16,4,128]{2,1,0:T(4,128)(2,1)}, bf16[16,4,128]{2,1,0:T(4,128)(2,1)S(1)}, u32[]{:S(2)}, u32[]{:S(2)}) collective-permute-start(bf16[16,4,128]{2,1,0:T(4,128)(2,1)} %get-tuple-element.25), channel_id=1, source_target_pairs={{1,0},{2,1},{3,2},{4,3},{5,4},{6,5},{7,6},{8,7},{9,8},{10,9},{11,1... | collective-permute-start | bytes 49160 | tf_op jit(solution)/shard_map/ppermute | solution.py:486
  16.8 0.0 copy-start.8
  16.8 0.0 copy-start.5
  16.8 0.0 copy-start.3
  16.8 8.2 %early.1 = (f32[2048,512]{1,0:T(8,128)}, f32[512,512]{1,0:T(8,128)}) custom-call(s32[16]{0:T(128)} %tiles.3, bf16[2048,512]{1,0:T(8,128)(2,1)} %refs_9_.1, s32[4,4,128]{2,1,0:T(4,128)} %bitcast.20, bf16[512,512]{1,0:T(8,128)(2,1)} %bitcast.13, bf16[1536,512]{1,0:T(8,128)(2,1)} %refs_12_.1, bf16[1536,512]{1,0:T(8,128)(2,1)} %refs_12_.1, ...), custom_call_target="tpu_custom_call" | custom-call | flops 3000000000 | bytes 10000000 | tf_op jit(solution)/shard_map/early/pallas_call | solution.py:313
  25.0 0.0 copy-done.8
  25.0 0.7 bitcast_reduce_fusion
  25.7 0.0 collective-permute-done.refs_0_
  25.7 0.0 copy-start.6
  25.7 0.0 collective-permute-done.1.refs_1_
  25.7 0.0 copy-start.7
  25.8 0.0 copy-done.5
  25.8 4.5 %collective-permute-start.2 = (bf16[34,4,128]{2,1,0:T(4,128)(2,1)S(1)}, bf16[34,4,128]{2,1,0:T(4,128)(2,1)S(1)}, u32[]{:S(2)}, u32[]{:S(2)}) collective-permute-start(bf16[34,4,128]{2,1,0:T(4,128)(2,1)S(1)} %pad_maximum_fusion), channel_id=1, source_target_pairs={{0,16},{16,32},{32,48},{48,64},{64,80},{80,96},{96,112},{1,17},{17... | collective-permute-start | bytes 104456 | tf_op jit(solution)/shard_map/ppermute | solution.py:489
  30.3 0.0 copy-done.4
  30.4 1.9 %collective-permute-start.3 = (bf16[34,4,128]{2,1,0:T(4,128)(2,1)S(1)}, bf16[34,4,128]{2,1,0:T(4,128)(2,1)S(1)}, u32[]{:S(2)}, u32[]{:S(2)}) collective-permute-start(bf16[34,4,128]{2,1,0:T(4,128)(2,1)S(1)} %pad_maximum_fusion.1), channel_id=1, source_target_pairs={{16,0},{32,16},{48,32},{64,48},{80,64},{96,80},{112,96},{17,1},{33... | collective-permute-start | bytes 104456 | tf_op jit(solution)/shard_map/ppermute | solution.py:490
  32.3 0.0 copy-done.3
  32.4 0.0 collective-permute-done.2.refs_2_
  32.4 0.0 copy-start.1
  32.4 3.2 %collective-permute-done.3.refs_3_ = bf16[34,4,128]{2,1,0:T(4,128)(2,1)S(1)} collective-permute-done((bf16[34,4,128]{2,1,0:T(4,128)(2,1)S(1)}, bf16[34,4,128]{2,1,0:T(4,128)(2,1)S(1)}, u32[]{:S(2)}, u32[]{:S(2)}) %collective-permute-start.3) | collective-permute-done | bytes 34848 | tf_op jit(solution)/shard_map/ppermute | solution.py:490
  35.6 0.0 copy-start.2
  35.6 0.0 all-to-all-done
  35.6 0.0 copy-start
  35.6 0.1 collective-permute-start.4
  35.7 0.7 fusion.9
  36.4 0.1 iota_compare_fusion.1
  36.5 0.6 select_reduce_fusion.1
  37.2 1.5 %collective-permute-start.6 = (bf16[512,4,128]{2,1,0:T(4,128)(2,1)S(1)}, bf16[512,4,128]{2,1,0:T(4,128)(2,1)S(1)}, u32[]{:S(2)}, u32[]{:S(2)}) collective-permute-start(bf16[512,4,128]{2,1,0:T(4,128)(2,1)S(1)} %bitcast.17), channel_id=1, source_target_pairs={{0,96},{1,97},{2,98},{3,99},{4,100},{5,101},{6,102},{7,103},{8,104... | collective-permute-start | bytes 1572872 | tf_op jit(solution)/shard_map/ppermute | solution.py:47
  38.7 0.0 copy-done.6
  38.7 0.0 copy-done.7
  38.7 0.0 copy-done.1
  38.7 0.0 copy-done.2
  38.7 8.6 %near.1.refs_8_ = bf16[2048,512]{1,0:T(8,128)(2,1)} custom-call(s32[2048]{0:T(1024)} %get-tuple-element.51.near_index, bf16[512,512]{1,0:T(8,128)(2,1)} %bitcast.14, bf16[16,4,128]{2,1,0:T(4,128)(2,1)} %copy-done.6, bf16[16,4,128]{2,1,0:T(4,128)(2,1)} %copy-done.7, bf16[34,4,128]{2,1,0:T(4,128)(2,1)} %copy-done.1, bf16[34,4,128]{2,1,0:T(4,128)(2,1)} %copy-done.2, ...), custom_call_target="tpu_custom_call" | custom-call | flops 2000000000 | bytes 8000000 | tf_op jit(solution)/shard_map/near/pallas_call | solution.py:338
  47.3 0.0 collective-permute-done.4.refs_1_
  47.3 1.4 %collective-permute-start.5 = (bf16[512,4,128]{2,1,0:T(4,128)(2,1)S(1)}, bf16[512,4,128]{2,1,0:T(4,128)(2,1)S(1)}, u32[]{:S(2)}, u32[]{:S(2)}) collective-permute-start(bf16[512,4,128]{2,1,0:T(4,128)(2,1)S(1)} %collective-permute-done.4.refs_1_), channel_id=1, source_target_pairs={{0,32},{1,33},{2,34},{3,35},{4,36},{5,37},{6,38},{7,39},{8,40},{9,... | collective-permute-start | bytes 1572872 | tf_op jit(solution)/shard_map/ppermute | solution.py:47
  48.7 1.0 %select_reduce_fusion = s32[4,512]{1,0:T(4,128)S(1)} fusion(s32[4,512]{1,0:T(4,128)S(1)} %broadcast_in_dim.55, s32[4,512]{1,0:T(4,128)S(1)} %select_reduce_fusion.1, pred[4,512]{1,0:T(4,128)(4,1)S(1)} %reshape.61), kind=kLoop, calls=%fused_computation | loop fusion | flops 4192256 | bytes 26624 | tf_op jit(solution)/shard_map/reduce_sum | solution.py:298
  49.7 0.6 copy.13
  50.3 0.7 convert_reduce_fusion.far_count
  51.0 0.0 copy-done
  51.0 0.0 collective-permute-start.7
  51.0 0.5 collective-permute-start.8
  51.5 0.0 collective-permute-done.6.refs_2_
  51.5 0.0 copy-start.10
  51.5 0.1 collective-permute-start.9
  51.6 4.1 %collective-permute-done.5.refs_3_ = bf16[512,4,128]{2,1,0:T(4,128)(2,1)S(1)} collective-permute-done((bf16[512,4,128]{2,1,0:T(4,128)(2,1)S(1)}, bf16[512,4,128]{2,1,0:T(4,128)(2,1)S(1)}, u32[]{:S(2)}, u32[]{:S(2)}) %collective-permute-start.5) | collective-permute-done | bytes 524320 | tf_op jit(solution)/shard_map/ppermute | solution.py:47
  55.7 0.0 copy-start.11
  55.7 2.3 %collective-permute-start.10 = (bf16[512,4,128]{2,1,0:T(4,128)(2,1)S(1)}, bf16[512,4,128]{2,1,0:T(4,128)(2,1)S(1)}, u32[]{:S(2)}, u32[]{:S(2)}) collective-permute-start(bf16[512,4,128]{2,1,0:T(4,128)(2,1)S(1)} %collective-permute-done.5.refs_3_), channel_id=1, source_target_pairs={{0,16},{1,17},{2,18},{3,19},{4,20},{5,21},{6,22},{7,23},{8,24},{9,... | collective-permute-start | bytes 1572872 | tf_op jit(solution)/shard_map/ppermute | solution.py:43
  58.0 0.0 collective-permute-done.7.refs_4_
  58.0 0.0 copy-start.12
  58.0 0.0 collective-permute-done.9.refs_6_
  58.0 0.0 copy-start.14
  58.1 0.0 collective-permute-done.8.refs_5_
  58.1 0.0 copy-start.13
  58.1 1.5 %collective-permute-done.10.refs_7_ = bf16[512,4,128]{2,1,0:T(4,128)(2,1)S(1)} collective-permute-done((bf16[512,4,128]{2,1,0:T(4,128)(2,1)S(1)}, bf16[512,4,128]{2,1,0:T(4,128)(2,1)S(1)}, u32[]{:S(2)}, u32[]{:S(2)}) %collective-permute-start.10) | collective-permute-done | bytes 524320 | tf_op jit(solution)/shard_map/ppermute | solution.py:43
  59.6 0.0 copy-done.9
  59.6 0.0 copy-done.10
  59.6 0.0 copy-done.11
  59.6 0.0 copy-done.12
  59.6 0.0 copy-done.14
  59.6 0.0 copy-done.13
  59.6 0.7 copy-done.15
  60.4 14.1 %late.1 = (bf16[2048,512]{1,0:T(8,128)(2,1)}, bf16[512,512]{1,0:T(8,128)(2,1)}) custom-call(s32[2048]{0:T(1024)} %bitcast.22, s32[4]{0:T(128)} %convert_reduce_fusion.far_count, s32[16]{0:T(128)} %tiles.3, s32[16]{0:T(128)} %get-tuple-element.36.lives, bf16[512,4,128]{2,1,0:T(4,128)(2,1)} %bitcast.19, bf16[512,4,128]{2,1,0:T(4,128)(2,1)} %copy-done.9, ...), custom_call_target="tpu_custom_call" | custom-call | flops 4000000000 | bytes 14000000 | tf_op jit(solution)/shard_map/late/pallas_call | solution.py:384
  (12 shorter events, 0.1 us)
Async XLA Ops:
  3.3 32.3 %all-to-all-start = ((bf16[16,32,4,128]{3,2,1,0:T(4,128)(2,1)}), bf16[16,32,4,128]{3,2,1,0:T(4,128)(2,1)S(1)}, u32[]{:S(2)}, u32[]{:S(2)}) async-start(bf16[16,32,4,128]{3,2,1,0:T(4,128)(2,1)} %get-tuple-element.22), calls=%async_computation | async-start | bytes 1048576 | tf_op jit(solution)/shard_map/all_to_all | solution.py:487
  11.9 13.8 %collective-permute-start = (bf16[16,4,128]{2,1,0:T(4,128)(2,1)}, bf16[16,4,128]{2,1,0:T(4,128)(2,1)S(1)}, u32[]{:S(2)}, u32[]{:S(2)}) collective-permute-start(bf16[16,4,128]{2,1,0:T(4,128)(2,1)} %get-tuple-element.23), channel_id=1, source_target_pairs={{0,1},{1,2},{2,3},{3,4},{4,5},{5,6},{6,7},{7,8},{8,9},{9,10},{10,1... | collective-permute-start | bytes 49160 | tf_op jit(solution)/shard_map/ppermute | solution.py:485
  13.3 12.4 %collective-permute-start.1 = (bf16[16,4,128]{2,1,0:T(4,128)(2,1)}, bf16[16,4,128]{2,1,0:T(4,128)(2,1)S(1)}, u32[]{:S(2)}, u32[]{:S(2)}) collective-permute-start(bf16[16,4,128]{2,1,0:T(4,128)(2,1)} %get-tuple-element.25), channel_id=1, source_target_pairs={{1,0},{2,1},{3,2},{4,3},{5,4},{6,5},{7,6},{8,7},{9,8},{10,9},{11,1... | collective-permute-start | bytes 49160 | tf_op jit(solution)/shard_map/ppermute | solution.py:486
  16.8 8.2 %copy-start.8 = (s32[2048]{0:T(1024)S(1)}, s32[2048]{0:T(1024)}, u32[]{:S(2)}) copy-start(s32[2048]{0:T(1024)} %param.14) | copy-start | bytes 24580
  16.8 8.9 %copy-start.5 = (bf16[32,4,128]{2,1,0:T(4,128)(2,1)S(1)}, bf16[32,4,128]{2,1,0:T(4,128)(2,1)}, u32[]{:S(2)}) copy-start(bf16[32,4,128]{2,1,0:T(4,128)(2,1)} %get-tuple-element.24) | copy-start | bytes 98308
  16.8 13.5 %copy-start.4 = (bf16[32,4,128]{2,1,0:T(4,128)(2,1)S(1)}, bf16[32,4,128]{2,1,0:T(4,128)(2,1)}, u32[]{:S(2)}) copy-start(bf16[32,4,128]{2,1,0:T(4,128)(2,1)} %get-tuple-element.26) | copy-start | bytes 98308
  16.8 15.5 %copy-start.3 = (s32[2048]{0:T(1024)S(1)}, s32[2048]{0:T(1024)}, u32[]{:S(2)}) copy-start(s32[2048]{0:T(1024)} %param.13) | copy-start | bytes 24580
  25.7 12.9 %copy-start.6 = (bf16[16,4,128]{2,1,0:T(4,128)(2,1)}, bf16[16,4,128]{2,1,0:T(4,128)(2,1)S(1)}, u32[]{:S(2)}) copy-start(bf16[16,4,128]{2,1,0:T(4,128)(2,1)S(1)} %collective-permute-done.refs_0_) | copy-start | bytes 49156
  25.7 12.9 %copy-start.7 = (bf16[16,4,128]{2,1,0:T(4,128)(2,1)}, bf16[16,4,128]{2,1,0:T(4,128)(2,1)S(1)}, u32[]{:S(2)}) copy-start(bf16[16,4,128]{2,1,0:T(4,128)(2,1)S(1)} %collective-permute-done.1.refs_1_) | copy-start | bytes 49156
  25.8 6.6 %collective-permute-start.2 = (bf16[34,4,128]{2,1,0:T(4,128)(2,1)S(1)}, bf16[34,4,128]{2,1,0:T(4,128)(2,1)S(1)}, u32[]{:S(2)}, u32[]{:S(2)}) collective-permute-start(bf16[34,4,128]{2,1,0:T(4,128)(2,1)S(1)} %pad_maximum_fusion), channel_id=1, source_target_pairs={{0,16},{16,32},{32,48},{48,64},{64,80},{80,96},{96,112},{1,17},{17... | collective-permute-start | bytes 104456 | tf_op jit(solution)/shard_map/ppermute | solution.py:489
  30.4 5.3 %collective-permute-start.3 = (bf16[34,4,128]{2,1,0:T(4,128)(2,1)S(1)}, bf16[34,4,128]{2,1,0:T(4,128)(2,1)S(1)}, u32[]{:S(2)}, u32[]{:S(2)}) collective-permute-start(bf16[34,4,128]{2,1,0:T(4,128)(2,1)S(1)} %pad_maximum_fusion.1), channel_id=1, source_target_pairs={{16,0},{32,16},{48,32},{64,48},{80,64},{96,80},{112,96},{17,1},{33... | collective-permute-start | bytes 104456 | tf_op jit(solution)/shard_map/ppermute | solution.py:490
  32.4 6.3 %copy-start.1 = (bf16[34,4,128]{2,1,0:T(4,128)(2,1)}, bf16[34,4,128]{2,1,0:T(4,128)(2,1)S(1)}, u32[]{:S(2)}) copy-start(bf16[34,4,128]{2,1,0:T(4,128)(2,1)S(1)} %collective-permute-done.2.refs_2_) | copy-start | bytes 104452
  35.6 3.0 %copy-start.2 = (bf16[34,4,128]{2,1,0:T(4,128)(2,1)}, bf16[34,4,128]{2,1,0:T(4,128)(2,1)S(1)}, u32[]{:S(2)}) copy-start(bf16[34,4,128]{2,1,0:T(4,128)(2,1)S(1)} %collective-permute-done.3.refs_3_) | copy-start | bytes 104452
  35.6 15.3 %copy-start = (bf16[16,32,4,128]{3,2,1,0:T(4,128)(2,1)}, bf16[16,32,4,128]{3,2,1,0:T(4,128)(2,1)S(1)}, u32[]{:S(2)}) copy-start(bf16[16,32,4,128]{3,2,1,0:T(4,128)(2,1)S(1)} %all-to-all-done) | copy-start | bytes 1572868
  35.6 11.7 %collective-permute-start.4 = (bf16[512,4,128]{2,1,0:T(4,128)(2,1)S(1)}, bf16[512,4,128]{2,1,0:T(4,128)(2,1)S(1)}, u32[]{:S(2)}, u32[]{:S(2)}) collective-permute-start(bf16[512,4,128]{2,1,0:T(4,128)(2,1)S(1)} %bitcast.16), channel_id=1, source_target_pairs={{0,32},{1,33},{2,34},{3,35},{4,36},{5,37},{6,38},{7,39},{8,40},{9,... | collective-permute-start | bytes 1572872 | tf_op jit(solution)/shard_map/ppermute | solution.py:47
  37.2 14.3 %collective-permute-start.6 = (bf16[512,4,128]{2,1,0:T(4,128)(2,1)S(1)}, bf16[512,4,128]{2,1,0:T(4,128)(2,1)S(1)}, u32[]{:S(2)}, u32[]{:S(2)}) collective-permute-start(bf16[512,4,128]{2,1,0:T(4,128)(2,1)S(1)} %bitcast.17), channel_id=1, source_target_pairs={{0,96},{1,97},{2,98},{3,99},{4,100},{5,101},{6,102},{7,103},{8,104... | collective-permute-start | bytes 1572872 | tf_op jit(solution)/shard_map/ppermute | solution.py:47
  47.3 12.3 %copy-start.9 = (bf16[512,4,128]{2,1,0:T(4,128)(2,1)}, bf16[512,4,128]{2,1,0:T(4,128)(2,1)S(1)}, u32[]{:S(2)}) copy-start(bf16[512,4,128]{2,1,0:T(4,128)(2,1)S(1)} %collective-permute-done.4.refs_1_) | copy-start | bytes 1572868
  47.3 8.4 %collective-permute-start.5 = (bf16[512,4,128]{2,1,0:T(4,128)(2,1)S(1)}, bf16[512,4,128]{2,1,0:T(4,128)(2,1)S(1)}, u32[]{:S(2)}, u32[]{:S(2)}) collective-permute-start(bf16[512,4,128]{2,1,0:T(4,128)(2,1)S(1)} %collective-permute-done.4.refs_1_), channel_id=1, source_target_pairs={{0,32},{1,33},{2,34},{3,35},{4,36},{5,37},{6,38},{7,39},{8,40},{9,... | collective-permute-start | bytes 1572872 | tf_op jit(solution)/shard_map/ppermute | solution.py:47
  51.0 7.1 %collective-permute-start.7 = (bf16[512,4,128]{2,1,0:T(4,128)(2,1)S(1)}, bf16[512,4,128]{2,1,0:T(4,128)(2,1)S(1)}, u32[]{:S(2)}, u32[]{:S(2)}) collective-permute-start(bf16[512,4,128]{2,1,0:T(4,128)(2,1)S(1)} %bitcast.18), channel_id=1, source_target_pairs={{0,16},{1,17},{2,18},{3,19},{4,20},{5,21},{6,22},{7,23},{8,24},{9,... | collective-permute-start | bytes 1572872 | tf_op jit(solution)/shard_map/ppermute | solution.py:43
  51.0 7.1 %collective-permute-start.8 = (bf16[512,4,128]{2,1,0:T(4,128)(2,1)S(1)}, bf16[512,4,128]{2,1,0:T(4,128)(2,1)S(1)}, u32[]{:S(2)}, u32[]{:S(2)}) collective-permute-start(bf16[512,4,128]{2,1,0:T(4,128)(2,1)S(1)} %collective-permute-done.4.refs_1_), channel_id=1, source_target_pairs={{0,16},{1,17},{2,18},{3,19},{4,20},{5,21},{6,22},{7,23},{8,24},{9,... | collective-permute-start | bytes 1572872 | tf_op jit(solution)/shard_map/ppermute | solution.py:43
  51.5 8.1 %copy-start.10 = (bf16[512,4,128]{2,1,0:T(4,128)(2,1)}, bf16[512,4,128]{2,1,0:T(4,128)(2,1)S(1)}, u32[]{:S(2)}) copy-start(bf16[512,4,128]{2,1,0:T(4,128)(2,1)S(1)} %collective-permute-done.6.refs_2_) | copy-start | bytes 1572868
  51.5 6.5 %collective-permute-start.9 = (bf16[512,4,128]{2,1,0:T(4,128)(2,1)S(1)}, bf16[512,4,128]{2,1,0:T(4,128)(2,1)S(1)}, u32[]{:S(2)}, u32[]{:S(2)}) collective-permute-start(bf16[512,4,128]{2,1,0:T(4,128)(2,1)S(1)} %collective-permute-done.6.refs_2_), channel_id=1, source_target_pairs={{0,16},{1,17},{2,18},{3,19},{4,20},{5,21},{6,22},{7,23},{8,24},{9,... | collective-permute-start | bytes 1572872 | tf_op jit(solution)/shard_map/ppermute | solution.py:43
  55.7 3.9 %copy-start.11 = (bf16[512,4,128]{2,1,0:T(4,128)(2,1)}, bf16[512,4,128]{2,1,0:T(4,128)(2,1)S(1)}, u32[]{:S(2)}) copy-start(bf16[512,4,128]{2,1,0:T(4,128)(2,1)S(1)} %collective-permute-done.5.refs_3_) | copy-start | bytes 1572868
  55.7 3.9 %collective-permute-start.10 = (bf16[512,4,128]{2,1,0:T(4,128)(2,1)S(1)}, bf16[512,4,128]{2,1,0:T(4,128)(2,1)S(1)}, u32[]{:S(2)}, u32[]{:S(2)}) collective-permute-start(bf16[512,4,128]{2,1,0:T(4,128)(2,1)S(1)} %collective-permute-done.5.refs_3_), channel_id=1, source_target_pairs={{0,16},{1,17},{2,18},{3,19},{4,20},{5,21},{6,22},{7,23},{8,24},{9,... | collective-permute-start | bytes 1572872 | tf_op jit(solution)/shard_map/ppermute | solution.py:43
  58.0 1.5 %copy-start.12 = (bf16[512,4,128]{2,1,0:T(4,128)(2,1)}, bf16[512,4,128]{2,1,0:T(4,128)(2,1)S(1)}, u32[]{:S(2)}) copy-start(bf16[512,4,128]{2,1,0:T(4,128)(2,1)S(1)} %collective-permute-done.7.refs_4_) | copy-start | bytes 1572868
  58.0 1.6 %copy-start.14 = (bf16[512,4,128]{2,1,0:T(4,128)(2,1)}, bf16[512,4,128]{2,1,0:T(4,128)(2,1)S(1)}, u32[]{:S(2)}) copy-start(bf16[512,4,128]{2,1,0:T(4,128)(2,1)S(1)} %collective-permute-done.9.refs_6_) | copy-start | bytes 1572868
  58.1 1.5 %copy-start.13 = (bf16[512,4,128]{2,1,0:T(4,128)(2,1)}, bf16[512,4,128]{2,1,0:T(4,128)(2,1)S(1)}, u32[]{:S(2)}) copy-start(bf16[512,4,128]{2,1,0:T(4,128)(2,1)S(1)} %collective-permute-done.8.refs_5_) | copy-start | bytes 1572868
  59.6 0.8 %copy-start.15 = (bf16[512,4,128]{2,1,0:T(4,128)(2,1)}, bf16[512,4,128]{2,1,0:T(4,128)(2,1)S(1)}, u32[]{:S(2)}) copy-start(bf16[512,4,128]{2,1,0:T(4,128)(2,1)S(1)} %collective-permute-done.10.refs_7_) | copy-start | bytes 1572868

commit v5 on v4

--- a/solution.py
+++ b/solution.py
@@ -482,22 +482,6 @@
         ],
         compiler_params=pltpu.CompilerParams(vmem_limit_bytes=VMEM),
     )(own_rows)
-    west = lax.ppermute(last_col, "lon", right)
-    east = lax.ppermute(first_col, "lon", left)
-    plane = lanes(lax.all_to_all(copies, "lon", split_axis=0, concat_axis=0, tiled=True))
-    wide = lambda r, rows: jnp.concatenate([west[r : r + 1], rows, east[r : r + 1]], 0)
-    north = lax.ppermute(wide(patch_rows - 1, bottom), "lat", up)
-    south = lax.ppermute(wide(0, top), "lat", down)
-    recv_rows = receiver.reshape(steps, GROUP, BLK)
-    copies, edges = lax.optimization_barrier((copies, edge_latent))
-    partial, node_first = early_call(
-        block_tile, edges, recv_rows, own_rows, w_first, w_node_first
-    )
-    plane, north, south, partial = lax.optimization_barrier((plane, north, south, partial))
-
-    ahead, behind = move(plane, "x", (1, -1)), move(plane, "x", (-1, 1))
-    plane_other = other_core(plane)
-
     senders = jnp.maximum(sender, 0)
     send_row = senders // grid_cols
     send_col = senders % grid_cols
@@ -518,15 +502,29 @@
     within = send_row % patch_rows // 4 * (patch_cols // 4) + send_col % patch_cols // 4
     far_index = ((half * 4 + at_x) * lon_count + src_lon) * per + within
     far_list, far_count = far_lists((receiver >= 0) & ~is_near, far_index, steps)
+    recv_rows = receiver.reshape(steps, GROUP, BLK)
     lives = jnp.sum((receiver >= 0).astype(jnp.int32).reshape(blocks, BLK), 1)
 
+    west = lax.ppermute(last_col, "lon", right)
+    east = lax.ppermute(first_col, "lon", left)
+    plane = lanes(lax.all_to_all(copies, "lon", split_axis=0, concat_axis=0, tiled=True))
+    wide = lambda r, rows: jnp.concatenate([west[r : r + 1], rows, east[r : r + 1]], 0)
+    north = lax.ppermute(wide(patch_rows - 1, bottom), "lat", up)
+    south = lax.ppermute(wide(0, top), "lat", down)
+    plane, north, south, edges, near_index, far_list, far_count, lives = lax.optimization_barrier(
+        (plane, north, south, edge_latent, near_index, far_list, far_count, lives)
+    )
+
+    ahead, behind = move(plane, "x", (1, -1)), move(plane, "x", (-1, 1))
+    plane_other = other_core(plane)
+    partial, node_first = early_call(
+        block_tile, edges, recv_rows, own_rows, w_first, w_node_first
+    )
+    ahead, partial = lax.optimization_barrier((ahead, partial))
+    across = move(ahead, "x", (1, -1))
     rims = [west, east, north, south]
     pre = near_call(near_index, own_rows, rims, partial, w_first)
-    ahead, pre = lax.optimization_barrier((ahead, pre))
-    across = move(ahead, "x", (1, -1))
-    across, far_list, far_count, lives = lax.optimization_barrier(
-        (across, far_list, far_count, lives)
-    )
+    across, pre = lax.optimization_barrier((across, pre))
     far_pieces = [plane, ahead, behind, across, plane_other]
     far_pieces += [other_core(piece) for piece in (ahead, behind, across)]
     edge_out, node_out = late_call(

time: 75.2 us -> 72.4 us (0.963)
  waiting for transfers between devices: 8.89 us -> 2.97 us
  other arithmetic: 3.87 us -> 7.47 us
    all_to_all x1, starting transfers between devices: 8.61 us -> 3.57 us  [per_device(): lax.all_to_all(copies, 'lon', split_axis=0, concat_axis=0, tiled=True)]
    ppermute x1, waiting for transfers between devices: 3.24 us -> 0.01 us  [per_device(): south = lax.ppermute(wide(0, top), 'lat', down)]
    ppermute x3, waiting for transfers between devices: 4.14 us -> 1.45 us  [move(): return lax.ppermute(value, ('lat', 'lon'), shift(axis, by_core))]
    concatenate x2, other arithmetic: 0.06 us -> 1.58 us  [per_device(): jnp.concatenate([west[r:r + 1], rows, east[r:r + 1]], 0)]
    ppermute x1, starting transfers between devices: 4.52 us -> 3.02 us  [per_device(): north = lax.ppermute(wide(patch_rows - 1, bottom), 'lat', up)]
    ppermute x4, starting transfers between devices: 2.91 us -> 4.24 us  [other_core(): return lax.ppermute(value, ('lat', 'lon'), pairs)]
    ppermute x1, starting transfers between devices: 1.37 us -> 2.54 us  [per_device(): west = lax.ppermute(last_col, 'lon', right)]
    ppermute x3, starting transfers between devices: 2.93 us -> 4.1 us  [move(): return lax.ppermute(value, ('lat', 'lon'), shift(axis, by_core))]
  transfers between devices with their start and end apart: 12 -> 12, of which waited for: 3 -> 2; matrix products, arithmetic and copies ran while one was open for 6% -> 11% of each run, Pallas kernels for 23% -> 23%
where the time goes in v5:
time: 72.4 us; the launch traced here: 71.6 us
  Pallas kernels  33.7 us (47%)
  starting transfers between devices  25 us (35%)
  other arithmetic  7.47 us (10%)
  waiting for transfers between devices  2.97 us (4%)
  local copies, waits for them, and re-layouts  1.45 us (2%)
  between operations  1.03 us (1%)
    pallas_call x1, Pallas kernels, late_call(): pl.pallas_call(late_kernel, name='late', in_specs=[scalars] * 4 + [anywhe...  14.3 us
    pallas_call x1, Pallas kernels, near_call(): pl.pallas_call(near_kernel, name='near', grid_spec=pltpu.PrefetchScalarGr...  8.63 us
    pallas_call x1, Pallas kernels, early_call(): pl.pallas_call(early_kernel, name='early', grid_spec=pltpu.PrefetchScalar...  8.08 us
    ppermute x1, starting transfers between devices, per_device(): east = lax.ppermute(first_col, 'lon', left)  4.65 us
    ppermute x4, starting transfers between devices, other_core(): return lax.ppermute(value, ('lat', 'lon'), pairs)  4.24 us
    ppermute x3, starting transfers between devices, move(): return lax.ppermute(value, ('lat', 'lon'), shift(axis, by_core))  4.1 us
    all_to_all x1, starting transfers between devices, per_device(): lax.all_to_all(copies, 'lon', split_axis=0, concat_axis=0, tiled=True)  3.57 us
    ppermute x1, starting transfers between devices, per_device(): north = lax.ppermute(wide(patch_rows - 1, bottom), 'lat', up)  3.02 us
  transfers between devices with their start and end apart: 12, of which 2 were waited for; matrix products, arithmetic and copies ran while one was open for 11% of the time, Pallas kernels for 23%

profile of v5, /device:TPU:1, one launch (start us, length us, event | category | flops | bytes accessed | tf_op | source)
XLA Modules:
  0.0 71.6 jit_solution(5881549326273279569)
XLA Ops:
  0.6 2.7 %coarse.1 = (bf16[16,32,4,128]{3,2,1,0:T(4,128)(2,1)}, bf16[16,4,128]{2,1,0:T(4,128)(2,1)}, bf16[16,4,128]{2,1,0:T(4,128)(2,1)}, bf16[32,4,128]{2,1,0:T(4,128)(2,1)}, bf16[32,4,128]{2,1,0:T(4,128)(2,1)}) custom-call(bf16[512,512]{1,0:T(8,128)(2,1)} %bitcast.12), custom_call_target="tpu_custom_call" | custom-call | tf_op jit(solution)/shard_map/coarse/pallas_call | solution.py:465
  3.3 2.5 %collective-permute-start = (bf16[16,4,128]{2,1,0:T(4,128)(2,1)}, bf16[16,4,128]{2,1,0:T(4,128)(2,1)S(1)}, u32[]{:S(2)}, u32[]{:S(2)}) collective-permute-start(bf16[16,4,128]{2,1,0:T(4,128)(2,1)} %get-tuple-element.24), channel_id=1, source_target_pairs={{0,1},{1,2},{2,3},{3,4},{4,5},{5,6},{6,7},{7,8},{8,9},{9,10},{10,1... | collective-permute-start | bytes 49160 | tf_op jit(solution)/shard_map/ppermute | solution.py:508
  5.9 4.7 %collective-permute-start.1 = (bf16[16,4,128]{2,1,0:T(4,128)(2,1)}, bf16[16,4,128]{2,1,0:T(4,128)(2,1)S(1)}, u32[]{:S(2)}, u32[]{:S(2)}) collective-permute-start(bf16[16,4,128]{2,1,0:T(4,128)(2,1)} %get-tuple-element.26), channel_id=1, source_target_pairs={{1,0},{2,1},{3,2},{4,3},{5,4},{6,5},{7,6},{8,7},{9,8},{10,9},{11,1... | collective-permute-start | bytes 49160 | tf_op jit(solution)/shard_map/ppermute | solution.py:509
  10.5 3.6 %all-to-all-start = ((bf16[16,32,4,128]{3,2,1,0:T(4,128)(2,1)}), bf16[16,32,4,128]{3,2,1,0:T(4,128)(2,1)S(1)}, u32[]{:S(2)}, u32[]{:S(2)}) async-start(bf16[16,32,4,128]{3,2,1,0:T(4,128)(2,1)} %get-tuple-element.23), calls=%async_computation | async-start | bytes 1048576 | tf_op jit(solution)/shard_map/all_to_all | solution.py:510
  14.1 0.1 iota_compare_fusion.1
  14.2 1.4 %bitcast_reduce_fusion = (s32[16]{0:T(128)}, pred[2048]{0:T(1024)(128)(4,1)S(1)}) fusion(s32[2048]{0:T(1024)} %param.14), kind=kLoop, calls=%fused_computation.51 | loop fusion | flops 6128 | bytes 10304 | tf_op jit(solution)/shard_map/reduce_sum | solution.py:506
  15.6 0.7 %not_and_fusion = (pred[2048]{0:T(1024)(128)(4,1)S(1)}, pred[2048]{0:T(1024)(128)(4,1)S(1)}) fusion(pred[2048]{0:T(1024)(128)(4,1)S(1)} %get-tuple-element.45, s32[]{:T(128)S(6)} %mul.32, s32[]{:T(128)S(6)} %mul.31, s32[2048]{0:T(1024)} %param.13), kind=kLoop, calls=%fused_computation.68 | loop fusion | flops 71680 | bytes 14344 | tf_op jit(solution)/shard_map/and | solution.py:504
  16.3 1.4 %fusion.9 = (s32[2048]{0:T(1024)S(1)}, s32[2048]{0:T(1024)}) fusion(s32[2048]{0:T(1024)} %param.13, s32[]{:T(128)S(6)} %select_n.109, s32[]{:T(128)S(6)} %select_n.106, pred[2048]{0:T(1024)(128)(4,1)S(1)} %get-tuple-element.47, s32[]{:T(128)S(6)} %mul.32, s32[]{:T(128)S(6)} %mul.31), kind=kLoop, calls=%fused_computation.46 | loop fusion | flops 335872 | bytes 26640 | tf_op jit(solution)/shard_map/sub | solution.py:296
  17.7 0.6 select_reduce_fusion.1
  18.4 1.0 %select_reduce_fusion = s32[4,512]{1,0:T(4,128)S(1)} fusion(s32[4,512]{1,0:T(4,128)S(1)} %broadcast_in_dim.55, s32[4,512]{1,0:T(4,128)S(1)} %select_reduce_fusion.1, pred[4,512]{1,0:T(4,128)(4,1)S(1)} %reshape.60), kind=kLoop, calls=%fused_computation | loop fusion | flops 4192256 | bytes 26624 | tf_op jit(solution)/shard_map/reduce_sum | solution.py:298
  19.3 0.0 collective-permute-done.refs_0_
  19.4 0.0 copy-start.3
  19.4 0.0 collective-permute-done.1.refs_1_
  19.4 0.0 copy-start.4
  19.4 0.8 %pad_maximum_fusion.1 = bf16[34,4,128]{2,1,0:T(4,128)(2,1)S(1)} fusion(bf16[1,4,128]{2,1,0:T(4,128)(2,1)S(1)} %get-tuple-element.50, bf16[32,4,128]{2,1,0:T(4,128)(2,1)} %get-tuple-element.27, bf16[1,4,128]{2,1,0:T(4,128)(2,1)S(1)} %get-tuple-element.48), kind=kLoop, calls=%fused_computation.6 | loop fusion | flops 34816 | bytes 69632 | tf_op jit(solution)/shard_map/concatenate | solution.py:511
  20.2 2.9 %collective-permute-start.3 = (bf16[34,4,128]{2,1,0:T(4,128)(2,1)S(1)}, bf16[34,4,128]{2,1,0:T(4,128)(2,1)S(1)}, u32[]{:S(2)}, u32[]{:S(2)}) collective-permute-start(bf16[34,4,128]{2,1,0:T(4,128)(2,1)S(1)} %pad_maximum_fusion.1), channel_id=1, source_target_pairs={{16,0},{32,16},{48,32},{64,48},{80,64},{96,80},{112,96},{17,1},{33... | collective-permute-start | bytes 104456 | tf_op jit(solution)/shard_map/ppermute | solution.py:513
  23.1 0.8 %pad_maximum_fusion = bf16[34,4,128]{2,1,0:T(4,128)(2,1)S(1)} fusion(bf16[1,4,128]{2,1,0:T(4,128)(2,1)S(1)} %get-tuple-element.51, bf16[32,4,128]{2,1,0:T(4,128)(2,1)} %get-tuple-element.25, bf16[1,4,128]{2,1,0:T(4,128)(2,1)S(1)} %get-tuple-element.49), kind=kLoop, calls=%fused_computation.5 | loop fusion | flops 34816 | bytes 69632 | tf_op jit(solution)/shard_map/concatenate | solution.py:511
  23.9 3.0 %collective-permute-start.2 = (bf16[34,4,128]{2,1,0:T(4,128)(2,1)S(1)}, bf16[34,4,128]{2,1,0:T(4,128)(2,1)S(1)}, u32[]{:S(2)}, u32[]{:S(2)}) collective-permute-start(bf16[34,4,128]{2,1,0:T(4,128)(2,1)S(1)} %pad_maximum_fusion), channel_id=1, source_target_pairs={{0,16},{16,32},{32,48},{48,64},{64,80},{80,96},{96,112},{1,17},{17... | collective-permute-start | bytes 104456 | tf_op jit(solution)/shard_map/ppermute | solution.py:512
  26.9 0.7 convert_reduce_fusion.far_count
  27.6 0.6 copy.13
  28.2 0.0 collective-permute-done.3.refs_3_
  28.2 0.0 copy-start.1
  28.2 0.0 collective-permute-done.2.refs_2_
  28.2 0.0 copy-start.2
  28.2 0.0 all-to-all-done
  28.2 0.0 copy-start
  28.2 1.3 %collective-permute-start.4 = (bf16[512,4,128]{2,1,0:T(4,128)(2,1)S(1)}, bf16[512,4,128]{2,1,0:T(4,128)(2,1)S(1)}, u32[]{:S(2)}, u32[]{:S(2)}) collective-permute-start(bf16[512,4,128]{2,1,0:T(4,128)(2,1)S(1)} %bitcast.16), channel_id=1, source_target_pairs={{0,32},{1,33},{2,34},{3,35},{4,36},{5,37},{6,38},{7,39},{8,40},{9,... | collective-permute-start | bytes 1572872 | tf_op jit(solution)/shard_map/ppermute | solution.py:47
  29.5 0.3 collective-permute-start.5
  29.8 8.1 %early.1 = (f32[2048,512]{1,0:T(8,128)}, f32[512,512]{1,0:T(8,128)}) custom-call(s32[16]{0:T(128)} %tiles.3, bf16[2048,512]{1,0:T(8,128)(2,1)} %refs_9_.1, s32[4,4,128]{2,1,0:T(4,128)} %bitcast.20, bf16[512,512]{1,0:T(8,128)(2,1)} %bitcast.13, bf16[1536,512]{1,0:T(8,128)(2,1)} %refs_12_.1, bf16[1536,512]{1,0:T(8,128)(2,1)} %refs_12_.1, ...), custom_call_target="tpu_custom_call" | custom-call | flops 3000000000 | bytes 10000000 | tf_op jit(solution)/shard_map/early/pallas_call | solution.py:313
  37.9 0.0 copy-done.3
  37.9 0.0 copy-done.4
  37.9 0.0 copy-done.1
  37.9 0.0 copy-done.2
  37.9 1.4 %collective-permute-done.4.refs_1_ = bf16[512,4,128]{2,1,0:T(4,128)(2,1)S(1)} collective-permute-done((bf16[512,4,128]{2,1,0:T(4,128)(2,1)S(1)}, bf16[512,4,128]{2,1,0:T(4,128)(2,1)S(1)}, u32[]{:S(2)}, u32[]{:S(2)}) %collective-permute-start.4) | collective-permute-done | bytes 524320 | tf_op jit(solution)/shard_map/ppermute | solution.py:47
  39.3 0.0 copy-start.5
  39.3 2.6 %collective-permute-start.6 = (bf16[512,4,128]{2,1,0:T(4,128)(2,1)S(1)}, bf16[512,4,128]{2,1,0:T(4,128)(2,1)S(1)}, u32[]{:S(2)}, u32[]{:S(2)}) collective-permute-start(bf16[512,4,128]{2,1,0:T(4,128)(2,1)S(1)} %collective-permute-done.4.refs_1_), channel_id=1, source_target_pairs={{0,32},{1,33},{2,34},{3,35},{4,36},{5,37},{6,38},{7,39},{8,40},{9,... | collective-permute-start | bytes 1572872 | tf_op jit(solution)/shard_map/ppermute | solution.py:47
  41.9 0.0 copy-done
  41.9 2.6 %collective-permute-start.7 = (bf16[512,4,128]{2,1,0:T(4,128)(2,1)S(1)}, bf16[512,4,128]{2,1,0:T(4,128)(2,1)S(1)}, u32[]{:S(2)}, u32[]{:S(2)}) collective-permute-start(bf16[512,4,128]{2,1,0:T(4,128)(2,1)S(1)} %bitcast.18), channel_id=1, source_target_pairs={{0,16},{1,17},{2,18},{3,19},{4,20},{5,21},{6,22},{7,23},{8,24},{9,... | collective-permute-start | bytes 1572872 | tf_op jit(solution)/shard_map/ppermute | solution.py:43
  44.5 0.1 collective-permute-start.8
  44.6 0.0 collective-permute-done.5.refs_2_
  44.6 0.0 copy-start.6
  44.6 0.4 collective-permute-start.9
  45.0 8.6 %near.1.refs_8_ = bf16[2048,512]{1,0:T(8,128)(2,1)} custom-call(s32[2048]{0:T(1024)} %get-tuple-element.35.near_index, bf16[512,512]{1,0:T(8,128)(2,1)} %bitcast.14, bf16[16,4,128]{2,1,0:T(4,128)(2,1)} %copy-done.3, bf16[16,4,128]{2,1,0:T(4,128)(2,1)} %copy-done.4, bf16[34,4,128]{2,1,0:T(4,128)(2,1)} %copy-done.2, bf16[34,4,128]{2,1,0:T(4,128)(2,1)} %copy-done.1, ...), custom_call_target="tpu_custom_call" | custom-call | flops 2000000000 | bytes 8000000 | tf_op jit(solution)/shard_map/near/pallas_call | solution.py:338
  53.7 0.0 copy-done.5
  53.7 0.0 copy-done.6
  53.7 0.0 collective-permute-done.6.refs_3_
  53.7 0.0 copy-start.7
  53.7 1.1 %collective-permute-start.10 = (bf16[512,4,128]{2,1,0:T(4,128)(2,1)S(1)}, bf16[512,4,128]{2,1,0:T(4,128)(2,1)S(1)}, u32[]{:S(2)}, u32[]{:S(2)}) collective-permute-start(bf16[512,4,128]{2,1,0:T(4,128)(2,1)S(1)} %collective-permute-done.6.refs_3_), channel_id=1, source_target_pairs={{0,16},{1,17},{2,18},{3,19},{4,20},{5,21},{6,22},{7,23},{8,24},{9,... | collective-permute-start | bytes 1572872 | tf_op jit(solution)/shard_map/ppermute | solution.py:43
  54.8 0.0 collective-permute-done.7.refs_4_
  54.8 0.0 copy-start.8
  54.8 0.0 collective-permute-done.8.refs_5_
  54.8 0.0 copy-start.9
  54.8 0.0 collective-permute-done.9.refs_6_
  54.8 0.0 copy-start.10
  54.9 1.5 %collective-permute-done.10.refs_7_ = bf16[512,4,128]{2,1,0:T(4,128)(2,1)S(1)} collective-permute-done((bf16[512,4,128]{2,1,0:T(4,128)(2,1)S(1)}, bf16[512,4,128]{2,1,0:T(4,128)(2,1)S(1)}, u32[]{:S(2)}, u32[]{:S(2)}) %collective-permute-start.10) | collective-permute-done | bytes 524320 | tf_op jit(solution)/shard_map/ppermute | solution.py:43
  56.4 0.0 copy-start.11
  56.4 0.0 copy-done.7
  56.4 0.0 copy-done.8
  56.4 0.0 copy-done.9
  56.4 0.0 copy-done.10
  56.4 0.8 %copy-done.11 = bf16[512,4,128]{2,1,0:T(4,128)(2,1)} copy-done((bf16[512,4,128]{2,1,0:T(4,128)(2,1)}, bf16[512,4,128]{2,1,0:T(4,128)(2,1)S(1)}, u32[]{:S(2)}) %copy-start.11) | copy-done | bytes 524312
  57.1 14.3 %late.1 = (bf16[2048,512]{1,0:T(8,128)(2,1)}, bf16[512,512]{1,0:T(8,128)(2,1)}) custom-call(s32[2048]{0:T(1024)} %bitcast.22, s32[4]{0:T(128)} %convert_reduce_fusion.far_count, s32[16]{0:T(128)} %tiles.3, s32[16]{0:T(128)} %get-tuple-element.30.lives, bf16[512,4,128]{2,1,0:T(4,128)(2,1)} %bitcast.19, bf16[512,4,128]{2,1,0:T(4,128)(2,1)} %copy-done.5, ...), custom_call_target="tpu_custom_call" | custom-call | flops 4000000000 | bytes 14000000 | tf_op jit(solution)/shard_map/late/pallas_call | solution.py:384
  (6 shorter events, 0.0 us)
Async XLA Ops:
  3.3 16.0 %collective-permute-start = (bf16[16,4,128]{2,1,0:T(4,128)(2,1)}, bf16[16,4,128]{2,1,0:T(4,128)(2,1)S(1)}, u32[]{:S(2)}, u32[]{:S(2)}) collective-permute-start(bf16[16,4,128]{2,1,0:T(4,128)(2,1)} %get-tuple-element.24), channel_id=1, source_target_pairs={{0,1},{1,2},{2,3},{3,4},{4,5},{5,6},{6,7},{7,8},{8,9},{9,10},{10,1... | collective-permute-start | bytes 49160 | tf_op jit(solution)/shard_map/ppermute | solution.py:508
  5.9 13.5 %collective-permute-start.1 = (bf16[16,4,128]{2,1,0:T(4,128)(2,1)}, bf16[16,4,128]{2,1,0:T(4,128)(2,1)S(1)}, u32[]{:S(2)}, u32[]{:S(2)}) collective-permute-start(bf16[16,4,128]{2,1,0:T(4,128)(2,1)} %get-tuple-element.26), channel_id=1, source_target_pairs={{1,0},{2,1},{3,2},{4,3},{5,4},{6,5},{7,6},{8,7},{9,8},{10,9},{11,1... | collective-permute-start | bytes 49160 | tf_op jit(solution)/shard_map/ppermute | solution.py:509
  10.5 17.7 %all-to-all-start = ((bf16[16,32,4,128]{3,2,1,0:T(4,128)(2,1)}), bf16[16,32,4,128]{3,2,1,0:T(4,128)(2,1)S(1)}, u32[]{:S(2)}, u32[]{:S(2)}) async-start(bf16[16,32,4,128]{3,2,1,0:T(4,128)(2,1)} %get-tuple-element.23), calls=%async_computation | async-start | bytes 1048576 | tf_op jit(solution)/shard_map/all_to_all | solution.py:510
  19.4 18.5 %copy-start.3 = (bf16[16,4,128]{2,1,0:T(4,128)(2,1)}, bf16[16,4,128]{2,1,0:T(4,128)(2,1)S(1)}, u32[]{:S(2)}) copy-start(bf16[16,4,128]{2,1,0:T(4,128)(2,1)S(1)} %collective-permute-done.refs_0_) | copy-start | bytes 49156
  19.4 18.5 %copy-start.4 = (bf16[16,4,128]{2,1,0:T(4,128)(2,1)}, bf16[16,4,128]{2,1,0:T(4,128)(2,1)S(1)}, u32[]{:S(2)}) copy-start(bf16[16,4,128]{2,1,0:T(4,128)(2,1)S(1)} %collective-permute-done.1.refs_1_) | copy-start | bytes 49156
  20.2 8.0 %collective-permute-start.3 = (bf16[34,4,128]{2,1,0:T(4,128)(2,1)S(1)}, bf16[34,4,128]{2,1,0:T(4,128)(2,1)S(1)}, u32[]{:S(2)}, u32[]{:S(2)}) collective-permute-start(bf16[34,4,128]{2,1,0:T(4,128)(2,1)S(1)} %pad_maximum_fusion.1), channel_id=1, source_target_pairs={{16,0},{32,16},{48,32},{64,48},{80,64},{96,80},{112,96},{17,1},{33... | collective-permute-start | bytes 104456 | tf_op jit(solution)/shard_map/ppermute | solution.py:513
  23.9 4.3 %collective-permute-start.2 = (bf16[34,4,128]{2,1,0:T(4,128)(2,1)S(1)}, bf16[34,4,128]{2,1,0:T(4,128)(2,1)S(1)}, u32[]{:S(2)}, u32[]{:S(2)}) collective-permute-start(bf16[34,4,128]{2,1,0:T(4,128)(2,1)S(1)} %pad_maximum_fusion), channel_id=1, source_target_pairs={{0,16},{16,32},{32,48},{48,64},{64,80},{80,96},{96,112},{1,17},{17... | collective-permute-start | bytes 104456 | tf_op jit(solution)/shard_map/ppermute | solution.py:512
  28.2 9.7 %copy-start.1 = (bf16[34,4,128]{2,1,0:T(4,128)(2,1)}, bf16[34,4,128]{2,1,0:T(4,128)(2,1)S(1)}, u32[]{:S(2)}) copy-start(bf16[34,4,128]{2,1,0:T(4,128)(2,1)S(1)} %collective-permute-done.3.refs_3_) | copy-start | bytes 104452
  28.2 9.7 %copy-start.2 = (bf16[34,4,128]{2,1,0:T(4,128)(2,1)}, bf16[34,4,128]{2,1,0:T(4,128)(2,1)S(1)}, u32[]{:S(2)}) copy-start(bf16[34,4,128]{2,1,0:T(4,128)(2,1)S(1)} %collective-permute-done.2.refs_2_) | copy-start | bytes 104452
  28.2 13.7 %copy-start = (bf16[16,32,4,128]{3,2,1,0:T(4,128)(2,1)}, bf16[16,32,4,128]{3,2,1,0:T(4,128)(2,1)S(1)}, u32[]{:S(2)}) copy-start(bf16[16,32,4,128]{3,2,1,0:T(4,128)(2,1)S(1)} %all-to-all-done) | copy-start | bytes 1572868
  28.2 11.1 %collective-permute-start.4 = (bf16[512,4,128]{2,1,0:T(4,128)(2,1)S(1)}, bf16[512,4,128]{2,1,0:T(4,128)(2,1)S(1)}, u32[]{:S(2)}, u32[]{:S(2)}) collective-permute-start(bf16[512,4,128]{2,1,0:T(4,128)(2,1)S(1)} %bitcast.16), channel_id=1, source_target_pairs={{0,32},{1,33},{2,34},{3,35},{4,36},{5,37},{6,38},{7,39},{8,40},{9,... | collective-permute-start | bytes 1572872 | tf_op jit(solution)/shard_map/ppermute | solution.py:47
  29.5 15.1 %collective-permute-start.5 = (bf16[512,4,128]{2,1,0:T(4,128)(2,1)S(1)}, bf16[512,4,128]{2,1,0:T(4,128)(2,1)S(1)}, u32[]{:S(2)}, u32[]{:S(2)}) collective-permute-start(bf16[512,4,128]{2,1,0:T(4,128)(2,1)S(1)} %bitcast.17), channel_id=1, source_target_pairs={{0,96},{1,97},{2,98},{3,99},{4,100},{5,101},{6,102},{7,103},{8,104... | collective-permute-start | bytes 1572872 | tf_op jit(solution)/shard_map/ppermute | solution.py:47
  39.3 14.3 %copy-start.5 = (bf16[512,4,128]{2,1,0:T(4,128)(2,1)}, bf16[512,4,128]{2,1,0:T(4,128)(2,1)S(1)}, u32[]{:S(2)}) copy-start(bf16[512,4,128]{2,1,0:T(4,128)(2,1)S(1)} %collective-permute-done.4.refs_1_) | copy-start | bytes 1572868
  39.3 14.3 %collective-permute-start.6 = (bf16[512,4,128]{2,1,0:T(4,128)(2,1)S(1)}, bf16[512,4,128]{2,1,0:T(4,128)(2,1)S(1)}, u32[]{:S(2)}, u32[]{:S(2)}) collective-permute-start(bf16[512,4,128]{2,1,0:T(4,128)(2,1)S(1)} %collective-permute-done.4.refs_1_), channel_id=1, source_target_pairs={{0,32},{1,33},{2,34},{3,35},{4,36},{5,37},{6,38},{7,39},{8,40},{9,... | collective-permute-start | bytes 1572872 | tf_op jit(solution)/shard_map/ppermute | solution.py:47
  41.9 12.9 %collective-permute-start.7 = (bf16[512,4,128]{2,1,0:T(4,128)(2,1)S(1)}, bf16[512,4,128]{2,1,0:T(4,128)(2,1)S(1)}, u32[]{:S(2)}, u32[]{:S(2)}) collective-permute-start(bf16[512,4,128]{2,1,0:T(4,128)(2,1)S(1)} %bitcast.18), channel_id=1, source_target_pairs={{0,16},{1,17},{2,18},{3,19},{4,20},{5,21},{6,22},{7,23},{8,24},{9,... | collective-permute-start | bytes 1572872 | tf_op jit(solution)/shard_map/ppermute | solution.py:43
  44.5 10.3 %collective-permute-start.8 = (bf16[512,4,128]{2,1,0:T(4,128)(2,1)S(1)}, bf16[512,4,128]{2,1,0:T(4,128)(2,1)S(1)}, u32[]{:S(2)}, u32[]{:S(2)}) collective-permute-start(bf16[512,4,128]{2,1,0:T(4,128)(2,1)S(1)} %collective-permute-done.4.refs_1_), channel_id=1, source_target_pairs={{0,16},{1,17},{2,18},{3,19},{4,20},{5,21},{6,22},{7,23},{8,24},{9,... | collective-permute-start | bytes 1572872 | tf_op jit(solution)/shard_map/ppermute | solution.py:43
  44.6 9.1 %copy-start.6 = (bf16[512,4,128]{2,1,0:T(4,128)(2,1)}, bf16[512,4,128]{2,1,0:T(4,128)(2,1)S(1)}, u32[]{:S(2)}) copy-start(bf16[512,4,128]{2,1,0:T(4,128)(2,1)S(1)} %collective-permute-done.5.refs_2_) | copy-start | bytes 1572868
  44.6 10.2 %collective-permute-start.9 = (bf16[512,4,128]{2,1,0:T(4,128)(2,1)S(1)}, bf16[512,4,128]{2,1,0:T(4,128)(2,1)S(1)}, u32[]{:S(2)}, u32[]{:S(2)}) collective-permute-start(bf16[512,4,128]{2,1,0:T(4,128)(2,1)S(1)} %collective-permute-done.5.refs_2_), channel_id=1, source_target_pairs={{0,16},{1,17},{2,18},{3,19},{4,20},{5,21},{6,22},{7,23},{8,24},{9,... | collective-permute-start | bytes 1572872 | tf_op jit(solution)/shard_map/ppermute | solution.py:43
  53.7 2.7 %copy-start.7 = (bf16[512,4,128]{2,1,0:T(4,128)(2,1)}, bf16[512,4,128]{2,1,0:T(4,128)(2,1)S(1)}, u32[]{:S(2)}) copy-start(bf16[512,4,128]{2,1,0:T(4,128)(2,1)S(1)} %collective-permute-done.6.refs_3_) | copy-start | bytes 1572868
  53.7 2.7 %collective-permute-start.10 = (bf16[512,4,128]{2,1,0:T(4,128)(2,1)S(1)}, bf16[512,4,128]{2,1,0:T(4,128)(2,1)S(1)}, u32[]{:S(2)}, u32[]{:S(2)}) collective-permute-start(bf16[512,4,128]{2,1,0:T(4,128)(2,1)S(1)} %collective-permute-done.6.refs_3_), channel_id=1, source_target_pairs={{0,16},{1,17},{2,18},{3,19},{4,20},{5,21},{6,22},{7,23},{8,24},{9,... | collective-permute-start | bytes 1572872 | tf_op jit(solution)/shard_map/ppermute | solution.py:43
  54.8 1.5 %copy-start.8 = (bf16[512,4,128]{2,1,0:T(4,128)(2,1)}, bf16[512,4,128]{2,1,0:T(4,128)(2,1)S(1)}, u32[]{:S(2)}) copy-start(bf16[512,4,128]{2,1,0:T(4,128)(2,1)S(1)} %collective-permute-done.7.refs_4_) | copy-start | bytes 1572868
  54.8 1.5 %copy-start.9 = (bf16[512,4,128]{2,1,0:T(4,128)(2,1)}, bf16[512,4,128]{2,1,0:T(4,128)(2,1)S(1)}, u32[]{:S(2)}) copy-start(bf16[512,4,128]{2,1,0:T(4,128)(2,1)S(1)} %collective-permute-done.8.refs_5_) | copy-start | bytes 1572868
  54.8 1.5 %copy-start.10 = (bf16[512,4,128]{2,1,0:T(4,128)(2,1)}, bf16[512,4,128]{2,1,0:T(4,128)(2,1)S(1)}, u32[]{:S(2)}) copy-start(bf16[512,4,128]{2,1,0:T(4,128)(2,1)S(1)} %collective-permute-done.9.refs_6_) | copy-start | bytes 1572868
  56.4 0.8 %copy-start.11 = (bf16[512,4,128]{2,1,0:T(4,128)(2,1)}, bf16[512,4,128]{2,1,0:T(4,128)(2,1)S(1)}, u32[]{:S(2)}) copy-start(bf16[512,4,128]{2,1,0:T(4,128)(2,1)S(1)} %collective-permute-done.10.refs_7_) | copy-start | bytes 1572868

commit v6 on v5

--- a/solution.py
+++ b/solution.py
@@ -137,12 +137,8 @@
         store.wait()
 
 
-def early_kernel(tiles, edge_ref, recv_ref, node_ref, we_ref, wr_ref, wn_ref, part_ref, nf_ref, got_ref):
+def early_kernel(tiles, edge_ref, recv_ref, node_ref, we_ref, wr_ref, part_ref, got_ref):
     step = pl.program_id(0)
-
-    @pl.when(step == 0)
-    def _():
-        nf_ref[...] = dot(node_ref[...], wn_ref[...])
 
     for k in range(GROUP):
         tile = pl.multiple_of(tiles[step * GROUP + k] * BLK, BLK)
@@ -154,7 +150,8 @@
             preferred_element_type=F32,
         )
         got_ref[k * BLK : (k + 1) * BLK, :] = rows.astype(BF)
-    part_ref[...] = dot(edge_ref[...], we_ref[...]) + dot(got_ref[...], wr_ref[...])
+    total = dot(edge_ref[...], we_ref[...]) + dot(got_ref[...], wr_ref[...])
+    part_ref[...] = total.astype(BF)
 
 
 def near_kernel(near_index, node_ref, *refs):
@@ -184,7 +181,8 @@
         return carry
 
     lax.fori_loop(0, ROWS // 16, body, 0)
-    pre_ref[...] = (part_ref[...] + dot(sent_rows(sent), ws_ref[...])).astype(BF)
+    total = part_ref[...].astype(F32) + dot(sent_rows(sent), ws_ref[...])
+    pre_ref[...] = total.astype(BF)
 
 
 def late_kernel(far_list, far_count, tiles, lives, *refs):
@@ -192,7 +190,6 @@
     (
         pre_hbm,
         edge_hbm,
-        nf_hbm,
         node_hbm,
         w1_hbm,
         w2_hbm,
@@ -209,7 +206,6 @@
         edge,
         out,
         agg,
-        nf,
         node,
         ws,
         w2,
@@ -235,17 +231,18 @@
             ]
         )
     last = [
-        pltpu.make_async_copy(nf_hbm, nf, in_sem.at[2]),
         pltpu.make_async_copy(node_hbm, node, in_sem.at[3]),
-        pltpu.make_async_copy(wn_hbm.at[pl.ds(F, F)], wn, in_sem.at[4]),
+        pltpu.make_async_copy(wn_hbm, wn, in_sem.at[4]),
         pltpu.make_async_copy(wn2_hbm, wn2, in_sem.at[5]),
     ]
-    for copy in first + sum(parts, []) + last:
+    for copy in first:
         copy.start()
     sent[...] = jnp.zeros_like(sent)
     agg[...] = jnp.zeros_like(agg)
     for copy in copies:
         copy.wait()
+    for copy in sum(parts, []) + last:
+        copy.start()
 
     for g in range(steps):
 
@@ -253,7 +250,7 @@
             packed = far_list[g * ROWS + i]
             return packed & 4095, packed >> 12
 
-        fetch((far_count[g] + 7) >> 3, 8, entry, table, sent)
+        fetch((far_count[g] + 15) >> 4, 16, entry, table, sent)
     for copy in first:
         copy.wait()
     place = lax.broadcasted_iota(jnp.int32, (BLK, F), 0)
@@ -279,7 +276,7 @@
         stores.append(store)
     for copy in last:
         copy.wait()
-    first_sum = nf[...] + dot(agg[...].astype(BF), wn[...])
+    first_sum = dot(node[...], wn[:F, :]) + dot(agg[...].astype(BF), wn[F:, :])
     second = dot(silu(first_sum).astype(BF), wn2[...])
     node_out_ref[...] = (node[...].astype(F32) + normed(second, ng_ref[...])).astype(BF)
     for store in stores:
@@ -307,7 +304,7 @@
     return whole, part, recv_spec, weight, anywhere
 
 
-def early_call(block_tile, edge_latent, recv_rows, own_rows, w_first, w_node_first):
+def early_call(block_tile, edge_latent, recv_rows, own_rows, w_first):
     whole, part, recv_spec, weight, anywhere = specs()
     blocks, nodes = block_tile.shape[0], own_rows.shape[0]
     return pl.pallas_call(
@@ -316,19 +313,16 @@
         grid_spec=pltpu.PrefetchScalarGridSpec(
             num_scalar_prefetch=1,
             grid=(blocks // GROUP,),
-            in_specs=[part, recv_spec, whole((nodes, F)), weight(0), weight(2), weight(0)],
-            out_specs=[part, whole((nodes, F))],
+            in_specs=[part, recv_spec, whole((nodes, F)), weight(0), weight(2)],
+            out_specs=part,
             scratch_shapes=[pltpu.VMEM((ROWS, F), BF)],
         ),
-        out_shape=[
-            jax.ShapeDtypeStruct((blocks * BLK, F), F32),
-            jax.ShapeDtypeStruct((nodes, F), F32),
-        ],
+        out_shape=jax.ShapeDtypeStruct((blocks * BLK, F), BF),
         compiler_params=pltpu.CompilerParams(vmem_limit_bytes=VMEM),
         cost_estimate=pl.CostEstimate(
             flops=3 * 10**9, bytes_accessed=10 * 10**6, transcendentals=0
         ),
-    )(block_tile, edge_latent, recv_rows, own_rows, w_first, w_first, w_node_first)
+    )(block_tile, edge_latent, recv_rows, own_rows, w_first, w_first)
 
 
 def near_call(near_index, own_rows, rims, partial, w_first):
@@ -365,7 +359,6 @@
     pre,
     edge_latent,
     receiver,
-    node_first,
     own_rows,
     w_first,
     w_second,
@@ -384,7 +377,7 @@
     return pl.pallas_call(
         late_kernel,
         name="late",
-        in_specs=[scalars] * 4 + [anywhere] * (FAR + 8) + [local] * 3,
+        in_specs=[scalars] * 4 + [anywhere] * (FAR + 7) + [local] * 3,
         out_specs=[anywhere, local],
         scratch_shapes=[
             pltpu.VMEM((far_rows, 4, 128), BF),
@@ -393,11 +386,10 @@
             pltpu.VMEM((slots, F), BF),
             pltpu.VMEM((slots, F), BF),
             pltpu.VMEM((nodes, F), F32),
-            pltpu.VMEM((nodes, F), F32),
             pltpu.VMEM((nodes, F), BF),
             square,
             square,
-            square,
+            pltpu.VMEM((2 * F, F), BF),
             square,
             pltpu.SemaphoreType.DMA((FAR,)),
             pltpu.SemaphoreType.DMA((6 + 2 * steps,)),
@@ -419,7 +411,6 @@
         *far_pieces,
         pre,
         edge_latent,
-        node_first,
         own_rows,
         w_first,
         w_second,
@@ -515,16 +506,16 @@
         (plane, north, south, edge_latent, near_index, far_list, far_count, lives)
     )
 
-    ahead, behind = move(plane, "x", (1, -1)), move(plane, "x", (-1, 1))
+    ahead = move(plane, "x", (1, -1))
     plane_other = other_core(plane)
-    partial, node_first = early_call(
-        block_tile, edges, recv_rows, own_rows, w_first, w_node_first
-    )
+    partial = early_call(block_tile, edges, recv_rows, own_rows, w_first)
+    later, partial = lax.optimization_barrier((plane, partial))
+    behind = move(later, "x", (-1, 1))
     ahead, partial = lax.optimization_barrier((ahead, partial))
     across = move(ahead, "x", (1, -1))
     rims = [west, east, north, south]
     pre = near_call(near_index, own_rows, rims, partial, w_first)
-    across, pre = lax.optimization_barrier((across, pre))
+    across, behind, pre = lax.optimization_barrier((across, behind, pre))
     far_pieces = [plane, ahead, behind, across, plane_other]
     far_pieces += [other_core(piece) for piece in (ahead, behind, across)]
     edge_out, node_out = late_call(
@@ -536,7 +527,6 @@
         pre,
         edge_latent,
         receiver,
-        node_first,
         own_rows,
         w_first,
         w_second,

time: 72.4 us -> 73.6 us (1.017)
  waiting for transfers between devices: 2.97 us -> 7.72 us
  Pallas kernels: 33.7 us -> 30.5 us
    all_to_all x1, starting transfers between devices: 3.57 us -> 8.61 us  [per_device(): lax.all_to_all(copies, 'lon', split_axis=0, concat_axis=0, tiled=True)]
    ppermute x4, starting transfers between devices: 4.24 us -> 1.38 us  [other_core(): return lax.ppermute(value, ('lat', 'lon'), pairs)]
    ppermute x1, starting transfers between devices: 3.02 us -> 5.08 us  [per_device(): north = lax.ppermute(wide(patch_rows - 1, bottom), 'lat', up)]
    ppermute x1, waiting for transfers between devices: 0.01 us -> 2.02 us  [per_device(): south = lax.ppermute(wide(0, top), 'lat', down)]
    pallas_call x1, Pallas kernels: 14.3 us -> 12.4 us  [late_call(): pl.pallas_call(late_kernel, name='late', in_specs=[scalars] * 4 + [anywhe...]
    ppermute x3, waiting for transfers between devices: 1.45 us -> 2.99 us  [move(): return lax.ppermute(value, ('lat', 'lon'), shift(axis, by_core))]
    ppermute x1, starting transfers between devices: 2.54 us -> 1.37 us  [per_device(): west = lax.ppermute(last_col, 'lon', right)]
    ppermute x3, starting transfers between devices: 4.1 us -> 2.93 us  [move(): return lax.ppermute(value, ('lat', 'lon'), shift(axis, by_core))]
  transfers between devices with their start and end apart: 12 -> 12, of which waited for: 2 -> 6; matrix products, arithmetic and copies ran while one was open for 11% -> 11% of each run, Pallas kernels for 23% -> 21%
where the time goes in v6:
time: 73.6 us; the launch traced here: 72.8 us
  Pallas kernels  30.5 us (41%)
  starting transfers between devices  24.8 us (34%)
  waiting for transfers between devices  7.72 us (10%)
  other arithmetic  7.39 us (10%)
  local copies, waits for them, and re-layouts  1.45 us (2%)
  between operations  0.97 us (1%)
    pallas_call x1, Pallas kernels, late_call(): pl.pallas_call(late_kernel, name='late', in_specs=[scalars] * 4 + [anywhe...  12.4 us
    all_to_all x1, starting transfers between devices, per_device(): lax.all_to_all(copies, 'lon', split_axis=0, concat_axis=0, tiled=True)  8.61 us
    pallas_call x1, Pallas kernels, near_call(): pl.pallas_call(near_kernel, name='near', grid_spec=pltpu.PrefetchScalarGr...  8.4 us
    pallas_call x1, Pallas kernels, early_call(): pl.pallas_call(early_kernel, name='early', grid_spec=pltpu.PrefetchScalar...  6.95 us
    ppermute x1, starting transfers between devices, per_device(): north = lax.ppermute(wide(patch_rows - 1, bottom), 'lat', up)  5.08 us
    ppermute x1, starting transfers between devices, per_device(): east = lax.ppermute(first_col, 'lon', left)  3.49 us
    ppermute x3, waiting for transfers between devices, move(): return lax.ppermute(value, ('lat', 'lon'), shift(axis, by_core))  2.99 us
    ppermute x3, starting transfers between devices, move(): return lax.ppermute(value, ('lat', 'lon'), shift(axis, by_core))  2.93 us
  transfers between devices with their start and end apart: 12, of which 6 were waited for; matrix products, arithmetic and copies ran while one was open for 11% of the time, Pallas kernels for 21%

profile of v6, /device:TPU:1, one launch (start us, length us, event | category | flops | bytes accessed | tf_op | source)
XLA Modules:
  0.0 72.8 jit_solution(7397499848869567284)
XLA Ops:
  0.6 2.7 %coarse.1 = (bf16[16,32,4,128]{3,2,1,0:T(4,128)(2,1)}, bf16[16,4,128]{2,1,0:T(4,128)(2,1)}, bf16[16,4,128]{2,1,0:T(4,128)(2,1)}, bf16[32,4,128]{2,1,0:T(4,128)(2,1)}, bf16[32,4,128]{2,1,0:T(4,128)(2,1)}) custom-call(bf16[512,512]{1,0:T(8,128)(2,1)} %bitcast.12), custom_call_target="tpu_custom_call" | custom-call | tf_op jit(solution)/shard_map/coarse/pallas_call | solution.py:456
  3.3 8.6 %all-to-all-start = ((bf16[16,32,4,128]{3,2,1,0:T(4,128)(2,1)}), bf16[16,32,4,128]{3,2,1,0:T(4,128)(2,1)S(1)}, u32[]{:S(2)}, u32[]{:S(2)}) async-start(bf16[16,32,4,128]{3,2,1,0:T(4,128)(2,1)} %get-tuple-element.24), calls=%async_computation | async-start | bytes 1048576 | tf_op jit(solution)/shard_map/all_to_all | solution.py:501
  12.0 1.4 %collective-permute-start = (bf16[16,4,128]{2,1,0:T(4,128)(2,1)}, bf16[16,4,128]{2,1,0:T(4,128)(2,1)S(1)}, u32[]{:S(2)}, u32[]{:S(2)}) collective-permute-start(bf16[16,4,128]{2,1,0:T(4,128)(2,1)} %get-tuple-element.25), channel_id=1, source_target_pairs={{0,1},{1,2},{2,3},{3,4},{4,5},{5,6},{6,7},{7,8},{8,9},{9,10},{10,1... | collective-permute-start | bytes 49160 | tf_op jit(solution)/shard_map/ppermute | solution.py:499
  13.3 3.5 %collective-permute-start.1 = (bf16[16,4,128]{2,1,0:T(4,128)(2,1)}, bf16[16,4,128]{2,1,0:T(4,128)(2,1)S(1)}, u32[]{:S(2)}, u32[]{:S(2)}) collective-permute-start(bf16[16,4,128]{2,1,0:T(4,128)(2,1)} %get-tuple-element.27), channel_id=1, source_target_pairs={{1,0},{2,1},{3,2},{4,3},{5,4},{6,5},{7,6},{8,7},{9,8},{10,9},{11,1... | collective-permute-start | bytes 49160 | tf_op jit(solution)/shard_map/ppermute | solution.py:500
  16.8 0.1 iota_compare_fusion.1
  16.9 1.3 %bitcast_reduce_fusion = (s32[16]{0:T(128)}, pred[2048]{0:T(1024)(128)(4,1)S(1)}) fusion(s32[2048]{0:T(1024)} %param.14), kind=kLoop, calls=%fused_computation.51 | loop fusion | flops 6128 | bytes 10304 | tf_op jit(solution)/shard_map/reduce_sum | solution.py:497
  18.2 0.7 not_and_fusion
  19.0 1.4 %fusion.9 = (s32[2048]{0:T(1024)S(1)}, s32[2048]{0:T(1024)}) fusion(s32[2048]{0:T(1024)} %param.13, s32[]{:T(128)S(6)} %select_n.109, s32[]{:T(128)S(6)} %select_n.106, pred[2048]{0:T(1024)(128)(4,1)S(1)} %get-tuple-element.49, s32[]{:T(128)S(6)} %mul.32, s32[]{:T(128)S(6)} %mul.31), kind=kLoop, calls=%fused_computation.46 | loop fusion | flops 335872 | bytes 26640 | tf_op jit(solution)/shard_map/sub | solution.py:293
  20.3 0.6 select_reduce_fusion.1
  21.0 1.0 %select_reduce_fusion = s32[4,512]{1,0:T(4,128)S(1)} fusion(s32[4,512]{1,0:T(4,128)S(1)} %broadcast_in_dim.55, s32[4,512]{1,0:T(4,128)S(1)} %select_reduce_fusion.1, pred[4,512]{1,0:T(4,128)(4,1)S(1)} %reshape.60), kind=kLoop, calls=%fused_computation | loop fusion | flops 4192256 | bytes 26624 | tf_op jit(solution)/shard_map/reduce_sum | solution.py:295
  22.0 0.4 collective-permute-done.refs_0_
  22.4 0.0 copy-start.1
  22.4 0.0 collective-permute-done.1.refs_1_
  22.4 0.0 copy-start.2
  22.5 0.8 %pad_maximum_fusion = bf16[34,4,128]{2,1,0:T(4,128)(2,1)S(1)} fusion(bf16[1,4,128]{2,1,0:T(4,128)(2,1)S(1)} %get-tuple-element.53, bf16[32,4,128]{2,1,0:T(4,128)(2,1)} %get-tuple-element.26, bf16[1,4,128]{2,1,0:T(4,128)(2,1)S(1)} %get-tuple-element.51), kind=kLoop, calls=%fused_computation.5 | loop fusion | flops 34816 | bytes 69632 | tf_op jit(solution)/shard_map/concatenate | solution.py:502
  23.3 5.1 %collective-permute-start.2 = (bf16[34,4,128]{2,1,0:T(4,128)(2,1)S(1)}, bf16[34,4,128]{2,1,0:T(4,128)(2,1)S(1)}, u32[]{:S(2)}, u32[]{:S(2)}) collective-permute-start(bf16[34,4,128]{2,1,0:T(4,128)(2,1)S(1)} %pad_maximum_fusion), channel_id=1, source_target_pairs={{0,16},{16,32},{32,48},{48,64},{64,80},{80,96},{96,112},{1,17},{17... | collective-permute-start | bytes 104456 | tf_op jit(solution)/shard_map/ppermute | solution.py:503
  28.3 0.8 %pad_maximum_fusion.1 = bf16[34,4,128]{2,1,0:T(4,128)(2,1)S(1)} fusion(bf16[1,4,128]{2,1,0:T(4,128)(2,1)S(1)} %get-tuple-element.52, bf16[32,4,128]{2,1,0:T(4,128)(2,1)} %get-tuple-element.28, bf16[1,4,128]{2,1,0:T(4,128)(2,1)S(1)} %get-tuple-element.50), kind=kLoop, calls=%fused_computation.6 | loop fusion | flops 34816 | bytes 69632 | tf_op jit(solution)/shard_map/concatenate | solution.py:502
  29.1 1.9 %collective-permute-start.3 = (bf16[34,4,128]{2,1,0:T(4,128)(2,1)S(1)}, bf16[34,4,128]{2,1,0:T(4,128)(2,1)S(1)}, u32[]{:S(2)}, u32[]{:S(2)}) collective-permute-start(bf16[34,4,128]{2,1,0:T(4,128)(2,1)S(1)} %pad_maximum_fusion.1), channel_id=1, source_target_pairs={{16,0},{32,16},{48,32},{64,48},{80,64},{96,80},{112,96},{17,1},{33... | collective-permute-start | bytes 104456 | tf_op jit(solution)/shard_map/ppermute | solution.py:504
  31.1 0.7 convert_reduce_fusion.far_count
  31.8 0.6 copy.13
  32.4 0.0 collective-permute-done.2.refs_2_
  32.4 0.0 copy-start.10
  32.4 2.0 %collective-permute-done.3.refs_3_ = bf16[34,4,128]{2,1,0:T(4,128)(2,1)S(1)} collective-permute-done((bf16[34,4,128]{2,1,0:T(4,128)(2,1)S(1)}, bf16[34,4,128]{2,1,0:T(4,128)(2,1)S(1)}, u32[]{:S(2)}, u32[]{:S(2)}) %collective-permute-start.3) | collective-permute-done | bytes 34848 | tf_op jit(solution)/shard_map/ppermute | solution.py:504
  34.4 0.0 copy-start.11
  34.4 0.0 all-to-all-done
  34.4 0.0 copy-start
  34.4 0.1 collective-permute-start.4
  34.5 6.9 %early.1.refs_4_ = bf16[2048,512]{1,0:T(8,128)(2,1)} custom-call(s32[16]{0:T(128)} %tiles.3, bf16[2048,512]{1,0:T(8,128)(2,1)} %refs_9_.1, s32[4,4,128]{2,1,0:T(4,128)} %bitcast.20, bf16[512,512]{1,0:T(8,128)(2,1)} %bitcast.13, bf16[1536,512]{1,0:T(8,128)(2,1)} %refs_11_.1, bf16[1536,512]{1,0:T(8,128)(2,1)} %refs_11_.1), custom_call_target="tpu_custom_call" | custom-call | flops 3000000000 | bytes 10000000 | tf_op jit(solution)/shard_map/early/pallas_call | solution.py:310
  41.4 0.0 copy-done.1
  41.4 0.0 copy-done.2
  41.4 0.0 copy-done.10
  41.4 0.0 copy-done.11
  41.5 1.5 %collective-permute-start.6 = (bf16[512,4,128]{2,1,0:T(4,128)(2,1)S(1)}, bf16[512,4,128]{2,1,0:T(4,128)(2,1)S(1)}, u32[]{:S(2)}, u32[]{:S(2)}) collective-permute-start(bf16[512,4,128]{2,1,0:T(4,128)(2,1)S(1)} %bitcast.17), channel_id=1, source_target_pairs={{0,96},{1,97},{2,98},{3,99},{4,100},{5,101},{6,102},{7,103},{8,104... | collective-permute-start | bytes 1572872 | tf_op jit(solution)/shard_map/ppermute | solution.py:47
  43.0 0.0 collective-permute-done.4.refs_1_
  43.0 0.0 copy-start.3
  43.0 1.4 %collective-permute-start.5 = (bf16[512,4,128]{2,1,0:T(4,128)(2,1)S(1)}, bf16[512,4,128]{2,1,0:T(4,128)(2,1)S(1)}, u32[]{:S(2)}, u32[]{:S(2)}) collective-permute-start(bf16[512,4,128]{2,1,0:T(4,128)(2,1)S(1)} %collective-permute-done.4.refs_1_), channel_id=1, source_target_pairs={{0,32},{1,33},{2,34},{3,35},{4,36},{5,37},{6,38},{7,39},{8,40},{9,... | collective-permute-start | bytes 1572872 | tf_op jit(solution)/shard_map/ppermute | solution.py:47
  44.3 0.0 copy-done
  44.3 0.0 collective-permute-start.7
  44.3 0.5 collective-permute-start.8
  44.8 8.4 %near.1.refs_8_ = bf16[2048,512]{1,0:T(8,128)(2,1)} custom-call(s32[2048]{0:T(1024)} %get-tuple-element.37.near_index, bf16[512,512]{1,0:T(8,128)(2,1)} %bitcast.14, bf16[16,4,128]{2,1,0:T(4,128)(2,1)} %copy-done.1, bf16[16,4,128]{2,1,0:T(4,128)(2,1)} %copy-done.2, bf16[34,4,128]{2,1,0:T(4,128)(2,1)} %copy-done.10, bf16[34,4,128]{2,1,0:T(4,128)(2,1)} %copy-done.11, ...), custom_call_target="tpu_custom_call" | custom-call | flops 2000000000 | bytes 8000000 | tf_op jit(solution)/shard_map/near/pallas_call | solution.py:332
  53.2 0.0 copy-done.3
  53.2 1.3 %collective-permute-done.6.refs_2_ = bf16[512,4,128]{2,1,0:T(4,128)(2,1)S(1)} collective-permute-done((bf16[512,4,128]{2,1,0:T(4,128)(2,1)S(1)}, bf16[512,4,128]{2,1,0:T(4,128)(2,1)S(1)}, u32[]{:S(2)}, u32[]{:S(2)}) %collective-permute-start.6) | collective-permute-done | bytes 524320 | tf_op jit(solution)/shard_map/ppermute | solution.py:47
  54.5 0.0 copy-start.4
  54.5 1.7 %collective-permute-done.5.refs_3_ = bf16[512,4,128]{2,1,0:T(4,128)(2,1)S(1)} collective-permute-done((bf16[512,4,128]{2,1,0:T(4,128)(2,1)S(1)}, bf16[512,4,128]{2,1,0:T(4,128)(2,1)S(1)}, u32[]{:S(2)}, u32[]{:S(2)}) %collective-permute-start.5) | collective-permute-done | bytes 524320 | tf_op jit(solution)/shard_map/ppermute | solution.py:47
  56.2 0.0 copy-start.5
  56.2 0.9 %collective-permute-start.9 = (bf16[512,4,128]{2,1,0:T(4,128)(2,1)S(1)}, bf16[512,4,128]{2,1,0:T(4,128)(2,1)S(1)}, u32[]{:S(2)}, u32[]{:S(2)}) collective-permute-start(bf16[512,4,128]{2,1,0:T(4,128)(2,1)S(1)} %collective-permute-done.6.refs_2_), channel_id=1, source_target_pairs={{0,16},{1,17},{2,18},{3,19},{4,20},{5,21},{6,22},{7,23},{8,24},{9,... | collective-permute-start | bytes 1572872 | tf_op jit(solution)/shard_map/ppermute | solution.py:43
  57.1 0.0 collective-permute-start.10
  57.1 0.0 collective-permute-done.7.refs_4_
  57.1 0.0 copy-start.6
  57.1 0.0 collective-permute-done.8.refs_5_
  57.1 0.0 copy-start.7
  57.1 1.5 %collective-permute-done.9.refs_6_ = bf16[512,4,128]{2,1,0:T(4,128)(2,1)S(1)} collective-permute-done((bf16[512,4,128]{2,1,0:T(4,128)(2,1)S(1)}, bf16[512,4,128]{2,1,0:T(4,128)(2,1)S(1)}, u32[]{:S(2)}, u32[]{:S(2)}) %collective-permute-start.9) | collective-permute-done | bytes 524320 | tf_op jit(solution)/shard_map/ppermute | solution.py:43
  58.6 0.0 copy-start.8
  58.6 0.7 %collective-permute-done.10.refs_7_ = bf16[512,4,128]{2,1,0:T(4,128)(2,1)S(1)} collective-permute-done((bf16[512,4,128]{2,1,0:T(4,128)(2,1)S(1)}, bf16[512,4,128]{2,1,0:T(4,128)(2,1)S(1)}, u32[]{:S(2)}, u32[]{:S(2)}) %collective-permute-start.10) | collective-permute-done | bytes 524320 | tf_op jit(solution)/shard_map/ppermute | solution.py:43
  59.4 0.0 copy-start.9
  59.4 0.0 copy-done.4
  59.4 0.0 copy-done.5
  59.4 0.0 copy-done.6
  59.4 0.0 copy-done.7
  59.4 0.0 copy-done.8
  59.5 0.7 %copy-done.9 = bf16[512,4,128]{2,1,0:T(4,128)(2,1)} copy-done((bf16[512,4,128]{2,1,0:T(4,128)(2,1)}, bf16[512,4,128]{2,1,0:T(4,128)(2,1)S(1)}, u32[]{:S(2)}) %copy-start.9) | copy-done | bytes 524312
  60.2 12.4 %late.1 = (bf16[2048,512]{1,0:T(8,128)(2,1)}, bf16[512,512]{1,0:T(8,128)(2,1)}) custom-call(s32[2048]{0:T(1024)} %bitcast.22, s32[4]{0:T(128)} %convert_reduce_fusion.far_count, s32[16]{0:T(128)} %tiles.3, s32[16]{0:T(128)} %get-tuple-element.31.lives, bf16[512,4,128]{2,1,0:T(4,128)(2,1)} %bitcast.19, bf16[512,4,128]{2,1,0:T(4,128)(2,1)} %copy-done.3, ...), custom_call_target="tpu_custom_call" | custom-call | flops 4000000000 | bytes 14000000 | tf_op jit(solution)/shard_map/late/pallas_call | solution.py:377
  (6 shorter events, 0.0 us)
Async XLA Ops:
  3.3 31.1 %all-to-all-start = ((bf16[16,32,4,128]{3,2,1,0:T(4,128)(2,1)}), bf16[16,32,4,128]{3,2,1,0:T(4,128)(2,1)S(1)}, u32[]{:S(2)}, u32[]{:S(2)}) async-start(bf16[16,32,4,128]{3,2,1,0:T(4,128)(2,1)} %get-tuple-element.24), calls=%async_computation | async-start | bytes 1048576 | tf_op jit(solution)/shard_map/all_to_all | solution.py:501
  12.0 10.5 %collective-permute-start = (bf16[16,4,128]{2,1,0:T(4,128)(2,1)}, bf16[16,4,128]{2,1,0:T(4,128)(2,1)S(1)}, u32[]{:S(2)}, u32[]{:S(2)}) collective-permute-start(bf16[16,4,128]{2,1,0:T(4,128)(2,1)} %get-tuple-element.25), channel_id=1, source_target_pairs={{0,1},{1,2},{2,3},{3,4},{4,5},{5,6},{6,7},{7,8},{8,9},{9,10},{10,1... | collective-permute-start | bytes 49160 | tf_op jit(solution)/shard_map/ppermute | solution.py:499
  13.3 9.1 %collective-permute-start.1 = (bf16[16,4,128]{2,1,0:T(4,128)(2,1)}, bf16[16,4,128]{2,1,0:T(4,128)(2,1)S(1)}, u32[]{:S(2)}, u32[]{:S(2)}) collective-permute-start(bf16[16,4,128]{2,1,0:T(4,128)(2,1)} %get-tuple-element.27), channel_id=1, source_target_pairs={{1,0},{2,1},{3,2},{4,3},{5,4},{6,5},{7,6},{8,7},{9,8},{10,9},{11,1... | collective-permute-start | bytes 49160 | tf_op jit(solution)/shard_map/ppermute | solution.py:500
  22.4 19.0 %copy-start.1 = (bf16[16,4,128]{2,1,0:T(4,128)(2,1)}, bf16[16,4,128]{2,1,0:T(4,128)(2,1)S(1)}, u32[]{:S(2)}) copy-start(bf16[16,4,128]{2,1,0:T(4,128)(2,1)S(1)} %collective-permute-done.refs_0_) | copy-start | bytes 49156
  22.4 19.0 %copy-start.2 = (bf16[16,4,128]{2,1,0:T(4,128)(2,1)}, bf16[16,4,128]{2,1,0:T(4,128)(2,1)S(1)}, u32[]{:S(2)}) copy-start(bf16[16,4,128]{2,1,0:T(4,128)(2,1)S(1)} %collective-permute-done.1.refs_1_) | copy-start | bytes 49156
  23.3 9.1 %collective-permute-start.2 = (bf16[34,4,128]{2,1,0:T(4,128)(2,1)S(1)}, bf16[34,4,128]{2,1,0:T(4,128)(2,1)S(1)}, u32[]{:S(2)}, u32[]{:S(2)}) collective-permute-start(bf16[34,4,128]{2,1,0:T(4,128)(2,1)S(1)} %pad_maximum_fusion), channel_id=1, source_target_pairs={{0,16},{16,32},{32,48},{48,64},{64,80},{80,96},{96,112},{1,17},{17... | collective-permute-start | bytes 104456 | tf_op jit(solution)/shard_map/ppermute | solution.py:503
  29.1 5.3 %collective-permute-start.3 = (bf16[34,4,128]{2,1,0:T(4,128)(2,1)S(1)}, bf16[34,4,128]{2,1,0:T(4,128)(2,1)S(1)}, u32[]{:S(2)}, u32[]{:S(2)}) collective-permute-start(bf16[34,4,128]{2,1,0:T(4,128)(2,1)S(1)} %pad_maximum_fusion.1), channel_id=1, source_target_pairs={{16,0},{32,16},{48,32},{64,48},{80,64},{96,80},{112,96},{17,1},{33... | collective-permute-start | bytes 104456 | tf_op jit(solution)/shard_map/ppermute | solution.py:504
  32.4 9.1 %copy-start.10 = (bf16[34,4,128]{2,1,0:T(4,128)(2,1)}, bf16[34,4,128]{2,1,0:T(4,128)(2,1)S(1)}, u32[]{:S(2)}) copy-start(bf16[34,4,128]{2,1,0:T(4,128)(2,1)S(1)} %collective-permute-done.2.refs_2_) | copy-start | bytes 104452
  34.4 7.1 %copy-start.11 = (bf16[34,4,128]{2,1,0:T(4,128)(2,1)}, bf16[34,4,128]{2,1,0:T(4,128)(2,1)S(1)}, u32[]{:S(2)}) copy-start(bf16[34,4,128]{2,1,0:T(4,128)(2,1)S(1)} %collective-permute-done.3.refs_3_) | copy-start | bytes 104452
  34.4 9.9 %copy-start = (bf16[16,32,4,128]{3,2,1,0:T(4,128)(2,1)}, bf16[16,32,4,128]{3,2,1,0:T(4,128)(2,1)S(1)}, u32[]{:S(2)}) copy-start(bf16[16,32,4,128]{3,2,1,0:T(4,128)(2,1)S(1)} %all-to-all-done) | copy-start | bytes 1572868
  34.4 8.6 %collective-permute-start.4 = (bf16[512,4,128]{2,1,0:T(4,128)(2,1)S(1)}, bf16[512,4,128]{2,1,0:T(4,128)(2,1)S(1)}, u32[]{:S(2)}, u32[]{:S(2)}) collective-permute-start(bf16[512,4,128]{2,1,0:T(4,128)(2,1)S(1)} %bitcast.16), channel_id=1, source_target_pairs={{0,32},{1,33},{2,34},{3,35},{4,36},{5,37},{6,38},{7,39},{8,40},{9,... | collective-permute-start | bytes 1572872 | tf_op jit(solution)/shard_map/ppermute | solution.py:47
  41.5 13.0 %collective-permute-start.6 = (bf16[512,4,128]{2,1,0:T(4,128)(2,1)S(1)}, bf16[512,4,128]{2,1,0:T(4,128)(2,1)S(1)}, u32[]{:S(2)}, u32[]{:S(2)}) collective-permute-start(bf16[512,4,128]{2,1,0:T(4,128)(2,1)S(1)} %bitcast.17), channel_id=1, source_target_pairs={{0,96},{1,97},{2,98},{3,99},{4,100},{5,101},{6,102},{7,103},{8,104... | collective-permute-start | bytes 1572872 | tf_op jit(solution)/shard_map/ppermute | solution.py:47
  43.0 10.3 %copy-start.3 = (bf16[512,4,128]{2,1,0:T(4,128)(2,1)}, bf16[512,4,128]{2,1,0:T(4,128)(2,1)S(1)}, u32[]{:S(2)}) copy-start(bf16[512,4,128]{2,1,0:T(4,128)(2,1)S(1)} %collective-permute-done.4.refs_1_) | copy-start | bytes 1572868
  43.0 13.3 %collective-permute-start.5 = (bf16[512,4,128]{2,1,0:T(4,128)(2,1)S(1)}, bf16[512,4,128]{2,1,0:T(4,128)(2,1)S(1)}, u32[]{:S(2)}, u32[]{:S(2)}) collective-permute-start(bf16[512,4,128]{2,1,0:T(4,128)(2,1)S(1)} %collective-permute-done.4.refs_1_), channel_id=1, source_target_pairs={{0,32},{1,33},{2,34},{3,35},{4,36},{5,37},{6,38},{7,39},{8,40},{9,... | collective-permute-start | bytes 1572872 | tf_op jit(solution)/shard_map/ppermute | solution.py:47
  44.3 12.8 %collective-permute-start.7 = (bf16[512,4,128]{2,1,0:T(4,128)(2,1)S(1)}, bf16[512,4,128]{2,1,0:T(4,128)(2,1)S(1)}, u32[]{:S(2)}, u32[]{:S(2)}) collective-permute-start(bf16[512,4,128]{2,1,0:T(4,128)(2,1)S(1)} %bitcast.18), channel_id=1, source_target_pairs={{0,16},{1,17},{2,18},{3,19},{4,20},{5,21},{6,22},{7,23},{8,24},{9,... | collective-permute-start | bytes 1572872 | tf_op jit(solution)/shard_map/ppermute | solution.py:43
  44.3 12.8 %collective-permute-start.8 = (bf16[512,4,128]{2,1,0:T(4,128)(2,1)S(1)}, bf16[512,4,128]{2,1,0:T(4,128)(2,1)S(1)}, u32[]{:S(2)}, u32[]{:S(2)}) collective-permute-start(bf16[512,4,128]{2,1,0:T(4,128)(2,1)S(1)} %collective-permute-done.4.refs_1_), channel_id=1, source_target_pairs={{0,16},{1,17},{2,18},{3,19},{4,20},{5,21},{6,22},{7,23},{8,24},{9,... | collective-permute-start | bytes 1572872 | tf_op jit(solution)/shard_map/ppermute | solution.py:43
  54.5 4.9 %copy-start.4 = (bf16[512,4,128]{2,1,0:T(4,128)(2,1)}, bf16[512,4,128]{2,1,0:T(4,128)(2,1)S(1)}, u32[]{:S(2)}) copy-start(bf16[512,4,128]{2,1,0:T(4,128)(2,1)S(1)} %collective-permute-done.6.refs_2_) | copy-start | bytes 1572868
  56.2 3.2 %copy-start.5 = (bf16[512,4,128]{2,1,0:T(4,128)(2,1)}, bf16[512,4,128]{2,1,0:T(4,128)(2,1)S(1)}, u32[]{:S(2)}) copy-start(bf16[512,4,128]{2,1,0:T(4,128)(2,1)S(1)} %collective-permute-done.5.refs_3_) | copy-start | bytes 1572868
  56.2 2.4 %collective-permute-start.9 = (bf16[512,4,128]{2,1,0:T(4,128)(2,1)S(1)}, bf16[512,4,128]{2,1,0:T(4,128)(2,1)S(1)}, u32[]{:S(2)}, u32[]{:S(2)}) collective-permute-start(bf16[512,4,128]{2,1,0:T(4,128)(2,1)S(1)} %collective-permute-done.6.refs_2_), channel_id=1, source_target_pairs={{0,16},{1,17},{2,18},{3,19},{4,20},{5,21},{6,22},{7,23},{8,24},{9,... | collective-permute-start | bytes 1572872 | tf_op jit(solution)/shard_map/ppermute | solution.py:43
  57.1 2.3 %collective-permute-start.10 = (bf16[512,4,128]{2,1,0:T(4,128)(2,1)S(1)}, bf16[512,4,128]{2,1,0:T(4,128)(2,1)S(1)}, u32[]{:S(2)}, u32[]{:S(2)}) collective-permute-start(bf16[512,4,128]{2,1,0:T(4,128)(2,1)S(1)} %collective-permute-done.5.refs_3_), channel_id=1, source_target_pairs={{0,16},{1,17},{2,18},{3,19},{4,20},{5,21},{6,22},{7,23},{8,24},{9,... | collective-permute-start | bytes 1572872 | tf_op jit(solution)/shard_map/ppermute | solution.py:43
  57.1 2.3 %copy-start.6 = (bf16[512,4,128]{2,1,0:T(4,128)(2,1)}, bf16[512,4,128]{2,1,0:T(4,128)(2,1)S(1)}, u32[]{:S(2)}) copy-start(bf16[512,4,128]{2,1,0:T(4,128)(2,1)S(1)} %collective-permute-done.7.refs_4_) | copy-start | bytes 1572868
  57.1 2.3 %copy-start.7 = (bf16[512,4,128]{2,1,0:T(4,128)(2,1)}, bf16[512,4,128]{2,1,0:T(4,128)(2,1)S(1)}, u32[]{:S(2)}) copy-start(bf16[512,4,128]{2,1,0:T(4,128)(2,1)S(1)} %collective-permute-done.8.refs_5_) | copy-start | bytes 1572868
  58.6 0.8 %copy-start.8 = (bf16[512,4,128]{2,1,0:T(4,128)(2,1)}, bf16[512,4,128]{2,1,0:T(4,128)(2,1)S(1)}, u32[]{:S(2)}) copy-start(bf16[512,4,128]{2,1,0:T(4,128)(2,1)S(1)} %collective-permute-done.9.refs_6_) | copy-start | bytes 1572868
  59.4 0.8 %copy-start.9 = (bf16[512,4,128]{2,1,0:T(4,128)(2,1)}, bf16[512,4,128]{2,1,0:T(4,128)(2,1)S(1)}, u32[]{:S(2)}) copy-start(bf16[512,4,128]{2,1,0:T(4,128)(2,1)S(1)} %collective-permute-done.10.refs_7_) | copy-start | bytes 1572868

commit v7 on v6

--- a/solution.py
+++ b/solution.py
@@ -11,7 +11,7 @@
 ROWS = GROUP * BLK
 RIMS = 4
 FAR = 8
-VMEM = 56 << 20
+VMEM = 16 << 20
 BF = jnp.bfloat16
 F32 = jnp.float32
 
@@ -318,7 +318,7 @@
             scratch_shapes=[pltpu.VMEM((ROWS, F), BF)],
         ),
         out_shape=jax.ShapeDtypeStruct((blocks * BLK, F), BF),
-        compiler_params=pltpu.CompilerParams(vmem_limit_bytes=VMEM),
+        compiler_params=pltpu.CompilerParams(vmem_limit_bytes=16 << 20),
         cost_estimate=pl.CostEstimate(
             flops=3 * 10**9, bytes_accessed=10 * 10**6, transcendentals=0
         ),
@@ -343,7 +343,7 @@
             ],
         ),
         out_shape=jax.ShapeDtypeStruct((slots, F), BF),
-        compiler_params=pltpu.CompilerParams(vmem_limit_bytes=VMEM),
+        compiler_params=pltpu.CompilerParams(vmem_limit_bytes=16 << 20),
         cost_estimate=pl.CostEstimate(
             flops=2 * 10**9, bytes_accessed=8 * 10**6, transcendentals=0
         ),
@@ -399,7 +399,7 @@
             jax.ShapeDtypeStruct((slots, F), BF),
             jax.ShapeDtypeStruct((nodes, F), BF),
         ],
-        compiler_params=pltpu.CompilerParams(vmem_limit_bytes=VMEM),
+        compiler_params=pltpu.CompilerParams(vmem_limit_bytes=40 << 20),
         cost_estimate=pl.CostEstimate(
             flops=4 * 10**9, bytes_accessed=14 * 10**6, transcendentals=2 * 10**6
         ),
@@ -502,13 +502,13 @@
     wide = lambda r, rows: jnp.concatenate([west[r : r + 1], rows, east[r : r + 1]], 0)
     north = lax.ppermute(wide(patch_rows - 1, bottom), "lat", up)
     south = lax.ppermute(wide(0, top), "lat", down)
-    plane, north, south, edges, near_index, far_list, far_count, lives = lax.optimization_barrier(
-        (plane, north, south, edge_latent, near_index, far_list, far_count, lives)
+    plane, north, south, tiles, near_index, far_list, far_count, lives = lax.optimization_barrier(
+        (plane, north, south, block_tile, near_index, far_list, far_count, lives)
     )
 
     ahead = move(plane, "x", (1, -1))
     plane_other = other_core(plane)
-    partial = early_call(block_tile, edges, recv_rows, own_rows, w_first)
+    partial = early_call(tiles, edge_latent, recv_rows, own_rows, w_first)
     later, partial = lax.optimization_barrier((plane, partial))
     behind = move(later, "x", (-1, 1))
     ahead, partial = lax.optimization_barrier((ahead, partial))

time: 73.6 us -> 67.5 us (0.917)
  Pallas kernels: 30.5 us -> 21.8 us
  waiting for transfers between devices: 7.72 us -> 13 us
  other arithmetic: 7.39 us -> 4.2 us
  local copies, waits for them, and re-layouts: 1.45 us -> 2.72 us
    ppermute x3, waiting for transfers between devices: 2.99 us -> 6.03 us  [move(): return lax.ppermute(value, ('lat', 'lon'), shift(axis, by_core))]
    pallas_call x1, Pallas kernels: 6.95 us -> 4.04 us  [early_call(): pl.pallas_call(early_kernel, name='early', grid_spec=pltpu.PrefetchScalar...]
    pallas_call x1, Pallas kernels: 8.4 us -> 5.87 us  [near_call(): pl.pallas_call(near_kernel, name='near', grid_spec=pltpu.PrefetchScalarGr...]
    pallas_call x1, Pallas kernels: 2.7 us -> 1.02 us  [per_device(): pl.pallas_call(coarse_kernel, name='coarse', in_specs=[pl.BlockSpec(memor...]
    pallas_call x1, Pallas kernels: 12.4 us -> 10.9 us  [late_call(): pl.pallas_call(late_kernel, name='late', in_specs=[scalars] * 4 + [anywhe...]
    concatenate x2, other arithmetic: 1.58 us -> 0.06 us  [per_device(): jnp.concatenate([west[r:r + 1], rows, east[r:r + 1]], 0)]
    unnamed x25, local copies, waits for them, and re-layouts: 1.42 us -> 2.68 us
    ppermute x1, waiting for transfers between devices: 2.02 us -> 3.19 us  [per_device(): south = lax.ppermute(wide(0, top), 'lat', down)]
  transfers between devices with their start and end apart: 12 -> 12, of which waited for: 6 -> 7; matrix products, arithmetic and copies ran while one was open for 11% -> 6% of each run, Pallas kernels for 21% -> 15%
where the time goes in v7:
time: 67.5 us; the launch traced here: 67 us
  starting transfers between devices  24.2 us (36%)
  Pallas kernels  21.8 us (32%)
  waiting for transfers between devices  13 us (19%)
  other arithmetic  4.2 us (6%)
  local copies, waits for them, and re-layouts  2.72 us (4%)
  between operations  1.05 us (2%)
    pallas_call x1, Pallas kernels, late_call(): pl.pallas_call(late_kernel, name='late', in_specs=[scalars] * 4 + [anywhe...  10.9 us
    all_to_all x1, starting transfers between devices, per_device(): lax.all_to_all(copies, 'lon', split_axis=0, concat_axis=0, tiled=True)  8.61 us
    ppermute x3, waiting for transfers between devices, move(): return lax.ppermute(value, ('lat', 'lon'), shift(axis, by_core))  6.03 us
    pallas_call x1, Pallas kernels, near_call(): pl.pallas_call(near_kernel, name='near', grid_spec=pltpu.PrefetchScalarGr...  5.87 us
    ppermute x1, starting transfers between devices, per_device(): north = lax.ppermute(wide(patch_rows - 1, bottom), 'lat', up)  5.08 us
    pallas_call x1, Pallas kernels, early_call(): pl.pallas_call(early_kernel, name='early', grid_spec=pltpu.PrefetchScalar...  4.04 us
    ppermute x1, starting transfers between devices, per_device(): east = lax.ppermute(first_col, 'lon', left)  3.49 us
    ppermute x1, waiting for transfers between devices, per_device(): south = lax.ppermute(wide(0, top), 'lat', down)  3.19 us
  transfers between devices with their start and end apart: 12, of which 7 were waited for; matrix products, arithmetic and copies ran while one was open for 6% of the time, Pallas kernels for 15%

profile of v7, /device:TPU:1, one launch (start us, length us, event | category | flops | bytes accessed | tf_op | source)
XLA Modules:
  0.0 67.0 jit_solution(9967884959667466180)
XLA Ops:
  0.6 0.0 copy-start.11
  0.6 0.0 copy-start
  0.6 1.0 %copy-done = bf16[16,32,512]{2,1,0:T(8,128)(2,1)S(1)} copy-done((bf16[16,32,512]{2,1,0:T(8,128)(2,1)S(1)}, bf16[16,32,512]{2,1,0:T(8,128)(2,1)}, u32[]{:S(2)}) %copy-start) | copy-done | bytes 524312
  1.7 0.0 copy-start.1
  1.7 0.0 copy-start.2
  1.7 0.0 copy-start.5
  1.7 1.0 %coarse.1 = (bf16[16,32,4,128]{3,2,1,0:T(4,128)(2,1)}, bf16[16,4,128]{2,1,0:T(4,128)(2,1)S(1)}, bf16[16,4,128]{2,1,0:T(4,128)(2,1)S(1)}, bf16[32,4,128]{2,1,0:T(4,128)(2,1)S(1)}, bf16[32,4,128]{2,1,0:T(4,128)(2,1)S(1)}) custom-call(bf16[512,512]{1,0:T(8,128)(2,1)S(1)} %bitcast.12), custom_call_target="tpu_custom_call" | custom-call | tf_op jit(solution)/shard_map/coarse/pallas_call | solution.py:456
  2.7 8.6 %all-to-all-start = ((bf16[16,32,4,128]{3,2,1,0:T(4,128)(2,1)}), bf16[16,32,4,128]{3,2,1,0:T(4,128)(2,1)S(1)}, u32[]{:S(2)}, u32[]{:S(2)}) async-start(bf16[16,32,4,128]{3,2,1,0:T(4,128)(2,1)} %get-tuple-element.24), calls=%async_computation | async-start | bytes 1048576 | tf_op jit(solution)/shard_map/all_to_all | solution.py:501
  11.3 1.4 %collective-permute-start = (bf16[16,4,128]{2,1,0:T(4,128)(2,1)S(1)}, bf16[16,4,128]{2,1,0:T(4,128)(2,1)S(1)}, u32[]{:S(2)}, u32[]{:S(2)}) collective-permute-start(bf16[16,4,128]{2,1,0:T(4,128)(2,1)S(1)} %get-tuple-element.25), channel_id=1, source_target_pairs={{0,1},{1,2},{2,3},{3,4},{4,5},{5,6},{6,7},{7,8},{8,9},{9,10},{10,1... | collective-permute-start | bytes 49160 | tf_op jit(solution)/shard_map/ppermute | solution.py:499
  12.7 3.5 %collective-permute-start.1 = (bf16[16,4,128]{2,1,0:T(4,128)(2,1)S(1)}, bf16[16,4,128]{2,1,0:T(4,128)(2,1)S(1)}, u32[]{:S(2)}, u32[]{:S(2)}) collective-permute-start(bf16[16,4,128]{2,1,0:T(4,128)(2,1)S(1)} %get-tuple-element.27), channel_id=1, source_target_pairs={{1,0},{2,1},{3,2},{4,3},{5,4},{6,5},{7,6},{8,7},{9,8},{10,9},{11,1... | collective-permute-start | bytes 49160 | tf_op jit(solution)/shard_map/ppermute | solution.py:500
  16.2 0.1 iota_compare_fusion.1
  16.3 0.8 %bitcast_reduce_fusion = (s32[16]{0:T(128)S(1)}, pred[2048]{0:T(1024)(128)(4,1)S(1)}) fusion(s32[2048]{0:T(1024)} %param.14), kind=kLoop, calls=%fused_computation.51 | loop fusion | flops 6128 | bytes 10304 | tf_op jit(solution)/shard_map/reduce_sum | solution.py:497
  17.1 0.7 %not_and_fusion = (pred[2048]{0:T(1024)(128)(4,1)S(1)}, pred[2048]{0:T(1024)(128)(4,1)S(1)}) fusion(pred[2048]{0:T(1024)(128)(4,1)S(1)} %get-tuple-element.47, s32[]{:T(128)S(6)} %mul.32, s32[]{:T(128)S(6)} %mul.31, s32[2048]{0:T(1024)} %param.13), kind=kLoop, calls=%fused_computation.68 | loop fusion | flops 71680 | bytes 14344 | tf_op jit(solution)/shard_map/and | solution.py:495
  17.9 0.8 %fusion.9 = (s32[2048]{0:T(1024)S(1)}, s32[2048]{0:T(1024)S(1)}) fusion(s32[2048]{0:T(1024)} %param.13, s32[]{:T(128)S(6)} %select_n.109, s32[]{:T(128)S(6)} %select_n.106, pred[2048]{0:T(1024)(128)(4,1)S(1)} %get-tuple-element.49, s32[]{:T(128)S(6)} %mul.32, s32[]{:T(128)S(6)} %mul.31), kind=kLoop, calls=%fused_computation.46 | loop fusion | flops 335872 | bytes 26640 | tf_op jit(solution)/shard_map/sub | solution.py:293
  18.7 0.6 select_reduce_fusion.1
  19.3 1.0 %select_reduce_fusion = s32[4,512]{1,0:T(4,128)S(1)} fusion(s32[4,512]{1,0:T(4,128)S(1)} %broadcast_in_dim.55, s32[4,512]{1,0:T(4,128)S(1)} %select_reduce_fusion.1, pred[4,512]{1,0:T(4,128)(4,1)S(1)} %reshape.60), kind=kLoop, calls=%fused_computation | loop fusion | flops 4192256 | bytes 26624 | tf_op jit(solution)/shard_map/reduce_sum | solution.py:295
  20.3 1.5 %collective-permute-done.refs_0_ = bf16[16,4,128]{2,1,0:T(4,128)(2,1)S(1)} collective-permute-done((bf16[16,4,128]{2,1,0:T(4,128)(2,1)S(1)}, bf16[16,4,128]{2,1,0:T(4,128)(2,1)S(1)}, u32[]{:S(2)}, u32[]{:S(2)}) %collective-permute-start) | collective-permute-done | bytes 16416 | tf_op jit(solution)/shard_map/ppermute | solution.py:499
  21.8 0.0 collective-permute-done.1.refs_1_
  21.9 5.1 %collective-permute-start.2 = (bf16[34,4,128]{2,1,0:T(4,128)(2,1)S(1)}, bf16[34,4,128]{2,1,0:T(4,128)(2,1)S(1)}, u32[]{:S(2)}, u32[]{:S(2)}) collective-permute-start(bf16[34,4,128]{2,1,0:T(4,128)(2,1)S(1)} %pad_maximum_fusion), channel_id=1, source_target_pairs={{0,16},{16,32},{32,48},{48,64},{64,80},{80,96},{96,112},{1,17},{17... | collective-permute-start | bytes 104456 | tf_op jit(solution)/shard_map/ppermute | solution.py:503
  27.0 1.9 %collective-permute-start.3 = (bf16[34,4,128]{2,1,0:T(4,128)(2,1)S(1)}, bf16[34,4,128]{2,1,0:T(4,128)(2,1)S(1)}, u32[]{:S(2)}, u32[]{:S(2)}) collective-permute-start(bf16[34,4,128]{2,1,0:T(4,128)(2,1)S(1)} %pad_maximum_fusion.1), channel_id=1, source_target_pairs={{16,0},{32,16},{48,32},{64,48},{80,64},{96,80},{112,96},{17,1},{33... | collective-permute-start | bytes 104456 | tf_op jit(solution)/shard_map/ppermute | solution.py:504
  28.9 0.1 convert_reduce_fusion.far_count
  29.1 0.0 collective-permute-done.2.refs_2_
  29.1 3.2 %collective-permute-done.3.refs_3_ = bf16[34,4,128]{2,1,0:T(4,128)(2,1)S(1)} collective-permute-done((bf16[34,4,128]{2,1,0:T(4,128)(2,1)S(1)}, bf16[34,4,128]{2,1,0:T(4,128)(2,1)S(1)}, u32[]{:S(2)}, u32[]{:S(2)}) %collective-permute-start.3) | collective-permute-done | bytes 34848 | tf_op jit(solution)/shard_map/ppermute | solution.py:504
  32.3 0.0 all-to-all-done
  32.3 0.0 collective-permute-start.4
  32.3 0.0 copy-done.11
  32.3 0.0 copy-done.1
  32.3 0.0 copy-done.2
  32.3 0.0 copy-done.5
  32.3 0.0 copy-start.3
  32.3 1.6 %copy-done.3 = bf16[2048,512]{1,0:T(8,128)(2,1)S(1)} copy-done((bf16[2048,512]{1,0:T(8,128)(2,1)S(1)}, bf16[2048,512]{1,0:T(8,128)(2,1)}, u32[]{:S(2)}) %copy-start.3) | copy-done | bytes 2097176
  33.9 4.0 %early.1.refs_4_ = bf16[2048,512]{1,0:T(8,128)(2,1)S(1)} custom-call(s32[16]{0:T(128)S(1)} %copy-done.11, bf16[2048,512]{1,0:T(8,128)(2,1)S(1)} %copy-done.3, s32[4,4,128]{2,1,0:T(4,128)S(1)} %bitcast.20, bf16[512,512]{1,0:T(8,128)(2,1)S(1)} %bitcast.13, bf16[1536,512]{1,0:T(8,128)(2,1)S(1)} %copy-done.5, bf16[1536,512]{1,0:T(8,128)(2,1)S(1)} %copy-done.5), custom_call_target="tpu_custom_call" | custom-call | flops 3000000000 | bytes 10000000 | tf_op jit(solution)/shard_map/early/pallas_call | solution.py:310
  37.9 0.0 copy-start.4
  38.0 0.0 copy-start.6
  38.0 0.0 copy-start.7
  38.0 0.0 copy-start.8
  38.0 0.0 copy-start.9
  38.0 0.0 copy-start.10
  38.0 1.5 %collective-permute-start.6 = (bf16[512,4,128]{2,1,0:T(4,128)(2,1)S(1)}, bf16[512,4,128]{2,1,0:T(4,128)(2,1)S(1)}, u32[]{:S(2)}, u32[]{:S(2)}) collective-permute-start(bf16[512,4,128]{2,1,0:T(4,128)(2,1)S(1)} %bitcast.17), channel_id=1, source_target_pairs={{0,96},{1,97},{2,98},{3,99},{4,100},{5,101},{6,102},{7,103},{8,104... | collective-permute-start | bytes 1572872 | tf_op jit(solution)/shard_map/ppermute | solution.py:47
  39.5 1.1 %collective-permute-done.4.refs_1_ = bf16[512,4,128]{2,1,0:T(4,128)(2,1)S(1)} collective-permute-done((bf16[512,4,128]{2,1,0:T(4,128)(2,1)S(1)}, bf16[512,4,128]{2,1,0:T(4,128)(2,1)S(1)}, u32[]{:S(2)}, u32[]{:S(2)}) %collective-permute-start.4) | collective-permute-done | bytes 524320 | tf_op jit(solution)/shard_map/ppermute | solution.py:47
  40.6 0.9 %collective-permute-start.5 = (bf16[512,4,128]{2,1,0:T(4,128)(2,1)S(1)}, bf16[512,4,128]{2,1,0:T(4,128)(2,1)S(1)}, u32[]{:S(2)}, u32[]{:S(2)}) collective-permute-start(bf16[512,4,128]{2,1,0:T(4,128)(2,1)S(1)} %collective-permute-done.4.refs_1_), channel_id=1, source_target_pairs={{0,32},{1,33},{2,34},{3,35},{4,36},{5,37},{6,38},{7,39},{8,40},{9,... | collective-permute-start | bytes 1572872 | tf_op jit(solution)/shard_map/ppermute | solution.py:47
  41.5 0.3 collective-permute-start.7
  41.8 0.2 collective-permute-start.8
  42.0 5.9 %near.1.refs_8_ = bf16[2048,512]{1,0:T(8,128)(2,1)S(1)} custom-call(s32[2048]{0:T(1024)S(1)} %get-tuple-element.37.near_index, bf16[512,512]{1,0:T(8,128)(2,1)S(1)} %bitcast.14, bf16[16,4,128]{2,1,0:T(4,128)(2,1)S(1)} %collective-permute-done.refs_0_, bf16[16,4,128]{2,1,0:T(4,128)(2,1)S(1)} %collective-permute-done.1.refs_1_, ...), custom_call_target="tpu_custom_call" | custom-call | flops 2000000000 | bytes 8000000 | tf_op jit(solution)/shard_map/near/pallas_call | solution.py:332
  47.9 1.9 %collective-permute-done.6.refs_2_ = bf16[512,4,128]{2,1,0:T(4,128)(2,1)S(1)} collective-permute-done((bf16[512,4,128]{2,1,0:T(4,128)(2,1)S(1)}, bf16[512,4,128]{2,1,0:T(4,128)(2,1)S(1)}, u32[]{:S(2)}, u32[]{:S(2)}) %collective-permute-start.6) | collective-permute-done | bytes 524320 | tf_op jit(solution)/shard_map/ppermute | solution.py:47
  49.8 3.1 %collective-permute-done.5.refs_3_ = bf16[512,4,128]{2,1,0:T(4,128)(2,1)S(1)} collective-permute-done((bf16[512,4,128]{2,1,0:T(4,128)(2,1)S(1)}, bf16[512,4,128]{2,1,0:T(4,128)(2,1)S(1)}, u32[]{:S(2)}, u32[]{:S(2)}) %collective-permute-start.5) | collective-permute-done | bytes 524320 | tf_op jit(solution)/shard_map/ppermute | solution.py:47
  52.9 0.8 %collective-permute-start.9 = (bf16[512,4,128]{2,1,0:T(4,128)(2,1)S(1)}, bf16[512,4,128]{2,1,0:T(4,128)(2,1)S(1)}, u32[]{:S(2)}, u32[]{:S(2)}) collective-permute-start(bf16[512,4,128]{2,1,0:T(4,128)(2,1)S(1)} %collective-permute-done.6.refs_2_), channel_id=1, source_target_pairs={{0,16},{1,17},{2,18},{3,19},{4,20},{5,21},{6,22},{7,23},{8,24},{9,... | collective-permute-start | bytes 1572872 | tf_op jit(solution)/shard_map/ppermute | solution.py:43
  53.7 0.0 collective-permute-start.10
  53.7 0.0 collective-permute-done.7.refs_4_
  53.7 0.0 collective-permute-done.8.refs_5_
  53.7 1.5 %collective-permute-done.9.refs_6_ = bf16[512,4,128]{2,1,0:T(4,128)(2,1)S(1)} collective-permute-done((bf16[512,4,128]{2,1,0:T(4,128)(2,1)S(1)}, bf16[512,4,128]{2,1,0:T(4,128)(2,1)S(1)}, u32[]{:S(2)}, u32[]{:S(2)}) %collective-permute-start.9) | collective-permute-done | bytes 524320 | tf_op jit(solution)/shard_map/ppermute | solution.py:43
  55.2 0.7 %collective-permute-done.10.refs_7_ = bf16[512,4,128]{2,1,0:T(4,128)(2,1)S(1)} collective-permute-done((bf16[512,4,128]{2,1,0:T(4,128)(2,1)S(1)}, bf16[512,4,128]{2,1,0:T(4,128)(2,1)S(1)}, u32[]{:S(2)}, u32[]{:S(2)}) %collective-permute-start.10) | collective-permute-done | bytes 524320 | tf_op jit(solution)/shard_map/ppermute | solution.py:43
  56.0 0.0 copy-done.4
  56.0 0.0 copy-done.6
  56.0 0.0 copy-done.7
  56.0 0.0 copy-done.8
  56.0 0.0 copy-done.9
  56.0 0.0 copy-done.10
  56.0 10.9 %late.1 = (bf16[2048,512]{1,0:T(8,128)(2,1)}, bf16[512,512]{1,0:T(8,128)(2,1)}) custom-call(s32[2048]{0:T(1024)S(1)} %bitcast.22, s32[4]{0:T(128)S(1)} %convert_reduce_fusion.far_count, s32[16]{0:T(128)S(1)} %copy-done.11, s32[16]{0:T(128)S(1)} %get-tuple-element.31.lives, bf16[512,4,128]{2,1,0:T(4,128)(2,1)S(1)} %bitcast.19, ...), custom_call_target="tpu_custom_call" | custom-call | flops 4000000000 | bytes 14000000 | tf_op jit(solution)/shard_map/late/pallas_call | solution.py:377
  (9 shorter events, 0.1 us)
Async XLA Ops:
  0.6 31.6 %copy-start.11 = (s32[16]{0:T(128)S(1)}, s32[16]{0:T(128)}, u32[]{:S(2)}) copy-start(s32[16]{0:T(128)} %tiles.2) | copy-start | bytes 196
  0.6 1.0 %copy-start = (bf16[16,32,512]{2,1,0:T(8,128)(2,1)S(1)}, bf16[16,32,512]{2,1,0:T(8,128)(2,1)}, u32[]{:S(2)}) copy-start(bf16[16,32,512]{2,1,0:T(8,128)(2,1)} %param.11) | copy-start | bytes 1572868
  1.7 30.6 %copy-start.1 = (bf16[16,32,512]{2,1,0:T(8,128)(2,1)S(1)}, bf16[16,32,512]{2,1,0:T(8,128)(2,1)}, u32[]{:S(2)}) copy-start(bf16[16,32,512]{2,1,0:T(8,128)(2,1)} %param.11) | copy-start | bytes 1572868
  1.7 30.6 %copy-start.2 = (s32[2048]{0:T(1024)S(1)}, s32[2048]{0:T(1024)}, u32[]{:S(2)}) copy-start(s32[2048]{0:T(1024)} %param.14) | copy-start | bytes 24580
  1.7 30.6 %copy-start.5 = (bf16[1536,512]{1,0:T(8,128)(2,1)S(1)}, bf16[1536,512]{1,0:T(8,128)(2,1)}, u32[]{:S(2)}) copy-start(bf16[1536,512]{1,0:T(8,128)(2,1)} %refs_11_.1) | copy-start | bytes 4718596
  2.7 29.5 %all-to-all-start = ((bf16[16,32,4,128]{3,2,1,0:T(4,128)(2,1)}), bf16[16,32,4,128]{3,2,1,0:T(4,128)(2,1)S(1)}, u32[]{:S(2)}, u32[]{:S(2)}) async-start(bf16[16,32,4,128]{3,2,1,0:T(4,128)(2,1)} %get-tuple-element.24), calls=%async_computation | async-start | bytes 1048576 | tf_op jit(solution)/shard_map/all_to_all | solution.py:501
  11.3 10.5 %collective-permute-start = (bf16[16,4,128]{2,1,0:T(4,128)(2,1)S(1)}, bf16[16,4,128]{2,1,0:T(4,128)(2,1)S(1)}, u32[]{:S(2)}, u32[]{:S(2)}) collective-permute-start(bf16[16,4,128]{2,1,0:T(4,128)(2,1)S(1)} %get-tuple-element.25), channel_id=1, source_target_pairs={{0,1},{1,2},{2,3},{3,4},{4,5},{5,6},{6,7},{7,8},{8,9},{9,10},{10,1... | collective-permute-start | bytes 49160 | tf_op jit(solution)/shard_map/ppermute | solution.py:499
  12.7 9.1 %collective-permute-start.1 = (bf16[16,4,128]{2,1,0:T(4,128)(2,1)S(1)}, bf16[16,4,128]{2,1,0:T(4,128)(2,1)S(1)}, u32[]{:S(2)}, u32[]{:S(2)}) collective-permute-start(bf16[16,4,128]{2,1,0:T(4,128)(2,1)S(1)} %get-tuple-element.27), channel_id=1, source_target_pairs={{1,0},{2,1},{3,2},{4,3},{5,4},{6,5},{7,6},{8,7},{9,8},{10,9},{11,1... | collective-permute-start | bytes 49160 | tf_op jit(solution)/shard_map/ppermute | solution.py:500
  21.9 7.2 %collective-permute-start.2 = (bf16[34,4,128]{2,1,0:T(4,128)(2,1)S(1)}, bf16[34,4,128]{2,1,0:T(4,128)(2,1)S(1)}, u32[]{:S(2)}, u32[]{:S(2)}) collective-permute-start(bf16[34,4,128]{2,1,0:T(4,128)(2,1)S(1)} %pad_maximum_fusion), channel_id=1, source_target_pairs={{0,16},{16,32},{32,48},{48,64},{64,80},{80,96},{96,112},{1,17},{17... | collective-permute-start | bytes 104456 | tf_op jit(solution)/shard_map/ppermute | solution.py:503
  27.0 5.3 %collective-permute-start.3 = (bf16[34,4,128]{2,1,0:T(4,128)(2,1)S(1)}, bf16[34,4,128]{2,1,0:T(4,128)(2,1)S(1)}, u32[]{:S(2)}, u32[]{:S(2)}) collective-permute-start(bf16[34,4,128]{2,1,0:T(4,128)(2,1)S(1)} %pad_maximum_fusion.1), channel_id=1, source_target_pairs={{16,0},{32,16},{48,32},{64,48},{80,64},{96,80},{112,96},{17,1},{33... | collective-permute-start | bytes 104456 | tf_op jit(solution)/shard_map/ppermute | solution.py:504
  32.3 8.3 %collective-permute-start.4 = (bf16[512,4,128]{2,1,0:T(4,128)(2,1)S(1)}, bf16[512,4,128]{2,1,0:T(4,128)(2,1)S(1)}, u32[]{:S(2)}, u32[]{:S(2)}) collective-permute-start(bf16[512,4,128]{2,1,0:T(4,128)(2,1)S(1)} %bitcast.16), channel_id=1, source_target_pairs={{0,32},{1,33},{2,34},{3,35},{4,36},{5,37},{6,38},{7,39},{8,40},{9,... | collective-permute-start | bytes 1572872 | tf_op jit(solution)/shard_map/ppermute | solution.py:47
  32.3 1.6 %copy-start.3 = (bf16[2048,512]{1,0:T(8,128)(2,1)S(1)}, bf16[2048,512]{1,0:T(8,128)(2,1)}, u32[]{:S(2)}) copy-start(bf16[2048,512]{1,0:T(8,128)(2,1)} %refs_9_.1) | copy-start | bytes 6291460
  37.9 18.0 %copy-start.4 = (bf16[2048,512]{1,0:T(8,128)(2,1)S(1)}, bf16[2048,512]{1,0:T(8,128)(2,1)}, u32[]{:S(2)}) copy-start(bf16[2048,512]{1,0:T(8,128)(2,1)} %refs_9_.1) | copy-start | bytes 6291460
  38.0 18.0 %copy-start.6 = (bf16[1024,512]{1,0:T(8,128)(2,1)S(1)}, bf16[1024,512]{1,0:T(8,128)(2,1)}, u32[]{:S(2)}) copy-start(bf16[1024,512]{1,0:T(8,128)(2,1)} %refs_13_.1) | copy-start | bytes 3145732
  38.0 18.0 %copy-start.7 = (bf16[512,512]{1,0:T(8,128)(2,1)S(1)}, bf16[512,512]{1,0:T(8,128)(2,1)}, u32[]{:S(2)}) copy-start(bf16[512,512]{1,0:T(8,128)(2,1)} %refs_12_.1) | copy-start | bytes 1572868
  38.0 18.0 %copy-start.8 = (bf16[512,512]{1,0:T(8,128)(2,1)S(1)}, bf16[512,512]{1,0:T(8,128)(2,1)}, u32[]{:S(2)}) copy-start(bf16[512,512]{1,0:T(8,128)(2,1)} %refs_14_.1) | copy-start | bytes 1572868
  38.0 18.0 %copy-start.9 = (f32[512]{0:T(512)S(1)}, f32[512]{0:T(512)}, u32[]{:S(2)}) copy-start(f32[512]{0:T(512)} %param.18) | copy-start | bytes 6148
  38.0 18.0 %copy-start.10 = (f32[512]{0:T(512)S(1)}, f32[512]{0:T(512)}, u32[]{:S(2)}) copy-start(f32[512]{0:T(512)} %param.21) | copy-start | bytes 6148
  38.0 11.8 %collective-permute-start.6 = (bf16[512,4,128]{2,1,0:T(4,128)(2,1)S(1)}, bf16[512,4,128]{2,1,0:T(4,128)(2,1)S(1)}, u32[]{:S(2)}, u32[]{:S(2)}) collective-permute-start(bf16[512,4,128]{2,1,0:T(4,128)(2,1)S(1)} %bitcast.17), channel_id=1, source_target_pairs={{0,96},{1,97},{2,98},{3,99},{4,100},{5,101},{6,102},{7,103},{8,104... | collective-permute-start | bytes 1572872 | tf_op jit(solution)/shard_map/ppermute | solution.py:47
  40.6 12.3 %collective-permute-start.5 = (bf16[512,4,128]{2,1,0:T(4,128)(2,1)S(1)}, bf16[512,4,128]{2,1,0:T(4,128)(2,1)S(1)}, u32[]{:S(2)}, u32[]{:S(2)}) collective-permute-start(bf16[512,4,128]{2,1,0:T(4,128)(2,1)S(1)} %collective-permute-done.4.refs_1_), channel_id=1, source_target_pairs={{0,32},{1,33},{2,34},{3,35},{4,36},{5,37},{6,38},{7,39},{8,40},{9,... | collective-permute-start | bytes 1572872 | tf_op jit(solution)/shard_map/ppermute | solution.py:47
  41.5 12.2 %collective-permute-start.7 = (bf16[512,4,128]{2,1,0:T(4,128)(2,1)S(1)}, bf16[512,4,128]{2,1,0:T(4,128)(2,1)S(1)}, u32[]{:S(2)}, u32[]{:S(2)}) collective-permute-start(bf16[512,4,128]{2,1,0:T(4,128)(2,1)S(1)} %bitcast.18), channel_id=1, source_target_pairs={{0,16},{1,17},{2,18},{3,19},{4,20},{5,21},{6,22},{7,23},{8,24},{9,... | collective-permute-start | bytes 1572872 | tf_op jit(solution)/shard_map/ppermute | solution.py:43
  41.8 11.8 %collective-permute-start.8 = (bf16[512,4,128]{2,1,0:T(4,128)(2,1)S(1)}, bf16[512,4,128]{2,1,0:T(4,128)(2,1)S(1)}, u32[]{:S(2)}, u32[]{:S(2)}) collective-permute-start(bf16[512,4,128]{2,1,0:T(4,128)(2,1)S(1)} %collective-permute-done.4.refs_1_), channel_id=1, source_target_pairs={{0,16},{1,17},{2,18},{3,19},{4,20},{5,21},{6,22},{7,23},{8,24},{9,... | collective-permute-start | bytes 1572872 | tf_op jit(solution)/shard_map/ppermute | solution.py:43
  52.9 2.4 %collective-permute-start.9 = (bf16[512,4,128]{2,1,0:T(4,128)(2,1)S(1)}, bf16[512,4,128]{2,1,0:T(4,128)(2,1)S(1)}, u32[]{:S(2)}, u32[]{:S(2)}) collective-permute-start(bf16[512,4,128]{2,1,0:T(4,128)(2,1)S(1)} %collective-permute-done.6.refs_2_), channel_id=1, source_target_pairs={{0,16},{1,17},{2,18},{3,19},{4,20},{5,21},{6,22},{7,23},{8,24},{9,... | collective-permute-start | bytes 1572872 | tf_op jit(solution)/shard_map/ppermute | solution.py:43
  53.7 2.3 %collective-permute-start.10 = (bf16[512,4,128]{2,1,0:T(4,128)(2,1)S(1)}, bf16[512,4,128]{2,1,0:T(4,128)(2,1)S(1)}, u32[]{:S(2)}, u32[]{:S(2)}) collective-permute-start(bf16[512,4,128]{2,1,0:T(4,128)(2,1)S(1)} %collective-permute-done.5.refs_3_), channel_id=1, source_target_pairs={{0,16},{1,17},{2,18},{3,19},{4,20},{5,21},{6,22},{7,23},{8,24},{9,... | collective-permute-start | bytes 1572872 | tf_op jit(solution)/shard_map/ppermute | solution.py:43

commit v8 on v7

--- a/solution.py
+++ b/solution.py
@@ -99,8 +99,10 @@
     return copies
 
 
-def coarse_kernel(node_ref, out_hbm, west_ref, east_ref, top_ref, bottom_ref, wide, tall, block, sem):
-    nodes, sides, cols = node_ref.shape[0], west_ref.shape[0], top_ref.shape[0]
+def coarse_kernel(odd, node_ref, out_hbm, *refs):
+    col_refs, row_refs = refs[0:2], refs[2:4]
+    wide, tall, block, sem = refs[4:]
+    nodes, sides, cols = node_ref.shape[0], col_refs[0].shape[0], row_refs[0].shape[0]
     per = block.shape[0]
     run = cols // 4
     starts = []
@@ -122,17 +124,19 @@
         take(starts[2], sides, j, cols - 1, cols)
         take(starts[3], cols, j, 0, 1)
         take(starts[4], cols, j, nodes - cols, 1)
-    outs = (block, west_ref, east_ref, top_ref, bottom_ref)
-    for start, out in zip(starts, outs):
-        for i in range(out.shape[0]):
-            out[i] = tall[(start + i) * 4 : (start + i) * 4 + 4, :].astype(BF)
-        if out is block:
-            stores = [
-                pltpu.make_async_copy(block, out_hbm.at[d], sem.at[d])
-                for d in range(out_hbm.shape[0])
-            ]
-            for store in stores:
-                store.start()
+    row = lambda k, i: tall[(starts[k] + i) * 4 : (starts[k] + i) * 4 + 4, :]
+    for i in range(per):
+        block[i] = row(0, i).astype(BF)
+    stores = [
+        pltpu.make_async_copy(block, out_hbm.at[d], sem.at[d]) for d in range(out_hbm.shape[0])
+    ]
+    for store in stores:
+        store.start()
+    for refs_of, low, high, is_odd in ((col_refs, 1, 2, odd[1] == 1), (row_refs, 3, 4, odd[0] == 1)):
+        for i in range(refs_of[0].shape[0]):
+            first, last = row(low, i), row(high, i)
+            refs_of[0][i] = jnp.where(is_odd, first, last).astype(BF)
+            refs_of[1][i] = jnp.where(is_odd, last, first).astype(BF)
     for store in stores:
         store.wait()
 
@@ -188,13 +192,13 @@
 def late_kernel(far_list, far_count, tiles, lives, *refs):
     pieces = refs[:FAR]
     (
-        pre_hbm,
-        edge_hbm,
-        node_hbm,
-        w1_hbm,
-        w2_hbm,
-        wn_hbm,
-        wn2_hbm,
+        pre,
+        edge,
+        node,
+        w1,
+        w2,
+        wn,
+        wn2,
         recv_ref,
         eg_ref,
         ng_ref,
@@ -202,47 +206,17 @@
         node_out_ref,
         table,
         sent,
-        pre,
-        edge,
         out,
         agg,
-        node,
-        ws,
-        w2,
-        wn,
-        wn2,
         sem,
-        in_sem,
         out_sem,
     ) = refs[FAR:]
     steps = recv_ref.shape[0] // GROUP
-    rows_of = lambda g: pl.ds(g * ROWS, ROWS)
     copies = load_table(pieces, table, sem)
-    first = [
-        pltpu.make_async_copy(w1_hbm.at[pl.ds(F, F)], ws, in_sem.at[0]),
-        pltpu.make_async_copy(w2_hbm, w2, in_sem.at[1]),
-    ]
-    parts = []
-    for g in range(steps):
-        parts.append(
-            [
-                pltpu.make_async_copy(pre_hbm.at[rows_of(g)], pre.at[rows_of(g)], in_sem.at[6 + 2 * g]),
-                pltpu.make_async_copy(edge_hbm.at[rows_of(g)], edge.at[rows_of(g)], in_sem.at[7 + 2 * g]),
-            ]
-        )
-    last = [
-        pltpu.make_async_copy(node_hbm, node, in_sem.at[3]),
-        pltpu.make_async_copy(wn_hbm, wn, in_sem.at[4]),
-        pltpu.make_async_copy(wn2_hbm, wn2, in_sem.at[5]),
-    ]
-    for copy in first:
-        copy.start()
     sent[...] = jnp.zeros_like(sent)
     agg[...] = jnp.zeros_like(agg)
     for copy in copies:
         copy.wait()
-    for copy in sum(parts, []) + last:
-        copy.start()
 
     for g in range(steps):
 
@@ -251,15 +225,12 @@
             return packed & 4095, packed >> 12
 
         fetch((far_count[g] + 15) >> 4, 16, entry, table, sent)
-    for copy in first:
-        copy.wait()
     place = lax.broadcasted_iota(jnp.int32, (BLK, F), 0)
     stores = []
     for g in range(steps):
-        for copy in parts[g]:
-            copy.wait()
         base = g * ROWS
-        total = pre[rows_of(g), :].astype(F32) + dot(sent_rows(sent, base), ws[...])
+        rows = pl.ds(base, ROWS)
+        total = pre[rows, :].astype(F32) + dot(sent_rows(sent, base), w1[F : 2 * F, :])
         message = normed(dot(silu(total).astype(BF), w2[...]), eg_ref[...]).astype(BF)
         for k in range(GROUP):
             b = g * GROUP + k
@@ -271,11 +242,9 @@
             ).astype(BF)
             tile = pl.multiple_of(tiles[b] * BLK, BLK)
             agg[pl.ds(tile, BLK), :] += dot(chosen(recv_ref[b : b + 1, :]), part)
-        store = pltpu.make_async_copy(out.at[rows_of(g)], out_hbm.at[rows_of(g)], out_sem.at[g])
+        store = pltpu.make_async_copy(out.at[rows], out_hbm.at[rows], out_sem.at[g])
         store.start()
         stores.append(store)
-    for copy in last:
-        copy.wait()
     first_sum = dot(node[...], wn[:F, :]) + dot(agg[...].astype(BF), wn[F:, :])
     second = dot(silu(first_sum).astype(BF), wn2[...])
     node_out_ref[...] = (node[...].astype(F32) + normed(second, ng_ref[...])).astype(BF)
@@ -373,26 +342,17 @@
     anywhere = pl.BlockSpec(memory_space=pl.ANY)
     local = pl.BlockSpec(memory_space=pltpu.VMEM)
     scalars = pl.BlockSpec(memory_space=pltpu.SMEM)
-    square = pltpu.VMEM((F, F), BF)
     return pl.pallas_call(
         late_kernel,
         name="late",
-        in_specs=[scalars] * 4 + [anywhere] * (FAR + 7) + [local] * 3,
+        in_specs=[scalars] * 4 + [anywhere] * FAR + [local] * 10,
         out_specs=[anywhere, local],
         scratch_shapes=[
             pltpu.VMEM((far_rows, 4, 128), BF),
             pltpu.VMEM((slots * 4 + 32, 128), F32),
             pltpu.VMEM((slots, F), BF),
-            pltpu.VMEM((slots, F), BF),
-            pltpu.VMEM((slots, F), BF),
             pltpu.VMEM((nodes, F), F32),
-            pltpu.VMEM((nodes, F), BF),
-            square,
-            square,
-            pltpu.VMEM((2 * F, F), BF),
-            square,
             pltpu.SemaphoreType.DMA((FAR,)),
-            pltpu.SemaphoreType.DMA((6 + 2 * steps,)),
             pltpu.SemaphoreType.DMA((steps,)),
         ],
         out_shape=[
@@ -446,17 +406,17 @@
     own_rows = node_latent.reshape(nodes, features)
     lanes = lambda a: a.reshape(-1, 4, 128)
 
-    right = [(i, (i + 1) % lon_count) for i in range(lon_count)]
-    left = [(j, i) for i, j in right]
-    up = [(i, i + 1) for i in range(lat_count - 1)]
-    down = [(j, i) for i, j in up]
-
+    def pairs(first, count, wrap):
+        couples = [(i, (i + 1) % count) for i in range(first, count if wrap else count - 1, 2)]
+        return couples + [(j, i) for i, j in couples]
+
+    lat_odd, lon_odd = lat_index % 2, lon_index % 2
     per = patch_rows // 4 * (patch_cols // 4)
     lane_rows = lambda rows: jax.ShapeDtypeStruct((rows, 4, 128), BF)
-    copies, first_col, last_col, top, bottom = pl.pallas_call(
+    copies, col_a, col_b, row_a, row_b = pl.pallas_call(
         coarse_kernel,
         name="coarse",
-        in_specs=[pl.BlockSpec(memory_space=pltpu.VMEM)],
+        in_specs=[pl.BlockSpec(memory_space=pltpu.SMEM), pl.BlockSpec(memory_space=pltpu.VMEM)],
         out_specs=[pl.BlockSpec(memory_space=pl.ANY)] + [pl.BlockSpec(memory_space=pltpu.VMEM)] * 4,
         scratch_shapes=[
             pltpu.VMEM((nodes * 4, 128), F32),
@@ -472,19 +432,18 @@
             lane_rows(patch_cols),
         ],
         compiler_params=pltpu.CompilerParams(vmem_limit_bytes=VMEM),
-    )(own_rows)
+    )(jnp.stack([lat_odd, lon_odd]).astype(jnp.int32), own_rows)
     senders = jnp.maximum(sender, 0)
     send_row = senders // grid_cols
     send_col = senders % grid_cols
     row = send_row - lat_index * patch_rows
     col = (send_col - lon_index * patch_cols + 1) % grid_cols - 1
     is_near = (row >= -1) & (row <= patch_rows) & (col <= patch_cols)
-    side = jnp.where(col < 0, nodes + row, nodes + patch_rows + row)
+    side = nodes + row + patch_rows * jnp.where(col < 0, 1 - lon_odd, lon_odd)
     inner = jnp.where((col < 0) | (col >= patch_cols), side, row * patch_cols + col)
     rim, span = nodes + 2 * patch_rows, patch_cols + 2
-    near_index = jnp.where(
-        row < 0, rim + col + 1, jnp.where(row >= patch_rows, rim + span + col + 1, inner)
-    )
+    strip = rim + col + 1 + span * jnp.where(row < 0, 1 - lat_odd, lat_odd)
+    near_index = jnp.where((row < 0) | (row >= patch_rows), strip, inner)
     near_index = jnp.where(is_near, near_index, rim + 2 * span)
     src_lat, src_lon = send_row // patch_rows, send_col // patch_cols
     src_core, core = src_lat % 2, lat_index % 2
@@ -496,14 +455,21 @@
     recv_rows = receiver.reshape(steps, GROUP, BLK)
     lives = jnp.sum((receiver >= 0).astype(jnp.int32).reshape(blocks, BLK), 1)
 
-    west = lax.ppermute(last_col, "lon", right)
-    east = lax.ppermute(first_col, "lon", left)
+    side_a = lax.ppermute(col_a, "lon", pairs(0, lon_count, True))
+    side_b = lax.ppermute(col_b, "lon", pairs(1, lon_count, True))
     plane = lanes(lax.all_to_all(copies, "lon", split_axis=0, concat_axis=0, tiled=True))
-    wide = lambda r, rows: jnp.concatenate([west[r : r + 1], rows, east[r : r + 1]], 0)
-    north = lax.ppermute(wide(patch_rows - 1, bottom), "lat", up)
-    south = lax.ppermute(wide(0, top), "lat", down)
-    plane, north, south, tiles, near_index, far_list, far_count, lives = lax.optimization_barrier(
-        (plane, north, south, block_tile, near_index, far_list, far_count, lives)
+    west = jnp.where(lon_odd == 1, side_a, side_b)
+    east = jnp.where(lon_odd == 1, side_b, side_a)
+    wide = lambda r, rows: jnp.concatenate(
+        [lax.dynamic_slice_in_dim(west, r, 1), rows, lax.dynamic_slice_in_dim(east, r, 1)], 0
+    )
+    edge_row = (1 - lat_odd) * (patch_rows - 1)
+    strip_a = lax.ppermute(wide(edge_row, row_a), "lat", pairs(0, lat_count, False))
+    strip_b = lax.ppermute(
+        wide(patch_rows - 1 - edge_row, row_b), "lat", pairs(1, lat_count, False)
+    )
+    plane, strip_a, strip_b, tiles, near_index, far_list, far_count, lives = lax.optimization_barrier(
+        (plane, strip_a, strip_b, block_tile, near_index, far_list, far_count, lives)
     )
 
     ahead = move(plane, "x", (1, -1))
@@ -513,7 +479,7 @@
     behind = move(later, "x", (-1, 1))
     ahead, partial = lax.optimization_barrier((ahead, partial))
     across = move(ahead, "x", (1, -1))
-    rims = [west, east, north, south]
+    rims = [side_a, side_b, strip_a, strip_b]
     pre = near_call(near_index, own_rows, rims, partial, w_first)
     across, behind, pre = lax.optimization_barrier((across, behind, pre))
     far_pieces = [plane, ahead, behind, across, plane_other]

time: 67.5 us -> 64.7 us (0.959)
  waiting for transfers between devices: 13 us -> 11.3 us
  starting transfers between devices: 24.2 us -> 23.5 us
    ppermute x4, waiting for transfers between devices: 4.72 us -> 3.19 us  [the longest x1 2.09 us: per_device(): lax.ppermute(wide(patch_rows - 1 - edge_row, row_b), 'lat', pairs(1, lat_...]
    ppermute x4, starting transfers between devices: 11.9 us -> 10.5 us  [the longest x1 3.9 us: per_device(): side_b = lax.ppermute(col_b, 'lon', pairs(1, lon_count, True))]
    pallas_call x1, Pallas kernels: 10.9 us -> 10.1 us  [late_call(): pl.pallas_call(late_kernel, name='late', in_specs=[scalars] * 4 + [anywhe...]
  transfers between devices with their start and end apart: 12 -> 12, of which waited for: 7 -> 7; matrix products, arithmetic and copies ran while one was open for 6% -> 7% of each run, Pallas kernels for 15% -> 15%
where the time goes in v8:
time: 64.7 us; the launch traced here: 64.3 us
  starting transfers between devices  23.5 us (36%)
  Pallas kernels  21.5 us (33%)
  waiting for transfers between devices  11.3 us (17%)
  other arithmetic  4.29 us (7%)
  local copies, waits for them, and re-layouts  2.72 us (4%)
  between operations  1.08 us (2%)
    pallas_call x1, Pallas kernels, late_call(): pl.pallas_call(late_kernel, name='late', in_specs=[scalars] * 4 + [anywhe...  10.1 us
    all_to_all x1, starting transfers between devices, per_device(): lax.all_to_all(copies, 'lon', split_axis=0, concat_axis=0, tiled=True)  8.61 us
    ppermute x3, waiting for transfers between devices, move(): return lax.ppermute(value, ('lat', 'lon'), shift(axis, by_core))  5.92 us
    pallas_call x1, Pallas kernels, near_call(): pl.pallas_call(near_kernel, name='near', grid_spec=pltpu.PrefetchScalarGr...  5.87 us
    pallas_call x1, Pallas kernels, early_call(): pl.pallas_call(early_kernel, name='early', grid_spec=pltpu.PrefetchScalar...  4.03 us
    ppermute x1, starting transfers between devices, per_device(): side_b = lax.ppermute(col_b, 'lon', pairs(1, lon_count, True))  3.9 us
    ppermute x1, starting transfers between devices, per_device(): lax.ppermute(wide(patch_rows - 1 - edge_row, row_b), 'lat', pairs(1, lat_...  3.02 us
    unnamed x25, local copies, waits for them, and re-layouts  2.69 us
  transfers between devices with their start and end apart: 12, of which 7 were waited for; matrix products, arithmetic and copies ran while one was open for 7% of the time, Pallas kernels for 15%

profile of v8, /device:TPU:1, one launch (start us, length us, event | category | flops | bytes accessed | tf_op | source)
XLA Modules:
  0.0 64.3 jit_solution(15977227268806584351)
XLA Ops:
  0.6 0.0 copy-start.2
  0.6 0.0 copy-start.11
  0.7 0.1 pad_add_fusion.odd
  0.7 0.0 copy-start
  0.8 1.0 %copy-done = bf16[16,32,512]{2,1,0:T(8,128)(2,1)S(1)} copy-done((bf16[16,32,512]{2,1,0:T(8,128)(2,1)S(1)}, bf16[16,32,512]{2,1,0:T(8,128)(2,1)}, u32[]{:S(2)}) %copy-start) | copy-done | bytes 524312
  1.8 0.0 copy-start.1
  1.8 0.0 copy-start.5
  1.8 1.6 %coarse.1 = (bf16[16,32,4,128]{3,2,1,0:T(4,128)(2,1)}, bf16[16,4,128]{2,1,0:T(4,128)(2,1)S(1)}, bf16[16,4,128]{2,1,0:T(4,128)(2,1)S(1)}, bf16[32,4,128]{2,1,0:T(4,128)(2,1)S(1)}, bf16[32,4,128]{2,1,0:T(4,128)(2,1)S(1)}) custom-call(s32[2]{0:T(128)S(1)} %pad_add_fusion.odd, bf16[512,512]{1,0:T(8,128)(2,1)S(1)} %bitcast.18), custom_call_target="tpu_custom_call" | custom-call | tf_op jit(solution)/shard_map/coarse/pallas_call | solution.py:416
  3.4 8.6 %all-to-all-start = ((bf16[16,32,4,128]{3,2,1,0:T(4,128)(2,1)}), bf16[16,32,4,128]{3,2,1,0:T(4,128)(2,1)S(1)}, u32[]{:S(2)}, u32[]{:S(2)}) async-start(bf16[16,32,4,128]{3,2,1,0:T(4,128)(2,1)} %get-tuple-element.24), calls=%async_computation | async-start | bytes 1048576 | tf_op jit(solution)/shard_map/all_to_all | solution.py:460
  12.0 1.4 %collective-permute-start = (bf16[16,4,128]{2,1,0:T(4,128)(2,1)S(1)}, bf16[16,4,128]{2,1,0:T(4,128)(2,1)S(1)}, u32[]{:S(2)}, u32[]{:S(2)}) collective-permute-start(bf16[16,4,128]{2,1,0:T(4,128)(2,1)S(1)} %get-tuple-element.25), channel_id=1, source_target_pairs={{0,1},{2,3},{4,5},{6,7},{8,9},{10,11},{12,13},{14,15},{1,0},{3,2},... | collective-permute-start | bytes 49160 | tf_op jit(solution)/shard_map/ppermute | solution.py:458
  13.3 3.9 %collective-permute-start.1 = (bf16[16,4,128]{2,1,0:T(4,128)(2,1)S(1)}, bf16[16,4,128]{2,1,0:T(4,128)(2,1)S(1)}, u32[]{:S(2)}, u32[]{:S(2)}) collective-permute-start(bf16[16,4,128]{2,1,0:T(4,128)(2,1)S(1)} %get-tuple-element.26), channel_id=1, source_target_pairs={{1,2},{3,4},{5,6},{7,8},{9,10},{11,12},{13,14},{15,0},{2,1},{4,3},... | collective-permute-start | bytes 49160 | tf_op jit(solution)/shard_map/ppermute | solution.py:459
  17.3 0.1 iota_compare_fusion.1
  17.3 0.8 %bitcast_reduce_fusion = (s32[16]{0:T(128)S(1)}, pred[2048]{0:T(1024)(128)(4,1)S(1)}) fusion(s32[2048]{0:T(1024)} %param.14), kind=kLoop, calls=%fused_computation.53 | loop fusion | flops 6128 | bytes 10304 | tf_op jit(solution)/shard_map/reduce_sum | solution.py:456
  18.2 0.7 %not_and_fusion = (pred[2048]{0:T(1024)(128)(4,1)S(1)}, pred[2048]{0:T(1024)(128)(4,1)S(1)}) fusion(pred[2048]{0:T(1024)(128)(4,1)S(1)} %get-tuple-element.47, s32[]{:T(128)S(6)} %mul.45, s32[]{:T(128)S(6)} %mul.44, s32[2048]{0:T(1024)} %param.13), kind=kLoop, calls=%fused_computation.70 | loop fusion | flops 71680 | bytes 14344 | tf_op jit(solution)/shard_map/and | solution.py:454
  18.9 0.8 %fusion.9 = (s32[2048]{0:T(1024)S(1)}, s32[2048]{0:T(1024)S(1)}) fusion(s32[2048]{0:T(1024)} %param.13, s32[]{:T(128)S(6)} %select_n.142, s32[]{:T(128)} %select_n.122, pred[2048]{0:T(1024)(128)(4,1)S(1)} %get-tuple-element.49, s32[]{:T(128)} %select_n.123, s32[]{:T(128)S(6)} %sub.73, s32[]{:T(128)S(6)} %sub.65, s32[]{:T(128)S(6)} %mul.45, s32[]{:T(128)S(6)} %mul.44), kind=kLoop, calls=%fused_computation.48 | loop fusion | flops 342016 | bytes 26652 | tf_op jit(solution)/shard_map/sub | solution.py:262
  19.7 0.6 %select_reduce_fusion.1 = s32[4,512]{1,0:T(4,128)S(1)} fusion(s32[4,512]{1,0:T(4,128)S(1)} %convert_element_type.8, pred[512,512]{1,0:T(8,128)(4,1)S(1)} %iota_compare_fusion.1), kind=kLoop, calls=%fused_computation.2 | loop fusion | flops 2095104 | bytes 278528 | tf_op jit(solution)/shard_map/reduce_sum | solution.py:261
  20.3 1.0 %select_reduce_fusion = s32[4,512]{1,0:T(4,128)S(1)} fusion(s32[4,512]{1,0:T(4,128)S(1)} %broadcast_in_dim.73, s32[4,512]{1,0:T(4,128)S(1)} %select_reduce_fusion.1, pred[4,512]{1,0:T(4,128)(4,1)S(1)} %reshape.60), kind=kLoop, calls=%fused_computation | loop fusion | flops 4192256 | bytes 26624 | tf_op jit(solution)/shard_map/reduce_sum | solution.py:264
  21.4 0.0 collective-permute-done.refs_0_
  21.4 1.1 %collective-permute-done.1.refs_1_ = bf16[16,4,128]{2,1,0:T(4,128)(2,1)S(1)} collective-permute-done((bf16[16,4,128]{2,1,0:T(4,128)(2,1)S(1)}, bf16[16,4,128]{2,1,0:T(4,128)(2,1)S(1)}, u32[]{:S(2)}, u32[]{:S(2)}) %collective-permute-start.1) | collective-permute-done | bytes 16416 | tf_op jit(solution)/shard_map/ppermute | solution.py:459
  22.5 2.2 %collective-permute-start.2 = (bf16[34,4,128]{2,1,0:T(4,128)(2,1)S(1)}, bf16[34,4,128]{2,1,0:T(4,128)(2,1)S(1)}, u32[]{:S(2)}, u32[]{:S(2)}) collective-permute-start(bf16[34,4,128]{2,1,0:T(4,128)(2,1)S(1)} %pad_maximum_fusion), channel_id=1, source_target_pairs={{0,16},{32,48},{64,80},{96,112},{16,0},{48,32},{80,64},{112,96},{1... | collective-permute-start | bytes 104456 | tf_op jit(solution)/shard_map/ppermute | solution.py:467
  24.7 3.0 %collective-permute-start.3 = (bf16[34,4,128]{2,1,0:T(4,128)(2,1)S(1)}, bf16[34,4,128]{2,1,0:T(4,128)(2,1)S(1)}, u32[]{:S(2)}, u32[]{:S(2)}) collective-permute-start(bf16[34,4,128]{2,1,0:T(4,128)(2,1)S(1)} %pad_maximum_fusion.1), channel_id=1, source_target_pairs={{16,32},{48,64},{80,96},{32,16},{64,48},{96,80},{17,33},{49,65},{8... | collective-permute-start | bytes 104456 | tf_op jit(solution)/shard_map/ppermute | solution.py:468
  27.7 0.1 convert_reduce_fusion.far_count
  27.9 0.0 collective-permute-done.2.refs_2_
  27.9 2.1 %collective-permute-done.3.refs_3_ = bf16[34,4,128]{2,1,0:T(4,128)(2,1)S(1)} collective-permute-done((bf16[34,4,128]{2,1,0:T(4,128)(2,1)S(1)}, bf16[34,4,128]{2,1,0:T(4,128)(2,1)S(1)}, u32[]{:S(2)}, u32[]{:S(2)}) %collective-permute-start.3) | collective-permute-done | bytes 34848 | tf_op jit(solution)/shard_map/ppermute | solution.py:468
  30.0 0.0 all-to-all-done
  30.0 0.0 collective-permute-start.4
  30.0 0.0 copy-done.2
  30.0 0.0 copy-done.11
  30.0 0.0 copy-done.1
  30.0 0.0 copy-done.5
  30.0 0.0 copy-start.3
  30.0 1.6 %copy-done.3 = bf16[2048,512]{1,0:T(8,128)(2,1)S(1)} copy-done((bf16[2048,512]{1,0:T(8,128)(2,1)S(1)}, bf16[2048,512]{1,0:T(8,128)(2,1)}, u32[]{:S(2)}) %copy-start.3) | copy-done | bytes 2097176
  31.6 4.0 %early.1.refs_4_ = bf16[2048,512]{1,0:T(8,128)(2,1)S(1)} custom-call(s32[16]{0:T(128)S(1)} %copy-done.11, bf16[2048,512]{1,0:T(8,128)(2,1)S(1)} %copy-done.3, s32[4,4,128]{2,1,0:T(4,128)S(1)} %bitcast.28, bf16[512,512]{1,0:T(8,128)(2,1)S(1)} %bitcast.19, bf16[1536,512]{1,0:T(8,128)(2,1)S(1)} %copy-done.5, bf16[1536,512]{1,0:T(8,128)(2,1)S(1)} %copy-done.5), custom_call_target="tpu_custom_call" | custom-call | flops 3000000000 | bytes 10000000 | tf_op jit(solution)/shard_map/early/pallas_call | solution.py:279
  35.6 0.0 copy-start.4
  35.7 0.0 copy-start.6
  35.7 0.0 copy-start.7
  35.7 0.0 copy-start.8
  35.7 0.0 copy-start.9
  35.7 0.0 copy-start.10
  35.7 1.5 %collective-permute-start.6 = (bf16[512,4,128]{2,1,0:T(4,128)(2,1)S(1)}, bf16[512,4,128]{2,1,0:T(4,128)(2,1)S(1)}, u32[]{:S(2)}, u32[]{:S(2)}) collective-permute-start(bf16[512,4,128]{2,1,0:T(4,128)(2,1)S(1)} %bitcast.23), channel_id=1, source_target_pairs={{0,96},{1,97},{2,98},{3,99},{4,100},{5,101},{6,102},{7,103},{8,104... | collective-permute-start | bytes 1572872 | tf_op jit(solution)/shard_map/ppermute | solution.py:47
  37.2 1.1 %collective-permute-done.4.refs_1_ = bf16[512,4,128]{2,1,0:T(4,128)(2,1)S(1)} collective-permute-done((bf16[512,4,128]{2,1,0:T(4,128)(2,1)S(1)}, bf16[512,4,128]{2,1,0:T(4,128)(2,1)S(1)}, u32[]{:S(2)}, u32[]{:S(2)}) %collective-permute-start.4) | collective-permute-done | bytes 524320 | tf_op jit(solution)/shard_map/ppermute | solution.py:47
  38.3 0.9 %collective-permute-start.5 = (bf16[512,4,128]{2,1,0:T(4,128)(2,1)S(1)}, bf16[512,4,128]{2,1,0:T(4,128)(2,1)S(1)}, u32[]{:S(2)}, u32[]{:S(2)}) collective-permute-start(bf16[512,4,128]{2,1,0:T(4,128)(2,1)S(1)} %collective-permute-done.4.refs_1_), channel_id=1, source_target_pairs={{0,32},{1,33},{2,34},{3,35},{4,36},{5,37},{6,38},{7,39},{8,40},{9,... | collective-permute-start | bytes 1572872 | tf_op jit(solution)/shard_map/ppermute | solution.py:47
  39.2 1.4 %collective-permute-start.7 = (bf16[512,4,128]{2,1,0:T(4,128)(2,1)S(1)}, bf16[512,4,128]{2,1,0:T(4,128)(2,1)S(1)}, u32[]{:S(2)}, u32[]{:S(2)}) collective-permute-start(bf16[512,4,128]{2,1,0:T(4,128)(2,1)S(1)} %bitcast.24), channel_id=1, source_target_pairs={{0,16},{1,17},{2,18},{3,19},{4,20},{5,21},{6,22},{7,23},{8,24},{9,... | collective-permute-start | bytes 1572872 | tf_op jit(solution)/shard_map/ppermute | solution.py:43
  40.7 0.0 collective-permute-start.8
  40.7 5.9 %near.1.refs_8_ = bf16[2048,512]{1,0:T(8,128)(2,1)S(1)} custom-call(s32[2048]{0:T(1024)S(1)} %get-tuple-element.37.near_index, bf16[512,512]{1,0:T(8,128)(2,1)S(1)} %bitcast.20, bf16[16,4,128]{2,1,0:T(4,128)(2,1)S(1)} %collective-permute-done.refs_0_, bf16[16,4,128]{2,1,0:T(4,128)(2,1)S(1)} %collective-permute-done.1.refs_1_, ...), custom_call_target="tpu_custom_call" | custom-call | flops 2000000000 | bytes 8000000 | tf_op jit(solution)/shard_map/near/pallas_call | solution.py:301
  46.5 0.4 collective-permute-done.6.refs_2_
  46.9 4.4 %collective-permute-done.5.refs_3_ = bf16[512,4,128]{2,1,0:T(4,128)(2,1)S(1)} collective-permute-done((bf16[512,4,128]{2,1,0:T(4,128)(2,1)S(1)}, bf16[512,4,128]{2,1,0:T(4,128)(2,1)S(1)}, u32[]{:S(2)}, u32[]{:S(2)}) %collective-permute-start.5) | collective-permute-done | bytes 524320 | tf_op jit(solution)/shard_map/ppermute | solution.py:47
  51.4 0.3 collective-permute-start.9
  51.7 0.2 collective-permute-start.10
  51.9 0.0 collective-permute-done.7.refs_4_
  51.9 0.0 collective-permute-done.8.refs_5_
  51.9 1.4 %collective-permute-done.9.refs_6_ = bf16[512,4,128]{2,1,0:T(4,128)(2,1)S(1)} collective-permute-done((bf16[512,4,128]{2,1,0:T(4,128)(2,1)S(1)}, bf16[512,4,128]{2,1,0:T(4,128)(2,1)S(1)}, u32[]{:S(2)}, u32[]{:S(2)}) %collective-permute-start.9) | collective-permute-done | bytes 524320 | tf_op jit(solution)/shard_map/ppermute | solution.py:43
  53.3 0.7 %collective-permute-done.10.refs_7_ = bf16[512,4,128]{2,1,0:T(4,128)(2,1)S(1)} collective-permute-done((bf16[512,4,128]{2,1,0:T(4,128)(2,1)S(1)}, bf16[512,4,128]{2,1,0:T(4,128)(2,1)S(1)}, u32[]{:S(2)}, u32[]{:S(2)}) %collective-permute-start.10) | collective-permute-done | bytes 524320 | tf_op jit(solution)/shard_map/ppermute | solution.py:43
  54.1 0.0 copy-done.4
  54.1 0.0 copy-done.6
  54.1 0.0 copy-done.7
  54.1 0.0 copy-done.8
  54.1 0.0 copy-done.9
  54.1 0.0 copy-done.10
  54.1 10.1 %late.1 = (bf16[2048,512]{1,0:T(8,128)(2,1)}, bf16[512,512]{1,0:T(8,128)(2,1)}) custom-call(s32[2048]{0:T(1024)S(1)} %bitcast.30, s32[4]{0:T(128)S(1)} %convert_reduce_fusion.far_count, s32[16]{0:T(128)S(1)} %copy-done.11, s32[16]{0:T(128)S(1)} %get-tuple-element.31.lives, bf16[512,4,128]{2,1,0:T(4,128)(2,1)S(1)} %bitcast.25, ...), custom_call_target="tpu_custom_call" | custom-call | flops 4000000000 | bytes 14000000 | tf_op jit(solution)/shard_map/late/pallas_call | solution.py:345
  (9 shorter events, 0.1 us)
Async XLA Ops:
  0.6 29.3 %copy-start.2 = (s32[2048]{0:T(1024)S(1)}, s32[2048]{0:T(1024)}, u32[]{:S(2)}) copy-start(s32[2048]{0:T(1024)} %param.14) | copy-start | bytes 24580
  0.6 29.3 %copy-start.11 = (s32[16]{0:T(128)S(1)}, s32[16]{0:T(128)}, u32[]{:S(2)}) copy-start(s32[16]{0:T(128)} %tiles.2) | copy-start | bytes 196
  0.7 1.0 %copy-start = (bf16[16,32,512]{2,1,0:T(8,128)(2,1)S(1)}, bf16[16,32,512]{2,1,0:T(8,128)(2,1)}, u32[]{:S(2)}) copy-start(bf16[16,32,512]{2,1,0:T(8,128)(2,1)} %param.11) | copy-start | bytes 1572868
  1.8 28.2 %copy-start.1 = (bf16[16,32,512]{2,1,0:T(8,128)(2,1)S(1)}, bf16[16,32,512]{2,1,0:T(8,128)(2,1)}, u32[]{:S(2)}) copy-start(bf16[16,32,512]{2,1,0:T(8,128)(2,1)} %param.11) | copy-start | bytes 1572868
  1.8 28.2 %copy-start.5 = (bf16[1536,512]{1,0:T(8,128)(2,1)S(1)}, bf16[1536,512]{1,0:T(8,128)(2,1)}, u32[]{:S(2)}) copy-start(bf16[1536,512]{1,0:T(8,128)(2,1)} %refs_11_.1) | copy-start | bytes 4718596
  3.4 26.6 %all-to-all-start = ((bf16[16,32,4,128]{3,2,1,0:T(4,128)(2,1)}), bf16[16,32,4,128]{3,2,1,0:T(4,128)(2,1)S(1)}, u32[]{:S(2)}, u32[]{:S(2)}) async-start(bf16[16,32,4,128]{3,2,1,0:T(4,128)(2,1)} %get-tuple-element.24), calls=%async_computation | async-start | bytes 1048576 | tf_op jit(solution)/shard_map/all_to_all | solution.py:460
  12.0 9.4 %collective-permute-start = (bf16[16,4,128]{2,1,0:T(4,128)(2,1)S(1)}, bf16[16,4,128]{2,1,0:T(4,128)(2,1)S(1)}, u32[]{:S(2)}, u32[]{:S(2)}) collective-permute-start(bf16[16,4,128]{2,1,0:T(4,128)(2,1)S(1)} %get-tuple-element.25), channel_id=1, source_target_pairs={{0,1},{2,3},{4,5},{6,7},{8,9},{10,11},{12,13},{14,15},{1,0},{3,2},... | collective-permute-start | bytes 49160 | tf_op jit(solution)/shard_map/ppermute | solution.py:458
  13.3 9.1 %collective-permute-start.1 = (bf16[16,4,128]{2,1,0:T(4,128)(2,1)S(1)}, bf16[16,4,128]{2,1,0:T(4,128)(2,1)S(1)}, u32[]{:S(2)}, u32[]{:S(2)}) collective-permute-start(bf16[16,4,128]{2,1,0:T(4,128)(2,1)S(1)} %get-tuple-element.26), channel_id=1, source_target_pairs={{1,2},{3,4},{5,6},{7,8},{9,10},{11,12},{13,14},{15,0},{2,1},{4,3},... | collective-permute-start | bytes 49160 | tf_op jit(solution)/shard_map/ppermute | solution.py:459
  22.5 5.3 %collective-permute-start.2 = (bf16[34,4,128]{2,1,0:T(4,128)(2,1)S(1)}, bf16[34,4,128]{2,1,0:T(4,128)(2,1)S(1)}, u32[]{:S(2)}, u32[]{:S(2)}) collective-permute-start(bf16[34,4,128]{2,1,0:T(4,128)(2,1)S(1)} %pad_maximum_fusion), channel_id=1, source_target_pairs={{0,16},{32,48},{64,80},{96,112},{16,0},{48,32},{80,64},{112,96},{1... | collective-permute-start | bytes 104456 | tf_op jit(solution)/shard_map/ppermute | solution.py:467
  24.7 5.3 %collective-permute-start.3 = (bf16[34,4,128]{2,1,0:T(4,128)(2,1)S(1)}, bf16[34,4,128]{2,1,0:T(4,128)(2,1)S(1)}, u32[]{:S(2)}, u32[]{:S(2)}) collective-permute-start(bf16[34,4,128]{2,1,0:T(4,128)(2,1)S(1)} %pad_maximum_fusion.1), channel_id=1, source_target_pairs={{16,32},{48,64},{80,96},{32,16},{64,48},{96,80},{17,33},{49,65},{8... | collective-permute-start | bytes 104456 | tf_op jit(solution)/shard_map/ppermute | solution.py:468
  30.0 8.3 %collective-permute-start.4 = (bf16[512,4,128]{2,1,0:T(4,128)(2,1)S(1)}, bf16[512,4,128]{2,1,0:T(4,128)(2,1)S(1)}, u32[]{:S(2)}, u32[]{:S(2)}) collective-permute-start(bf16[512,4,128]{2,1,0:T(4,128)(2,1)S(1)} %bitcast.22), channel_id=1, source_target_pairs={{0,32},{1,33},{2,34},{3,35},{4,36},{5,37},{6,38},{7,39},{8,40},{9,... | collective-permute-start | bytes 1572872 | tf_op jit(solution)/shard_map/ppermute | solution.py:47
  30.0 1.6 %copy-start.3 = (bf16[2048,512]{1,0:T(8,128)(2,1)S(1)}, bf16[2048,512]{1,0:T(8,128)(2,1)}, u32[]{:S(2)}) copy-start(bf16[2048,512]{1,0:T(8,128)(2,1)} %refs_9_.1) | copy-start | bytes 6291460
  35.6 18.4 %copy-start.4 = (bf16[2048,512]{1,0:T(8,128)(2,1)S(1)}, bf16[2048,512]{1,0:T(8,128)(2,1)}, u32[]{:S(2)}) copy-start(bf16[2048,512]{1,0:T(8,128)(2,1)} %refs_9_.1) | copy-start | bytes 6291460
  35.7 18.4 %copy-start.6 = (bf16[1024,512]{1,0:T(8,128)(2,1)S(1)}, bf16[1024,512]{1,0:T(8,128)(2,1)}, u32[]{:S(2)}) copy-start(bf16[1024,512]{1,0:T(8,128)(2,1)} %refs_13_.1) | copy-start | bytes 3145732
  35.7 18.4 %copy-start.7 = (bf16[512,512]{1,0:T(8,128)(2,1)S(1)}, bf16[512,512]{1,0:T(8,128)(2,1)}, u32[]{:S(2)}) copy-start(bf16[512,512]{1,0:T(8,128)(2,1)} %refs_12_.1) | copy-start | bytes 1572868
  35.7 18.4 %copy-start.8 = (bf16[512,512]{1,0:T(8,128)(2,1)S(1)}, bf16[512,512]{1,0:T(8,128)(2,1)}, u32[]{:S(2)}) copy-start(bf16[512,512]{1,0:T(8,128)(2,1)} %refs_14_.1) | copy-start | bytes 1572868
  35.7 18.4 %copy-start.9 = (f32[512]{0:T(512)S(1)}, f32[512]{0:T(512)}, u32[]{:S(2)}) copy-start(f32[512]{0:T(512)} %param.18) | copy-start | bytes 6148
  35.7 18.4 %copy-start.10 = (f32[512]{0:T(512)S(1)}, f32[512]{0:T(512)}, u32[]{:S(2)}) copy-start(f32[512]{0:T(512)} %param.21) | copy-start | bytes 6148
  35.7 11.2 %collective-permute-start.6 = (bf16[512,4,128]{2,1,0:T(4,128)(2,1)S(1)}, bf16[512,4,128]{2,1,0:T(4,128)(2,1)S(1)}, u32[]{:S(2)}, u32[]{:S(2)}) collective-permute-start(bf16[512,4,128]{2,1,0:T(4,128)(2,1)S(1)} %bitcast.23), channel_id=1, source_target_pairs={{0,96},{1,97},{2,98},{3,99},{4,100},{5,101},{6,102},{7,103},{8,104... | collective-permute-start | bytes 1572872 | tf_op jit(solution)/shard_map/ppermute | solution.py:47
  38.3 13.1 %collective-permute-start.5 = (bf16[512,4,128]{2,1,0:T(4,128)(2,1)S(1)}, bf16[512,4,128]{2,1,0:T(4,128)(2,1)S(1)}, u32[]{:S(2)}, u32[]{:S(2)}) collective-permute-start(bf16[512,4,128]{2,1,0:T(4,128)(2,1)S(1)} %collective-permute-done.4.refs_1_), channel_id=1, source_target_pairs={{0,32},{1,33},{2,34},{3,35},{4,36},{5,37},{6,38},{7,39},{8,40},{9,... | collective-permute-start | bytes 1572872 | tf_op jit(solution)/shard_map/ppermute | solution.py:47
  39.2 12.7 %collective-permute-start.7 = (bf16[512,4,128]{2,1,0:T(4,128)(2,1)S(1)}, bf16[512,4,128]{2,1,0:T(4,128)(2,1)S(1)}, u32[]{:S(2)}, u32[]{:S(2)}) collective-permute-start(bf16[512,4,128]{2,1,0:T(4,128)(2,1)S(1)} %bitcast.24), channel_id=1, source_target_pairs={{0,16},{1,17},{2,18},{3,19},{4,20},{5,21},{6,22},{7,23},{8,24},{9,... | collective-permute-start | bytes 1572872 | tf_op jit(solution)/shard_map/ppermute | solution.py:43
  40.7 11.2 %collective-permute-start.8 = (bf16[512,4,128]{2,1,0:T(4,128)(2,1)S(1)}, bf16[512,4,128]{2,1,0:T(4,128)(2,1)S(1)}, u32[]{:S(2)}, u32[]{:S(2)}) collective-permute-start(bf16[512,4,128]{2,1,0:T(4,128)(2,1)S(1)} %collective-permute-done.4.refs_1_), channel_id=1, source_target_pairs={{0,16},{1,17},{2,18},{3,19},{4,20},{5,21},{6,22},{7,23},{8,24},{9,... | collective-permute-start | bytes 1572872 | tf_op jit(solution)/shard_map/ppermute | solution.py:43
  51.4 1.9 %collective-permute-start.9 = (bf16[512,4,128]{2,1,0:T(4,128)(2,1)S(1)}, bf16[512,4,128]{2,1,0:T(4,128)(2,1)S(1)}, u32[]{:S(2)}, u32[]{:S(2)}) collective-permute-start(bf16[512,4,128]{2,1,0:T(4,128)(2,1)S(1)} %collective-permute-done.6.refs_2_), channel_id=1, source_target_pairs={{0,16},{1,17},{2,18},{3,19},{4,20},{5,21},{6,22},{7,23},{8,24},{9,... | collective-permute-start | bytes 1572872 | tf_op jit(solution)/shard_map/ppermute | solution.py:43
  51.7 2.4 %collective-permute-start.10 = (bf16[512,4,128]{2,1,0:T(4,128)(2,1)S(1)}, bf16[512,4,128]{2,1,0:T(4,128)(2,1)S(1)}, u32[]{:S(2)}, u32[]{:S(2)}) collective-permute-start(bf16[512,4,128]{2,1,0:T(4,128)(2,1)S(1)} %collective-permute-done.5.refs_3_), channel_id=1, source_target_pairs={{0,16},{1,17},{2,18},{3,19},{4,20},{5,21},{6,22},{7,23},{8,24},{9,... | collective-permute-start | bytes 1572872 | tf_op jit(solution)/shard_map/ppermute | solution.py:43

commit v9 on v8

--- a/solution.py
+++ b/solution.py
@@ -458,6 +458,12 @@
     side_a = lax.ppermute(col_a, "lon", pairs(0, lon_count, True))
     side_b = lax.ppermute(col_b, "lon", pairs(1, lon_count, True))
     plane = lanes(lax.all_to_all(copies, "lon", split_axis=0, concat_axis=0, tiled=True))
+    plane, side_a, side_b, tiles, near_index, far_list, far_count, lives = lax.optimization_barrier(
+        (plane, side_a, side_b, block_tile, near_index, far_list, far_count, lives)
+    )
+
+    ahead = move(plane, "x", (1, -1))
+    plane_other = other_core(plane)
     west = jnp.where(lon_odd == 1, side_a, side_b)
     east = jnp.where(lon_odd == 1, side_b, side_a)
     wide = lambda r, rows: jnp.concatenate(
@@ -468,12 +474,6 @@
     strip_b = lax.ppermute(
         wide(patch_rows - 1 - edge_row, row_b), "lat", pairs(1, lat_count, False)
     )
-    plane, strip_a, strip_b, tiles, near_index, far_list, far_count, lives = lax.optimization_barrier(
-        (plane, strip_a, strip_b, block_tile, near_index, far_list, far_count, lives)
-    )
-
-    ahead = move(plane, "x", (1, -1))
-    plane_other = other_core(plane)
     partial = early_call(tiles, edge_latent, recv_rows, own_rows, w_first)
     later, partial = lax.optimization_barrier((plane, partial))
     behind = move(later, "x", (-1, 1))

time: 64.7 us -> 64.6 us (level)
  waiting for transfers between devices: 11.3 us -> 7.48 us
  starting transfers between devices: 23.5 us -> 27.2 us
    ppermute x3, waiting for transfers between devices: 5.92 us -> 0.39 us  [move(): return lax.ppermute(value, ('lat', 'lon'), shift(axis, by_core))]
    ppermute x3, starting transfers between devices: 2.44 us -> 5.67 us  [move(): return lax.ppermute(value, ('lat', 'lon'), shift(axis, by_core))]
    ppermute x1, waiting for transfers between devices: 2.09 us -> 3.95 us  [per_device(): lax.ppermute(wide(patch_rows - 1 - edge_row, row_b), 'lat', pairs(1, lat_...]
    ppermute x1, starting transfers between devices: 3.02 us -> 4.28 us  [per_device(): lax.ppermute(wide(patch_rows - 1 - edge_row, row_b), 'lat', pairs(1, lat_...]
    ppermute x4, starting transfers between devices: 1.96 us -> 1.16 us  [other_core(): return lax.ppermute(value, ('lat', 'lon'), pairs)]
  transfers between devices with their start and end apart: 12 -> 12, of which waited for: 7 -> 5; matrix products, arithmetic and copies ran while one was open for 7% -> 7% of each run, Pallas kernels for 15% -> 15%
where the time goes in v9:
time: 64.6 us; the launch traced here: 64.2 us
  starting transfers between devices  27.2 us (42%)
  Pallas kernels  21.4 us (33%)
  waiting for transfers between devices  7.48 us (12%)
  other arithmetic  4.29 us (7%)
  local copies, waits for them, and re-layouts  2.72 us (4%)
  between operations  1.07 us (2%)
    pallas_call x1, Pallas kernels, late_call(): pl.pallas_call(late_kernel, name='late', in_specs=[scalars] * 4 + [anywhe...  9.99 us
    all_to_all x1, starting transfers between devices, per_device(): lax.all_to_all(copies, 'lon', split_axis=0, concat_axis=0, tiled=True)  8.61 us
    pallas_call x1, Pallas kernels, near_call(): pl.pallas_call(near_kernel, name='near', grid_spec=pltpu.PrefetchScalarGr...  5.87 us
    ppermute x3, starting transfers between devices, move(): return lax.ppermute(value, ('lat', 'lon'), shift(axis, by_core))  5.67 us
    ppermute x1, starting transfers between devices, per_device(): lax.ppermute(wide(patch_rows - 1 - edge_row, row_b), 'lat', pairs(1, lat_...  4.28 us
    pallas_call x1, Pallas kernels, early_call(): pl.pallas_call(early_kernel, name='early', grid_spec=pltpu.PrefetchScalar...  4.03 us
    ppermute x1, waiting for transfers between devices, per_device(): lax.ppermute(wide(patch_rows - 1 - edge_row, row_b), 'lat', pairs(1, lat_...  3.95 us
    ppermute x1, starting transfers between devices, per_device(): side_b = lax.ppermute(col_b, 'lon', pairs(1, lon_count, True))  3.9 us
  transfers between devices with their start and end apart: 12, of which 5 were waited for; matrix products, arithmetic and copies ran while one was open for 7% of the time, Pallas kernels for 15%

profile of v9, /device:TPU:1, one launch (start us, length us, event | category | flops | bytes accessed | tf_op | source)
XLA Modules:
  0.0 64.2 jit_solution(7045662435810675713)
XLA Ops:
  0.6 0.0 copy-start.2
  0.6 0.0 copy-start.11
  0.7 0.1 pad_add_fusion.odd
  0.7 0.0 copy-start
  0.8 1.0 %copy-done = bf16[16,32,512]{2,1,0:T(8,128)(2,1)S(1)} copy-done((bf16[16,32,512]{2,1,0:T(8,128)(2,1)S(1)}, bf16[16,32,512]{2,1,0:T(8,128)(2,1)}, u32[]{:S(2)}) %copy-start) | copy-done | bytes 524312
  1.8 0.0 copy-start.1
  1.8 0.0 copy-start.5
  1.8 1.6 %coarse.1 = (bf16[16,32,4,128]{3,2,1,0:T(4,128)(2,1)}, bf16[16,4,128]{2,1,0:T(4,128)(2,1)S(1)}, bf16[16,4,128]{2,1,0:T(4,128)(2,1)S(1)}, bf16[32,4,128]{2,1,0:T(4,128)(2,1)S(1)}, bf16[32,4,128]{2,1,0:T(4,128)(2,1)S(1)}) custom-call(s32[2]{0:T(128)S(1)} %pad_add_fusion.odd, bf16[512,512]{1,0:T(8,128)(2,1)S(1)} %bitcast.18), custom_call_target="tpu_custom_call" | custom-call | tf_op jit(solution)/shard_map/coarse/pallas_call | solution.py:416
  3.4 8.6 %all-to-all-start = ((bf16[16,32,4,128]{3,2,1,0:T(4,128)(2,1)}), bf16[16,32,4,128]{3,2,1,0:T(4,128)(2,1)S(1)}, u32[]{:S(2)}, u32[]{:S(2)}) async-start(bf16[16,32,4,128]{3,2,1,0:T(4,128)(2,1)} %get-tuple-element.24), calls=%async_computation | async-start | bytes 1048576 | tf_op jit(solution)/shard_map/all_to_all | solution.py:460
  12.0 1.4 %collective-permute-start = (bf16[16,4,128]{2,1,0:T(4,128)(2,1)S(1)}, bf16[16,4,128]{2,1,0:T(4,128)(2,1)S(1)}, u32[]{:S(2)}, u32[]{:S(2)}) collective-permute-start(bf16[16,4,128]{2,1,0:T(4,128)(2,1)S(1)} %get-tuple-element.25), channel_id=1, source_target_pairs={{0,1},{2,3},{4,5},{6,7},{8,9},{10,11},{12,13},{14,15},{1,0},{3,2},... | collective-permute-start | bytes 49160 | tf_op jit(solution)/shard_map/ppermute | solution.py:458
  13.3 3.9 %collective-permute-start.1 = (bf16[16,4,128]{2,1,0:T(4,128)(2,1)S(1)}, bf16[16,4,128]{2,1,0:T(4,128)(2,1)S(1)}, u32[]{:S(2)}, u32[]{:S(2)}) collective-permute-start(bf16[16,4,128]{2,1,0:T(4,128)(2,1)S(1)} %get-tuple-element.26), channel_id=1, source_target_pairs={{1,2},{3,4},{5,6},{7,8},{9,10},{11,12},{13,14},{15,0},{2,1},{4,3},... | collective-permute-start | bytes 49160 | tf_op jit(solution)/shard_map/ppermute | solution.py:459
  17.3 0.1 iota_compare_fusion.1
  17.3 0.8 %bitcast_reduce_fusion = (s32[16]{0:T(128)S(1)}, pred[2048]{0:T(1024)(128)(4,1)S(1)}) fusion(s32[2048]{0:T(1024)} %param.14), kind=kLoop, calls=%fused_computation.53 | loop fusion | flops 6128 | bytes 10304 | tf_op jit(solution)/shard_map/reduce_sum | solution.py:456
  18.2 0.7 %not_and_fusion = (pred[2048]{0:T(1024)(128)(4,1)S(1)}, pred[2048]{0:T(1024)(128)(4,1)S(1)}) fusion(pred[2048]{0:T(1024)(128)(4,1)S(1)} %get-tuple-element.47, s32[]{:T(128)S(6)} %mul.44, s32[]{:T(128)S(6)} %mul.43, s32[2048]{0:T(1024)} %param.13), kind=kLoop, calls=%fused_computation.70 | loop fusion | flops 71680 | bytes 14344 | tf_op jit(solution)/shard_map/and | solution.py:454
  18.9 0.8 %fusion.9 = (s32[2048]{0:T(1024)S(1)}, s32[2048]{0:T(1024)S(1)}) fusion(s32[2048]{0:T(1024)} %param.13, s32[]{:T(128)S(6)} %select_n.137, s32[]{:T(128)} %select_n.122, pred[2048]{0:T(1024)(128)(4,1)S(1)} %get-tuple-element.49, s32[]{:T(128)} %select_n.123, s32[]{:T(128)S(6)} %sub.72, s32[]{:T(128)S(6)} %sub.71, s32[]{:T(128)S(6)} %mul.44, s32[]{:T(128)S(6)} %mul.43), kind=kLoop, calls=%fused_computation.48 | loop fusion | flops 342016 | bytes 26652 | tf_op jit(solution)/shard_map/sub | solution.py:262
  19.7 0.6 %select_reduce_fusion.1 = s32[4,512]{1,0:T(4,128)S(1)} fusion(s32[4,512]{1,0:T(4,128)S(1)} %convert_element_type.8, pred[512,512]{1,0:T(8,128)(4,1)S(1)} %iota_compare_fusion.1), kind=kLoop, calls=%fused_computation.2 | loop fusion | flops 2095104 | bytes 278528 | tf_op jit(solution)/shard_map/reduce_sum | solution.py:261
  20.3 1.0 %select_reduce_fusion = s32[4,512]{1,0:T(4,128)S(1)} fusion(s32[4,512]{1,0:T(4,128)S(1)} %broadcast_in_dim.73, s32[4,512]{1,0:T(4,128)S(1)} %select_reduce_fusion.1, pred[4,512]{1,0:T(4,128)(4,1)S(1)} %reshape.60), kind=kLoop, calls=%fused_computation | loop fusion | flops 4192256 | bytes 26624 | tf_op jit(solution)/shard_map/reduce_sum | solution.py:264
  21.3 0.1 convert_reduce_fusion.far_count
  21.5 0.0 collective-permute-done.refs_0_
  21.5 1.0 %collective-permute-done.1.refs_1_ = bf16[16,4,128]{2,1,0:T(4,128)(2,1)S(1)} collective-permute-done((bf16[16,4,128]{2,1,0:T(4,128)(2,1)S(1)}, bf16[16,4,128]{2,1,0:T(4,128)(2,1)S(1)}, u32[]{:S(2)}, u32[]{:S(2)}) %collective-permute-start.1) | collective-permute-done | bytes 16416 | tf_op jit(solution)/shard_map/ppermute | solution.py:459
  22.5 0.0 all-to-all-done
  22.5 2.5 %collective-permute-start.2 = (bf16[512,4,128]{2,1,0:T(4,128)(2,1)S(1)}, bf16[512,4,128]{2,1,0:T(4,128)(2,1)S(1)}, u32[]{:S(2)}, u32[]{:S(2)}) collective-permute-start(bf16[512,4,128]{2,1,0:T(4,128)(2,1)S(1)} %bitcast.22), channel_id=1, source_target_pairs={{0,32},{1,33},{2,34},{3,35},{4,36},{5,37},{6,38},{7,39},{8,40},{9,... | collective-permute-start | bytes 1572872 | tf_op jit(solution)/shard_map/ppermute | solution.py:47
  24.9 0.0 copy-done.2
  24.9 0.0 copy-done.11
  24.9 0.0 copy-done.1
  25.0 0.0 copy-done.5
  25.0 0.0 copy-start.3
  25.0 1.6 %copy-done.3 = bf16[2048,512]{1,0:T(8,128)(2,1)S(1)} copy-done((bf16[2048,512]{1,0:T(8,128)(2,1)S(1)}, bf16[2048,512]{1,0:T(8,128)(2,1)}, u32[]{:S(2)}) %copy-start.3) | copy-done | bytes 2097176
  26.6 4.0 %early.1.refs_4_ = bf16[2048,512]{1,0:T(8,128)(2,1)S(1)} custom-call(s32[16]{0:T(128)S(1)} %copy-done.11, bf16[2048,512]{1,0:T(8,128)(2,1)S(1)} %copy-done.3, s32[4,4,128]{2,1,0:T(4,128)S(1)} %bitcast.28, bf16[512,512]{1,0:T(8,128)(2,1)S(1)} %bitcast.19, bf16[1536,512]{1,0:T(8,128)(2,1)S(1)} %copy-done.5, bf16[1536,512]{1,0:T(8,128)(2,1)S(1)} %copy-done.5), custom_call_target="tpu_custom_call" | custom-call | flops 3000000000 | bytes 10000000 | tf_op jit(solution)/shard_map/early/pallas_call | solution.py:279
  30.6 0.1 collective-permute-start.4
  30.7 0.4 collective-permute-done.2.refs_1_
  31.1 3.1 %collective-permute-start.3 = (bf16[512,4,128]{2,1,0:T(4,128)(2,1)S(1)}, bf16[512,4,128]{2,1,0:T(4,128)(2,1)S(1)}, u32[]{:S(2)}, u32[]{:S(2)}) collective-permute-start(bf16[512,4,128]{2,1,0:T(4,128)(2,1)S(1)} %collective-permute-done.2.refs_1_), channel_id=1, source_target_pairs={{0,32},{1,33},{2,34},{3,35},{4,36},{5,37},{6,38},{7,39},{8,40},{9,... | collective-permute-start | bytes 1572872 | tf_op jit(solution)/shard_map/ppermute | solution.py:47
  34.2 2.2 %collective-permute-start.5 = (bf16[34,4,128]{2,1,0:T(4,128)(2,1)S(1)}, bf16[34,4,128]{2,1,0:T(4,128)(2,1)S(1)}, u32[]{:S(2)}, u32[]{:S(2)}) collective-permute-start(bf16[34,4,128]{2,1,0:T(4,128)(2,1)S(1)} %pad_maximum_fusion), channel_id=1, source_target_pairs={{0,16},{32,48},{64,80},{96,112},{16,0},{48,32},{80,64},{112,96},{1... | collective-permute-start | bytes 104456 | tf_op jit(solution)/shard_map/ppermute | solution.py:473
  36.5 0.0 copy-start.4
  36.5 0.0 copy-start.6
  36.5 0.0 copy-start.7
  36.5 0.0 copy-start.8
  36.5 0.0 copy-start.9
  36.5 0.0 copy-start.10
  36.6 4.3 %collective-permute-start.6 = (bf16[34,4,128]{2,1,0:T(4,128)(2,1)S(1)}, bf16[34,4,128]{2,1,0:T(4,128)(2,1)S(1)}, u32[]{:S(2)}, u32[]{:S(2)}) collective-permute-start(bf16[34,4,128]{2,1,0:T(4,128)(2,1)S(1)} %pad_maximum_fusion.1), channel_id=1, source_target_pairs={{16,32},{48,64},{80,96},{32,16},{64,48},{96,80},{17,33},{49,65},{8... | collective-permute-start | bytes 104456 | tf_op jit(solution)/shard_map/ppermute | solution.py:474
  40.8 0.1 collective-permute-start.7
  40.9 0.0 collective-permute-done.5.refs_2_
  40.9 0.5 collective-permute-start.8
  41.4 4.0 %collective-permute-done.6.refs_3_ = bf16[34,4,128]{2,1,0:T(4,128)(2,1)S(1)} collective-permute-done((bf16[34,4,128]{2,1,0:T(4,128)(2,1)S(1)}, bf16[34,4,128]{2,1,0:T(4,128)(2,1)S(1)}, u32[]{:S(2)}, u32[]{:S(2)}) %collective-permute-start.6) | collective-permute-done | bytes 34848 | tf_op jit(solution)/shard_map/ppermute | solution.py:474
  45.4 5.9 %near.1.refs_8_ = bf16[2048,512]{1,0:T(8,128)(2,1)S(1)} custom-call(s32[2048]{0:T(1024)S(1)} %get-tuple-element.35.near_index, bf16[512,512]{1,0:T(8,128)(2,1)S(1)} %bitcast.20, bf16[16,4,128]{2,1,0:T(4,128)(2,1)S(1)} %collective-permute-done.refs_0_, bf16[16,4,128]{2,1,0:T(4,128)(2,1)S(1)} %collective-permute-done.1.refs_1_, ...), custom_call_target="tpu_custom_call" | custom-call | flops 2000000000 | bytes 8000000 | tf_op jit(solution)/shard_map/near/pallas_call | solution.py:301
  51.3 0.0 collective-permute-done.4.refs_2_
  51.3 0.0 collective-permute-done.3.refs_3_
  51.3 0.1 collective-permute-start.9
  51.4 0.5 collective-permute-start.10
  51.9 0.0 collective-permute-done.7.refs_4_
  51.9 0.0 collective-permute-done.8.refs_5_
  51.9 1.4 %collective-permute-done.9.refs_6_ = bf16[512,4,128]{2,1,0:T(4,128)(2,1)S(1)} collective-permute-done((bf16[512,4,128]{2,1,0:T(4,128)(2,1)S(1)}, bf16[512,4,128]{2,1,0:T(4,128)(2,1)S(1)}, u32[]{:S(2)}, u32[]{:S(2)}) %collective-permute-start.9) | collective-permute-done | bytes 524320 | tf_op jit(solution)/shard_map/ppermute | solution.py:43
  53.3 0.7 %collective-permute-done.10.refs_7_ = bf16[512,4,128]{2,1,0:T(4,128)(2,1)S(1)} collective-permute-done((bf16[512,4,128]{2,1,0:T(4,128)(2,1)S(1)}, bf16[512,4,128]{2,1,0:T(4,128)(2,1)S(1)}, u32[]{:S(2)}, u32[]{:S(2)}) %collective-permute-start.10) | collective-permute-done | bytes 524320 | tf_op jit(solution)/shard_map/ppermute | solution.py:43
  54.0 0.0 copy-done.4
  54.0 0.0 copy-done.6
  54.0 0.0 copy-done.7
  54.0 0.0 copy-done.8
  54.0 0.0 copy-done.9
  54.1 0.0 copy-done.10
  54.1 10.0 %late.1 = (bf16[2048,512]{1,0:T(8,128)(2,1)}, bf16[512,512]{1,0:T(8,128)(2,1)}) custom-call(s32[2048]{0:T(1024)S(1)} %bitcast.30, s32[4]{0:T(128)S(1)} %convert_reduce_fusion.far_count, s32[16]{0:T(128)S(1)} %copy-done.11, s32[16]{0:T(128)S(1)} %get-tuple-element.29.lives, bf16[512,4,128]{2,1,0:T(4,128)(2,1)S(1)} %bitcast.25, ...), custom_call_target="tpu_custom_call" | custom-call | flops 4000000000 | bytes 14000000 | tf_op jit(solution)/shard_map/late/pallas_call | solution.py:345
  (9 shorter events, 0.1 us)
Async XLA Ops:
  0.6 24.3 %copy-start.2 = (s32[2048]{0:T(1024)S(1)}, s32[2048]{0:T(1024)}, u32[]{:S(2)}) copy-start(s32[2048]{0:T(1024)} %param.14) | copy-start | bytes 24580
  0.6 24.3 %copy-start.11 = (s32[16]{0:T(128)S(1)}, s32[16]{0:T(128)}, u32[]{:S(2)}) copy-start(s32[16]{0:T(128)} %tiles.2) | copy-start | bytes 196
  0.7 1.0 %copy-start = (bf16[16,32,512]{2,1,0:T(8,128)(2,1)S(1)}, bf16[16,32,512]{2,1,0:T(8,128)(2,1)}, u32[]{:S(2)}) copy-start(bf16[16,32,512]{2,1,0:T(8,128)(2,1)} %param.11) | copy-start | bytes 1572868
  1.8 23.2 %copy-start.1 = (bf16[16,32,512]{2,1,0:T(8,128)(2,1)S(1)}, bf16[16,32,512]{2,1,0:T(8,128)(2,1)}, u32[]{:S(2)}) copy-start(bf16[16,32,512]{2,1,0:T(8,128)(2,1)} %param.11) | copy-start | bytes 1572868
  1.8 23.2 %copy-start.5 = (bf16[1536,512]{1,0:T(8,128)(2,1)S(1)}, bf16[1536,512]{1,0:T(8,128)(2,1)}, u32[]{:S(2)}) copy-start(bf16[1536,512]{1,0:T(8,128)(2,1)} %refs_11_.1) | copy-start | bytes 4718596
  3.4 19.1 %all-to-all-start = ((bf16[16,32,4,128]{3,2,1,0:T(4,128)(2,1)}), bf16[16,32,4,128]{3,2,1,0:T(4,128)(2,1)S(1)}, u32[]{:S(2)}, u32[]{:S(2)}) async-start(bf16[16,32,4,128]{3,2,1,0:T(4,128)(2,1)} %get-tuple-element.24), calls=%async_computation | async-start | bytes 1048576 | tf_op jit(solution)/shard_map/all_to_all | solution.py:460
  12.0 9.5 %collective-permute-start = (bf16[16,4,128]{2,1,0:T(4,128)(2,1)S(1)}, bf16[16,4,128]{2,1,0:T(4,128)(2,1)S(1)}, u32[]{:S(2)}, u32[]{:S(2)}) collective-permute-start(bf16[16,4,128]{2,1,0:T(4,128)(2,1)S(1)} %get-tuple-element.25), channel_id=1, source_target_pairs={{0,1},{2,3},{4,5},{6,7},{8,9},{10,11},{12,13},{14,15},{1,0},{3,2},... | collective-permute-start | bytes 49160 | tf_op jit(solution)/shard_map/ppermute | solution.py:458
  13.3 9.1 %collective-permute-start.1 = (bf16[16,4,128]{2,1,0:T(4,128)(2,1)S(1)}, bf16[16,4,128]{2,1,0:T(4,128)(2,1)S(1)}, u32[]{:S(2)}, u32[]{:S(2)}) collective-permute-start(bf16[16,4,128]{2,1,0:T(4,128)(2,1)S(1)} %get-tuple-element.26), channel_id=1, source_target_pairs={{1,2},{3,4},{5,6},{7,8},{9,10},{11,12},{13,14},{15,0},{2,1},{4,3},... | collective-permute-start | bytes 49160 | tf_op jit(solution)/shard_map/ppermute | solution.py:459
  22.5 8.6 %collective-permute-start.2 = (bf16[512,4,128]{2,1,0:T(4,128)(2,1)S(1)}, bf16[512,4,128]{2,1,0:T(4,128)(2,1)S(1)}, u32[]{:S(2)}, u32[]{:S(2)}) collective-permute-start(bf16[512,4,128]{2,1,0:T(4,128)(2,1)S(1)} %bitcast.22), channel_id=1, source_target_pairs={{0,32},{1,33},{2,34},{3,35},{4,36},{5,37},{6,38},{7,39},{8,40},{9,... | collective-permute-start | bytes 1572872 | tf_op jit(solution)/shard_map/ppermute | solution.py:47
  25.0 1.6 %copy-start.3 = (bf16[2048,512]{1,0:T(8,128)(2,1)S(1)}, bf16[2048,512]{1,0:T(8,128)(2,1)}, u32[]{:S(2)}) copy-start(bf16[2048,512]{1,0:T(8,128)(2,1)} %refs_9_.1) | copy-start | bytes 6291460
  30.6 20.7 %collective-permute-start.4 = (bf16[512,4,128]{2,1,0:T(4,128)(2,1)S(1)}, bf16[512,4,128]{2,1,0:T(4,128)(2,1)S(1)}, u32[]{:S(2)}, u32[]{:S(2)}) collective-permute-start(bf16[512,4,128]{2,1,0:T(4,128)(2,1)S(1)} %bitcast.23), channel_id=1, source_target_pairs={{0,96},{1,97},{2,98},{3,99},{4,100},{5,101},{6,102},{7,103},{8,104... | collective-permute-start | bytes 1572872 | tf_op jit(solution)/shard_map/ppermute | solution.py:47
  31.1 20.2 %collective-permute-start.3 = (bf16[512,4,128]{2,1,0:T(4,128)(2,1)S(1)}, bf16[512,4,128]{2,1,0:T(4,128)(2,1)S(1)}, u32[]{:S(2)}, u32[]{:S(2)}) collective-permute-start(bf16[512,4,128]{2,1,0:T(4,128)(2,1)S(1)} %collective-permute-done.2.refs_1_), channel_id=1, source_target_pairs={{0,32},{1,33},{2,34},{3,35},{4,36},{5,37},{6,38},{7,39},{8,40},{9,... | collective-permute-start | bytes 1572872 | tf_op jit(solution)/shard_map/ppermute | solution.py:47
  34.2 6.7 %collective-permute-start.5 = (bf16[34,4,128]{2,1,0:T(4,128)(2,1)S(1)}, bf16[34,4,128]{2,1,0:T(4,128)(2,1)S(1)}, u32[]{:S(2)}, u32[]{:S(2)}) collective-permute-start(bf16[34,4,128]{2,1,0:T(4,128)(2,1)S(1)} %pad_maximum_fusion), channel_id=1, source_target_pairs={{0,16},{32,48},{64,80},{96,112},{16,0},{48,32},{80,64},{112,96},{1... | collective-permute-start | bytes 104456 | tf_op jit(solution)/shard_map/ppermute | solution.py:473
  36.5 17.5 %copy-start.4 = (bf16[2048,512]{1,0:T(8,128)(2,1)S(1)}, bf16[2048,512]{1,0:T(8,128)(2,1)}, u32[]{:S(2)}) copy-start(bf16[2048,512]{1,0:T(8,128)(2,1)} %refs_9_.1) | copy-start | bytes 6291460
  36.5 17.5 %copy-start.6 = (bf16[1024,512]{1,0:T(8,128)(2,1)S(1)}, bf16[1024,512]{1,0:T(8,128)(2,1)}, u32[]{:S(2)}) copy-start(bf16[1024,512]{1,0:T(8,128)(2,1)} %refs_13_.1) | copy-start | bytes 3145732
  36.5 17.5 %copy-start.7 = (bf16[512,512]{1,0:T(8,128)(2,1)S(1)}, bf16[512,512]{1,0:T(8,128)(2,1)}, u32[]{:S(2)}) copy-start(bf16[512,512]{1,0:T(8,128)(2,1)} %refs_12_.1) | copy-start | bytes 1572868
  36.5 17.5 %copy-start.8 = (bf16[512,512]{1,0:T(8,128)(2,1)S(1)}, bf16[512,512]{1,0:T(8,128)(2,1)}, u32[]{:S(2)}) copy-start(bf16[512,512]{1,0:T(8,128)(2,1)} %refs_14_.1) | copy-start | bytes 1572868
  36.5 17.5 %copy-start.9 = (f32[512]{0:T(512)S(1)}, f32[512]{0:T(512)}, u32[]{:S(2)}) copy-start(f32[512]{0:T(512)} %param.18) | copy-start | bytes 6148
  36.5 17.5 %copy-start.10 = (f32[512]{0:T(512)S(1)}, f32[512]{0:T(512)}, u32[]{:S(2)}) copy-start(f32[512]{0:T(512)} %param.21) | copy-start | bytes 6148
  36.6 8.8 %collective-permute-start.6 = (bf16[34,4,128]{2,1,0:T(4,128)(2,1)S(1)}, bf16[34,4,128]{2,1,0:T(4,128)(2,1)S(1)}, u32[]{:S(2)}, u32[]{:S(2)}) collective-permute-start(bf16[34,4,128]{2,1,0:T(4,128)(2,1)S(1)} %pad_maximum_fusion.1), channel_id=1, source_target_pairs={{16,32},{48,64},{80,96},{32,16},{64,48},{96,80},{17,33},{49,65},{8... | collective-permute-start | bytes 104456 | tf_op jit(solution)/shard_map/ppermute | solution.py:474
  40.8 11.0 %collective-permute-start.7 = (bf16[512,4,128]{2,1,0:T(4,128)(2,1)S(1)}, bf16[512,4,128]{2,1,0:T(4,128)(2,1)S(1)}, u32[]{:S(2)}, u32[]{:S(2)}) collective-permute-start(bf16[512,4,128]{2,1,0:T(4,128)(2,1)S(1)} %bitcast.24), channel_id=1, source_target_pairs={{0,16},{1,17},{2,18},{3,19},{4,20},{5,21},{6,22},{7,23},{8,24},{9,... | collective-permute-start | bytes 1572872 | tf_op jit(solution)/shard_map/ppermute | solution.py:43
  40.9 10.9 %collective-permute-start.8 = (bf16[512,4,128]{2,1,0:T(4,128)(2,1)S(1)}, bf16[512,4,128]{2,1,0:T(4,128)(2,1)S(1)}, u32[]{:S(2)}, u32[]{:S(2)}) collective-permute-start(bf16[512,4,128]{2,1,0:T(4,128)(2,1)S(1)} %collective-permute-done.2.refs_1_), channel_id=1, source_target_pairs={{0,16},{1,17},{2,18},{3,19},{4,20},{5,21},{6,22},{7,23},{8,24},{9,... | collective-permute-start | bytes 1572872 | tf_op jit(solution)/shard_map/ppermute | solution.py:43
  51.3 2.0 %collective-permute-start.9 = (bf16[512,4,128]{2,1,0:T(4,128)(2,1)S(1)}, bf16[512,4,128]{2,1,0:T(4,128)(2,1)S(1)}, u32[]{:S(2)}, u32[]{:S(2)}) collective-permute-start(bf16[512,4,128]{2,1,0:T(4,128)(2,1)S(1)} %collective-permute-done.4.refs_2_), channel_id=1, source_target_pairs={{0,16},{1,17},{2,18},{3,19},{4,20},{5,21},{6,22},{7,23},{8,24},{9,... | collective-permute-start | bytes 1572872 | tf_op jit(solution)/shard_map/ppermute | solution.py:43
  51.4 2.6 %collective-permute-start.10 = (bf16[512,4,128]{2,1,0:T(4,128)(2,1)S(1)}, bf16[512,4,128]{2,1,0:T(4,128)(2,1)S(1)}, u32[]{:S(2)}, u32[]{:S(2)}) collective-permute-start(bf16[512,4,128]{2,1,0:T(4,128)(2,1)S(1)} %collective-permute-done.3.refs_3_), channel_id=1, source_target_pairs={{0,16},{1,17},{2,18},{3,19},{4,20},{5,21},{6,22},{7,23},{8,24},{9,... | collective-permute-start | bytes 1572872 | tf_op jit(solution)/shard_map/ppermute | solution.py:43

commit v10 on v9

--- a/solution.py
+++ b/solution.py
@@ -475,7 +475,7 @@
         wide(patch_rows - 1 - edge_row, row_b), "lat", pairs(1, lat_count, False)
     )
     partial = early_call(tiles, edge_latent, recv_rows, own_rows, w_first)
-    later, partial = lax.optimization_barrier((plane, partial))
+    later, partial, strip_a, strip_b = lax.optimization_barrier((plane, partial, strip_a, strip_b))
     behind = move(later, "x", (-1, 1))
     ahead, partial = lax.optimization_barrier((ahead, partial))
     across = move(ahead, "x", (1, -1))

time: 64.6 us -> 63.6 us (0.985)
  starting transfers between devices: 27.2 us -> 25.1 us
  waiting for transfers between devices: 7.48 us -> 8.4 us
    ppermute x3, waiting for transfers between devices: 0.39 us -> 5.15 us  [move(): return lax.ppermute(value, ('lat', 'lon'), shift(axis, by_core))]
    ppermute x1, waiting for transfers between devices: 3.95 us -> 0.01 us  [per_device(): lax.ppermute(wide(patch_rows - 1 - edge_row, row_b), 'lat', pairs(1, lat_...]
    ppermute x1, starting transfers between devices: 4.28 us -> 3.02 us  [per_device(): lax.ppermute(wide(patch_rows - 1 - edge_row, row_b), 'lat', pairs(1, lat_...]
    ppermute x1, starting transfers between devices: 2.22 us -> 1.17 us  [per_device(): lax.ppermute(wide(edge_row, row_a), 'lat', pairs(0, lat_count, False))]
    ppermute x4, starting transfers between devices: 1.16 us -> 1.85 us  [other_core(): return lax.ppermute(value, ('lat', 'lon'), pairs)]
  transfers between devices with their start and end apart: 12 -> 12, of which waited for: 5 -> 5; matrix products, arithmetic and copies ran while one was open for 7% -> 7% of each run, Pallas kernels for 15% -> 16%
where the time goes in v10:
time: 63.6 us; the launch traced here: 63.1 us
  starting transfers between devices  25.1 us (39%)
  Pallas kernels  21.4 us (34%)
  waiting for transfers between devices  8.4 us (13%)
  other arithmetic  4.29 us (7%)
  local copies, waits for them, and re-layouts  2.72 us (4%)
  between operations  1.09 us (2%)
    pallas_call x1, Pallas kernels, late_call(): pl.pallas_call(late_kernel, name='late', in_specs=[scalars] * 4 + [anywhe...  9.98 us
    all_to_all x1, starting transfers between devices, per_device(): lax.all_to_all(copies, 'lon', split_axis=0, concat_axis=0, tiled=True)  8.61 us
    pallas_call x1, Pallas kernels, near_call(): pl.pallas_call(near_kernel, name='near', grid_spec=pltpu.PrefetchScalarGr...  5.86 us
    ppermute x3, starting transfers between devices, move(): return lax.ppermute(value, ('lat', 'lon'), shift(axis, by_core))  5.23 us
    ppermute x3, waiting for transfers between devices, move(): return lax.ppermute(value, ('lat', 'lon'), shift(axis, by_core))  5.15 us
    pallas_call x1, Pallas kernels, early_call(): pl.pallas_call(early_kernel, name='early', grid_spec=pltpu.PrefetchScalar...  4.03 us
    ppermute x1, starting transfers between devices, per_device(): side_b = lax.ppermute(col_b, 'lon', pairs(1, lon_count, True))  3.9 us
    ppermute x1, starting transfers between devices, per_device(): lax.ppermute(wide(patch_rows - 1 - edge_row, row_b), 'lat', pairs(1, lat_...  3.02 us
  transfers between devices with their start and end apart: 12, of which 5 were waited for; matrix products, arithmetic and copies ran while one was open for 7% of the time, Pallas kernels for 16%

profile of v10, /device:TPU:1, one launch (start us, length us, event | category | flops | bytes accessed | tf_op | source)
XLA Modules:
  0.0 63.1 jit_solution(1532460870791823182)
XLA Ops:
  0.6 0.0 copy-start.2
  0.6 0.0 copy-start.11
  0.7 0.1 pad_add_fusion.odd
  0.7 0.0 copy-start
  0.8 1.0 %copy-done = bf16[16,32,512]{2,1,0:T(8,128)(2,1)S(1)} copy-done((bf16[16,32,512]{2,1,0:T(8,128)(2,1)S(1)}, bf16[16,32,512]{2,1,0:T(8,128)(2,1)}, u32[]{:S(2)}) %copy-start) | copy-done | bytes 524312
  1.8 0.0 copy-start.1
  1.8 0.0 copy-start.5
  1.8 1.6 %coarse.1 = (bf16[16,32,4,128]{3,2,1,0:T(4,128)(2,1)}, bf16[16,4,128]{2,1,0:T(4,128)(2,1)S(1)}, bf16[16,4,128]{2,1,0:T(4,128)(2,1)S(1)}, bf16[32,4,128]{2,1,0:T(4,128)(2,1)S(1)}, bf16[32,4,128]{2,1,0:T(4,128)(2,1)S(1)}) custom-call(s32[2]{0:T(128)S(1)} %pad_add_fusion.odd, bf16[512,512]{1,0:T(8,128)(2,1)S(1)} %bitcast.18), custom_call_target="tpu_custom_call" | custom-call | tf_op jit(solution)/shard_map/coarse/pallas_call | solution.py:416
  3.4 8.6 %all-to-all-start = ((bf16[16,32,4,128]{3,2,1,0:T(4,128)(2,1)}), bf16[16,32,4,128]{3,2,1,0:T(4,128)(2,1)S(1)}, u32[]{:S(2)}, u32[]{:S(2)}) async-start(bf16[16,32,4,128]{3,2,1,0:T(4,128)(2,1)} %get-tuple-element.26), calls=%async_computation | async-start | bytes 1048576 | tf_op jit(solution)/shard_map/all_to_all | solution.py:460
  12.0 1.4 %collective-permute-start = (bf16[16,4,128]{2,1,0:T(4,128)(2,1)S(1)}, bf16[16,4,128]{2,1,0:T(4,128)(2,1)S(1)}, u32[]{:S(2)}, u32[]{:S(2)}) collective-permute-start(bf16[16,4,128]{2,1,0:T(4,128)(2,1)S(1)} %get-tuple-element.27), channel_id=1, source_target_pairs={{0,1},{2,3},{4,5},{6,7},{8,9},{10,11},{12,13},{14,15},{1,0},{3,2},... | collective-permute-start | bytes 49160 | tf_op jit(solution)/shard_map/ppermute | solution.py:458
  13.3 3.9 %collective-permute-start.1 = (bf16[16,4,128]{2,1,0:T(4,128)(2,1)S(1)}, bf16[16,4,128]{2,1,0:T(4,128)(2,1)S(1)}, u32[]{:S(2)}, u32[]{:S(2)}) collective-permute-start(bf16[16,4,128]{2,1,0:T(4,128)(2,1)S(1)} %get-tuple-element.28), channel_id=1, source_target_pairs={{1,2},{3,4},{5,6},{7,8},{9,10},{11,12},{13,14},{15,0},{2,1},{4,3},... | collective-permute-start | bytes 49160 | tf_op jit(solution)/shard_map/ppermute | solution.py:459
  17.3 0.1 iota_compare_fusion.1
  17.3 0.8 %bitcast_reduce_fusion = (s32[16]{0:T(128)S(1)}, pred[2048]{0:T(1024)(128)(4,1)S(1)}) fusion(s32[2048]{0:T(1024)} %param.14), kind=kLoop, calls=%fused_computation.53 | loop fusion | flops 6128 | bytes 10304 | tf_op jit(solution)/shard_map/reduce_sum | solution.py:456
  18.2 0.7 %not_and_fusion = (pred[2048]{0:T(1024)(128)(4,1)S(1)}, pred[2048]{0:T(1024)(128)(4,1)S(1)}) fusion(pred[2048]{0:T(1024)(128)(4,1)S(1)} %get-tuple-element.51, s32[]{:T(128)S(6)} %mul.44, s32[]{:T(128)S(6)} %mul.43, s32[2048]{0:T(1024)} %param.13), kind=kLoop, calls=%fused_computation.70 | loop fusion | flops 71680 | bytes 14344 | tf_op jit(solution)/shard_map/and | solution.py:454
  18.9 0.8 %fusion.9 = (s32[2048]{0:T(1024)S(1)}, s32[2048]{0:T(1024)S(1)}) fusion(s32[2048]{0:T(1024)} %param.13, s32[]{:T(128)S(6)} %select_n.137, s32[]{:T(128)} %select_n.122, pred[2048]{0:T(1024)(128)(4,1)S(1)} %get-tuple-element.53, s32[]{:T(128)} %select_n.123, s32[]{:T(128)S(6)} %sub.72, s32[]{:T(128)S(6)} %sub.71, s32[]{:T(128)S(6)} %mul.44, s32[]{:T(128)S(6)} %mul.43), kind=kLoop, calls=%fused_computation.48 | loop fusion | flops 342016 | bytes 26652 | tf_op jit(solution)/shard_map/sub | solution.py:262
  19.7 0.6 %select_reduce_fusion.1 = s32[4,512]{1,0:T(4,128)S(1)} fusion(s32[4,512]{1,0:T(4,128)S(1)} %convert_element_type.8, pred[512,512]{1,0:T(8,128)(4,1)S(1)} %iota_compare_fusion.1), kind=kLoop, calls=%fused_computation.2 | loop fusion | flops 2095104 | bytes 278528 | tf_op jit(solution)/shard_map/reduce_sum | solution.py:261
  20.3 1.0 %select_reduce_fusion = s32[4,512]{1,0:T(4,128)S(1)} fusion(s32[4,512]{1,0:T(4,128)S(1)} %broadcast_in_dim.73, s32[4,512]{1,0:T(4,128)S(1)} %select_reduce_fusion.1, pred[4,512]{1,0:T(4,128)(4,1)S(1)} %reshape.60), kind=kLoop, calls=%fused_computation | loop fusion | flops 4192256 | bytes 26624 | tf_op jit(solution)/shard_map/reduce_sum | solution.py:264
  21.3 0.1 convert_reduce_fusion.far_count
  21.5 0.0 collective-permute-done.refs_0_
  21.5 1.0 %collective-permute-done.1.refs_1_ = bf16[16,4,128]{2,1,0:T(4,128)(2,1)S(1)} collective-permute-done((bf16[16,4,128]{2,1,0:T(4,128)(2,1)S(1)}, bf16[16,4,128]{2,1,0:T(4,128)(2,1)S(1)}, u32[]{:S(2)}, u32[]{:S(2)}) %collective-permute-start.1) | collective-permute-done | bytes 16416 | tf_op jit(solution)/shard_map/ppermute | solution.py:459
  22.5 0.0 all-to-all-done
  22.5 2.5 %collective-permute-start.2 = (bf16[512,4,128]{2,1,0:T(4,128)(2,1)S(1)}, bf16[512,4,128]{2,1,0:T(4,128)(2,1)S(1)}, u32[]{:S(2)}, u32[]{:S(2)}) collective-permute-start(bf16[512,4,128]{2,1,0:T(4,128)(2,1)S(1)} %bitcast.22), channel_id=1, source_target_pairs={{0,32},{1,33},{2,34},{3,35},{4,36},{5,37},{6,38},{7,39},{8,40},{9,... | collective-permute-start | bytes 1572872 | tf_op jit(solution)/shard_map/ppermute | solution.py:47
  25.0 1.2 %collective-permute-start.3 = (bf16[34,4,128]{2,1,0:T(4,128)(2,1)S(1)}, bf16[34,4,128]{2,1,0:T(4,128)(2,1)S(1)}, u32[]{:S(2)}, u32[]{:S(2)}) collective-permute-start(bf16[34,4,128]{2,1,0:T(4,128)(2,1)S(1)} %pad_maximum_fusion), channel_id=1, source_target_pairs={{0,16},{32,48},{64,80},{96,112},{16,0},{48,32},{80,64},{112,96},{1... | collective-permute-start | bytes 104456 | tf_op jit(solution)/shard_map/ppermute | solution.py:473
  26.2 3.0 %collective-permute-start.4 = (bf16[34,4,128]{2,1,0:T(4,128)(2,1)S(1)}, bf16[34,4,128]{2,1,0:T(4,128)(2,1)S(1)}, u32[]{:S(2)}, u32[]{:S(2)}) collective-permute-start(bf16[34,4,128]{2,1,0:T(4,128)(2,1)S(1)} %pad_maximum_fusion.1), channel_id=1, source_target_pairs={{16,32},{48,64},{80,96},{32,16},{64,48},{96,80},{17,33},{49,65},{8... | collective-permute-start | bytes 104456 | tf_op jit(solution)/shard_map/ppermute | solution.py:474
  29.2 0.0 copy-done.2
  29.2 0.0 copy-done.11
  29.3 0.0 copy-done.1
  29.3 0.0 copy-done.5
  29.3 0.0 copy-start.3
  29.3 1.6 %copy-done.3 = bf16[2048,512]{1,0:T(8,128)(2,1)S(1)} copy-done((bf16[2048,512]{1,0:T(8,128)(2,1)S(1)}, bf16[2048,512]{1,0:T(8,128)(2,1)}, u32[]{:S(2)}) %copy-start.3) | copy-done | bytes 2097176
  30.9 4.0 %early.1.refs_4_ = bf16[2048,512]{1,0:T(8,128)(2,1)S(1)} custom-call(s32[16]{0:T(128)S(1)} %copy-done.11, bf16[2048,512]{1,0:T(8,128)(2,1)S(1)} %copy-done.3, s32[4,4,128]{2,1,0:T(4,128)S(1)} %bitcast.28, bf16[512,512]{1,0:T(8,128)(2,1)S(1)} %bitcast.19, bf16[1536,512]{1,0:T(8,128)(2,1)S(1)} %copy-done.5, bf16[1536,512]{1,0:T(8,128)(2,1)S(1)} %copy-done.5), custom_call_target="tpu_custom_call" | custom-call | flops 3000000000 | bytes 10000000 | tf_op jit(solution)/shard_map/early/pallas_call | solution.py:279
  34.9 0.0 copy-start.4
  34.9 0.0 copy-start.6
  34.9 0.0 copy-start.7
  34.9 0.0 copy-start.8
  35.0 0.0 copy-start.9
  35.0 0.0 copy-start.10
  35.0 0.0 collective-permute-done.3.refs_2_
  35.0 0.0 collective-permute-done.4.refs_3_
  35.0 1.0 %collective-permute-start.6 = (bf16[512,4,128]{2,1,0:T(4,128)(2,1)S(1)}, bf16[512,4,128]{2,1,0:T(4,128)(2,1)S(1)}, u32[]{:S(2)}, u32[]{:S(2)}) collective-permute-start(bf16[512,4,128]{2,1,0:T(4,128)(2,1)S(1)} %bitcast.23), channel_id=1, source_target_pairs={{0,96},{1,97},{2,98},{3,99},{4,100},{5,101},{6,102},{7,103},{8,104... | collective-permute-start | bytes 1572872 | tf_op jit(solution)/shard_map/ppermute | solution.py:47
  36.0 0.0 collective-permute-done.2.refs_1_
  36.0 1.8 %collective-permute-start.5 = (bf16[512,4,128]{2,1,0:T(4,128)(2,1)S(1)}, bf16[512,4,128]{2,1,0:T(4,128)(2,1)S(1)}, u32[]{:S(2)}, u32[]{:S(2)}) collective-permute-start(bf16[512,4,128]{2,1,0:T(4,128)(2,1)S(1)} %collective-permute-done.2.refs_1_), channel_id=1, source_target_pairs={{0,32},{1,33},{2,34},{3,35},{4,36},{5,37},{6,38},{7,39},{8,40},{9,... | collective-permute-start | bytes 1572872 | tf_op jit(solution)/shard_map/ppermute | solution.py:47
  37.8 0.0 collective-permute-start.7
  37.8 0.5 collective-permute-start.8
  38.3 5.9 %near.1.refs_8_ = bf16[2048,512]{1,0:T(8,128)(2,1)S(1)} custom-call(s32[2048]{0:T(1024)S(1)} %get-tuple-element.41.near_index, bf16[512,512]{1,0:T(8,128)(2,1)S(1)} %bitcast.20, bf16[16,4,128]{2,1,0:T(4,128)(2,1)S(1)} %collective-permute-done.refs_0_, bf16[16,4,128]{2,1,0:T(4,128)(2,1)S(1)} %collective-permute-done.1.refs_1_, ...), custom_call_target="tpu_custom_call" | custom-call | flops 2000000000 | bytes 8000000 | tf_op jit(solution)/shard_map/near/pallas_call | solution.py:301
  44.1 3.3 %collective-permute-done.6.refs_2_ = bf16[512,4,128]{2,1,0:T(4,128)(2,1)S(1)} collective-permute-done((bf16[512,4,128]{2,1,0:T(4,128)(2,1)S(1)}, bf16[512,4,128]{2,1,0:T(4,128)(2,1)S(1)}, u32[]{:S(2)}, u32[]{:S(2)}) %collective-permute-start.6) | collective-permute-done | bytes 524320 | tf_op jit(solution)/shard_map/ppermute | solution.py:47
  47.4 1.9 %collective-permute-done.5.refs_3_ = bf16[512,4,128]{2,1,0:T(4,128)(2,1)S(1)} collective-permute-done((bf16[512,4,128]{2,1,0:T(4,128)(2,1)S(1)}, bf16[512,4,128]{2,1,0:T(4,128)(2,1)S(1)}, u32[]{:S(2)}, u32[]{:S(2)}) %collective-permute-start.5) | collective-permute-done | bytes 524320 | tf_op jit(solution)/shard_map/ppermute | solution.py:47
  49.3 1.3 %collective-permute-start.9 = (bf16[512,4,128]{2,1,0:T(4,128)(2,1)S(1)}, bf16[512,4,128]{2,1,0:T(4,128)(2,1)S(1)}, u32[]{:S(2)}, u32[]{:S(2)}) collective-permute-start(bf16[512,4,128]{2,1,0:T(4,128)(2,1)S(1)} %collective-permute-done.6.refs_2_), channel_id=1, source_target_pairs={{0,16},{1,17},{2,18},{3,19},{4,20},{5,21},{6,22},{7,23},{8,24},{9,... | collective-permute-start | bytes 1572872 | tf_op jit(solution)/shard_map/ppermute | solution.py:43
  50.6 0.0 collective-permute-start.10
  50.6 0.0 collective-permute-done.7.refs_4_
  50.6 0.0 collective-permute-done.8.refs_5_
  50.6 1.5 %collective-permute-done.9.refs_6_ = bf16[512,4,128]{2,1,0:T(4,128)(2,1)S(1)} collective-permute-done((bf16[512,4,128]{2,1,0:T(4,128)(2,1)S(1)}, bf16[512,4,128]{2,1,0:T(4,128)(2,1)S(1)}, u32[]{:S(2)}, u32[]{:S(2)}) %collective-permute-start.9) | collective-permute-done | bytes 524320 | tf_op jit(solution)/shard_map/ppermute | solution.py:43
  52.2 0.7 %collective-permute-done.10.refs_7_ = bf16[512,4,128]{2,1,0:T(4,128)(2,1)S(1)} collective-permute-done((bf16[512,4,128]{2,1,0:T(4,128)(2,1)S(1)}, bf16[512,4,128]{2,1,0:T(4,128)(2,1)S(1)}, u32[]{:S(2)}, u32[]{:S(2)}) %collective-permute-start.10) | collective-permute-done | bytes 524320 | tf_op jit(solution)/shard_map/ppermute | solution.py:43
  52.9 0.0 copy-done.4
  52.9 0.0 copy-done.6
  52.9 0.0 copy-done.7
  52.9 0.0 copy-done.8
  52.9 0.0 copy-done.9
  52.9 0.0 copy-done.10
  52.9 10.0 %late.1 = (bf16[2048,512]{1,0:T(8,128)(2,1)}, bf16[512,512]{1,0:T(8,128)(2,1)}) custom-call(s32[2048]{0:T(1024)S(1)} %bitcast.30, s32[4]{0:T(128)S(1)} %convert_reduce_fusion.far_count, s32[16]{0:T(128)S(1)} %copy-done.11, s32[16]{0:T(128)S(1)} %get-tuple-element.31.lives, bf16[512,4,128]{2,1,0:T(4,128)(2,1)S(1)} %bitcast.25, ...), custom_call_target="tpu_custom_call" | custom-call | flops 4000000000 | bytes 14000000 | tf_op jit(solution)/shard_map/late/pallas_call | solution.py:345
  (9 shorter events, 0.1 us)
Async XLA Ops:
  0.6 28.6 %copy-start.2 = (s32[2048]{0:T(1024)S(1)}, s32[2048]{0:T(1024)}, u32[]{:S(2)}) copy-start(s32[2048]{0:T(1024)} %param.14) | copy-start | bytes 24580
  0.6 28.6 %copy-start.11 = (s32[16]{0:T(128)S(1)}, s32[16]{0:T(128)}, u32[]{:S(2)}) copy-start(s32[16]{0:T(128)} %tiles.2) | copy-start | bytes 196
  0.7 1.0 %copy-start = (bf16[16,32,512]{2,1,0:T(8,128)(2,1)S(1)}, bf16[16,32,512]{2,1,0:T(8,128)(2,1)}, u32[]{:S(2)}) copy-start(bf16[16,32,512]{2,1,0:T(8,128)(2,1)} %param.11) | copy-start | bytes 1572868
  1.8 27.5 %copy-start.1 = (bf16[16,32,512]{2,1,0:T(8,128)(2,1)S(1)}, bf16[16,32,512]{2,1,0:T(8,128)(2,1)}, u32[]{:S(2)}) copy-start(bf16[16,32,512]{2,1,0:T(8,128)(2,1)} %param.11) | copy-start | bytes 1572868
  1.8 27.5 %copy-start.5 = (bf16[1536,512]{1,0:T(8,128)(2,1)S(1)}, bf16[1536,512]{1,0:T(8,128)(2,1)}, u32[]{:S(2)}) copy-start(bf16[1536,512]{1,0:T(8,128)(2,1)} %refs_11_.1) | copy-start | bytes 4718596
  3.4 19.1 %all-to-all-start = ((bf16[16,32,4,128]{3,2,1,0:T(4,128)(2,1)}), bf16[16,32,4,128]{3,2,1,0:T(4,128)(2,1)S(1)}, u32[]{:S(2)}, u32[]{:S(2)}) async-start(bf16[16,32,4,128]{3,2,1,0:T(4,128)(2,1)} %get-tuple-element.26), calls=%async_computation | async-start | bytes 1048576 | tf_op jit(solution)/shard_map/all_to_all | solution.py:460
  12.0 9.5 %collective-permute-start = (bf16[16,4,128]{2,1,0:T(4,128)(2,1)S(1)}, bf16[16,4,128]{2,1,0:T(4,128)(2,1)S(1)}, u32[]{:S(2)}, u32[]{:S(2)}) collective-permute-start(bf16[16,4,128]{2,1,0:T(4,128)(2,1)S(1)} %get-tuple-element.27), channel_id=1, source_target_pairs={{0,1},{2,3},{4,5},{6,7},{8,9},{10,11},{12,13},{14,15},{1,0},{3,2},... | collective-permute-start | bytes 49160 | tf_op jit(solution)/shard_map/ppermute | solution.py:458
  13.3 9.1 %collective-permute-start.1 = (bf16[16,4,128]{2,1,0:T(4,128)(2,1)S(1)}, bf16[16,4,128]{2,1,0:T(4,128)(2,1)S(1)}, u32[]{:S(2)}, u32[]{:S(2)}) collective-permute-start(bf16[16,4,128]{2,1,0:T(4,128)(2,1)S(1)} %get-tuple-element.28), channel_id=1, source_target_pairs={{1,2},{3,4},{5,6},{7,8},{9,10},{11,12},{13,14},{15,0},{2,1},{4,3},... | collective-permute-start | bytes 49160 | tf_op jit(solution)/shard_map/ppermute | solution.py:459
  22.5 13.5 %collective-permute-start.2 = (bf16[512,4,128]{2,1,0:T(4,128)(2,1)S(1)}, bf16[512,4,128]{2,1,0:T(4,128)(2,1)S(1)}, u32[]{:S(2)}, u32[]{:S(2)}) collective-permute-start(bf16[512,4,128]{2,1,0:T(4,128)(2,1)S(1)} %bitcast.22), channel_id=1, source_target_pairs={{0,32},{1,33},{2,34},{3,35},{4,36},{5,37},{6,38},{7,39},{8,40},{9,... | collective-permute-start | bytes 1572872 | tf_op jit(solution)/shard_map/ppermute | solution.py:47
  25.0 10.0 %collective-permute-start.3 = (bf16[34,4,128]{2,1,0:T(4,128)(2,1)S(1)}, bf16[34,4,128]{2,1,0:T(4,128)(2,1)S(1)}, u32[]{:S(2)}, u32[]{:S(2)}) collective-permute-start(bf16[34,4,128]{2,1,0:T(4,128)(2,1)S(1)} %pad_maximum_fusion), channel_id=1, source_target_pairs={{0,16},{32,48},{64,80},{96,112},{16,0},{48,32},{80,64},{112,96},{1... | collective-permute-start | bytes 104456 | tf_op jit(solution)/shard_map/ppermute | solution.py:473
  26.2 8.8 %collective-permute-start.4 = (bf16[34,4,128]{2,1,0:T(4,128)(2,1)S(1)}, bf16[34,4,128]{2,1,0:T(4,128)(2,1)S(1)}, u32[]{:S(2)}, u32[]{:S(2)}) collective-permute-start(bf16[34,4,128]{2,1,0:T(4,128)(2,1)S(1)} %pad_maximum_fusion.1), channel_id=1, source_target_pairs={{16,32},{48,64},{80,96},{32,16},{64,48},{96,80},{17,33},{49,65},{8... | collective-permute-start | bytes 104456 | tf_op jit(solution)/shard_map/ppermute | solution.py:474
  29.3 1.6 %copy-start.3 = (bf16[2048,512]{1,0:T(8,128)(2,1)S(1)}, bf16[2048,512]{1,0:T(8,128)(2,1)}, u32[]{:S(2)}) copy-start(bf16[2048,512]{1,0:T(8,128)(2,1)} %refs_9_.1) | copy-start | bytes 6291460
  34.9 18.0 %copy-start.4 = (bf16[2048,512]{1,0:T(8,128)(2,1)S(1)}, bf16[2048,512]{1,0:T(8,128)(2,1)}, u32[]{:S(2)}) copy-start(bf16[2048,512]{1,0:T(8,128)(2,1)} %refs_9_.1) | copy-start | bytes 6291460
  34.9 18.0 %copy-start.6 = (bf16[1024,512]{1,0:T(8,128)(2,1)S(1)}, bf16[1024,512]{1,0:T(8,128)(2,1)}, u32[]{:S(2)}) copy-start(bf16[1024,512]{1,0:T(8,128)(2,1)} %refs_13_.1) | copy-start | bytes 3145732
  34.9 18.0 %copy-start.7 = (bf16[512,512]{1,0:T(8,128)(2,1)S(1)}, bf16[512,512]{1,0:T(8,128)(2,1)}, u32[]{:S(2)}) copy-start(bf16[512,512]{1,0:T(8,128)(2,1)} %refs_12_.1) | copy-start | bytes 1572868
  34.9 18.0 %copy-start.8 = (bf16[512,512]{1,0:T(8,128)(2,1)S(1)}, bf16[512,512]{1,0:T(8,128)(2,1)}, u32[]{:S(2)}) copy-start(bf16[512,512]{1,0:T(8,128)(2,1)} %refs_14_.1) | copy-start | bytes 1572868
  35.0 18.0 %copy-start.9 = (f32[512]{0:T(512)S(1)}, f32[512]{0:T(512)}, u32[]{:S(2)}) copy-start(f32[512]{0:T(512)} %param.18) | copy-start | bytes 6148
  35.0 18.0 %copy-start.10 = (f32[512]{0:T(512)S(1)}, f32[512]{0:T(512)}, u32[]{:S(2)}) copy-start(f32[512]{0:T(512)} %param.21) | copy-start | bytes 6148
  35.0 12.4 %collective-permute-start.6 = (bf16[512,4,128]{2,1,0:T(4,128)(2,1)S(1)}, bf16[512,4,128]{2,1,0:T(4,128)(2,1)S(1)}, u32[]{:S(2)}, u32[]{:S(2)}) collective-permute-start(bf16[512,4,128]{2,1,0:T(4,128)(2,1)S(1)} %bitcast.23), channel_id=1, source_target_pairs={{0,96},{1,97},{2,98},{3,99},{4,100},{5,101},{6,102},{7,103},{8,104... | collective-permute-start | bytes 1572872 | tf_op jit(solution)/shard_map/ppermute | solution.py:47
  36.0 13.3 %collective-permute-start.5 = (bf16[512,4,128]{2,1,0:T(4,128)(2,1)S(1)}, bf16[512,4,128]{2,1,0:T(4,128)(2,1)S(1)}, u32[]{:S(2)}, u32[]{:S(2)}) collective-permute-start(bf16[512,4,128]{2,1,0:T(4,128)(2,1)S(1)} %collective-permute-done.2.refs_1_), channel_id=1, source_target_pairs={{0,32},{1,33},{2,34},{3,35},{4,36},{5,37},{6,38},{7,39},{8,40},{9,... | collective-permute-start | bytes 1572872 | tf_op jit(solution)/shard_map/ppermute | solution.py:47
  37.8 12.9 %collective-permute-start.7 = (bf16[512,4,128]{2,1,0:T(4,128)(2,1)S(1)}, bf16[512,4,128]{2,1,0:T(4,128)(2,1)S(1)}, u32[]{:S(2)}, u32[]{:S(2)}) collective-permute-start(bf16[512,4,128]{2,1,0:T(4,128)(2,1)S(1)} %bitcast.24), channel_id=1, source_target_pairs={{0,16},{1,17},{2,18},{3,19},{4,20},{5,21},{6,22},{7,23},{8,24},{9,... | collective-permute-start | bytes 1572872 | tf_op jit(solution)/shard_map/ppermute | solution.py:43
  37.8 12.9 %collective-permute-start.8 = (bf16[512,4,128]{2,1,0:T(4,128)(2,1)S(1)}, bf16[512,4,128]{2,1,0:T(4,128)(2,1)S(1)}, u32[]{:S(2)}, u32[]{:S(2)}) collective-permute-start(bf16[512,4,128]{2,1,0:T(4,128)(2,1)S(1)} %collective-permute-done.2.refs_1_), channel_id=1, source_target_pairs={{0,16},{1,17},{2,18},{3,19},{4,20},{5,21},{6,22},{7,23},{8,24},{9,... | collective-permute-start | bytes 1572872 | tf_op jit(solution)/shard_map/ppermute | solution.py:43
  49.3 2.9 %collective-permute-start.9 = (bf16[512,4,128]{2,1,0:T(4,128)(2,1)S(1)}, bf16[512,4,128]{2,1,0:T(4,128)(2,1)S(1)}, u32[]{:S(2)}, u32[]{:S(2)}) collective-permute-start(bf16[512,4,128]{2,1,0:T(4,128)(2,1)S(1)} %collective-permute-done.6.refs_2_), channel_id=1, source_target_pairs={{0,16},{1,17},{2,18},{3,19},{4,20},{5,21},{6,22},{7,23},{8,24},{9,... | collective-permute-start | bytes 1572872 | tf_op jit(solution)/shard_map/ppermute | solution.py:43
  50.6 2.3 %collective-permute-start.10 = (bf16[512,4,128]{2,1,0:T(4,128)(2,1)S(1)}, bf16[512,4,128]{2,1,0:T(4,128)(2,1)S(1)}, u32[]{:S(2)}, u32[]{:S(2)}) collective-permute-start(bf16[512,4,128]{2,1,0:T(4,128)(2,1)S(1)} %collective-permute-done.5.refs_3_), channel_id=1, source_target_pairs={{0,16},{1,17},{2,18},{3,19},{4,20},{5,21},{6,22},{7,23},{8,24},{9,... | collective-permute-start | bytes 1572872 | tf_op jit(solution)/shard_map/ppermute | solution.py:43

commit v11 on v10

--- a/solution.py
+++ b/solution.py
@@ -474,9 +474,9 @@
     strip_b = lax.ppermute(
         wide(patch_rows - 1 - edge_row, row_b), "lat", pairs(1, lat_count, False)
     )
+    later, tiles, strip_a, strip_b = lax.optimization_barrier((plane, tiles, strip_a, strip_b))
+    behind = move(later, "x", (-1, 1))
     partial = early_call(tiles, edge_latent, recv_rows, own_rows, w_first)
-    later, partial, strip_a, strip_b = lax.optimization_barrier((plane, partial, strip_a, strip_b))
-    behind = move(later, "x", (-1, 1))
     ahead, partial = lax.optimization_barrier((ahead, partial))
     across = move(ahead, "x", (1, -1))
     rims = [side_a, side_b, strip_a, strip_b]

time: 63.6 us -> 62.8 us (0.987)
  waiting for transfers between devices: 8.4 us -> 6.23 us
  starting transfers between devices: 25.1 us -> 26.6 us
    ppermute x3, waiting for transfers between devices: 5.15 us -> 0.48 us  [move(): return lax.ppermute(value, ('lat', 'lon'), shift(axis, by_core))]
    ppermute x1, waiting for transfers between devices: 0.01 us -> 2.51 us  [per_device(): lax.ppermute(wide(patch_rows - 1 - edge_row, row_b), 'lat', pairs(1, lat_...]
    ppermute x4, starting transfers between devices: 1.85 us -> 3.28 us  [other_core(): return lax.ppermute(value, ('lat', 'lon'), pairs)]
where the time goes in v11:
time: 62.8 us; the launch traced here: 62.4 us
  starting transfers between devices  26.6 us (42%)
  Pallas kernels  21.5 us (34%)
  waiting for transfers between devices  6.23 us (10%)
  other arithmetic  4.29 us (7%)
  local copies, waits for them, and re-layouts  2.72 us (4%)
  between operations  1.07 us (2%)
    pallas_call x1, Pallas kernels, late_call(): pl.pallas_call(late_kernel, name='late', in_specs=[scalars] * 4 + [anywhe...  10 us
    all_to_all x1, starting transfers between devices, per_device(): lax.all_to_all(copies, 'lon', split_axis=0, concat_axis=0, tiled=True)  8.61 us
    pallas_call x1, Pallas kernels, near_call(): pl.pallas_call(near_kernel, name='near', grid_spec=pltpu.PrefetchScalarGr...  5.86 us
    ppermute x3, starting transfers between devices, move(): return lax.ppermute(value, ('lat', 'lon'), shift(axis, by_core))  5.22 us
    pallas_call x1, Pallas kernels, early_call(): pl.pallas_call(early_kernel, name='early', grid_spec=pltpu.PrefetchScalar...  4.04 us
    ppermute x1, starting transfers between devices, per_device(): side_b = lax.ppermute(col_b, 'lon', pairs(1, lon_count, True))  3.9 us
    ppermute x4, starting transfers between devices, other_core(): return lax.ppermute(value, ('lat', 'lon'), pairs)  3.28 us
    ppermute x1, starting transfers between devices, per_device(): lax.ppermute(wide(patch_rows - 1 - edge_row, row_b), 'lat', pairs(1, lat_...  3.02 us
  transfers between devices with their start and end apart: 12, of which 5 were waited for; matrix products, arithmetic and copies ran while one was open for 7% of the time, Pallas kernels for 16%

profile of v11, /device:TPU:1, one launch (start us, length us, event | category | flops | bytes accessed | tf_op | source)
XLA Modules:
  0.0 62.4 jit_solution(6433499277674207542)
XLA Ops:
  0.6 0.0 copy-start.2
  0.6 0.0 copy-start.11
  0.7 0.1 pad_add_fusion.odd
  0.7 0.0 copy-start
  0.8 1.0 %copy-done = bf16[16,32,512]{2,1,0:T(8,128)(2,1)S(1)} copy-done((bf16[16,32,512]{2,1,0:T(8,128)(2,1)S(1)}, bf16[16,32,512]{2,1,0:T(8,128)(2,1)}, u32[]{:S(2)}) %copy-start) | copy-done | bytes 524312
  1.8 0.0 copy-start.1
  1.8 0.0 copy-start.5
  1.8 1.6 %coarse.1 = (bf16[16,32,4,128]{3,2,1,0:T(4,128)(2,1)}, bf16[16,4,128]{2,1,0:T(4,128)(2,1)S(1)}, bf16[16,4,128]{2,1,0:T(4,128)(2,1)S(1)}, bf16[32,4,128]{2,1,0:T(4,128)(2,1)S(1)}, bf16[32,4,128]{2,1,0:T(4,128)(2,1)S(1)}) custom-call(s32[2]{0:T(128)S(1)} %pad_add_fusion.odd, bf16[512,512]{1,0:T(8,128)(2,1)S(1)} %bitcast.18), custom_call_target="tpu_custom_call" | custom-call | tf_op jit(solution)/shard_map/coarse/pallas_call | solution.py:416
  3.4 8.6 %all-to-all-start = ((bf16[16,32,4,128]{3,2,1,0:T(4,128)(2,1)}), bf16[16,32,4,128]{3,2,1,0:T(4,128)(2,1)S(1)}, u32[]{:S(2)}, u32[]{:S(2)}) async-start(bf16[16,32,4,128]{3,2,1,0:T(4,128)(2,1)} %get-tuple-element.26), calls=%async_computation | async-start | bytes 1048576 | tf_op jit(solution)/shard_map/all_to_all | solution.py:460
  12.0 1.4 %collective-permute-start = (bf16[16,4,128]{2,1,0:T(4,128)(2,1)S(1)}, bf16[16,4,128]{2,1,0:T(4,128)(2,1)S(1)}, u32[]{:S(2)}, u32[]{:S(2)}) collective-permute-start(bf16[16,4,128]{2,1,0:T(4,128)(2,1)S(1)} %get-tuple-element.27), channel_id=1, source_target_pairs={{0,1},{2,3},{4,5},{6,7},{8,9},{10,11},{12,13},{14,15},{1,0},{3,2},... | collective-permute-start | bytes 49160 | tf_op jit(solution)/shard_map/ppermute | solution.py:458
  13.3 3.9 %collective-permute-start.1 = (bf16[16,4,128]{2,1,0:T(4,128)(2,1)S(1)}, bf16[16,4,128]{2,1,0:T(4,128)(2,1)S(1)}, u32[]{:S(2)}, u32[]{:S(2)}) collective-permute-start(bf16[16,4,128]{2,1,0:T(4,128)(2,1)S(1)} %get-tuple-element.28), channel_id=1, source_target_pairs={{1,2},{3,4},{5,6},{7,8},{9,10},{11,12},{13,14},{15,0},{2,1},{4,3},... | collective-permute-start | bytes 49160 | tf_op jit(solution)/shard_map/ppermute | solution.py:459
  17.3 0.1 iota_compare_fusion.1
  17.3 0.8 %bitcast_reduce_fusion = (s32[16]{0:T(128)S(1)}, pred[2048]{0:T(1024)(128)(4,1)S(1)}) fusion(s32[2048]{0:T(1024)} %param.14), kind=kLoop, calls=%fused_computation.53 | loop fusion | flops 6128 | bytes 10304 | tf_op jit(solution)/shard_map/reduce_sum | solution.py:456
  18.2 0.7 %not_and_fusion = (pred[2048]{0:T(1024)(128)(4,1)S(1)}, pred[2048]{0:T(1024)(128)(4,1)S(1)}) fusion(pred[2048]{0:T(1024)(128)(4,1)S(1)} %get-tuple-element.51, s32[]{:T(128)S(6)} %mul.44, s32[]{:T(128)S(6)} %mul.43, s32[2048]{0:T(1024)} %param.13), kind=kLoop, calls=%fused_computation.70 | loop fusion | flops 71680 | bytes 14344 | tf_op jit(solution)/shard_map/and | solution.py:454
  18.9 0.8 %fusion.9 = (s32[2048]{0:T(1024)S(1)}, s32[2048]{0:T(1024)S(1)}) fusion(s32[2048]{0:T(1024)} %param.13, s32[]{:T(128)S(6)} %select_n.137, s32[]{:T(128)} %select_n.122, pred[2048]{0:T(1024)(128)(4,1)S(1)} %get-tuple-element.53, s32[]{:T(128)} %select_n.123, s32[]{:T(128)S(6)} %sub.72, s32[]{:T(128)S(6)} %sub.71, s32[]{:T(128)S(6)} %mul.44, s32[]{:T(128)S(6)} %mul.43), kind=kLoop, calls=%fused_computation.48 | loop fusion | flops 342016 | bytes 26652 | tf_op jit(solution)/shard_map/sub | solution.py:262
  19.7 0.6 %select_reduce_fusion.1 = s32[4,512]{1,0:T(4,128)S(1)} fusion(s32[4,512]{1,0:T(4,128)S(1)} %convert_element_type.8, pred[512,512]{1,0:T(8,128)(4,1)S(1)} %iota_compare_fusion.1), kind=kLoop, calls=%fused_computation.2 | loop fusion | flops 2095104 | bytes 278528 | tf_op jit(solution)/shard_map/reduce_sum | solution.py:261
  20.3 1.0 %select_reduce_fusion = s32[4,512]{1,0:T(4,128)S(1)} fusion(s32[4,512]{1,0:T(4,128)S(1)} %broadcast_in_dim.73, s32[4,512]{1,0:T(4,128)S(1)} %select_reduce_fusion.1, pred[4,512]{1,0:T(4,128)(4,1)S(1)} %reshape.60), kind=kLoop, calls=%fused_computation | loop fusion | flops 4192256 | bytes 26624 | tf_op jit(solution)/shard_map/reduce_sum | solution.py:264
  21.3 0.1 convert_reduce_fusion.far_count
  21.5 0.0 collective-permute-done.refs_0_
  21.5 1.0 %collective-permute-done.1.refs_1_ = bf16[16,4,128]{2,1,0:T(4,128)(2,1)S(1)} collective-permute-done((bf16[16,4,128]{2,1,0:T(4,128)(2,1)S(1)}, bf16[16,4,128]{2,1,0:T(4,128)(2,1)S(1)}, u32[]{:S(2)}, u32[]{:S(2)}) %collective-permute-start.1) | collective-permute-done | bytes 16416 | tf_op jit(solution)/shard_map/ppermute | solution.py:459
  22.5 0.0 all-to-all-done
  22.5 2.5 %collective-permute-start.2 = (bf16[512,4,128]{2,1,0:T(4,128)(2,1)S(1)}, bf16[512,4,128]{2,1,0:T(4,128)(2,1)S(1)}, u32[]{:S(2)}, u32[]{:S(2)}) collective-permute-start(bf16[512,4,128]{2,1,0:T(4,128)(2,1)S(1)} %bitcast.22), channel_id=1, source_target_pairs={{0,32},{1,33},{2,34},{3,35},{4,36},{5,37},{6,38},{7,39},{8,40},{9,... | collective-permute-start | bytes 1572872 | tf_op jit(solution)/shard_map/ppermute | solution.py:47
  25.0 1.2 %collective-permute-start.3 = (bf16[34,4,128]{2,1,0:T(4,128)(2,1)S(1)}, bf16[34,4,128]{2,1,0:T(4,128)(2,1)S(1)}, u32[]{:S(2)}, u32[]{:S(2)}) collective-permute-start(bf16[34,4,128]{2,1,0:T(4,128)(2,1)S(1)} %pad_maximum_fusion), channel_id=1, source_target_pairs={{0,16},{32,48},{64,80},{96,112},{16,0},{48,32},{80,64},{112,96},{1... | collective-permute-start | bytes 104456 | tf_op jit(solution)/shard_map/ppermute | solution.py:473
  26.2 3.0 %collective-permute-start.4 = (bf16[34,4,128]{2,1,0:T(4,128)(2,1)S(1)}, bf16[34,4,128]{2,1,0:T(4,128)(2,1)S(1)}, u32[]{:S(2)}, u32[]{:S(2)}) collective-permute-start(bf16[34,4,128]{2,1,0:T(4,128)(2,1)S(1)} %pad_maximum_fusion.1), channel_id=1, source_target_pairs={{16,32},{48,64},{80,96},{32,16},{64,48},{96,80},{17,33},{49,65},{8... | collective-permute-start | bytes 104456 | tf_op jit(solution)/shard_map/ppermute | solution.py:474
  29.2 0.0 collective-permute-done.3.refs_2_
  29.2 2.5 %collective-permute-done.4.refs_3_ = bf16[34,4,128]{2,1,0:T(4,128)(2,1)S(1)} collective-permute-done((bf16[34,4,128]{2,1,0:T(4,128)(2,1)S(1)}, bf16[34,4,128]{2,1,0:T(4,128)(2,1)S(1)}, u32[]{:S(2)}, u32[]{:S(2)}) %collective-permute-start.4) | collective-permute-done | bytes 34848 | tf_op jit(solution)/shard_map/ppermute | solution.py:474
  31.8 1.2 %collective-permute-start.6 = (bf16[512,4,128]{2,1,0:T(4,128)(2,1)S(1)}, bf16[512,4,128]{2,1,0:T(4,128)(2,1)S(1)}, u32[]{:S(2)}, u32[]{:S(2)}) collective-permute-start(bf16[512,4,128]{2,1,0:T(4,128)(2,1)S(1)} %bitcast.23), channel_id=1, source_target_pairs={{0,96},{1,97},{2,98},{3,99},{4,100},{5,101},{6,102},{7,103},{8,104... | collective-permute-start | bytes 1572872 | tf_op jit(solution)/shard_map/ppermute | solution.py:47
  33.0 0.0 copy-done.2
  33.0 0.0 copy-done.11
  33.0 0.0 copy-done.1
  33.0 0.0 copy-done.5
  33.0 0.0 copy-start.3
  33.0 1.6 %copy-done.3 = bf16[2048,512]{1,0:T(8,128)(2,1)S(1)} copy-done((bf16[2048,512]{1,0:T(8,128)(2,1)S(1)}, bf16[2048,512]{1,0:T(8,128)(2,1)}, u32[]{:S(2)}) %copy-start.3) | copy-done | bytes 2097176
  34.6 4.0 %early.1.refs_4_ = bf16[2048,512]{1,0:T(8,128)(2,1)S(1)} custom-call(s32[16]{0:T(128)S(1)} %copy-done.11, bf16[2048,512]{1,0:T(8,128)(2,1)S(1)} %copy-done.3, s32[4,4,128]{2,1,0:T(4,128)S(1)} %bitcast.28, bf16[512,512]{1,0:T(8,128)(2,1)S(1)} %bitcast.19, bf16[1536,512]{1,0:T(8,128)(2,1)S(1)} %copy-done.5, bf16[1536,512]{1,0:T(8,128)(2,1)S(1)} %copy-done.5), custom_call_target="tpu_custom_call" | custom-call | flops 3000000000 | bytes 10000000 | tf_op jit(solution)/shard_map/early/pallas_call | solution.py:279
  38.6 0.0 copy-start.4
  38.6 0.0 copy-start.6
  38.6 0.0 copy-start.7
  38.7 0.0 copy-start.8
  38.7 0.0 copy-start.9
  38.7 0.0 copy-start.10
  38.7 0.0 collective-permute-done.2.refs_1_
  38.7 1.5 %collective-permute-start.5 = (bf16[512,4,128]{2,1,0:T(4,128)(2,1)S(1)}, bf16[512,4,128]{2,1,0:T(4,128)(2,1)S(1)}, u32[]{:S(2)}, u32[]{:S(2)}) collective-permute-start(bf16[512,4,128]{2,1,0:T(4,128)(2,1)S(1)} %collective-permute-done.2.refs_1_), channel_id=1, source_target_pairs={{0,32},{1,33},{2,34},{3,35},{4,36},{5,37},{6,38},{7,39},{8,40},{9,... | collective-permute-start | bytes 1572872 | tf_op jit(solution)/shard_map/ppermute | solution.py:47
  40.2 0.0 collective-permute-start.7
  40.2 0.5 collective-permute-start.8
  40.7 5.9 %near.1.refs_8_ = bf16[2048,512]{1,0:T(8,128)(2,1)S(1)} custom-call(s32[2048]{0:T(1024)S(1)} %get-tuple-element.41.near_index, bf16[512,512]{1,0:T(8,128)(2,1)S(1)} %bitcast.20, bf16[16,4,128]{2,1,0:T(4,128)(2,1)S(1)} %collective-permute-done.refs_0_, bf16[16,4,128]{2,1,0:T(4,128)(2,1)S(1)} %collective-permute-done.1.refs_1_, ...), custom_call_target="tpu_custom_call" | custom-call | flops 2000000000 | bytes 8000000 | tf_op jit(solution)/shard_map/near/pallas_call | solution.py:301
  46.6 0.0 collective-permute-done.6.refs_2_
  46.6 0.5 collective-permute-done.5.refs_3_
  47.1 2.8 %collective-permute-start.9 = (bf16[512,4,128]{2,1,0:T(4,128)(2,1)S(1)}, bf16[512,4,128]{2,1,0:T(4,128)(2,1)S(1)}, u32[]{:S(2)}, u32[]{:S(2)}) collective-permute-start(bf16[512,4,128]{2,1,0:T(4,128)(2,1)S(1)} %collective-permute-done.6.refs_2_), channel_id=1, source_target_pairs={{0,16},{1,17},{2,18},{3,19},{4,20},{5,21},{6,22},{7,23},{8,24},{9,... | collective-permute-start | bytes 1572872 | tf_op jit(solution)/shard_map/ppermute | solution.py:43
  49.9 0.0 collective-permute-start.10
  49.9 0.0 collective-permute-done.7.refs_4_
  49.9 0.0 collective-permute-done.8.refs_5_
  49.9 1.5 %collective-permute-done.9.refs_6_ = bf16[512,4,128]{2,1,0:T(4,128)(2,1)S(1)} collective-permute-done((bf16[512,4,128]{2,1,0:T(4,128)(2,1)S(1)}, bf16[512,4,128]{2,1,0:T(4,128)(2,1)S(1)}, u32[]{:S(2)}, u32[]{:S(2)}) %collective-permute-start.9) | collective-permute-done | bytes 524320 | tf_op jit(solution)/shard_map/ppermute | solution.py:43
  51.4 0.7 %collective-permute-done.10.refs_7_ = bf16[512,4,128]{2,1,0:T(4,128)(2,1)S(1)} collective-permute-done((bf16[512,4,128]{2,1,0:T(4,128)(2,1)S(1)}, bf16[512,4,128]{2,1,0:T(4,128)(2,1)S(1)}, u32[]{:S(2)}, u32[]{:S(2)}) %collective-permute-start.10) | collective-permute-done | bytes 524320 | tf_op jit(solution)/shard_map/ppermute | solution.py:43
  52.2 0.0 copy-done.4
  52.2 0.0 copy-done.6
  52.2 0.0 copy-done.7
  52.2 0.0 copy-done.8
  52.2 0.0 copy-done.9
  52.2 0.0 copy-done.10
  52.2 10.0 %late.1 = (bf16[2048,512]{1,0:T(8,128)(2,1)}, bf16[512,512]{1,0:T(8,128)(2,1)}) custom-call(s32[2048]{0:T(1024)S(1)} %bitcast.30, s32[4]{0:T(128)S(1)} %convert_reduce_fusion.far_count, s32[16]{0:T(128)S(1)} %copy-done.11, s32[16]{0:T(128)S(1)} %get-tuple-element.31.lives, bf16[512,4,128]{2,1,0:T(4,128)(2,1)S(1)} %bitcast.25, ...), custom_call_target="tpu_custom_call" | custom-call | flops 4000000000 | bytes 14000000 | tf_op jit(solution)/shard_map/late/pallas_call | solution.py:345
  (9 shorter events, 0.1 us)
Async XLA Ops:
  0.6 32.3 %copy-start.2 = (s32[2048]{0:T(1024)S(1)}, s32[2048]{0:T(1024)}, u32[]{:S(2)}) copy-start(s32[2048]{0:T(1024)} %param.14) | copy-start | bytes 24580
  0.6 32.3 %copy-start.11 = (s32[16]{0:T(128)S(1)}, s32[16]{0:T(128)}, u32[]{:S(2)}) copy-start(s32[16]{0:T(128)} %tiles.2) | copy-start | bytes 196
  0.7 1.0 %copy-start = (bf16[16,32,512]{2,1,0:T(8,128)(2,1)S(1)}, bf16[16,32,512]{2,1,0:T(8,128)(2,1)}, u32[]{:S(2)}) copy-start(bf16[16,32,512]{2,1,0:T(8,128)(2,1)} %param.11) | copy-start | bytes 1572868
  1.8 31.2 %copy-start.1 = (bf16[16,32,512]{2,1,0:T(8,128)(2,1)S(1)}, bf16[16,32,512]{2,1,0:T(8,128)(2,1)}, u32[]{:S(2)}) copy-start(bf16[16,32,512]{2,1,0:T(8,128)(2,1)} %param.11) | copy-start | bytes 1572868
  1.8 31.2 %copy-start.5 = (bf16[1536,512]{1,0:T(8,128)(2,1)S(1)}, bf16[1536,512]{1,0:T(8,128)(2,1)}, u32[]{:S(2)}) copy-start(bf16[1536,512]{1,0:T(8,128)(2,1)} %refs_11_.1) | copy-start | bytes 4718596
  3.4 19.1 %all-to-all-start = ((bf16[16,32,4,128]{3,2,1,0:T(4,128)(2,1)}), bf16[16,32,4,128]{3,2,1,0:T(4,128)(2,1)S(1)}, u32[]{:S(2)}, u32[]{:S(2)}) async-start(bf16[16,32,4,128]{3,2,1,0:T(4,128)(2,1)} %get-tuple-element.26), calls=%async_computation | async-start | bytes 1048576 | tf_op jit(solution)/shard_map/all_to_all | solution.py:460
  12.0 9.5 %collective-permute-start = (bf16[16,4,128]{2,1,0:T(4,128)(2,1)S(1)}, bf16[16,4,128]{2,1,0:T(4,128)(2,1)S(1)}, u32[]{:S(2)}, u32[]{:S(2)}) collective-permute-start(bf16[16,4,128]{2,1,0:T(4,128)(2,1)S(1)} %get-tuple-element.27), channel_id=1, source_target_pairs={{0,1},{2,3},{4,5},{6,7},{8,9},{10,11},{12,13},{14,15},{1,0},{3,2},... | collective-permute-start | bytes 49160 | tf_op jit(solution)/shard_map/ppermute | solution.py:458
  13.3 9.1 %collective-permute-start.1 = (bf16[16,4,128]{2,1,0:T(4,128)(2,1)S(1)}, bf16[16,4,128]{2,1,0:T(4,128)(2,1)S(1)}, u32[]{:S(2)}, u32[]{:S(2)}) collective-permute-start(bf16[16,4,128]{2,1,0:T(4,128)(2,1)S(1)} %get-tuple-element.28), channel_id=1, source_target_pairs={{1,2},{3,4},{5,6},{7,8},{9,10},{11,12},{13,14},{15,0},{2,1},{4,3},... | collective-permute-start | bytes 49160 | tf_op jit(solution)/shard_map/ppermute | solution.py:459
  22.5 16.2 %collective-permute-start.2 = (bf16[512,4,128]{2,1,0:T(4,128)(2,1)S(1)}, bf16[512,4,128]{2,1,0:T(4,128)(2,1)S(1)}, u32[]{:S(2)}, u32[]{:S(2)}) collective-permute-start(bf16[512,4,128]{2,1,0:T(4,128)(2,1)S(1)} %bitcast.22), channel_id=1, source_target_pairs={{0,32},{1,33},{2,34},{3,35},{4,36},{5,37},{6,38},{7,39},{8,40},{9,... | collective-permute-start | bytes 1572872 | tf_op jit(solution)/shard_map/ppermute | solution.py:47
  25.0 4.2 %collective-permute-start.3 = (bf16[34,4,128]{2,1,0:T(4,128)(2,1)S(1)}, bf16[34,4,128]{2,1,0:T(4,128)(2,1)S(1)}, u32[]{:S(2)}, u32[]{:S(2)}) collective-permute-start(bf16[34,4,128]{2,1,0:T(4,128)(2,1)S(1)} %pad_maximum_fusion), channel_id=1, source_target_pairs={{0,16},{32,48},{64,80},{96,112},{16,0},{48,32},{80,64},{112,96},{1... | collective-permute-start | bytes 104456 | tf_op jit(solution)/shard_map/ppermute | solution.py:473
  26.2 5.5 %collective-permute-start.4 = (bf16[34,4,128]{2,1,0:T(4,128)(2,1)S(1)}, bf16[34,4,128]{2,1,0:T(4,128)(2,1)S(1)}, u32[]{:S(2)}, u32[]{:S(2)}) collective-permute-start(bf16[34,4,128]{2,1,0:T(4,128)(2,1)S(1)} %pad_maximum_fusion.1), channel_id=1, source_target_pairs={{16,32},{48,64},{80,96},{32,16},{64,48},{96,80},{17,33},{49,65},{8... | collective-permute-start | bytes 104456 | tf_op jit(solution)/shard_map/ppermute | solution.py:474
  31.8 14.9 %collective-permute-start.6 = (bf16[512,4,128]{2,1,0:T(4,128)(2,1)S(1)}, bf16[512,4,128]{2,1,0:T(4,128)(2,1)S(1)}, u32[]{:S(2)}, u32[]{:S(2)}) collective-permute-start(bf16[512,4,128]{2,1,0:T(4,128)(2,1)S(1)} %bitcast.23), channel_id=1, source_target_pairs={{0,96},{1,97},{2,98},{3,99},{4,100},{5,101},{6,102},{7,103},{8,104... | collective-permute-start | bytes 1572872 | tf_op jit(solution)/shard_map/ppermute | solution.py:47
  33.0 1.6 %copy-start.3 = (bf16[2048,512]{1,0:T(8,128)(2,1)S(1)}, bf16[2048,512]{1,0:T(8,128)(2,1)}, u32[]{:S(2)}) copy-start(bf16[2048,512]{1,0:T(8,128)(2,1)} %refs_9_.1) | copy-start | bytes 6291460
  38.6 13.5 %copy-start.4 = (bf16[2048,512]{1,0:T(8,128)(2,1)S(1)}, bf16[2048,512]{1,0:T(8,128)(2,1)}, u32[]{:S(2)}) copy-start(bf16[2048,512]{1,0:T(8,128)(2,1)} %refs_9_.1) | copy-start | bytes 6291460
  38.6 13.5 %copy-start.6 = (bf16[1024,512]{1,0:T(8,128)(2,1)S(1)}, bf16[1024,512]{1,0:T(8,128)(2,1)}, u32[]{:S(2)}) copy-start(bf16[1024,512]{1,0:T(8,128)(2,1)} %refs_13_.1) | copy-start | bytes 3145732
  38.6 13.5 %copy-start.7 = (bf16[512,512]{1,0:T(8,128)(2,1)S(1)}, bf16[512,512]{1,0:T(8,128)(2,1)}, u32[]{:S(2)}) copy-start(bf16[512,512]{1,0:T(8,128)(2,1)} %refs_12_.1) | copy-start | bytes 1572868
  38.7 13.5 %copy-start.8 = (bf16[512,512]{1,0:T(8,128)(2,1)S(1)}, bf16[512,512]{1,0:T(8,128)(2,1)}, u32[]{:S(2)}) copy-start(bf16[512,512]{1,0:T(8,128)(2,1)} %refs_14_.1) | copy-start | bytes 1572868
  38.7 13.5 %copy-start.9 = (f32[512]{0:T(512)S(1)}, f32[512]{0:T(512)}, u32[]{:S(2)}) copy-start(f32[512]{0:T(512)} %param.18) | copy-start | bytes 6148
  38.7 13.5 %copy-start.10 = (f32[512]{0:T(512)S(1)}, f32[512]{0:T(512)}, u32[]{:S(2)}) copy-start(f32[512]{0:T(512)} %param.21) | copy-start | bytes 6148
  38.7 8.4 %collective-permute-start.5 = (bf16[512,4,128]{2,1,0:T(4,128)(2,1)S(1)}, bf16[512,4,128]{2,1,0:T(4,128)(2,1)S(1)}, u32[]{:S(2)}, u32[]{:S(2)}) collective-permute-start(bf16[512,4,128]{2,1,0:T(4,128)(2,1)S(1)} %collective-permute-done.2.refs_1_), channel_id=1, source_target_pairs={{0,32},{1,33},{2,34},{3,35},{4,36},{5,37},{6,38},{7,39},{8,40},{9,... | collective-permute-start | bytes 1572872 | tf_op jit(solution)/shard_map/ppermute | solution.py:47
  40.2 9.6 %collective-permute-start.7 = (bf16[512,4,128]{2,1,0:T(4,128)(2,1)S(1)}, bf16[512,4,128]{2,1,0:T(4,128)(2,1)S(1)}, u32[]{:S(2)}, u32[]{:S(2)}) collective-permute-start(bf16[512,4,128]{2,1,0:T(4,128)(2,1)S(1)} %bitcast.24), channel_id=1, source_target_pairs={{0,16},{1,17},{2,18},{3,19},{4,20},{5,21},{6,22},{7,23},{8,24},{9,... | collective-permute-start | bytes 1572872 | tf_op jit(solution)/shard_map/ppermute | solution.py:43
  40.2 9.6 %collective-permute-start.8 = (bf16[512,4,128]{2,1,0:T(4,128)(2,1)S(1)}, bf16[512,4,128]{2,1,0:T(4,128)(2,1)S(1)}, u32[]{:S(2)}, u32[]{:S(2)}) collective-permute-start(bf16[512,4,128]{2,1,0:T(4,128)(2,1)S(1)} %collective-permute-done.2.refs_1_), channel_id=1, source_target_pairs={{0,16},{1,17},{2,18},{3,19},{4,20},{5,21},{6,22},{7,23},{8,24},{9,... | collective-permute-start | bytes 1572872 | tf_op jit(solution)/shard_map/ppermute | solution.py:43
  47.1 4.3 %collective-permute-start.9 = (bf16[512,4,128]{2,1,0:T(4,128)(2,1)S(1)}, bf16[512,4,128]{2,1,0:T(4,128)(2,1)S(1)}, u32[]{:S(2)}, u32[]{:S(2)}) collective-permute-start(bf16[512,4,128]{2,1,0:T(4,128)(2,1)S(1)} %collective-permute-done.6.refs_2_), channel_id=1, source_target_pairs={{0,16},{1,17},{2,18},{3,19},{4,20},{5,21},{6,22},{7,23},{8,24},{9,... | collective-permute-start | bytes 1572872 | tf_op jit(solution)/shard_map/ppermute | solution.py:43
  49.9 2.3 %collective-permute-start.10 = (bf16[512,4,128]{2,1,0:T(4,128)(2,1)S(1)}, bf16[512,4,128]{2,1,0:T(4,128)(2,1)S(1)}, u32[]{:S(2)}, u32[]{:S(2)}) collective-permute-start(bf16[512,4,128]{2,1,0:T(4,128)(2,1)S(1)} %collective-permute-done.5.refs_3_), channel_id=1, source_target_pairs={{0,16},{1,17},{2,18},{3,19},{4,20},{5,21},{6,22},{7,23},{8,24},{9,... | collective-permute-start | bytes 1572872 | tf_op jit(solution)/shard_map/ppermute | solution.py:43

commit v12 on v11

--- a/solution.py
+++ b/solution.py
@@ -476,9 +476,9 @@
     )
     later, tiles, strip_a, strip_b = lax.optimization_barrier((plane, tiles, strip_a, strip_b))
     behind = move(later, "x", (-1, 1))
+    ahead, tiles, strip_a, strip_b = lax.optimization_barrier((ahead, tiles, strip_a, strip_b))
+    across = move(ahead, "x", (1, -1))
     partial = early_call(tiles, edge_latent, recv_rows, own_rows, w_first)
-    ahead, partial = lax.optimization_barrier((ahead, partial))
-    across = move(ahead, "x", (1, -1))
     rims = [side_a, side_b, strip_a, strip_b]
     pre = near_call(near_index, own_rows, rims, partial, w_first)
     across, behind, pre = lax.optimization_barrier((across, behind, pre))

time: 62.8 us -> 60.6 us (0.965)
  starting transfers between devices: 26.6 us -> 25.1 us
    ppermute x4, starting transfers between devices: 3.28 us -> 1.82 us  [other_core(): return lax.ppermute(value, ('lat', 'lon'), pairs)]
  transfers between devices with their start and end apart: 12 -> 12, of which waited for: 5 -> 4; matrix products, arithmetic and copies ran while one was open for 7% -> 7% of each run, Pallas kernels for 16% -> 16%
where the time goes in v12:
time: 60.6 us; the launch traced here: 60.3 us
  starting transfers between devices  25.1 us (41%)
  Pallas kernels  21.5 us (35%)
  waiting for transfers between devices  5.67 us (9%)
  other arithmetic  4.29 us (7%)
  local copies, waits for them, and re-layouts  2.72 us (4%)
  between operations  1.08 us (2%)
    pallas_call x1, Pallas kernels, late_call(): pl.pallas_call(late_kernel, name='late', in_specs=[scalars] * 4 + [anywhe...  9.99 us
    all_to_all x1, starting transfers between devices, per_device(): lax.all_to_all(copies, 'lon', split_axis=0, concat_axis=0, tiled=True)  8.61 us
    pallas_call x1, Pallas kernels, near_call(): pl.pallas_call(near_kernel, name='near', grid_spec=pltpu.PrefetchScalarGr...  5.87 us
    ppermute x3, starting transfers between devices, move(): return lax.ppermute(value, ('lat', 'lon'), shift(axis, by_core))  5.16 us
    pallas_call x1, Pallas kernels, early_call(): pl.pallas_call(early_kernel, name='early', grid_spec=pltpu.PrefetchScalar...  4.04 us
    ppermute x1, starting transfers between devices, per_device(): side_b = lax.ppermute(col_b, 'lon', pairs(1, lon_count, True))  3.9 us
    ppermute x1, starting transfers between devices, per_device(): lax.ppermute(wide(patch_rows - 1 - edge_row, row_b), 'lat', pairs(1, lat_...  3.02 us
    unnamed x25, local copies, waits for them, and re-layouts  2.69 us
  transfers between devices with their start and end apart: 12, of which 4 were waited for; matrix products, arithmetic and copies ran while one was open for 7% of the time, Pallas kernels for 16%

profile of v12, /device:TPU:1, one launch (start us, length us, event | category | flops | bytes accessed | tf_op | source)
XLA Modules:
  0.0 60.3 jit_solution(9259977392362533583)
XLA Ops:
  0.6 0.0 copy-start.2
  0.6 0.0 copy-start.11
  0.7 0.1 pad_add_fusion.odd
  0.7 0.0 copy-start
  0.8 1.0 %copy-done = bf16[16,32,512]{2,1,0:T(8,128)(2,1)S(1)} copy-done((bf16[16,32,512]{2,1,0:T(8,128)(2,1)S(1)}, bf16[16,32,512]{2,1,0:T(8,128)(2,1)}, u32[]{:S(2)}) %copy-start) | copy-done | bytes 524312
  1.8 0.0 copy-start.1
  1.8 0.0 copy-start.5
  1.8 1.6 %coarse.1 = (bf16[16,32,4,128]{3,2,1,0:T(4,128)(2,1)}, bf16[16,4,128]{2,1,0:T(4,128)(2,1)S(1)}, bf16[16,4,128]{2,1,0:T(4,128)(2,1)S(1)}, bf16[32,4,128]{2,1,0:T(4,128)(2,1)S(1)}, bf16[32,4,128]{2,1,0:T(4,128)(2,1)S(1)}) custom-call(s32[2]{0:T(128)S(1)} %pad_add_fusion.odd, bf16[512,512]{1,0:T(8,128)(2,1)S(1)} %bitcast.18), custom_call_target="tpu_custom_call" | custom-call | tf_op jit(solution)/shard_map/coarse/pallas_call | solution.py:416
  3.4 8.6 %all-to-all-start = ((bf16[16,32,4,128]{3,2,1,0:T(4,128)(2,1)}), bf16[16,32,4,128]{3,2,1,0:T(4,128)(2,1)S(1)}, u32[]{:S(2)}, u32[]{:S(2)}) async-start(bf16[16,32,4,128]{3,2,1,0:T(4,128)(2,1)} %get-tuple-element.28), calls=%async_computation | async-start | bytes 1048576 | tf_op jit(solution)/shard_map/all_to_all | solution.py:460
  12.0 1.4 %collective-permute-start = (bf16[16,4,128]{2,1,0:T(4,128)(2,1)S(1)}, bf16[16,4,128]{2,1,0:T(4,128)(2,1)S(1)}, u32[]{:S(2)}, u32[]{:S(2)}) collective-permute-start(bf16[16,4,128]{2,1,0:T(4,128)(2,1)S(1)} %get-tuple-element.29), channel_id=1, source_target_pairs={{0,1},{2,3},{4,5},{6,7},{8,9},{10,11},{12,13},{14,15},{1,0},{3,2},... | collective-permute-start | bytes 49160 | tf_op jit(solution)/shard_map/ppermute | solution.py:458
  13.3 3.9 %collective-permute-start.1 = (bf16[16,4,128]{2,1,0:T(4,128)(2,1)S(1)}, bf16[16,4,128]{2,1,0:T(4,128)(2,1)S(1)}, u32[]{:S(2)}, u32[]{:S(2)}) collective-permute-start(bf16[16,4,128]{2,1,0:T(4,128)(2,1)S(1)} %get-tuple-element.30), channel_id=1, source_target_pairs={{1,2},{3,4},{5,6},{7,8},{9,10},{11,12},{13,14},{15,0},{2,1},{4,3},... | collective-permute-start | bytes 49160 | tf_op jit(solution)/shard_map/ppermute | solution.py:459
  17.3 0.1 iota_compare_fusion.1
  17.3 0.8 %bitcast_reduce_fusion = (s32[16]{0:T(128)S(1)}, pred[2048]{0:T(1024)(128)(4,1)S(1)}) fusion(s32[2048]{0:T(1024)} %param.14), kind=kLoop, calls=%fused_computation.53 | loop fusion | flops 6128 | bytes 10304 | tf_op jit(solution)/shard_map/reduce_sum | solution.py:456
  18.2 0.7 %not_and_fusion = (pred[2048]{0:T(1024)(128)(4,1)S(1)}, pred[2048]{0:T(1024)(128)(4,1)S(1)}) fusion(pred[2048]{0:T(1024)(128)(4,1)S(1)} %get-tuple-element.55, s32[]{:T(128)S(6)} %mul.44, s32[]{:T(128)S(6)} %mul.43, s32[2048]{0:T(1024)} %param.13), kind=kLoop, calls=%fused_computation.70 | loop fusion | flops 71680 | bytes 14344 | tf_op jit(solution)/shard_map/and | solution.py:454
  18.9 0.8 %fusion.9 = (s32[2048]{0:T(1024)S(1)}, s32[2048]{0:T(1024)S(1)}) fusion(s32[2048]{0:T(1024)} %param.13, s32[]{:T(128)S(6)} %select_n.137, s32[]{:T(128)} %select_n.122, pred[2048]{0:T(1024)(128)(4,1)S(1)} %get-tuple-element.57, s32[]{:T(128)} %select_n.123, s32[]{:T(128)S(6)} %sub.72, s32[]{:T(128)S(6)} %sub.71, s32[]{:T(128)S(6)} %mul.44, s32[]{:T(128)S(6)} %mul.43), kind=kLoop, calls=%fused_computation.48 | loop fusion | flops 342016 | bytes 26652 | tf_op jit(solution)/shard_map/sub | solution.py:262
  19.7 0.6 %select_reduce_fusion.1 = s32[4,512]{1,0:T(4,128)S(1)} fusion(s32[4,512]{1,0:T(4,128)S(1)} %convert_element_type.8, pred[512,512]{1,0:T(8,128)(4,1)S(1)} %iota_compare_fusion.1), kind=kLoop, calls=%fused_computation.2 | loop fusion | flops 2095104 | bytes 278528 | tf_op jit(solution)/shard_map/reduce_sum | solution.py:261
  20.3 1.0 %select_reduce_fusion = s32[4,512]{1,0:T(4,128)S(1)} fusion(s32[4,512]{1,0:T(4,128)S(1)} %broadcast_in_dim.73, s32[4,512]{1,0:T(4,128)S(1)} %select_reduce_fusion.1, pred[4,512]{1,0:T(4,128)(4,1)S(1)} %reshape.60), kind=kLoop, calls=%fused_computation | loop fusion | flops 4192256 | bytes 26624 | tf_op jit(solution)/shard_map/reduce_sum | solution.py:264
  21.3 0.1 convert_reduce_fusion.far_count
  21.5 0.0 collective-permute-done.refs_0_
  21.5 1.0 %collective-permute-done.1.refs_1_ = bf16[16,4,128]{2,1,0:T(4,128)(2,1)S(1)} collective-permute-done((bf16[16,4,128]{2,1,0:T(4,128)(2,1)S(1)}, bf16[16,4,128]{2,1,0:T(4,128)(2,1)S(1)}, u32[]{:S(2)}, u32[]{:S(2)}) %collective-permute-start.1) | collective-permute-done | bytes 16416 | tf_op jit(solution)/shard_map/ppermute | solution.py:459
  22.5 0.0 all-to-all-done
  22.5 2.5 %collective-permute-start.2 = (bf16[512,4,128]{2,1,0:T(4,128)(2,1)S(1)}, bf16[512,4,128]{2,1,0:T(4,128)(2,1)S(1)}, u32[]{:S(2)}, u32[]{:S(2)}) collective-permute-start(bf16[512,4,128]{2,1,0:T(4,128)(2,1)S(1)} %bitcast.22), channel_id=1, source_target_pairs={{0,32},{1,33},{2,34},{3,35},{4,36},{5,37},{6,38},{7,39},{8,40},{9,... | collective-permute-start | bytes 1572872 | tf_op jit(solution)/shard_map/ppermute | solution.py:47
  25.0 1.2 %collective-permute-start.3 = (bf16[34,4,128]{2,1,0:T(4,128)(2,1)S(1)}, bf16[34,4,128]{2,1,0:T(4,128)(2,1)S(1)}, u32[]{:S(2)}, u32[]{:S(2)}) collective-permute-start(bf16[34,4,128]{2,1,0:T(4,128)(2,1)S(1)} %pad_maximum_fusion), channel_id=1, source_target_pairs={{0,16},{32,48},{64,80},{96,112},{16,0},{48,32},{80,64},{112,96},{1... | collective-permute-start | bytes 104456 | tf_op jit(solution)/shard_map/ppermute | solution.py:473
  26.2 3.0 %collective-permute-start.4 = (bf16[34,4,128]{2,1,0:T(4,128)(2,1)S(1)}, bf16[34,4,128]{2,1,0:T(4,128)(2,1)S(1)}, u32[]{:S(2)}, u32[]{:S(2)}) collective-permute-start(bf16[34,4,128]{2,1,0:T(4,128)(2,1)S(1)} %pad_maximum_fusion.1), channel_id=1, source_target_pairs={{16,32},{48,64},{80,96},{32,16},{64,48},{96,80},{17,33},{49,65},{8... | collective-permute-start | bytes 104456 | tf_op jit(solution)/shard_map/ppermute | solution.py:474
  29.2 0.0 collective-permute-done.3.refs_2_
  29.2 2.5 %collective-permute-done.4.refs_3_ = bf16[34,4,128]{2,1,0:T(4,128)(2,1)S(1)} collective-permute-done((bf16[34,4,128]{2,1,0:T(4,128)(2,1)S(1)}, bf16[34,4,128]{2,1,0:T(4,128)(2,1)S(1)}, u32[]{:S(2)}, u32[]{:S(2)}) %collective-permute-start.4) | collective-permute-done | bytes 34848 | tf_op jit(solution)/shard_map/ppermute | solution.py:474
  31.8 1.2 %collective-permute-start.6 = (bf16[512,4,128]{2,1,0:T(4,128)(2,1)S(1)}, bf16[512,4,128]{2,1,0:T(4,128)(2,1)S(1)}, u32[]{:S(2)}, u32[]{:S(2)}) collective-permute-start(bf16[512,4,128]{2,1,0:T(4,128)(2,1)S(1)} %bitcast.23), channel_id=1, source_target_pairs={{0,96},{1,97},{2,98},{3,99},{4,100},{5,101},{6,102},{7,103},{8,104... | collective-permute-start | bytes 1572872 | tf_op jit(solution)/shard_map/ppermute | solution.py:47
  33.0 0.0 collective-permute-done.2.refs_1_
  33.0 1.5 %collective-permute-start.5 = (bf16[512,4,128]{2,1,0:T(4,128)(2,1)S(1)}, bf16[512,4,128]{2,1,0:T(4,128)(2,1)S(1)}, u32[]{:S(2)}, u32[]{:S(2)}) collective-permute-start(bf16[512,4,128]{2,1,0:T(4,128)(2,1)S(1)} %collective-permute-done.2.refs_1_), channel_id=1, source_target_pairs={{0,32},{1,33},{2,34},{3,35},{4,36},{5,37},{6,38},{7,39},{8,40},{9,... | collective-permute-start | bytes 1572872 | tf_op jit(solution)/shard_map/ppermute | solution.py:47
  34.4 1.2 %collective-permute-start.7 = (bf16[512,4,128]{2,1,0:T(4,128)(2,1)S(1)}, bf16[512,4,128]{2,1,0:T(4,128)(2,1)S(1)}, u32[]{:S(2)}, u32[]{:S(2)}) collective-permute-start(bf16[512,4,128]{2,1,0:T(4,128)(2,1)S(1)} %bitcast.24), channel_id=1, source_target_pairs={{0,16},{1,17},{2,18},{3,19},{4,20},{5,21},{6,22},{7,23},{8,24},{9,... | collective-permute-start | bytes 1572872 | tf_op jit(solution)/shard_map/ppermute | solution.py:43
  35.6 0.0 collective-permute-start.8
  35.6 0.0 copy-done.2
  35.6 0.0 copy-done.11
  35.6 0.0 copy-done.1
  35.6 0.0 copy-done.5
  35.6 0.0 copy-start.3
  35.6 1.6 %copy-done.3 = bf16[2048,512]{1,0:T(8,128)(2,1)S(1)} copy-done((bf16[2048,512]{1,0:T(8,128)(2,1)S(1)}, bf16[2048,512]{1,0:T(8,128)(2,1)}, u32[]{:S(2)}) %copy-start.3) | copy-done | bytes 2097176
  37.2 4.0 %early.1.refs_4_ = bf16[2048,512]{1,0:T(8,128)(2,1)S(1)} custom-call(s32[16]{0:T(128)S(1)} %copy-done.11, bf16[2048,512]{1,0:T(8,128)(2,1)S(1)} %copy-done.3, s32[4,4,128]{2,1,0:T(4,128)S(1)} %bitcast.28, bf16[512,512]{1,0:T(8,128)(2,1)S(1)} %bitcast.19, bf16[1536,512]{1,0:T(8,128)(2,1)S(1)} %copy-done.5, bf16[1536,512]{1,0:T(8,128)(2,1)S(1)} %copy-done.5), custom_call_target="tpu_custom_call" | custom-call | flops 3000000000 | bytes 10000000 | tf_op jit(solution)/shard_map/early/pallas_call | solution.py:279
  41.3 0.0 copy-start.4
  41.3 0.0 copy-start.6
  41.3 0.0 copy-start.7
  41.3 0.0 copy-start.8
  41.3 0.0 copy-start.9
  41.3 0.0 copy-start.10
  41.3 5.9 %near.1.refs_8_ = bf16[2048,512]{1,0:T(8,128)(2,1)S(1)} custom-call(s32[2048]{0:T(1024)S(1)} %get-tuple-element.45.near_index, bf16[512,512]{1,0:T(8,128)(2,1)S(1)} %bitcast.20, bf16[16,4,128]{2,1,0:T(4,128)(2,1)S(1)} %collective-permute-done.refs_0_, bf16[16,4,128]{2,1,0:T(4,128)(2,1)S(1)} %collective-permute-done.1.refs_1_, ...), custom_call_target="tpu_custom_call" | custom-call | flops 2000000000 | bytes 8000000 | tf_op jit(solution)/shard_map/near/pallas_call | solution.py:301
  47.2 0.0 collective-permute-done.6.refs_2_
  47.2 0.0 collective-permute-done.5.refs_3_
  47.2 0.6 collective-permute-start.9
  47.8 0.1 collective-permute-start.10
  47.9 0.0 collective-permute-done.7.refs_4_
  47.9 0.0 collective-permute-done.8.refs_5_
  47.9 1.4 %collective-permute-done.9.refs_6_ = bf16[512,4,128]{2,1,0:T(4,128)(2,1)S(1)} collective-permute-done((bf16[512,4,128]{2,1,0:T(4,128)(2,1)S(1)}, bf16[512,4,128]{2,1,0:T(4,128)(2,1)S(1)}, u32[]{:S(2)}, u32[]{:S(2)}) %collective-permute-start.9) | collective-permute-done | bytes 524320 | tf_op jit(solution)/shard_map/ppermute | solution.py:43
  49.4 0.7 %collective-permute-done.10.refs_7_ = bf16[512,4,128]{2,1,0:T(4,128)(2,1)S(1)} collective-permute-done((bf16[512,4,128]{2,1,0:T(4,128)(2,1)S(1)}, bf16[512,4,128]{2,1,0:T(4,128)(2,1)S(1)}, u32[]{:S(2)}, u32[]{:S(2)}) %collective-permute-start.10) | collective-permute-done | bytes 524320 | tf_op jit(solution)/shard_map/ppermute | solution.py:43
  50.1 0.0 copy-done.4
  50.1 0.0 copy-done.6
  50.1 0.0 copy-done.7
  50.1 0.0 copy-done.8
  50.1 0.0 copy-done.9
  50.1 0.0 copy-done.10
  50.1 10.0 %late.1 = (bf16[2048,512]{1,0:T(8,128)(2,1)}, bf16[512,512]{1,0:T(8,128)(2,1)}) custom-call(s32[2048]{0:T(1024)S(1)} %bitcast.30, s32[4]{0:T(128)S(1)} %convert_reduce_fusion.far_count, s32[16]{0:T(128)S(1)} %copy-done.11, s32[16]{0:T(128)S(1)} %get-tuple-element.33.lives, bf16[512,4,128]{2,1,0:T(4,128)(2,1)S(1)} %bitcast.25, ...), custom_call_target="tpu_custom_call" | custom-call | flops 4000000000 | bytes 14000000 | tf_op jit(solution)/shard_map/late/pallas_call | solution.py:345
  (9 shorter events, 0.1 us)
Async XLA Ops:
  0.6 35.0 %copy-start.2 = (s32[2048]{0:T(1024)S(1)}, s32[2048]{0:T(1024)}, u32[]{:S(2)}) copy-start(s32[2048]{0:T(1024)} %param.14) | copy-start | bytes 24580
  0.6 35.0 %copy-start.11 = (s32[16]{0:T(128)S(1)}, s32[16]{0:T(128)}, u32[]{:S(2)}) copy-start(s32[16]{0:T(128)} %tiles.2) | copy-start | bytes 196
  0.7 1.0 %copy-start = (bf16[16,32,512]{2,1,0:T(8,128)(2,1)S(1)}, bf16[16,32,512]{2,1,0:T(8,128)(2,1)}, u32[]{:S(2)}) copy-start(bf16[16,32,512]{2,1,0:T(8,128)(2,1)} %param.11) | copy-start | bytes 1572868
  1.8 33.8 %copy-start.1 = (bf16[16,32,512]{2,1,0:T(8,128)(2,1)S(1)}, bf16[16,32,512]{2,1,0:T(8,128)(2,1)}, u32[]{:S(2)}) copy-start(bf16[16,32,512]{2,1,0:T(8,128)(2,1)} %param.11) | copy-start | bytes 1572868
  1.8 33.8 %copy-start.5 = (bf16[1536,512]{1,0:T(8,128)(2,1)S(1)}, bf16[1536,512]{1,0:T(8,128)(2,1)}, u32[]{:S(2)}) copy-start(bf16[1536,512]{1,0:T(8,128)(2,1)} %refs_11_.1) | copy-start | bytes 4718596
  3.4 19.1 %all-to-all-start = ((bf16[16,32,4,128]{3,2,1,0:T(4,128)(2,1)}), bf16[16,32,4,128]{3,2,1,0:T(4,128)(2,1)S(1)}, u32[]{:S(2)}, u32[]{:S(2)}) async-start(bf16[16,32,4,128]{3,2,1,0:T(4,128)(2,1)} %get-tuple-element.28), calls=%async_computation | async-start | bytes 1048576 | tf_op jit(solution)/shard_map/all_to_all | solution.py:460
  12.0 9.5 %collective-permute-start = (bf16[16,4,128]{2,1,0:T(4,128)(2,1)S(1)}, bf16[16,4,128]{2,1,0:T(4,128)(2,1)S(1)}, u32[]{:S(2)}, u32[]{:S(2)}) collective-permute-start(bf16[16,4,128]{2,1,0:T(4,128)(2,1)S(1)} %get-tuple-element.29), channel_id=1, source_target_pairs={{0,1},{2,3},{4,5},{6,7},{8,9},{10,11},{12,13},{14,15},{1,0},{3,2},... | collective-permute-start | bytes 49160 | tf_op jit(solution)/shard_map/ppermute | solution.py:458
  13.3 9.1 %collective-permute-start.1 = (bf16[16,4,128]{2,1,0:T(4,128)(2,1)S(1)}, bf16[16,4,128]{2,1,0:T(4,128)(2,1)S(1)}, u32[]{:S(2)}, u32[]{:S(2)}) collective-permute-start(bf16[16,4,128]{2,1,0:T(4,128)(2,1)S(1)} %get-tuple-element.30), channel_id=1, source_target_pairs={{1,2},{3,4},{5,6},{7,8},{9,10},{11,12},{13,14},{15,0},{2,1},{4,3},... | collective-permute-start | bytes 49160 | tf_op jit(solution)/shard_map/ppermute | solution.py:459
  22.5 10.5 %collective-permute-start.2 = (bf16[512,4,128]{2,1,0:T(4,128)(2,1)S(1)}, bf16[512,4,128]{2,1,0:T(4,128)(2,1)S(1)}, u32[]{:S(2)}, u32[]{:S(2)}) collective-permute-start(bf16[512,4,128]{2,1,0:T(4,128)(2,1)S(1)} %bitcast.22), channel_id=1, source_target_pairs={{0,32},{1,33},{2,34},{3,35},{4,36},{5,37},{6,38},{7,39},{8,40},{9,... | collective-permute-start | bytes 1572872 | tf_op jit(solution)/shard_map/ppermute | solution.py:47
  25.0 4.2 %collective-permute-start.3 = (bf16[34,4,128]{2,1,0:T(4,128)(2,1)S(1)}, bf16[34,4,128]{2,1,0:T(4,128)(2,1)S(1)}, u32[]{:S(2)}, u32[]{:S(2)}) collective-permute-start(bf16[34,4,128]{2,1,0:T(4,128)(2,1)S(1)} %pad_maximum_fusion), channel_id=1, source_target_pairs={{0,16},{32,48},{64,80},{96,112},{16,0},{48,32},{80,64},{112,96},{1... | collective-permute-start | bytes 104456 | tf_op jit(solution)/shard_map/ppermute | solution.py:473
  26.2 5.5 %collective-permute-start.4 = (bf16[34,4,128]{2,1,0:T(4,128)(2,1)S(1)}, bf16[34,4,128]{2,1,0:T(4,128)(2,1)S(1)}, u32[]{:S(2)}, u32[]{:S(2)}) collective-permute-start(bf16[34,4,128]{2,1,0:T(4,128)(2,1)S(1)} %pad_maximum_fusion.1), channel_id=1, source_target_pairs={{16,32},{48,64},{80,96},{32,16},{64,48},{96,80},{17,33},{49,65},{8... | collective-permute-start | bytes 104456 | tf_op jit(solution)/shard_map/ppermute | solution.py:474
  31.8 15.5 %collective-permute-start.6 = (bf16[512,4,128]{2,1,0:T(4,128)(2,1)S(1)}, bf16[512,4,128]{2,1,0:T(4,128)(2,1)S(1)}, u32[]{:S(2)}, u32[]{:S(2)}) collective-permute-start(bf16[512,4,128]{2,1,0:T(4,128)(2,1)S(1)} %bitcast.23), channel_id=1, source_target_pairs={{0,96},{1,97},{2,98},{3,99},{4,100},{5,101},{6,102},{7,103},{8,104... | collective-permute-start | bytes 1572872 | tf_op jit(solution)/shard_map/ppermute | solution.py:47
  33.0 14.3 %collective-permute-start.5 = (bf16[512,4,128]{2,1,0:T(4,128)(2,1)S(1)}, bf16[512,4,128]{2,1,0:T(4,128)(2,1)S(1)}, u32[]{:S(2)}, u32[]{:S(2)}) collective-permute-start(bf16[512,4,128]{2,1,0:T(4,128)(2,1)S(1)} %collective-permute-done.2.refs_1_), channel_id=1, source_target_pairs={{0,32},{1,33},{2,34},{3,35},{4,36},{5,37},{6,38},{7,39},{8,40},{9,... | collective-permute-start | bytes 1572872 | tf_op jit(solution)/shard_map/ppermute | solution.py:47
  34.4 13.5 %collective-permute-start.7 = (bf16[512,4,128]{2,1,0:T(4,128)(2,1)S(1)}, bf16[512,4,128]{2,1,0:T(4,128)(2,1)S(1)}, u32[]{:S(2)}, u32[]{:S(2)}) collective-permute-start(bf16[512,4,128]{2,1,0:T(4,128)(2,1)S(1)} %bitcast.24), channel_id=1, source_target_pairs={{0,16},{1,17},{2,18},{3,19},{4,20},{5,21},{6,22},{7,23},{8,24},{9,... | collective-permute-start | bytes 1572872 | tf_op jit(solution)/shard_map/ppermute | solution.py:43
  35.6 12.3 %collective-permute-start.8 = (bf16[512,4,128]{2,1,0:T(4,128)(2,1)S(1)}, bf16[512,4,128]{2,1,0:T(4,128)(2,1)S(1)}, u32[]{:S(2)}, u32[]{:S(2)}) collective-permute-start(bf16[512,4,128]{2,1,0:T(4,128)(2,1)S(1)} %collective-permute-done.2.refs_1_), channel_id=1, source_target_pairs={{0,16},{1,17},{2,18},{3,19},{4,20},{5,21},{6,22},{7,23},{8,24},{9,... | collective-permute-start | bytes 1572872 | tf_op jit(solution)/shard_map/ppermute | solution.py:43
  35.6 1.6 %copy-start.3 = (bf16[2048,512]{1,0:T(8,128)(2,1)S(1)}, bf16[2048,512]{1,0:T(8,128)(2,1)}, u32[]{:S(2)}) copy-start(bf16[2048,512]{1,0:T(8,128)(2,1)} %refs_9_.1) | copy-start | bytes 6291460
  41.3 8.8 %copy-start.4 = (bf16[2048,512]{1,0:T(8,128)(2,1)S(1)}, bf16[2048,512]{1,0:T(8,128)(2,1)}, u32[]{:S(2)}) copy-start(bf16[2048,512]{1,0:T(8,128)(2,1)} %refs_9_.1) | copy-start | bytes 6291460
  41.3 8.8 %copy-start.6 = (bf16[1024,512]{1,0:T(8,128)(2,1)S(1)}, bf16[1024,512]{1,0:T(8,128)(2,1)}, u32[]{:S(2)}) copy-start(bf16[1024,512]{1,0:T(8,128)(2,1)} %refs_13_.1) | copy-start | bytes 3145732
  41.3 8.8 %copy-start.7 = (bf16[512,512]{1,0:T(8,128)(2,1)S(1)}, bf16[512,512]{1,0:T(8,128)(2,1)}, u32[]{:S(2)}) copy-start(bf16[512,512]{1,0:T(8,128)(2,1)} %refs_12_.1) | copy-start | bytes 1572868
  41.3 8.8 %copy-start.8 = (bf16[512,512]{1,0:T(8,128)(2,1)S(1)}, bf16[512,512]{1,0:T(8,128)(2,1)}, u32[]{:S(2)}) copy-start(bf16[512,512]{1,0:T(8,128)(2,1)} %refs_14_.1) | copy-start | bytes 1572868
  41.3 8.8 %copy-start.9 = (f32[512]{0:T(512)S(1)}, f32[512]{0:T(512)}, u32[]{:S(2)}) copy-start(f32[512]{0:T(512)} %param.18) | copy-start | bytes 6148
  41.3 8.8 %copy-start.10 = (f32[512]{0:T(512)S(1)}, f32[512]{0:T(512)}, u32[]{:S(2)}) copy-start(f32[512]{0:T(512)} %param.21) | copy-start | bytes 6148
  47.2 2.1 %collective-permute-start.9 = (bf16[512,4,128]{2,1,0:T(4,128)(2,1)S(1)}, bf16[512,4,128]{2,1,0:T(4,128)(2,1)S(1)}, u32[]{:S(2)}, u32[]{:S(2)}) collective-permute-start(bf16[512,4,128]{2,1,0:T(4,128)(2,1)S(1)} %collective-permute-done.6.refs_2_), channel_id=1, source_target_pairs={{0,16},{1,17},{2,18},{3,19},{4,20},{5,21},{6,22},{7,23},{8,24},{9,... | collective-permute-start | bytes 1572872 | tf_op jit(solution)/shard_map/ppermute | solution.py:43
  47.8 2.3 %collective-permute-start.10 = (bf16[512,4,128]{2,1,0:T(4,128)(2,1)S(1)}, bf16[512,4,128]{2,1,0:T(4,128)(2,1)S(1)}, u32[]{:S(2)}, u32[]{:S(2)}) collective-permute-start(bf16[512,4,128]{2,1,0:T(4,128)(2,1)S(1)} %collective-permute-done.5.refs_3_), channel_id=1, source_target_pairs={{0,16},{1,17},{2,18},{3,19},{4,20},{5,21},{6,22},{7,23},{8,24},{9,... | collective-permute-start | bytes 1572872 | tf_op jit(solution)/shard_map/ppermute | solution.py:43

commit v13 on v12

--- a/solution.py
+++ b/solution.py
@@ -478,7 +478,8 @@
     behind = move(later, "x", (-1, 1))
     ahead, tiles, strip_a, strip_b = lax.optimization_barrier((ahead, tiles, strip_a, strip_b))
     across = move(ahead, "x", (1, -1))
-    partial = early_call(tiles, edge_latent, recv_rows, own_rows, w_first)
+    held = pltpu.with_memory_space_constraint(edge_latent, pltpu.HBM)
+    partial = early_call(tiles, held, recv_rows, own_rows, w_first)
     rims = [side_a, side_b, strip_a, strip_b]
     pre = near_call(near_index, own_rows, rims, partial, w_first)
     across, behind, pre = lax.optimization_barrier((across, behind, pre))

time: 60.6 us -> 60.5 us (level)
  local copies, waits for them, and re-layouts: 2.72 us -> 1.13 us
  Pallas kernels: 21.5 us -> 22.8 us
    unnamed x25 -> x23, local copies, waits for them, and re-layouts: 2.69 us -> 1.1 us
    pallas_call x1, Pallas kernels: 4.04 us -> 5.3 us  [early_call(): pl.pallas_call(early_kernel, name='early', grid_spec=pltpu.PrefetchScalar...]
  transfers between devices with their start and end apart: 12 -> 12, of which waited for: 4 -> 4; matrix products, arithmetic and copies ran while one was open for 7% -> 7% of each run, Pallas kernels for 16% -> 19%
where the time goes in v13:
time: 60.5 us; the launch traced here: 60.1 us
  starting transfers between devices  25.1 us (41%)
  Pallas kernels  22.8 us (38%)
  waiting for transfers between devices  5.67 us (9%)
  other arithmetic  4.29 us (7%)
  local copies, waits for them, and re-layouts  1.13 us (2%)
  between operations  1.08 us (2%)
    pallas_call x1, Pallas kernels, late_call(): pl.pallas_call(late_kernel, name='late', in_specs=[scalars] * 4 + [anywhe...  10.1 us
    all_to_all x1, starting transfers between devices, per_device(): lax.all_to_all(copies, 'lon', split_axis=0, concat_axis=0, tiled=True)  8.61 us
    pallas_call x1, Pallas kernels, near_call(): pl.pallas_call(near_kernel, name='near', grid_spec=pltpu.PrefetchScalarGr...  5.87 us
    pallas_call x1, Pallas kernels, early_call(): pl.pallas_call(early_kernel, name='early', grid_spec=pltpu.PrefetchScalar...  5.3 us
    ppermute x3, starting transfers between devices, move(): return lax.ppermute(value, ('lat', 'lon'), shift(axis, by_core))  5.16 us
    ppermute x1, starting transfers between devices, per_device(): side_b = lax.ppermute(col_b, 'lon', pairs(1, lon_count, True))  3.9 us
    ppermute x1, starting transfers between devices, per_device(): lax.ppermute(wide(patch_rows - 1 - edge_row, row_b), 'lat', pairs(1, lat_...  3.02 us
    ppermute x1, waiting for transfers between devices, per_device(): lax.ppermute(wide(patch_rows - 1 - edge_row, row_b), 'lat', pairs(1, lat_...  2.51 us
  transfers between devices with their start and end apart: 12, of which 4 were waited for; matrix products, arithmetic and copies ran while one was open for 7% of the time, Pallas kernels for 19%

profile of v13, /device:TPU:1, one launch (start us, length us, event | category | flops | bytes accessed | tf_op | source)
XLA Modules:
  0.0 60.1 jit_solution(5588119460867697447)
XLA Ops:
  0.6 0.0 copy-start.2
  0.6 0.0 copy-start.10
  0.7 0.1 pad_add_fusion.odd
  0.7 0.0 copy-start
  0.8 1.0 %copy-done = bf16[16,32,512]{2,1,0:T(8,128)(2,1)S(1)} copy-done((bf16[16,32,512]{2,1,0:T(8,128)(2,1)S(1)}, bf16[16,32,512]{2,1,0:T(8,128)(2,1)}, u32[]{:S(2)}) %copy-start) | copy-done | bytes 524312
  1.8 0.0 copy-start.1
  1.8 0.0 copy-start.4
  1.8 1.6 %coarse.1 = (bf16[16,32,4,128]{3,2,1,0:T(4,128)(2,1)}, bf16[16,4,128]{2,1,0:T(4,128)(2,1)S(1)}, bf16[16,4,128]{2,1,0:T(4,128)(2,1)S(1)}, bf16[32,4,128]{2,1,0:T(4,128)(2,1)S(1)}, bf16[32,4,128]{2,1,0:T(4,128)(2,1)S(1)}) custom-call(s32[2]{0:T(128)S(1)} %pad_add_fusion.odd, bf16[512,512]{1,0:T(8,128)(2,1)S(1)} %bitcast.18), custom_call_target="tpu_custom_call" | custom-call | tf_op jit(solution)/shard_map/coarse/pallas_call | solution.py:416
  3.4 8.6 %all-to-all-start = ((bf16[16,32,4,128]{3,2,1,0:T(4,128)(2,1)}), bf16[16,32,4,128]{3,2,1,0:T(4,128)(2,1)S(1)}, u32[]{:S(2)}, u32[]{:S(2)}) async-start(bf16[16,32,4,128]{3,2,1,0:T(4,128)(2,1)} %get-tuple-element.28), calls=%async_computation | async-start | bytes 1048576 | tf_op jit(solution)/shard_map/all_to_all | solution.py:460
  12.0 1.4 %collective-permute-start = (bf16[16,4,128]{2,1,0:T(4,128)(2,1)S(1)}, bf16[16,4,128]{2,1,0:T(4,128)(2,1)S(1)}, u32[]{:S(2)}, u32[]{:S(2)}) collective-permute-start(bf16[16,4,128]{2,1,0:T(4,128)(2,1)S(1)} %get-tuple-element.29), channel_id=1, source_target_pairs={{0,1},{2,3},{4,5},{6,7},{8,9},{10,11},{12,13},{14,15},{1,0},{3,2},... | collective-permute-start | bytes 49160 | tf_op jit(solution)/shard_map/ppermute | solution.py:458
  13.3 3.9 %collective-permute-start.1 = (bf16[16,4,128]{2,1,0:T(4,128)(2,1)S(1)}, bf16[16,4,128]{2,1,0:T(4,128)(2,1)S(1)}, u32[]{:S(2)}, u32[]{:S(2)}) collective-permute-start(bf16[16,4,128]{2,1,0:T(4,128)(2,1)S(1)} %get-tuple-element.30), channel_id=1, source_target_pairs={{1,2},{3,4},{5,6},{7,8},{9,10},{11,12},{13,14},{15,0},{2,1},{4,3},... | collective-permute-start | bytes 49160 | tf_op jit(solution)/shard_map/ppermute | solution.py:459
  17.3 0.1 iota_compare_fusion.1
  17.3 0.8 %bitcast_reduce_fusion = (s32[16]{0:T(128)S(1)}, pred[2048]{0:T(1024)(128)(4,1)S(1)}) fusion(s32[2048]{0:T(1024)} %param.14), kind=kLoop, calls=%fused_computation.53 | loop fusion | flops 6128 | bytes 10304 | tf_op jit(solution)/shard_map/reduce_sum | solution.py:456
  18.2 0.7 %not_and_fusion = (pred[2048]{0:T(1024)(128)(4,1)S(1)}, pred[2048]{0:T(1024)(128)(4,1)S(1)}) fusion(pred[2048]{0:T(1024)(128)(4,1)S(1)} %get-tuple-element.55, s32[]{:T(128)S(6)} %mul.44, s32[]{:T(128)S(6)} %mul.43, s32[2048]{0:T(1024)} %param.13), kind=kLoop, calls=%fused_computation.70 | loop fusion | flops 71680 | bytes 14344 | tf_op jit(solution)/shard_map/and | solution.py:454
  18.9 0.8 %fusion.9 = (s32[2048]{0:T(1024)S(1)}, s32[2048]{0:T(1024)S(1)}) fusion(s32[2048]{0:T(1024)} %param.13, s32[]{:T(128)S(6)} %select_n.137, s32[]{:T(128)} %select_n.122, pred[2048]{0:T(1024)(128)(4,1)S(1)} %get-tuple-element.57, s32[]{:T(128)} %select_n.123, s32[]{:T(128)S(6)} %sub.72, s32[]{:T(128)S(6)} %sub.71, s32[]{:T(128)S(6)} %mul.44, s32[]{:T(128)S(6)} %mul.43), kind=kLoop, calls=%fused_computation.48 | loop fusion | flops 342016 | bytes 26652 | tf_op jit(solution)/shard_map/sub | solution.py:262
  19.7 0.6 %select_reduce_fusion.1 = s32[4,512]{1,0:T(4,128)S(1)} fusion(s32[4,512]{1,0:T(4,128)S(1)} %convert_element_type.8, pred[512,512]{1,0:T(8,128)(4,1)S(1)} %iota_compare_fusion.1), kind=kLoop, calls=%fused_computation.2 | loop fusion | flops 2095104 | bytes 278528 | tf_op jit(solution)/shard_map/reduce_sum | solution.py:261
  20.3 1.0 %select_reduce_fusion = s32[4,512]{1,0:T(4,128)S(1)} fusion(s32[4,512]{1,0:T(4,128)S(1)} %broadcast_in_dim.73, s32[4,512]{1,0:T(4,128)S(1)} %select_reduce_fusion.1, pred[4,512]{1,0:T(4,128)(4,1)S(1)} %reshape.60), kind=kLoop, calls=%fused_computation | loop fusion | flops 4192256 | bytes 26624 | tf_op jit(solution)/shard_map/reduce_sum | solution.py:264
  21.3 0.1 convert_reduce_fusion.far_count
  21.5 0.0 collective-permute-done.refs_0_
  21.5 1.0 %collective-permute-done.1.refs_1_ = bf16[16,4,128]{2,1,0:T(4,128)(2,1)S(1)} collective-permute-done((bf16[16,4,128]{2,1,0:T(4,128)(2,1)S(1)}, bf16[16,4,128]{2,1,0:T(4,128)(2,1)S(1)}, u32[]{:S(2)}, u32[]{:S(2)}) %collective-permute-start.1) | collective-permute-done | bytes 16416 | tf_op jit(solution)/shard_map/ppermute | solution.py:459
  22.5 0.0 all-to-all-done
  22.5 2.5 %collective-permute-start.2 = (bf16[512,4,128]{2,1,0:T(4,128)(2,1)S(1)}, bf16[512,4,128]{2,1,0:T(4,128)(2,1)S(1)}, u32[]{:S(2)}, u32[]{:S(2)}) collective-permute-start(bf16[512,4,128]{2,1,0:T(4,128)(2,1)S(1)} %bitcast.22), channel_id=1, source_target_pairs={{0,32},{1,33},{2,34},{3,35},{4,36},{5,37},{6,38},{7,39},{8,40},{9,... | collective-permute-start | bytes 1572872 | tf_op jit(solution)/shard_map/ppermute | solution.py:47
  25.0 1.2 %collective-permute-start.3 = (bf16[34,4,128]{2,1,0:T(4,128)(2,1)S(1)}, bf16[34,4,128]{2,1,0:T(4,128)(2,1)S(1)}, u32[]{:S(2)}, u32[]{:S(2)}) collective-permute-start(bf16[34,4,128]{2,1,0:T(4,128)(2,1)S(1)} %pad_maximum_fusion), channel_id=1, source_target_pairs={{0,16},{32,48},{64,80},{96,112},{16,0},{48,32},{80,64},{112,96},{1... | collective-permute-start | bytes 104456 | tf_op jit(solution)/shard_map/ppermute | solution.py:473
  26.2 3.0 %collective-permute-start.4 = (bf16[34,4,128]{2,1,0:T(4,128)(2,1)S(1)}, bf16[34,4,128]{2,1,0:T(4,128)(2,1)S(1)}, u32[]{:S(2)}, u32[]{:S(2)}) collective-permute-start(bf16[34,4,128]{2,1,0:T(4,128)(2,1)S(1)} %pad_maximum_fusion.1), channel_id=1, source_target_pairs={{16,32},{48,64},{80,96},{32,16},{64,48},{96,80},{17,33},{49,65},{8... | collective-permute-start | bytes 104456 | tf_op jit(solution)/shard_map/ppermute | solution.py:474
  29.2 0.0 collective-permute-done.3.refs_2_
  29.2 2.5 %collective-permute-done.4.refs_3_ = bf16[34,4,128]{2,1,0:T(4,128)(2,1)S(1)} collective-permute-done((bf16[34,4,128]{2,1,0:T(4,128)(2,1)S(1)}, bf16[34,4,128]{2,1,0:T(4,128)(2,1)S(1)}, u32[]{:S(2)}, u32[]{:S(2)}) %collective-permute-start.4) | collective-permute-done | bytes 34848 | tf_op jit(solution)/shard_map/ppermute | solution.py:474
  31.8 1.2 %collective-permute-start.6 = (bf16[512,4,128]{2,1,0:T(4,128)(2,1)S(1)}, bf16[512,4,128]{2,1,0:T(4,128)(2,1)S(1)}, u32[]{:S(2)}, u32[]{:S(2)}) collective-permute-start(bf16[512,4,128]{2,1,0:T(4,128)(2,1)S(1)} %bitcast.23), channel_id=1, source_target_pairs={{0,96},{1,97},{2,98},{3,99},{4,100},{5,101},{6,102},{7,103},{8,104... | collective-permute-start | bytes 1572872 | tf_op jit(solution)/shard_map/ppermute | solution.py:47
  33.0 0.0 collective-permute-done.2.refs_1_
  33.0 1.5 %collective-permute-start.5 = (bf16[512,4,128]{2,1,0:T(4,128)(2,1)S(1)}, bf16[512,4,128]{2,1,0:T(4,128)(2,1)S(1)}, u32[]{:S(2)}, u32[]{:S(2)}) collective-permute-start(bf16[512,4,128]{2,1,0:T(4,128)(2,1)S(1)} %collective-permute-done.2.refs_1_), channel_id=1, source_target_pairs={{0,32},{1,33},{2,34},{3,35},{4,36},{5,37},{6,38},{7,39},{8,40},{9,... | collective-permute-start | bytes 1572872 | tf_op jit(solution)/shard_map/ppermute | solution.py:47
  34.4 1.2 %collective-permute-start.7 = (bf16[512,4,128]{2,1,0:T(4,128)(2,1)S(1)}, bf16[512,4,128]{2,1,0:T(4,128)(2,1)S(1)}, u32[]{:S(2)}, u32[]{:S(2)}) collective-permute-start(bf16[512,4,128]{2,1,0:T(4,128)(2,1)S(1)} %bitcast.24), channel_id=1, source_target_pairs={{0,16},{1,17},{2,18},{3,19},{4,20},{5,21},{6,22},{7,23},{8,24},{9,... | collective-permute-start | bytes 1572872 | tf_op jit(solution)/shard_map/ppermute | solution.py:43
  35.6 0.0 collective-permute-start.8
  35.6 0.0 copy-done.2
  35.6 0.0 copy-done.10
  35.6 0.0 copy-done.1
  35.6 0.0 copy-done.4
  35.6 5.3 %early.1.refs_4_ = bf16[2048,512]{1,0:T(8,128)(2,1)S(1)} custom-call(s32[16]{0:T(128)S(1)} %copy-done.10, bf16[2048,512]{1,0:T(8,128)(2,1)} %refs_9_.1, s32[4,4,128]{2,1,0:T(4,128)S(1)} %bitcast.28, bf16[512,512]{1,0:T(8,128)(2,1)S(1)} %bitcast.19, bf16[1536,512]{1,0:T(8,128)(2,1)S(1)} %copy-done.4, bf16[1536,512]{1,0:T(8,128)(2,1)S(1)} %copy-done.4), custom_call_target="tpu_custom_call" | custom-call | flops 3000000000 | bytes 10000000 | tf_op jit(solution)/shard_map/early/pallas_call | solution.py:279
  40.9 0.0 copy-start.3
  40.9 0.0 copy-start.5
  41.0 0.0 copy-start.6
  41.0 0.0 copy-start.7
  41.0 0.0 copy-start.8
  41.0 0.0 copy-start.9
  41.0 5.9 %near.1.refs_8_ = bf16[2048,512]{1,0:T(8,128)(2,1)S(1)} custom-call(s32[2048]{0:T(1024)S(1)} %get-tuple-element.45.near_index, bf16[512,512]{1,0:T(8,128)(2,1)S(1)} %bitcast.20, bf16[16,4,128]{2,1,0:T(4,128)(2,1)S(1)} %collective-permute-done.refs_0_, bf16[16,4,128]{2,1,0:T(4,128)(2,1)S(1)} %collective-permute-done.1.refs_1_, ...), custom_call_target="tpu_custom_call" | custom-call | flops 2000000000 | bytes 8000000 | tf_op jit(solution)/shard_map/near/pallas_call | solution.py:301
  46.9 0.0 collective-permute-done.6.refs_2_
  46.9 0.0 collective-permute-done.5.refs_3_
  46.9 0.6 collective-permute-start.9
  47.5 0.1 collective-permute-start.10
  47.6 0.0 collective-permute-done.7.refs_4_
  47.6 0.0 collective-permute-done.8.refs_5_
  47.6 1.4 %collective-permute-done.9.refs_6_ = bf16[512,4,128]{2,1,0:T(4,128)(2,1)S(1)} collective-permute-done((bf16[512,4,128]{2,1,0:T(4,128)(2,1)S(1)}, bf16[512,4,128]{2,1,0:T(4,128)(2,1)S(1)}, u32[]{:S(2)}, u32[]{:S(2)}) %collective-permute-start.9) | collective-permute-done | bytes 524320 | tf_op jit(solution)/shard_map/ppermute | solution.py:43
  49.0 0.7 %collective-permute-done.10.refs_7_ = bf16[512,4,128]{2,1,0:T(4,128)(2,1)S(1)} collective-permute-done((bf16[512,4,128]{2,1,0:T(4,128)(2,1)S(1)}, bf16[512,4,128]{2,1,0:T(4,128)(2,1)S(1)}, u32[]{:S(2)}, u32[]{:S(2)}) %collective-permute-start.10) | collective-permute-done | bytes 524320 | tf_op jit(solution)/shard_map/ppermute | solution.py:43
  49.8 0.0 copy-done.3
  49.8 0.0 copy-done.5
  49.8 0.0 copy-done.6
  49.8 0.0 copy-done.7
  49.8 0.0 copy-done.8
  49.8 0.0 copy-done.9
  49.8 10.1 %late.1 = (bf16[2048,512]{1,0:T(8,128)(2,1)}, bf16[512,512]{1,0:T(8,128)(2,1)}) custom-call(s32[2048]{0:T(1024)S(1)} %bitcast.30, s32[4]{0:T(128)S(1)} %convert_reduce_fusion.far_count, s32[16]{0:T(128)S(1)} %copy-done.10, s32[16]{0:T(128)S(1)} %get-tuple-element.33.lives, bf16[512,4,128]{2,1,0:T(4,128)(2,1)S(1)} %bitcast.25, ...), custom_call_target="tpu_custom_call" | custom-call | flops 4000000000 | bytes 14000000 | tf_op jit(solution)/shard_map/late/pallas_call | solution.py:345
  (9 shorter events, 0.1 us)
Async XLA Ops:
  0.6 35.0 %copy-start.2 = (s32[2048]{0:T(1024)S(1)}, s32[2048]{0:T(1024)}, u32[]{:S(2)}) copy-start(s32[2048]{0:T(1024)} %param.14) | copy-start | bytes 24580
  0.6 35.0 %copy-start.10 = (s32[16]{0:T(128)S(1)}, s32[16]{0:T(128)}, u32[]{:S(2)}) copy-start(s32[16]{0:T(128)} %tiles.2) | copy-start | bytes 196
  0.7 1.0 %copy-start = (bf16[16,32,512]{2,1,0:T(8,128)(2,1)S(1)}, bf16[16,32,512]{2,1,0:T(8,128)(2,1)}, u32[]{:S(2)}) copy-start(bf16[16,32,512]{2,1,0:T(8,128)(2,1)} %param.11) | copy-start | bytes 1572868
  1.8 33.8 %copy-start.1 = (bf16[16,32,512]{2,1,0:T(8,128)(2,1)S(1)}, bf16[16,32,512]{2,1,0:T(8,128)(2,1)}, u32[]{:S(2)}) copy-start(bf16[16,32,512]{2,1,0:T(8,128)(2,1)} %param.11) | copy-start | bytes 1572868
  1.8 33.8 %copy-start.4 = (bf16[1536,512]{1,0:T(8,128)(2,1)S(1)}, bf16[1536,512]{1,0:T(8,128)(2,1)}, u32[]{:S(2)}) copy-start(bf16[1536,512]{1,0:T(8,128)(2,1)} %refs_11_.1) | copy-start | bytes 4718596
  3.4 19.1 %all-to-all-start = ((bf16[16,32,4,128]{3,2,1,0:T(4,128)(2,1)}), bf16[16,32,4,128]{3,2,1,0:T(4,128)(2,1)S(1)}, u32[]{:S(2)}, u32[]{:S(2)}) async-start(bf16[16,32,4,128]{3,2,1,0:T(4,128)(2,1)} %get-tuple-element.28), calls=%async_computation | async-start | bytes 1048576 | tf_op jit(solution)/shard_map/all_to_all | solution.py:460
  12.0 9.5 %collective-permute-start = (bf16[16,4,128]{2,1,0:T(4,128)(2,1)S(1)}, bf16[16,4,128]{2,1,0:T(4,128)(2,1)S(1)}, u32[]{:S(2)}, u32[]{:S(2)}) collective-permute-start(bf16[16,4,128]{2,1,0:T(4,128)(2,1)S(1)} %get-tuple-element.29), channel_id=1, source_target_pairs={{0,1},{2,3},{4,5},{6,7},{8,9},{10,11},{12,13},{14,15},{1,0},{3,2},... | collective-permute-start | bytes 49160 | tf_op jit(solution)/shard_map/ppermute | solution.py:458
  13.3 9.1 %collective-permute-start.1 = (bf16[16,4,128]{2,1,0:T(4,128)(2,1)S(1)}, bf16[16,4,128]{2,1,0:T(4,128)(2,1)S(1)}, u32[]{:S(2)}, u32[]{:S(2)}) collective-permute-start(bf16[16,4,128]{2,1,0:T(4,128)(2,1)S(1)} %get-tuple-element.30), channel_id=1, source_target_pairs={{1,2},{3,4},{5,6},{7,8},{9,10},{11,12},{13,14},{15,0},{2,1},{4,3},... | collective-permute-start | bytes 49160 | tf_op jit(solution)/shard_map/ppermute | solution.py:459
  22.5 10.5 %collective-permute-start.2 = (bf16[512,4,128]{2,1,0:T(4,128)(2,1)S(1)}, bf16[512,4,128]{2,1,0:T(4,128)(2,1)S(1)}, u32[]{:S(2)}, u32[]{:S(2)}) collective-permute-start(bf16[512,4,128]{2,1,0:T(4,128)(2,1)S(1)} %bitcast.22), channel_id=1, source_target_pairs={{0,32},{1,33},{2,34},{3,35},{4,36},{5,37},{6,38},{7,39},{8,40},{9,... | collective-permute-start | bytes 1572872 | tf_op jit(solution)/shard_map/ppermute | solution.py:47
  25.0 4.2 %collective-permute-start.3 = (bf16[34,4,128]{2,1,0:T(4,128)(2,1)S(1)}, bf16[34,4,128]{2,1,0:T(4,128)(2,1)S(1)}, u32[]{:S(2)}, u32[]{:S(2)}) collective-permute-start(bf16[34,4,128]{2,1,0:T(4,128)(2,1)S(1)} %pad_maximum_fusion), channel_id=1, source_target_pairs={{0,16},{32,48},{64,80},{96,112},{16,0},{48,32},{80,64},{112,96},{1... | collective-permute-start | bytes 104456 | tf_op jit(solution)/shard_map/ppermute | solution.py:473
  26.2 5.5 %collective-permute-start.4 = (bf16[34,4,128]{2,1,0:T(4,128)(2,1)S(1)}, bf16[34,4,128]{2,1,0:T(4,128)(2,1)S(1)}, u32[]{:S(2)}, u32[]{:S(2)}) collective-permute-start(bf16[34,4,128]{2,1,0:T(4,128)(2,1)S(1)} %pad_maximum_fusion.1), channel_id=1, source_target_pairs={{16,32},{48,64},{80,96},{32,16},{64,48},{96,80},{17,33},{49,65},{8... | collective-permute-start | bytes 104456 | tf_op jit(solution)/shard_map/ppermute | solution.py:474
  31.8 15.1 %collective-permute-start.6 = (bf16[512,4,128]{2,1,0:T(4,128)(2,1)S(1)}, bf16[512,4,128]{2,1,0:T(4,128)(2,1)S(1)}, u32[]{:S(2)}, u32[]{:S(2)}) collective-permute-start(bf16[512,4,128]{2,1,0:T(4,128)(2,1)S(1)} %bitcast.23), channel_id=1, source_target_pairs={{0,96},{1,97},{2,98},{3,99},{4,100},{5,101},{6,102},{7,103},{8,104... | collective-permute-start | bytes 1572872 | tf_op jit(solution)/shard_map/ppermute | solution.py:47
  33.0 13.9 %collective-permute-start.5 = (bf16[512,4,128]{2,1,0:T(4,128)(2,1)S(1)}, bf16[512,4,128]{2,1,0:T(4,128)(2,1)S(1)}, u32[]{:S(2)}, u32[]{:S(2)}) collective-permute-start(bf16[512,4,128]{2,1,0:T(4,128)(2,1)S(1)} %collective-permute-done.2.refs_1_), channel_id=1, source_target_pairs={{0,32},{1,33},{2,34},{3,35},{4,36},{5,37},{6,38},{7,39},{8,40},{9,... | collective-permute-start | bytes 1572872 | tf_op jit(solution)/shard_map/ppermute | solution.py:47
  34.4 13.1 %collective-permute-start.7 = (bf16[512,4,128]{2,1,0:T(4,128)(2,1)S(1)}, bf16[512,4,128]{2,1,0:T(4,128)(2,1)S(1)}, u32[]{:S(2)}, u32[]{:S(2)}) collective-permute-start(bf16[512,4,128]{2,1,0:T(4,128)(2,1)S(1)} %bitcast.24), channel_id=1, source_target_pairs={{0,16},{1,17},{2,18},{3,19},{4,20},{5,21},{6,22},{7,23},{8,24},{9,... | collective-permute-start | bytes 1572872 | tf_op jit(solution)/shard_map/ppermute | solution.py:43
  35.6 12.0 %collective-permute-start.8 = (bf16[512,4,128]{2,1,0:T(4,128)(2,1)S(1)}, bf16[512,4,128]{2,1,0:T(4,128)(2,1)S(1)}, u32[]{:S(2)}, u32[]{:S(2)}) collective-permute-start(bf16[512,4,128]{2,1,0:T(4,128)(2,1)S(1)} %collective-permute-done.2.refs_1_), channel_id=1, source_target_pairs={{0,16},{1,17},{2,18},{3,19},{4,20},{5,21},{6,22},{7,23},{8,24},{9,... | collective-permute-start | bytes 1572872 | tf_op jit(solution)/shard_map/ppermute | solution.py:43
  40.9 8.8 %copy-start.3 = (bf16[2048,512]{1,0:T(8,128)(2,1)S(1)}, bf16[2048,512]{1,0:T(8,128)(2,1)}, u32[]{:S(2)}) copy-start(bf16[2048,512]{1,0:T(8,128)(2,1)} %refs_9_.1) | copy-start | bytes 6291460
  40.9 8.8 %copy-start.5 = (bf16[1024,512]{1,0:T(8,128)(2,1)S(1)}, bf16[1024,512]{1,0:T(8,128)(2,1)}, u32[]{:S(2)}) copy-start(bf16[1024,512]{1,0:T(8,128)(2,1)} %refs_13_.1) | copy-start | bytes 3145732
  41.0 8.8 %copy-start.6 = (bf16[512,512]{1,0:T(8,128)(2,1)S(1)}, bf16[512,512]{1,0:T(8,128)(2,1)}, u32[]{:S(2)}) copy-start(bf16[512,512]{1,0:T(8,128)(2,1)} %refs_12_.1) | copy-start | bytes 1572868
  41.0 8.8 %copy-start.7 = (bf16[512,512]{1,0:T(8,128)(2,1)S(1)}, bf16[512,512]{1,0:T(8,128)(2,1)}, u32[]{:S(2)}) copy-start(bf16[512,512]{1,0:T(8,128)(2,1)} %refs_14_.1) | copy-start | bytes 1572868
  41.0 8.8 %copy-start.8 = (f32[512]{0:T(512)S(1)}, f32[512]{0:T(512)}, u32[]{:S(2)}) copy-start(f32[512]{0:T(512)} %param.18) | copy-start | bytes 6148
  41.0 8.8 %copy-start.9 = (f32[512]{0:T(512)S(1)}, f32[512]{0:T(512)}, u32[]{:S(2)}) copy-start(f32[512]{0:T(512)} %param.21) | copy-start | bytes 6148
  46.9 2.1 %collective-permute-start.9 = (bf16[512,4,128]{2,1,0:T(4,128)(2,1)S(1)}, bf16[512,4,128]{2,1,0:T(4,128)(2,1)S(1)}, u32[]{:S(2)}, u32[]{:S(2)}) collective-permute-start(bf16[512,4,128]{2,1,0:T(4,128)(2,1)S(1)} %collective-permute-done.6.refs_2_), channel_id=1, source_target_pairs={{0,16},{1,17},{2,18},{3,19},{4,20},{5,21},{6,22},{7,23},{8,24},{9,... | collective-permute-start | bytes 1572872 | tf_op jit(solution)/shard_map/ppermute | solution.py:43
  47.5 2.3 %collective-permute-start.10 = (bf16[512,4,128]{2,1,0:T(4,128)(2,1)S(1)}, bf16[512,4,128]{2,1,0:T(4,128)(2,1)S(1)}, u32[]{:S(2)}, u32[]{:S(2)}) collective-permute-start(bf16[512,4,128]{2,1,0:T(4,128)(2,1)S(1)} %collective-permute-done.5.refs_3_), channel_id=1, source_target_pairs={{0,16},{1,17},{2,18},{3,19},{4,20},{5,21},{6,22},{7,23},{8,24},{9,... | collective-permute-start | bytes 1572872 | tf_op jit(solution)/shard_map/ppermute | solution.py:43
